TPU v7x, 256 devices: a whole 4x4x8 slice. The times are simulated.
256 devices in a mesh: replica: 4 (over z_lo), shard: 64 (over y, z_hi, x, core).
Axes of the slice: x: 4, y: 4, z: 8 (z_hi: 2, z_lo: 4; z = z_hi * 4 + z_lo), core: 2. Of those that a mesh axis runs over, the one named last changes fastest.
Arguments:
- activations: bfloat16 [32768, 512], P(('replica', 'shard')), may hold values from -6 to 6
- cotangents: bfloat16 [32768, 8192], P(('replica', 'shard')), may hold values from -0.005859375 to 0.005859375
- statistics: float32 [2, 8192, 512], P(None, 'shard'), may hold values from -8 to 32, as said below
- roots: bfloat16 [2, 8192, 512], P(None, 'shard'), may hold values from -0.25 to 0.25
- ages: int32 [32], replicated, may hold values from 1 to 16
- refresh: int32 [32], replicated, may hold values 0 or 1
Outputs:
- update: bfloat16 [8192, 512], P('shard')
- new_statistics: float32 [2, 8192, 512], P(None, 'shard')
- new_roots: bfloat16 [2, 8192, 512], P(None, 'shard')
Inputs may be any that keep to these rules, and one draw needn't show every extreme that they name: `statistics`: for each block k, rows k * 512 to (k + 1) * 512 - 1 of either layer hold a symmetric positive definite 512 x 512 matrix.
All inputs are finite; a program needn't handle non-finite values.
Results may differ from a plain program's by a relative error of at most 0.0064.
Values may be sent and summed in bfloat16 or wider, within the bound.
No kernel may reach another device: no remote copies, remote signals or barrier semaphores. Data moves between devices by JAX's collectives and lax.ppermute only.
A program may use at most 128 MiB of HBM per device.

v0:
```python
import math

import jax
import jax.numpy as jnp
from jax import lax
from jax.sharding import Mesh
from jax.sharding import PartitionSpec as P

ITERS = 3
SHARD = ("shard_0", "shard_1", "shard_2", "shard_3")
REPLICA_SHARD = ("replica", "shard_0", "shard_1", "shard_2", "shard_3")


decay_base = 0.9
tiny_term = 1e-06


def from_partner(x, axis, apart):
    return lax.ppermute(x, axis, [(i, i ^ 1 << apart) for i in range(lax.axis_size(axis))])


def split_up(x, dim, size):
    before, after = (x.shape[:dim], x.shape[dim + 1 :])
    return jnp.moveaxis(x.reshape(*before, size, -1, *after), dim, 0)


def scatter_pairs(x, chips, core, dim):
    sizes = (lax.axis_size(chips), lax.axis_size(core))
    pieces = split_up(x, dim, sizes[0] * sizes[1])
    inside = pieces.shape[1:]
    pieces = pieces.reshape(*sizes, *inside).swapaxes(0, 1).reshape(-1, *inside)
    pieces = lax.psum_scatter(pieces, core, scatter_dimension=0, tiled=True)
    return lax.psum_scatter(pieces, chips, scatter_dimension=0, tiled=True)[0]


def copy_for_each(x, axis):
    copies = jnp.broadcast_to(x, (lax.axis_size(axis), *x.shape))
    return lax.all_to_all(copies, axis, split_axis=0, concat_axis=0, tiled=True)


def over_copies(x, axis):
    everything = copy_for_each(x, axis)
    return jnp.sum(everything, axis=0)


def newton(matrix):
    identity = jnp.eye(matrix.shape[-1], dtype=jnp.float32)
    frobenius = jnp.sqrt(jnp.sum(matrix * matrix) + tiny_term)
    scaling = 2.5 / frobenius
    iterate = scaling**0.25 * identity
    residual_map = scaling * matrix
    for sweep_index in range(ITERS):
        factor = (5.0 * identity - residual_map) * 0.25
        iterate = jnp.matmul(iterate, factor, precision=lax.Precision.HIGHEST)
        square = jnp.matmul(factor, factor, precision=lax.Precision.HIGHEST)
        fourth = jnp.matmul(square, square, precision=lax.Precision.HIGHEST)
        residual_map = jnp.matmul(fourth, residual_map, precision=lax.Precision.HIGHEST)
    return iterate


def gram_pair(blocks):
    left_gram = jnp.einsum("nij,nkj->nik", blocks, blocks, preferred_element_type=jnp.float32)
    right_gram = jnp.einsum("nji,njk->nik", blocks, blocks, preferred_element_type=jnp.float32)
    return jnp.stack([left_gram, right_gram], axis=1)


def stat_swap(values, bit_number):
    return from_partner(values, SHARD, bit_number)


def block_swap(values, bit_number):
    return from_partner(values, SHARD, bit_number)


def team_block(values, mover, team_size):
    shard_index = lax.axis_index(SHARD)
    gathered = values
    for bit_number in range(team_size.bit_length() - 1):
        partner = mover(gathered, bit_number)
        upper_side = jnp.right_shift(shard_index, bit_number) % 2 == 1
        below = jnp.concatenate([partner, gathered], axis=1)
        above = jnp.concatenate([gathered, partner], axis=1)
        gathered = jnp.where(upper_side, below, above)
    return gathered


def per_device(activations, cotangents, statistics, roots, ages, refresh):
    block_order = activations.shape[1]
    rows_here = statistics.shape[1]
    group_total = scatter_pairs(
        lax.dot_general(
            cotangents, activations, (((0,), (0,)), ((), ())), preferred_element_type=jnp.float32
        ),
        ("shard_0", "shard_1", "shard_2"),
        "shard_3",
        0,
    )
    gradient = over_copies(group_total, "replica").astype(jnp.bfloat16)
    shard_index = lax.axis_index(SHARD)
    team_size = block_order // rows_here
    team_place = shard_index % team_size
    first_block = shard_index // team_size
    row_start = team_place * rows_here
    blocks_here = 1
    old_stats = team_block(statistics, stat_swap, team_size)[:, None]
    full_pair = team_block(jnp.stack([gradient, roots[1]]), block_swap, team_size)
    grad_blocks = full_pair[0][None]
    right_old = full_pair[1][None]

    def own_rows(blocks):
        return lax.dynamic_slice_in_dim(blocks[0], row_start, rows_here, 0)

    count_here = 2 * blocks_here
    gram_pairs = gram_pair(grad_blocks).reshape(count_here, block_order, block_order)
    previous = old_stats.transpose(1, 0, 2, 3).reshape(count_here, block_order, block_order)
    ages_here = lax.dynamic_slice_in_dim(ages, 2 * first_block, count_here, 0)
    fresh_here = lax.dynamic_slice_in_dim(refresh, 2 * first_block, count_here, 0) == 1
    decay_factor = (decay_base ** ages_here.astype(jnp.float32))[:, None, None]
    updated = jnp.where(
        fresh_here[:, None, None],
        decay_factor * previous + (1.0 - decay_factor) * gram_pairs,
        previous,
    )
    refreshed = jax.vmap(newton)(updated).astype(jnp.bfloat16)
    root_pairs = refreshed.reshape(blocks_here, 2, block_order, block_order)
    fresh_pairs = fresh_here.reshape(blocks_here, 2)
    right_full = jnp.where(fresh_pairs[:, 1, None, None], root_pairs[:, 1], right_old)
    left_mask = own_rows(
        jnp.broadcast_to(fresh_pairs[:, 0, None, None], (blocks_here, block_order, 1))
    )
    left_rows = jnp.where(left_mask, own_rows(root_pairs[:, 0]), roots[0])
    new_roots = jnp.stack([left_rows, own_rows(right_full)])
    stat_pairs = updated.reshape(blocks_here, 2, block_order, block_order)
    new_statistics = jnp.stack([own_rows(stat_pairs[:, 0]), own_rows(stat_pairs[:, 1])])
    mixed_blocks = jnp.einsum(
        "nij,njk->nik", grad_blocks, right_full, preferred_element_type=jnp.float32
    ).astype(jnp.bfloat16)
    left_blocks = left_rows.reshape(blocks_here, -1, block_order)
    product = jnp.einsum(
        "nij,njk->nik", left_blocks, mixed_blocks, preferred_element_type=jnp.float32
    )
    update = (product.reshape(rows_here, block_order) * math.sqrt(block_order)).astype(jnp.bfloat16)
    return (update, new_statistics, new_roots)


def solution(mesh):
    split = Mesh(
        mesh.devices.reshape(mesh.shape["replica"], 4, 2, 4, 2),
        ("replica", "shard_0", "shard_1", "shard_2", "shard_3"),
    )
    placed = (
        P(REPLICA_SHARD, None),
        P(REPLICA_SHARD, None),
        P(None, SHARD, None),
        P(None, SHARD, None),
        P(),
        P(),
    )
    return jax.shard_map(
        per_device,
        mesh=split,
        in_specs=placed,
        out_specs=(P(SHARD, None), P(None, SHARD, None), P(None, SHARD, None)),
        check_vma=False,
    )
```

profile of v0, /device:TPU:1, one launch (start us, length us, event | category | flops | bytes accessed | tf_op | source)
XLA Modules:
  0.0 439.5 jit_solution(15200567484628147271)
XLA Ops:
  7.2 1.5 copy-done
  8.8 3.3 fusion.49
  12.0 6.3 %copy.10 = f32[32,2,128,512]{3,2,0,1:T(8,128)} copy(f32[32,2,128,512]{3,2,1,0:T(8,128)S(1)} %bitcast.61) | data formatting | bytes 33554432 | tf_op jit(solution)/shard_map/reshape;reshape | solution.py:31
  18.4 36.1 %reduce-scatter.3.cloned.1.call-done = f32[32,128,512]{2,1,0:T(8,128)} async-done(((f32[64,128,512]{2,1,0:T(8,128)}), f32[32,128,512]{2,1,0:T(8,128)}) %reduce-scatter.3.cloned.1.call-update) | async-done | bytes 8388624 | tf_op jit(solution)/shard_map/reduce_scatter | solution.py:32
  54.5 249.0 %reduce-scatter.5.cloned.1.call-done = f32[1,128,512]{2,1,0:T(8,128)} async-done(((f32[32,128,512]{2,1,0:T(8,128)}), f32[1,128,512]{2,1,0:T(8,128)}) %reduce-scatter.5.cloned.1.call-update) | async-done | bytes 262160 | tf_op jit(solution)/shard_map/reduce_scatter | solution.py:33
  303.5 2.1 broadcast_in_dim.47
  305.6 4.2 all-to-all-start
  309.7 21.4 %collective-permute-start = (f32[2,128,512]{2,1,0:T(8,128)S(1)}, f32[2,128,512]{2,1,0:T(8,128)S(1)}, u32[]{:S(2)}, u32[]{:S(2)}) collective-permute-start(f32[2,128,512]{2,1,0:T(8,128)S(1)} %copy-done.4), channel_id=1, source_target_pairs={{0,1},{1,0},{2,3},{3,2},{4,5},{5,4},{6,7},{7,6},{8,9},{9,8},{10,11... | collective-permute-start | bytes 1572872 | tf_op jit(solution)/shard_map/ppermute | solution.py:19
  331.3 16.0 %collective-permute-start.2 = (bf16[2,128,512]{2,1,0:T(8,128)(2,1)S(1)}, bf16[2,128,512]{2,1,0:T(8,128)(2,1)S(1)}, u32[]{:S(2)}, u32[]{:S(2)}) collective-permute-start(bf16[2,128,512]{2,1,0:T(8,128)(2,1)S(1)} %pad_maximum_fusion.2), channel_id=1, source_target_pairs={{0,1},{1,0},{2,3},{3,2},{4,5},{5,4},{6,7},{7,6},{8,9},{9,8},{10,11... | collective-permute-start | bytes 786440 | tf_op jit(solution)/shard_map/ppermute | solution.py:19
  348.6 1.2 collective-permute-start.3
  350.8 32.8 %collective-permute-done.3 = bf16[2,256,512]{2,1,0:T(8,128)(2,1)} collective-permute-done((bf16[2,256,512]{2,1,0:T(8,128)(2,1)S(1)}, bf16[2,256,512]{2,1,0:T(8,128)(2,1)}, u32[]{:S(2)}, u32[]{:S(2)}) %collective-permute-start.3) | collective-permute-done | bytes 524320 | tf_op jit(solution)/shard_map/ppermute | solution.py:19
  383.6 1.6 maximum_select_fusion.3
  386.2 2.6 multiply_reduce_fusion
  388.8 4.0 fusion.11
  392.8 3.5 fusion.50
  396.3 3.7 fusion.7
  400.0 4.0 fusion.9
  404.0 3.5 fusion.51
  407.5 3.6 fusion.52
  411.1 4.1 fusion.5
  415.2 3.7 fusion.10
  418.9 3.7 fusion.15
  424.9 2.3 fusion.20
  428.0 2.7 add_select_fusion
  (47 shorter events, 8.3 us)
Async XLA Ops:
  7.2 1.6 copy-start
  7.2 47.3 %reduce-scatter.3.cloned.1.call-start = ((), (), s32[]{:S(2)}) async-start(), calls=%async_computation.3 | async-start | bytes 25165824 | tf_op jit(solution)/shard_map/reduce_scatter | solution.py:32
  18.3 285.2 %reduce-scatter.5.cloned.1.call-start = ((), (), s32[]{:S(2)}) async-start(), calls=%async_computation.4 | async-start | bytes 8650752 | tf_op jit(solution)/shard_map/reduce_scatter | solution.py:33
  54.5 255.2 %copy-start.4 = (f32[2,128,512]{2,1,0:T(8,128)S(1)}, f32[2,128,512]{2,1,0:T(8,128)}, u32[]{:S(2)}) copy-start(f32[2,128,512]{2,1,0:T(8,128)} %param.8) | copy-start | bytes 1572868
  54.5 276.6 %copy-start.5 = (bf16[2,128,512]{2,1,0:T(8,128)(2,1)S(1)}, bf16[2,128,512]{2,1,0:T(8,128)(2,1)}, u32[]{:S(2)}) copy-start(bf16[2,128,512]{2,1,0:T(8,128)(2,1)} %param.9) | copy-start | bytes 786436
  305.6 41.7 %copy-start.8 = (s32[32]{0:T(128)S(1)}, s32[32]{0:T(128)}, u32[]{:S(2)}) copy-start(s32[32]{0:T(128)} %param.11) | copy-start | bytes 388
  305.6 25.6 %all-to-all-start = ((f32[4,128,512]{2,1,0:T(8,128)}), f32[4,128,512]{2,1,0:T(8,128)S(1)}, u32[]{:S(2)}, u32[]{:S(2)}) async-start(f32[4,128,512]{2,1,0:T(8,128)} %broadcast_in_dim.47), calls=%async_computation.2 | async-start | bytes 2097152 | tf_op jit(solution)/shard_map/all_to_all | solution.py:38
  309.7 37.6 %collective-permute-start = (f32[2,128,512]{2,1,0:T(8,128)S(1)}, f32[2,128,512]{2,1,0:T(8,128)S(1)}, u32[]{:S(2)}, u32[]{:S(2)}) collective-permute-start(f32[2,128,512]{2,1,0:T(8,128)S(1)} %copy-done.4), channel_id=1, source_target_pairs={{0,1},{1,0},{2,3},{3,2},{4,5},{5,4},{6,7},{7,6},{8,9},{9,8},{10,11... | collective-permute-start | bytes 1572872 | tf_op jit(solution)/shard_map/ppermute | solution.py:19
  331.3 18.6 %copy-start.7 = (s32[32]{0:T(128)S(1)}, s32[32]{0:T(128)}, u32[]{:S(2)}) copy-start(s32[32]{0:T(128)} %param.10) | copy-start | bytes 388
  331.3 17.1 %collective-permute-start.2 = (bf16[2,128,512]{2,1,0:T(8,128)(2,1)S(1)}, bf16[2,128,512]{2,1,0:T(8,128)(2,1)S(1)}, u32[]{:S(2)}, u32[]{:S(2)}) collective-permute-start(bf16[2,128,512]{2,1,0:T(8,128)(2,1)S(1)} %pad_maximum_fusion.2), channel_id=1, source_target_pairs={{0,1},{1,0},{2,3},{3,2},{4,5},{5,4},{6,7},{7,6},{8,9},{9,8},{10,11... | collective-permute-start | bytes 786440 | tf_op jit(solution)/shard_map/ppermute | solution.py:19
  347.5 38.7 %collective-permute-start.1 = (f32[2,256,512]{2,1,0:T(8,128)S(1)}, f32[2,256,512]{2,1,0:T(8,128)}, u32[]{:S(2)}, u32[]{:S(2)}) collective-permute-start(f32[2,256,512]{2,1,0:T(8,128)S(1)} %maximum_select_fusion.2), channel_id=1, source_target_pairs={{0,2},{1,3},{2,0},{3,1},{4,6},{5,7},{6,4},{7,5},{8,10},{9,11},{10,... | collective-permute-start | bytes 3145736 | tf_op jit(solution)/shard_map/ppermute | solution.py:19
  348.6 35.0 %collective-permute-start.3 = (bf16[2,256,512]{2,1,0:T(8,128)(2,1)S(1)}, bf16[2,256,512]{2,1,0:T(8,128)(2,1)}, u32[]{:S(2)}, u32[]{:S(2)}) collective-permute-start(bf16[2,256,512]{2,1,0:T(8,128)(2,1)S(1)} %maximum_select_fusion.4), channel_id=1, source_target_pairs={{0,2},{1,3},{2,0},{3,1},{4,6},{5,7},{6,4},{7,5},{8,10},{9,11},{10,... | collective-permute-start | bytes 1572872 | tf_op jit(solution)/shard_map/ppermute | solution.py:19
  386.2 2.6 copy-start.2
  422.6 1.6 copy-start.6
  423.4 0.8 copy-start.3
  430.7 1.8 copy-start.1
Sparse Core Ops, SparseCore 0:
  18.5 35.9 reduce-scatter.2
  57.2 246.2 reduce-scatter.4
where the time goes:
time: 444 us; the launch traced here: 440 us
  waiting for transfers between devices  318 us (72%)
  starting transfers between devices  43.5 us (10%)
  matrix products  40.3 us (9%)
  between operations  14.5 us (3%)
  local copies, waits for them, and re-layouts  12.3 us (3%)
  other arithmetic  10.7 us (2%)
    reduce_scatter x1, waiting for transfers between devices, scatter_pairs(): return lax.psum_scatter(pieces, chips, scatter_dimension=0, tiled=True)[0]  249 us
    ppermute x4, starting transfers between devices, from_partner(): lax.ppermute(x, axis, [(i, i ^ 1 << apart) for i in range(lax.axis_size(a...  39.2 us
    reduce_scatter x1, waiting for transfers between devices, scatter_pairs(): pieces = lax.psum_scatter(pieces, core, scatter_dimension=0, tiled=True)  36.1 us
    ppermute x4, waiting for transfers between devices, from_partner(): lax.ppermute(x, axis, [(i, i ^ 1 << apart) for i in range(lax.axis_size(a...  33.1 us
    dot_general x3, matrix products, newton(): iterate = jnp.matmul(iterate, factor, precision=lax.Precision.HIGHEST)  11.5 us
  transfers between devices with their start and end apart: 7, of which 4 were waited for; matrix products, arithmetic and copies ran while one was open for 1% of the time, Pallas kernels for 0%

commit v1 on v0

v1 whole, which is shorter than its diff:
```python
import math

import jax
import jax.numpy as jnp
from jax import lax
from jax.experimental import pallas as pl
from jax.experimental.pallas import tpu as pltpu
from jax.sharding import Mesh
from jax.sharding import PartitionSpec as P

X = ("x_hi", "x_lo")
Z = ("z_lo", "z_hi")
SHARD = ("y", "z_hi", "x_hi", "x_lo", "core")
EVERY = ("z_lo",) + SHARD

B = 512
ROWS = 128
PART = 32
SEND = jnp.bfloat16

decay_base = 0.9
tiny_term = 1e-06


def shift(x, axis, by):
    n = lax.axis_size(axis)
    return lax.ppermute(x, axis, [(i, (i + by) % n) for i in range(n)])


def shift_z(x, by):
    spot = [(i % 4) * 2 + i // 4 for i in range(8)]
    return lax.ppermute(x, Z, [(spot[i], spot[(i + by) % 8]) for i in range(8)])


def partner(x, axis, bits=1):
    n = lax.axis_size(axis)
    return lax.ppermute(x, axis, [(i, i ^ bits) for i in range(n)])


def pick(x, index):
    return lax.dynamic_index_in_dim(x, index, 0, keepdims=False)


def dot(a, b, contract=(1, 0)):
    dims = (((contract[0],), (contract[1],)), ((), ()))
    return lax.dot_general(a, b, dims, preferred_element_type=jnp.float32)


def narrow(x):
    return x.astype(jnp.bfloat16)


def finish_kernel(place, fresh, decay, pieces, stats, right_old, left_old,
                  update, new_stats, new_roots, grad, full, right, work):
    x_lo, core, z_lo = place[0], place[1], place[2]
    quarter = x_lo * 2 + core
    own = pl.ds(pl.multiple_of(quarter * ROWS, ROWS), ROWS)
    for a in range(2):
        for b in range(2):
            top = ((x_lo ^ a) * 2 + (core ^ b)) * ROWS
            here = pl.ds(pl.multiple_of(top, ROWS), ROWS)
            right[here, :] = right_old[b, a]
            for layer in range(2):
                full[layer, here, :] = stats[b, a, layer]
            for k in range(4):
                rows = pl.multiple_of(top + (z_lo ^ k) * PART, PART)
                grad[pl.ds(rows, PART), :] = pieces[b, a, k]
    g = grad[...]

    def refresh_stats(layer, gram):
        old = full[layer]
        d = decay[layer]
        a = jnp.where(fresh[layer] == 1, d * old + (1.0 - d) * gram, old)
        full[layer] = a
        new_stats[layer] = full[layer, own, :]
        total = jnp.sum(jnp.sum(a * a, axis=0, keepdims=True), axis=1, keepdims=True)
        scaling = 2.5 / jnp.sqrt(total + tiny_term)
        return scaling * a, jnp.sqrt(jnp.sqrt(scaling))

    def advance(m):
        mb = narrow(m)
        u = narrow(dot(mb, mb) * 0.0625 - 0.625 * m)
        w = dot(u, mb)
        return 2.44140625 * m + 3.125 * w + dot(u, narrow(w))

    def root_of(m, m_rows, m2, m2_rows, m3, m3_rows, row0, scale):
        y = dot(narrow(m_rows), narrow(m2)) * 0.0625 - 0.3125 * (m_rows + m2_rows)
        r = lax.broadcasted_iota(jnp.int32, m_rows.shape, 0) + row0
        c = lax.broadcasted_iota(jnp.int32, m_rows.shape, 1)
        out = jnp.where(r == c, 1.953125, 0.0) + 1.25 * y - 0.390625 * m3_rows
        out = out - 0.25 * dot(narrow(y), narrow(m3))
        return narrow(scale * out)

    m, scale = refresh_stats(1, dot(g, g, (0, 0)))
    m2 = advance(m)
    m3 = advance(m2)
    root = root_of(m, m, m2, m2, m3, m3, 0, scale)
    root = jnp.where(fresh[1] == 1, root, right[...])
    right[...] = root
    new_roots[1] = right[own, :]
    mixed = narrow(dot(g, root))

    m, scale = refresh_stats(0, dot(g, g, (1, 1)))
    work[0] = m
    m2 = advance(m)
    work[1] = m2
    m3 = advance(m2)
    work[2] = m3
    rows = root_of(m, work[0, own, :], m2, work[1, own, :], m3, work[2, own, :], quarter * ROWS, scale)
    rows = jnp.where(fresh[0] == 1, rows, left_old[...])
    new_roots[0] = rows
    update[...] = narrow(dot(rows, mixed) * math.sqrt(B))


def finish(place, fresh, decay, pieces, stats, right_old, left_old):
    smem = pl.BlockSpec(memory_space=pltpu.SMEM)
    vmem = pl.BlockSpec(memory_space=pltpu.VMEM)
    return pl.pallas_call(
        finish_kernel,
        name="finish",
        out_shape=(
            jax.ShapeDtypeStruct((ROWS, B), jnp.bfloat16),
            jax.ShapeDtypeStruct((2, ROWS, B), jnp.float32),
            jax.ShapeDtypeStruct((2, ROWS, B), jnp.bfloat16),
        ),
        in_specs=[smem] * 3 + [vmem] * 4,
        out_specs=(vmem,) * 3,
        scratch_shapes=[
            pltpu.VMEM((B, B), jnp.bfloat16),
            pltpu.VMEM((2, B, B), jnp.float32),
            pltpu.VMEM((B, B), jnp.bfloat16),
            pltpu.VMEM((3, B, B), jnp.float32),
        ],
        compiler_params=pltpu.CompilerParams(vmem_limit_bytes=40 << 20),
        cost_estimate=pl.CostEstimate(flops=18 * 2 * B**3, bytes_accessed=6 << 20, transcendentals=0),
    )(place, fresh, decay, pieces, stats, right_old, left_old)


def per_device(activations, cotangents, statistics, roots, ages, refresh):
    x, y = lax.axis_index(X), lax.axis_index("y")
    x_hi, x_lo, z_hi, z_lo = (lax.axis_index(a) for a in ("x_hi", "x_lo", "z_hi", "z_lo"))
    core = lax.axis_index("core")
    z = z_hi * 4 + z_lo

    def y_piece(t):
        columns = lax.dynamic_slice_in_dim(cotangents, t * 4 * B, 2 * B, 1)
        return jnp.concatenate([columns, activations], axis=1)

    def x_piece(t):
        columns = [
            lax.dynamic_slice_in_dim(cotangents, (4 * j + 2) * B + t * B // 2, B // 2, 1)
            for j in range(4)
        ]
        return jnp.concatenate(columns + [activations], axis=1)

    def product(pieces):
        both = jnp.concatenate(pieces, axis=0)
        return dot(both[:, : 2 * B], both[:, 2 * B :], (0, 0))

    y_parts, x_parts = [y_piece(y)], [x_piece(x)]
    for k in (2, 1, 3):
        y_parts.append(shift(y_piece((y + k) % 4), "y", k))
        x_parts.append(shift(x_piece((x + k) % 4), X, k))

    def core_sum(total):
        halves = total.reshape(4, 2, ROWS, B).swapaxes(0, 1)
        return pick(halves, core) + partner(pick(halves, 1 - core), "core")

    y_sum = core_sum(product(y_parts))
    x_sum = core_sum(product(x_parts))
    y_total, x_total = pick(y_sum, x), pick(x_sum, y)
    for k in (2, 1, 3):
        y_total += shift(pick(y_sum, (x + k) % 4).astype(SEND), X, k).astype(jnp.float32)
        x_total += shift(pick(x_sum, (y + k) % 4).astype(SEND), "y", k).astype(jnp.float32)

    plane = jnp.stack([y_total, x_total]).reshape(8, PART, B)
    plane, statistics, roots = lax.optimization_barrier((plane, statistics, roots))
    part = pick(plane, z)
    for k in (4, 3, 5, 2, 6, 1, 7):
        part += shift_z(pick(plane, (z + k) % 8).astype(SEND), k).astype(jnp.float32)
    part = narrow(part)
    pieces = jnp.stack([part] + [partner(part, "z_lo", k) for k in (1, 2, 3)])
    pieces = jnp.stack([pieces, partner(pieces, "x_lo")])
    pieces = jnp.stack([pieces, partner(pieces, "core")])

    stats = jnp.stack([statistics, partner(statistics, "x_lo")])
    stats = jnp.stack([stats, partner(stats, "core")])
    right_old = jnp.stack([roots[1], partner(roots[1], "x_lo")])
    right_old = jnp.stack([right_old, partner(right_old, "core")])

    block = y * 4 + z_hi * 2 + x_hi
    ages_here = lax.dynamic_slice_in_dim(ages, 2 * block, 2, 0)
    fresh = lax.dynamic_slice_in_dim(refresh, 2 * block, 2, 0)
    decay = decay_base ** ages_here.astype(jnp.float32)
    place = jnp.stack([x_lo, core, z_lo]).astype(jnp.int32)
    return finish(place, fresh, decay, pieces, stats, right_old, roots[0])


def solution(mesh):
    split = Mesh(mesh.devices.reshape(4, 4, 2, 2, 2, 2), EVERY)
    placed = (P(EVERY, None), P(EVERY, None), P(None, SHARD, None), P(None, SHARD, None), P(), P())
    return jax.shard_map(
        per_device,
        mesh=split,
        in_specs=placed,
        out_specs=(P(SHARD, None), P(None, SHARD, None), P(None, SHARD, None)),
        check_vma=False,
    )
```

time: 444 us -> 117 us (0.26)
  waiting for transfers between devices: 318 us -> 28.5 us
  matrix products: 40.3 us -> 3.43 us
  between operations: 14.5 us -> 1.18 us
  Pallas kernels: 0 us -> 8.43 us
  starting transfers between devices: 43.5 us -> 51.3 us
    reduce_scatter x2 -> x0, waiting for transfers between devices: 285 us -> none  [the longest x1 249 us: scatter_pairs(): return lax.psum_scatter(pieces, chips, scatter_dimension=0, tiled=True)[0]]
    dot_general x13 -> x2, matrix products: 40.3 us -> 3.43 us  [dot(): return lax.dot_general(a, b, dims, preferred_element_type=jnp.float32)]
    ppermute x4 -> x30, starting transfers between devices: 39.2 us -> 51.3 us  [the longest x12 19.8 us: shift(): return lax.ppermute(x, axis, [(i, (i + by) % n) for i in range(n)])]
    pallas_call x0 -> x1, Pallas kernels: none -> 8.43 us  [finish(): pl.pallas_call(finish_kernel, name='finish', out_shape=(jax.ShapeDtypeStr...]
    unnamed x18 -> x22, local copies, waits for them, and re-layouts: 3.08 us -> 10.3 us
    another operation x2 -> x0, local copies, waits for them, and re-layouts: 6.32 us -> none  [the longest x1 6.27 us: scatter_pairs(): pieces = pieces.reshape(*sizes, *inside).swapaxes(0, 1).reshape(-1, *inside)]
    select_n x6 -> x0, other arithmetic: 6.01 us -> none  [the longest x1 2.7 us: per_device(): jnp.where(fresh_here[:, None, None], decay_factor * previous + (1.0 - dec...]
    ppermute x4 -> x30, waiting for transfers between devices: 33.1 us -> 28.5 us  [the longest x12 20.5 us: shift(): return lax.ppermute(x, axis, [(i, (i + by) % n) for i in range(n)])]
  transfers between devices with their start and end apart: 7 -> 30, of which waited for: 4 -> 10; matrix products, arithmetic and copies ran while one was open for 1% -> 13% of each run, Pallas kernels for 0% -> 0%
where the time goes in v1:
time: 117 us; the launch traced here: 116 us
  starting transfers between devices  51.3 us (44%)
  waiting for transfers between devices  28.5 us (24%)
  local copies, waits for them, and re-layouts  14.1 us (12%)
  other arithmetic  9.19 us (8%)
  Pallas kernels  8.43 us (7%)
  matrix products  3.43 us (3%)
  between operations  1.18 us (1%)
    ppermute x12, waiting for transfers between devices, shift(): return lax.ppermute(x, axis, [(i, (i + by) % n) for i in range(n)])  20.5 us
    ppermute x12, starting transfers between devices, shift(): return lax.ppermute(x, axis, [(i, (i + by) % n) for i in range(n)])  19.8 us
    ppermute x11, starting transfers between devices, partner(): return lax.ppermute(x, axis, [(i, i ^ bits) for i in range(n)])  16.5 us
    ppermute x7, starting transfers between devices, shift_z(): return lax.ppermute(x, Z, [(spot[i], spot[(i + by) % 8]) for i in range(8)])  15 us
    unnamed x22, local copies, waits for them, and re-layouts  10.3 us
    pallas_call x1, Pallas kernels, finish(): pl.pallas_call(finish_kernel, name='finish', out_shape=(jax.ShapeDtypeStr...  8.43 us
    ppermute x11, waiting for transfers between devices, partner(): return lax.ppermute(x, axis, [(i, i ^ bits) for i in range(n)])  4.95 us
    dot_general x2, matrix products, dot(): return lax.dot_general(a, b, dims, preferred_element_type=jnp.float32)  3.43 us
  transfers between devices with their start and end apart: 30, of which 10 were waited for; matrix products, arithmetic and copies ran while one was open for 13% of the time, Pallas kernels for 0%

profile of v1, /device:TPU:1, one launch (start us, length us, event | category | flops | bytes accessed | tf_op | source)
XLA Modules:
  0.0 116.1 jit_solution(3272196063172680374)
XLA Ops:
  3.2 1.8 %dynamic-slice_dynamic-update-slice_fusion.13 = (bf16[128,1536]{1,0:T(8,128)(2,1)S(1)}, bf16[128,1536]{1,0:T(8,128)(2,1)}, bf16[128,1536]{1,0:T(8,128)(2,1)S(1)}, bf16[128,1536]{1,0:T(8,128)(2,1)S(1)}) fusion(bf16[128,1536]{1,0:T(8,128)(2,1)S(1)} %get-tuple-element.21, bf16[128,8192]{1,0:T(8,128)(2,1)} %param.7, s32[]{:T(128)S(6)} %select_n.235, ...), kind=kLoop, calls=%fused_computation.86 | loop fusion | bytes 524304
  5.0 1.8 %dynamic-slice_dynamic-update-slice_fusion.12 = (bf16[128,1536]{1,0:T(8,128)(2,1)S(1)}, bf16[128,1536]{1,0:T(8,128)(2,1)}, bf16[128,1536]{1,0:T(8,128)(2,1)S(1)}, bf16[128,1536]{1,0:T(8,128)(2,1)S(1)}) fusion(bf16[128,1536]{1,0:T(8,128)(2,1)S(1)} %get-tuple-element.17, bf16[128,8192]{1,0:T(8,128)(2,1)} %param.7, s32[]{:T(128)S(6)} %select_n.236, ...), kind=kLoop, calls=%fused_computation.85 | loop fusion | bytes 524304
  10.6 3.3 %collective-permute-start.9 = (bf16[128,1536]{1,0:T(8,128)(2,1)}, bf16[128,1536]{1,0:T(8,128)(2,1)S(1)}, u32[]{:S(2)}, u32[]{:S(2)}) collective-permute-start(bf16[128,1536]{1,0:T(8,128)(2,1)} %get-tuple-element.56), channel_id=1, source_target_pairs={{0,6},{2,0},{4,2},{6,4},{1,7},{3,1},{5,3},{7,5},{8,14},{10,8},{12,... | collective-permute-start | bytes 1179656 | tf_op jit(solution)/shard_map/ppermute | solution.py:27
  13.9 1.7 %collective-permute-start.7 = (bf16[128,1536]{1,0:T(8,128)(2,1)}, bf16[128,1536]{1,0:T(8,128)(2,1)}, u32[]{:S(2)}, u32[]{:S(2)}) collective-permute-start(bf16[128,1536]{1,0:T(8,128)(2,1)} %get-tuple-element.55), channel_id=1, source_target_pairs={{0,4},{2,6},{4,0},{6,2},{1,5},{3,7},{5,1},{7,3},{8,12},{10,14},{12... | collective-permute-start | bytes 1179656 | tf_op jit(solution)/shard_map/ppermute | solution.py:27
  15.8 2.8 %collective-permute-start.2 = (bf16[128,1536]{1,0:T(8,128)(2,1)S(1)}, bf16[128,1536]{1,0:T(8,128)(2,1)}, u32[]{:S(2)}, u32[]{:S(2)}) collective-permute-start(bf16[128,1536]{1,0:T(8,128)(2,1)S(1)} %get-tuple-element.53), channel_id=1, source_target_pairs={{0,48},{16,0},{32,16},{48,32},{1,49},{17,1},{33,17},{49,33},{2,50}... | collective-permute-start | bytes 1179656 | tf_op jit(solution)/shard_map/ppermute | solution.py:27
  18.6 6.5 %collective-permute-done.9 = bf16[128,1536]{1,0:T(8,128)(2,1)S(1)} collective-permute-done((bf16[128,1536]{1,0:T(8,128)(2,1)}, bf16[128,1536]{1,0:T(8,128)(2,1)S(1)}, u32[]{:S(2)}, u32[]{:S(2)}) %collective-permute-start.9) | collective-permute-done | bytes 393248 | tf_op jit(solution)/shard_map/ppermute | solution.py:27
  26.0 6.6 %collective-permute-done.7 = bf16[128,1536]{1,0:T(8,128)(2,1)} collective-permute-done((bf16[128,1536]{1,0:T(8,128)(2,1)}, bf16[128,1536]{1,0:T(8,128)(2,1)}, u32[]{:S(2)}, u32[]{:S(2)}) %collective-permute-start.7) | collective-permute-done | bytes 393248 | tf_op jit(solution)/shard_map/ppermute | solution.py:27
  33.8 1.7 %fusion = f32[1024,512]{1,0:T(8,128)S(1)} fusion(bf16[512,1536]{1,0:T(8,128)(2,1)S(1)} %pad_maximum_fusion.2, bf16[128,1536]{1,0:T(8,128)(2,1)S(1)} %collective-permute-done.9, bf16[128,1536]{1,0:T(8,128)(2,1)} %collective-permute-done.8, bf16[128,1536]{1,0:T(8,128)(2,1)} %collective-permute-done.7, bf16[128,1536]{1,0:T(8,128)(2,1)S(1)} %get-tuple-element.54), kind=kOutput, calls=%fused_computation.3 | convolution fusion | flops 538968064 | bytes 4718592 | tf_op jit(solution)/shard_map/dot_general | solution.py:46
  37.9 2.8 %collective-permute-start.10 = (f32[4,128,512]{2,1,0:T(8,128)}, f32[4,128,512]{2,1,0:T(8,128)}, u32[]{:S(2)}, u32[]{:S(2)}) collective-permute-start(f32[4,128,512]{2,1,0:T(8,128)} %dynamic-slice_bitcast_fusion), channel_id=1, source_target_pairs={{0,1},{1,0},{2,3},{3,2},{4,5},{5,4},{6,7},{7,6},{8,9},{9,8},{10,11... | collective-permute-start | bytes 3145736 | tf_op jit(solution)/shard_map/ppermute | solution.py:37
  41.9 1.7 %fusion.2 = f32[1024,512]{1,0:T(8,128)S(1)} fusion(bf16[512,1536]{1,0:T(8,128)(2,1)S(1)} %pad_maximum_fusion.1, bf16[128,1536]{1,0:T(8,128)(2,1)} %collective-permute-done.2, bf16[128,1536]{1,0:T(8,128)(2,1)} %collective-permute-done.1, bf16[128,1536]{1,0:T(8,128)(2,1)S(1)} %collective-permute-done, bf16[128,512]{1,0:T(8,128)(2,1)S(1)} %copy-done.2, ...), kind=kOutput, calls=%fused_computation.5 | convolution fusion | flops 539492352 | bytes 4718592 | tf_op jit(solution)/shard_map/dot_general | solution.py:46
  44.3 1.7 %bitcast_add_fusion = f32[4,128,512]{2,1,0:T(8,128)S(1)} fusion(f32[4,128,512]{2,1,0:T(8,128)} %collective-permute-done.10, f32[4,2,128,512]{3,2,1,0:T(8,128)} %bitcast.102, s32[]{:T(128)S(6)} %select_n.223), kind=kLoop, calls=%fused_computation.8 | loop fusion | flops 262144 | bytes 3145732 | tf_op jit(solution)/shard_map/add | solution.py:167
  46.2 2.9 %collective-permute-start.13 = (bf16[128,512]{1,0:T(8,128)(2,1)S(1)}, bf16[128,512]{1,0:T(8,128)(2,1)S(1)}, u32[]{:S(2)}, u32[]{:S(2)}) collective-permute-start(bf16[128,512]{1,0:T(8,128)(2,1)S(1)} %get-tuple-element.33), channel_id=1, source_target_pairs={{0,48},{16,0},{32,16},{48,32},{1,49},{17,1},{33,17},{49,33},{2,50}... | collective-permute-start | bytes 393224 | tf_op jit(solution)/shard_map/ppermute | solution.py:27
  49.0 1.6 %collective-permute-start.11 = (bf16[128,512]{1,0:T(8,128)(2,1)S(1)}, bf16[128,512]{1,0:T(8,128)(2,1)S(1)}, u32[]{:S(2)}, u32[]{:S(2)}) collective-permute-start(bf16[128,512]{1,0:T(8,128)(2,1)S(1)} %get-tuple-element.32), channel_id=1, source_target_pairs={{0,32},{16,48},{32,0},{48,16},{1,33},{17,49},{33,1},{49,17},{2,34}... | collective-permute-start | bytes 393224 | tf_op jit(solution)/shard_map/ppermute | solution.py:27
  52.2 5.6 %collective-permute-start.6 = (bf16[128,512]{1,0:T(8,128)(2,1)S(1)}, bf16[128,512]{1,0:T(8,128)(2,1)S(1)}, u32[]{:S(2)}, u32[]{:S(2)}) collective-permute-start(bf16[128,512]{1,0:T(8,128)(2,1)S(1)} %get-tuple-element.30), channel_id=1, source_target_pairs={{0,6},{2,0},{4,2},{6,4},{1,7},{3,1},{5,3},{7,5},{8,14},{10,8},{12,... | collective-permute-start | bytes 393224 | tf_op jit(solution)/shard_map/ppermute | solution.py:27
  59.7 6.5 %collective-permute-done.5 = bf16[128,512]{1,0:T(8,128)(2,1)S(1)} collective-permute-done((bf16[128,512]{1,0:T(8,128)(2,1)S(1)}, bf16[128,512]{1,0:T(8,128)(2,1)S(1)}, u32[]{:S(2)}, u32[]{:S(2)}) %collective-permute-start.5) | collective-permute-done | bytes 131104 | tf_op jit(solution)/shard_map/ppermute | solution.py:27
  66.6 5.6 %collective-permute-start.20 = (bf16[32,512]{1,0:T(8,128)(2,1)S(1)}, bf16[32,512]{1,0:T(8,128)(2,1)S(1)}, u32[]{:S(2)}, u32[]{:S(2)}) collective-permute-start(bf16[32,512]{1,0:T(8,128)(2,1)S(1)} %get-tuple-element.36), channel_id=1, source_target_pairs={{0,200},{64,0},{128,64},{192,128},{8,192},{72,8},{136,72},{200,136... | collective-permute-start | bytes 98312 | tf_op jit(solution)/shard_map/ppermute | solution.py:32
  72.3 1.9 %collective-permute-start.18 = (bf16[32,512]{1,0:T(8,128)(2,1)S(1)}, bf16[32,512]{1,0:T(8,128)(2,1)S(1)}, u32[]{:S(2)}, u32[]{:S(2)}) collective-permute-start(bf16[32,512]{1,0:T(8,128)(2,1)S(1)} %get-tuple-element.38), channel_id=1, source_target_pairs={{0,136},{64,200},{128,0},{192,64},{8,128},{72,192},{136,8},{200,72... | collective-permute-start | bytes 98312 | tf_op jit(solution)/shard_map/ppermute | solution.py:32
  74.7 2.4 %collective-permute-start.16 = (bf16[32,512]{1,0:T(8,128)(2,1)S(1)}, bf16[32,512]{1,0:T(8,128)(2,1)S(1)}, u32[]{:S(2)}, u32[]{:S(2)}) collective-permute-start(bf16[32,512]{1,0:T(8,128)(2,1)S(1)} %get-tuple-element.40), channel_id=1, source_target_pairs={{0,72},{64,136},{128,200},{192,0},{8,64},{72,128},{136,192},{200,8... | collective-permute-start | bytes 98312 | tf_op jit(solution)/shard_map/ppermute | solution.py:32
  77.9 3.7 %collective-permute-start.14 = (bf16[32,512]{1,0:T(8,128)(2,1)S(1)}, bf16[32,512]{1,0:T(8,128)(2,1)S(1)}, u32[]{:S(2)}, u32[]{:S(2)}) collective-permute-start(bf16[32,512]{1,0:T(8,128)(2,1)S(1)} %get-tuple-element.35), channel_id=1, source_target_pairs={{0,8},{64,72},{128,136},{192,200},{8,0},{72,64},{136,128},{200,192... | collective-permute-start | bytes 98312 | tf_op jit(solution)/shard_map/ppermute | solution.py:32
  84.7 4.2 %collective-permute-start.23 = (bf16[32,512]{1,0:T(8,128)(2,1)S(1)}, bf16[32,512]{1,0:T(8,128)(2,1)S(1)}, u32[]{:S(2)}, u32[]{:S(2)}) collective-permute-start(bf16[32,512]{1,0:T(8,128)(2,1)S(1)} %fusion.38), channel_id=1, source_target_pairs={{0,192},{64,128},{128,64},{192,0},{1,193},{65,129},{129,65},{193,1... | collective-permute-start | bytes 98312 | tf_op jit(solution)/shard_map/ppermute | solution.py:37
  89.5 4.6 %collective-permute-start.27 = (f32[2,2,128,512]{3,2,1,0:T(8,128)S(1)}, f32[2,2,128,512]{3,2,1,0:T(8,128)S(1)}, u32[]{:S(2)}, u32[]{:S(2)}) collective-permute-start(f32[2,2,128,512]{3,2,1,0:T(8,128)S(1)} %get-tuple-element.28), channel_id=1, source_target_pairs={{0,1},{1,0},{2,3},{3,2},{4,5},{5,4},{6,7},{7,6},{8,9},{9,8},{10,11... | collective-permute-start | bytes 3145736 | tf_op jit(solution)/shard_map/ppermute | solution.py:37
  94.2 1.7 %slice_bitcast_fusion = (bf16[128,512]{1,0:T(8,128)(2,1)S(1)}, bf16[128,512]{1,0:T(8,128)(2,1)}, bf16[1,128,512]{2,1,0:T(8,128)(2,1)S(1)}) fusion(bf16[2,128,512]{2,1,0:T(8,128)(2,1)} %param.9), kind=kLoop, calls=%fused_computation.57 | loop fusion | bytes 655360 | tf_op jit(solution)/shard_map/squeeze | solution.py:196
  98.2 3.3 %collective-permute-done.28 = bf16[128,512]{1,0:T(8,128)(2,1)} collective-permute-done((bf16[128,512]{1,0:T(8,128)(2,1)}, bf16[128,512]{1,0:T(8,128)(2,1)}, u32[]{:S(2)}, u32[]{:S(2)}) %collective-permute-start.28) | collective-permute-done | bytes 131104 | tf_op jit(solution)/shard_map/ppermute | solution.py:37
  107.7 8.4 %finish.1 = (bf16[128,512]{1,0:T(8,128)(2,1)}, f32[2,128,512]{2,1,0:T(8,128)}, bf16[2,128,512]{2,1,0:T(8,128)(2,1)}) custom-call(s32[3]{0:T(128)S(1)} %pad_add_fusion.place, s32[2]{0:T(128)S(1)} %dynamic_slice.121.fresh, f32[2]{0:T(128)S(1)} %convert_power_fusion.decay, bf16[2,2,4,32,512]{4,3,2,1,0:T(8,128)(2,1)S(1)} %pad_maximum_fusion.8.pieces, ...), custom_call_target="tpu_custom_call" | custom-call | flops 4831838208 | bytes 6291456 | tf_op jit(solution)/shard_map/finish/pallas_call | solution.py:118
  (88 shorter events, 30.0 us)
Async XLA Ops:
  10.6 14.5 %collective-permute-start.9 = (bf16[128,1536]{1,0:T(8,128)(2,1)}, bf16[128,1536]{1,0:T(8,128)(2,1)S(1)}, u32[]{:S(2)}, u32[]{:S(2)}) collective-permute-start(bf16[128,1536]{1,0:T(8,128)(2,1)} %get-tuple-element.56), channel_id=1, source_target_pairs={{0,6},{2,0},{4,2},{6,4},{1,7},{3,1},{5,3},{7,5},{8,14},{10,8},{12,... | collective-permute-start | bytes 1179656 | tf_op jit(solution)/shard_map/ppermute | solution.py:27
  13.9 12.1 %collective-permute-start.8 = (bf16[128,1536]{1,0:T(8,128)(2,1)}, bf16[128,1536]{1,0:T(8,128)(2,1)}, u32[]{:S(2)}, u32[]{:S(2)}) collective-permute-start(bf16[128,1536]{1,0:T(8,128)(2,1)} %copy-done.4), channel_id=1, source_target_pairs={{0,2},{2,4},{4,6},{6,0},{1,3},{3,5},{5,7},{7,1},{8,10},{10,12},{12... | collective-permute-start | bytes 1179656 | tf_op jit(solution)/shard_map/ppermute | solution.py:27
  13.9 18.7 %collective-permute-start.7 = (bf16[128,1536]{1,0:T(8,128)(2,1)}, bf16[128,1536]{1,0:T(8,128)(2,1)}, u32[]{:S(2)}, u32[]{:S(2)}) collective-permute-start(bf16[128,1536]{1,0:T(8,128)(2,1)} %get-tuple-element.55), channel_id=1, source_target_pairs={{0,4},{2,6},{4,0},{6,2},{1,5},{3,7},{5,1},{7,3},{8,12},{10,14},{12... | collective-permute-start | bytes 1179656 | tf_op jit(solution)/shard_map/ppermute | solution.py:27
  15.8 24.9 %collective-permute-start.2 = (bf16[128,1536]{1,0:T(8,128)(2,1)S(1)}, bf16[128,1536]{1,0:T(8,128)(2,1)}, u32[]{:S(2)}, u32[]{:S(2)}) collective-permute-start(bf16[128,1536]{1,0:T(8,128)(2,1)S(1)} %get-tuple-element.53), channel_id=1, source_target_pairs={{0,48},{16,0},{32,16},{48,32},{1,49},{17,1},{33,17},{49,33},{2,50}... | collective-permute-start | bytes 1179656 | tf_op jit(solution)/shard_map/ppermute | solution.py:27
  18.6 22.1 %collective-permute-start.1 = (bf16[128,1536]{1,0:T(8,128)(2,1)S(1)}, bf16[128,1536]{1,0:T(8,128)(2,1)}, u32[]{:S(2)}, u32[]{:S(2)}) collective-permute-start(bf16[128,1536]{1,0:T(8,128)(2,1)S(1)} %get-tuple-element.52), channel_id=1, source_target_pairs={{0,16},{16,32},{32,48},{48,0},{1,17},{17,33},{33,49},{49,1},{2,18}... | collective-permute-start | bytes 1179656 | tf_op jit(solution)/shard_map/ppermute | solution.py:27
  25.1 15.6 %collective-permute-start = (bf16[128,1536]{1,0:T(8,128)(2,1)S(1)}, bf16[128,1536]{1,0:T(8,128)(2,1)S(1)}, u32[]{:S(2)}, u32[]{:S(2)}) collective-permute-start(bf16[128,1536]{1,0:T(8,128)(2,1)S(1)} %get-tuple-element.51), channel_id=1, source_target_pairs={{0,32},{16,48},{32,0},{48,16},{1,33},{17,49},{33,1},{49,17},{2,34}... | collective-permute-start | bytes 1179656 | tf_op jit(solution)/shard_map/ppermute | solution.py:27
  37.9 6.4 %collective-permute-start.10 = (f32[4,128,512]{2,1,0:T(8,128)}, f32[4,128,512]{2,1,0:T(8,128)}, u32[]{:S(2)}, u32[]{:S(2)}) collective-permute-start(f32[4,128,512]{2,1,0:T(8,128)} %dynamic-slice_bitcast_fusion), channel_id=1, source_target_pairs={{0,1},{1,0},{2,3},{3,2},{4,5},{5,4},{6,7},{7,6},{8,9},{9,8},{10,11... | collective-permute-start | bytes 3145736 | tf_op jit(solution)/shard_map/ppermute | solution.py:37
  43.7 7.0 %collective-permute-start.3 = (f32[4,128,512]{2,1,0:T(8,128)S(1)}, f32[4,128,512]{2,1,0:T(8,128)}, u32[]{:S(2)}, u32[]{:S(2)}) collective-permute-start(f32[4,128,512]{2,1,0:T(8,128)S(1)} %dynamic-slice_bitcast_fusion.1), channel_id=1, source_target_pairs={{0,1},{1,0},{2,3},{3,2},{4,5},{5,4},{6,7},{7,6},{8,9},{9,8},{10,11... | collective-permute-start | bytes 3145736 | tf_op jit(solution)/shard_map/ppermute | solution.py:37
  46.2 11.6 %collective-permute-start.13 = (bf16[128,512]{1,0:T(8,128)(2,1)S(1)}, bf16[128,512]{1,0:T(8,128)(2,1)S(1)}, u32[]{:S(2)}, u32[]{:S(2)}) collective-permute-start(bf16[128,512]{1,0:T(8,128)(2,1)S(1)} %get-tuple-element.33), channel_id=1, source_target_pairs={{0,48},{16,0},{32,16},{48,32},{1,49},{17,1},{33,17},{49,33},{2,50}... | collective-permute-start | bytes 393224 | tf_op jit(solution)/shard_map/ppermute | solution.py:27
  49.0 10.0 %collective-permute-start.12 = (bf16[128,512]{1,0:T(8,128)(2,1)S(1)}, bf16[128,512]{1,0:T(8,128)(2,1)S(1)}, u32[]{:S(2)}, u32[]{:S(2)}) collective-permute-start(bf16[128,512]{1,0:T(8,128)(2,1)S(1)} %get-tuple-element.34), channel_id=1, source_target_pairs={{0,16},{16,32},{32,48},{48,0},{1,17},{17,33},{33,49},{49,1},{2,18}... | collective-permute-start | bytes 393224 | tf_op jit(solution)/shard_map/ppermute | solution.py:27
  49.0 10.0 %collective-permute-start.11 = (bf16[128,512]{1,0:T(8,128)(2,1)S(1)}, bf16[128,512]{1,0:T(8,128)(2,1)S(1)}, u32[]{:S(2)}, u32[]{:S(2)}) collective-permute-start(bf16[128,512]{1,0:T(8,128)(2,1)S(1)} %get-tuple-element.32), channel_id=1, source_target_pairs={{0,32},{16,48},{32,0},{48,16},{1,33},{17,49},{33,1},{49,17},{2,34}... | collective-permute-start | bytes 393224 | tf_op jit(solution)/shard_map/ppermute | solution.py:27
  52.2 7.5 %collective-permute-start.6 = (bf16[128,512]{1,0:T(8,128)(2,1)S(1)}, bf16[128,512]{1,0:T(8,128)(2,1)S(1)}, u32[]{:S(2)}, u32[]{:S(2)}) collective-permute-start(bf16[128,512]{1,0:T(8,128)(2,1)S(1)} %get-tuple-element.30), channel_id=1, source_target_pairs={{0,6},{2,0},{4,2},{6,4},{1,7},{3,1},{5,3},{7,5},{8,14},{10,8},{12,... | collective-permute-start | bytes 393224 | tf_op jit(solution)/shard_map/ppermute | solution.py:27
  57.8 8.5 %collective-permute-start.5 = (bf16[128,512]{1,0:T(8,128)(2,1)S(1)}, bf16[128,512]{1,0:T(8,128)(2,1)S(1)}, u32[]{:S(2)}, u32[]{:S(2)}) collective-permute-start(bf16[128,512]{1,0:T(8,128)(2,1)S(1)} %get-tuple-element.31), channel_id=1, source_target_pairs={{0,2},{2,4},{4,6},{6,0},{1,3},{3,5},{5,7},{7,1},{8,10},{10,12},{12... | collective-permute-start | bytes 393224 | tf_op jit(solution)/shard_map/ppermute | solution.py:27
  57.8 8.5 %collective-permute-start.4 = (bf16[128,512]{1,0:T(8,128)(2,1)S(1)}, bf16[128,512]{1,0:T(8,128)(2,1)S(1)}, u32[]{:S(2)}, u32[]{:S(2)}) collective-permute-start(bf16[128,512]{1,0:T(8,128)(2,1)S(1)} %get-tuple-element.29), channel_id=1, source_target_pairs={{0,4},{2,6},{4,0},{6,2},{1,5},{3,7},{5,1},{7,3},{8,12},{10,14},{12... | collective-permute-start | bytes 393224 | tf_op jit(solution)/shard_map/ppermute | solution.py:27
  66.4 22.9 %collective-permute-start.26 = (f32[2,128,512]{2,1,0:T(8,128)S(1)}, f32[2,128,512]{2,1,0:T(8,128)S(1)}, u32[]{:S(2)}, u32[]{:S(2)}) collective-permute-start(f32[2,128,512]{2,1,0:T(8,128)S(1)} %copy-done.3), channel_id=1, source_target_pairs={{0,2},{2,0},{1,3},{3,1},{4,6},{6,4},{5,7},{7,5},{8,10},{10,8},{9,1... | collective-permute-start | bytes 1572872 | tf_op jit(solution)/shard_map/ppermute | solution.py:37
  66.6 8.0 %collective-permute-start.20 = (bf16[32,512]{1,0:T(8,128)(2,1)S(1)}, bf16[32,512]{1,0:T(8,128)(2,1)S(1)}, u32[]{:S(2)}, u32[]{:S(2)}) collective-permute-start(bf16[32,512]{1,0:T(8,128)(2,1)S(1)} %get-tuple-element.36), channel_id=1, source_target_pairs={{0,200},{64,0},{128,64},{192,128},{8,192},{72,8},{136,72},{200,136... | collective-permute-start | bytes 98312 | tf_op jit(solution)/shard_map/ppermute | solution.py:32
  74.2 7.4 %collective-permute-start.17 = (bf16[32,512]{1,0:T(8,128)(2,1)S(1)}, bf16[32,512]{1,0:T(8,128)(2,1)S(1)}, u32[]{:S(2)}, u32[]{:S(2)}) collective-permute-start(bf16[32,512]{1,0:T(8,128)(2,1)S(1)} %get-tuple-element.39), channel_id=1, source_target_pairs={{0,128},{64,192},{128,8},{192,72},{8,136},{72,200},{136,0},{200,64... | collective-permute-start | bytes 98312 | tf_op jit(solution)/shard_map/ppermute | solution.py:32
  74.7 7.0 %collective-permute-start.16 = (bf16[32,512]{1,0:T(8,128)(2,1)S(1)}, bf16[32,512]{1,0:T(8,128)(2,1)S(1)}, u32[]{:S(2)}, u32[]{:S(2)}) collective-permute-start(bf16[32,512]{1,0:T(8,128)(2,1)S(1)} %get-tuple-element.40), channel_id=1, source_target_pairs={{0,72},{64,136},{128,200},{192,0},{8,64},{72,128},{136,192},{200,8... | collective-permute-start | bytes 98312 | tf_op jit(solution)/shard_map/ppermute | solution.py:32
  77.9 6.7 %collective-permute-start.14 = (bf16[32,512]{1,0:T(8,128)(2,1)S(1)}, bf16[32,512]{1,0:T(8,128)(2,1)S(1)}, u32[]{:S(2)}, u32[]{:S(2)}) collective-permute-start(bf16[32,512]{1,0:T(8,128)(2,1)S(1)} %get-tuple-element.35), channel_id=1, source_target_pairs={{0,8},{64,72},{128,136},{192,200},{8,0},{72,64},{136,128},{200,192... | collective-permute-start | bytes 98312 | tf_op jit(solution)/shard_map/ppermute | solution.py:32
  84.7 12.8 %collective-permute-start.23 = (bf16[32,512]{1,0:T(8,128)(2,1)S(1)}, bf16[32,512]{1,0:T(8,128)(2,1)S(1)}, u32[]{:S(2)}, u32[]{:S(2)}) collective-permute-start(bf16[32,512]{1,0:T(8,128)(2,1)S(1)} %fusion.38), channel_id=1, source_target_pairs={{0,192},{64,128},{128,64},{192,0},{1,193},{65,129},{129,65},{193,1... | collective-permute-start | bytes 98312 | tf_op jit(solution)/shard_map/ppermute | solution.py:37
  88.9 8.6 %collective-permute-start.22 = (bf16[32,512]{1,0:T(8,128)(2,1)S(1)}, bf16[32,512]{1,0:T(8,128)(2,1)S(1)}, u32[]{:S(2)}, u32[]{:S(2)}) collective-permute-start(bf16[32,512]{1,0:T(8,128)(2,1)S(1)} %fusion.38), channel_id=1, source_target_pairs={{0,128},{64,192},{128,0},{192,64},{1,129},{65,193},{129,1},{193,65... | collective-permute-start | bytes 98312 | tf_op jit(solution)/shard_map/ppermute | solution.py:37
  88.9 8.6 %collective-permute-start.21 = (bf16[32,512]{1,0:T(8,128)(2,1)S(1)}, bf16[32,512]{1,0:T(8,128)(2,1)S(1)}, u32[]{:S(2)}, u32[]{:S(2)}) collective-permute-start(bf16[32,512]{1,0:T(8,128)(2,1)S(1)} %fusion.38), channel_id=1, source_target_pairs={{0,64},{64,0},{128,192},{192,128},{1,65},{65,1},{129,193},{193,129... | collective-permute-start | bytes 98312 | tf_op jit(solution)/shard_map/ppermute | solution.py:37
  89.5 18.0 %collective-permute-start.27 = (f32[2,2,128,512]{3,2,1,0:T(8,128)S(1)}, f32[2,2,128,512]{3,2,1,0:T(8,128)S(1)}, u32[]{:S(2)}, u32[]{:S(2)}) collective-permute-start(f32[2,2,128,512]{3,2,1,0:T(8,128)S(1)} %get-tuple-element.28), channel_id=1, source_target_pairs={{0,1},{1,0},{2,3},{3,2},{4,5},{5,4},{6,7},{7,6},{8,9},{9,8},{10,11... | collective-permute-start | bytes 3145736 | tf_op jit(solution)/shard_map/ppermute | solution.py:37
  98.2 6.2 %collective-permute-start.24 = (bf16[4,32,512]{2,1,0:T(8,128)(2,1)}, bf16[4,32,512]{2,1,0:T(8,128)(2,1)}, u32[]{:S(2)}, u32[]{:S(2)}) collective-permute-start(bf16[4,32,512]{2,1,0:T(8,128)(2,1)} %get-tuple-element.50), channel_id=1, source_target_pairs={{0,2},{2,0},{1,3},{3,1},{4,6},{6,4},{5,7},{7,5},{8,10},{10,8},{9,1... | collective-permute-start | bytes 393224 | tf_op jit(solution)/shard_map/ppermute | solution.py:37
  (14 other events, 94.6 us)

commit v2 on v1

v2 whole, which is shorter than its diff:
```python
import math

import jax
import jax.numpy as jnp
from jax import lax
from jax.experimental import pallas as pl
from jax.experimental.pallas import tpu as pltpu
from jax.sharding import Mesh
from jax.sharding import PartitionSpec as P

X = ("x_hi", "x_lo")
Z = ("z_lo", "z_hi")
SHARD = ("y", "z_hi", "x_hi", "x_lo", "core")
EVERY = ("z_lo",) + SHARD

B = 512
ROWS = 128
TOKENS = 128
WIDE = 3 * B
SEND = jnp.bfloat16

decay_base = 0.9
tiny_term = 1e-06


def shift(x, axis, by):
    n = lax.axis_size(axis)
    return lax.ppermute(x, axis, [(i, (i + by) % n) for i in range(n)])


def swap_z(x, bits):
    spot = [(i % 4) * 2 + i // 4 for i in range(8)]
    return lax.ppermute(x, Z, [(spot[i], spot[i ^ bits]) for i in range(8)])


def partner(x, axis, bits=1):
    n = lax.axis_size(axis)
    return lax.ppermute(x, axis, [(i, i ^ bits) for i in range(n)])


def dot(a, b, contract=(1, 0)):
    dims = (((contract[0],), (contract[1],)), ((), ()))
    return lax.dot_general(a, b, dims, preferred_element_type=jnp.float32)


def narrow(x):
    return x.astype(jnp.bfloat16)


def rounded(x):
    return lax.optimization_barrier(narrow(x))


def finish_kernel(place, fresh, decay, g0, g1, g2, g3, s0, s1, s2, s3, r0, r1, r2, r3, left_old,
                  update, new_stats, new_roots, grad, full, right, work):
    x_lo, core = place[0], place[1]
    pieces, stats, right_old = (g0, g1, g2, g3), (s0, s1, s2, s3), (r0, r1, r2, r3)
    quarter = x_lo * 2 + core
    own = pl.ds(pl.multiple_of(quarter * ROWS, ROWS), ROWS)
    for a in range(2):
        for b in range(2):
            top = ((x_lo ^ a) * 2 + (core ^ b)) * ROWS
            here = pl.ds(pl.multiple_of(top, ROWS), ROWS)
            right[here, :] = right_old[2 * b + a][...]
            grad[here, :] = pieces[2 * b + a][...]
            for layer in range(2):
                full[layer, here, :] = stats[2 * b + a][layer]
    g = grad[...]

    def refresh_stats(layer, gram):
        old = full[layer]
        d = decay[layer]
        a = jnp.where(fresh[layer] == 1, d * old + (1.0 - d) * gram, old)
        full[layer] = a
        new_stats[layer] = full[layer, own, :]
        total = jnp.sum(jnp.sum(a * a, axis=0, keepdims=True), axis=1, keepdims=True)
        scaling = 2.5 / jnp.sqrt(total + tiny_term)
        return scaling * a, jnp.sqrt(jnp.sqrt(scaling))

    def advance(m):
        mb = narrow(m)
        u = narrow(dot(mb, mb) * 0.0625 - 0.625 * m)
        w = dot(u, mb)
        return 2.44140625 * m + 3.125 * w + dot(u, narrow(w))

    def root_of(m, m_rows, m2, m2_rows, m3, m3_rows, row0, scale):
        y = dot(narrow(m_rows), narrow(m2)) * 0.0625 - 0.3125 * (m_rows + m2_rows)
        r = lax.broadcasted_iota(jnp.int32, m_rows.shape, 0) + row0
        c = lax.broadcasted_iota(jnp.int32, m_rows.shape, 1)
        out = jnp.where(r == c, 1.953125, 0.0) + 1.25 * y - 0.390625 * m3_rows
        out = out - 0.25 * dot(narrow(y), narrow(m3))
        return narrow(scale * out)

    m, scale = refresh_stats(1, dot(g, g, (0, 0)))
    m2 = advance(m)
    m3 = advance(m2)
    root = root_of(m, m, m2, m2, m3, m3, 0, scale)
    root = jnp.where(fresh[1] == 1, root, right[...])
    right[...] = root
    new_roots[1] = right[own, :]
    mixed = narrow(dot(g, root))

    m, scale = refresh_stats(0, dot(g, g, (1, 1)))
    work[0] = m
    m2 = advance(m)
    work[1] = m2
    m3 = advance(m2)
    work[2] = m3
    rows = root_of(m, work[0, own, :], m2, work[1, own, :], m3, work[2, own, :], quarter * ROWS, scale)
    rows = jnp.where(fresh[0] == 1, rows, left_old[...])
    new_roots[0] = rows
    update[...] = narrow(dot(rows, mixed) * math.sqrt(B))


def finish(place, fresh, decay, *arrays):
    smem = pl.BlockSpec(memory_space=pltpu.SMEM)
    vmem = pl.BlockSpec(memory_space=pltpu.VMEM)
    return pl.pallas_call(
        finish_kernel,
        name="finish",
        out_shape=(
            jax.ShapeDtypeStruct((ROWS, B), jnp.bfloat16),
            jax.ShapeDtypeStruct((2, ROWS, B), jnp.float32),
            jax.ShapeDtypeStruct((2, ROWS, B), jnp.bfloat16),
        ),
        in_specs=[smem] * 3 + [vmem] * 13,
        out_specs=(vmem,) * 3,
        scratch_shapes=[
            pltpu.VMEM((B, B), jnp.bfloat16),
            pltpu.VMEM((2, B, B), jnp.float32),
            pltpu.VMEM((B, B), jnp.bfloat16),
            pltpu.VMEM((3, B, B), jnp.float32),
        ],
        compiler_params=pltpu.CompilerParams(vmem_limit_bytes=40 << 20),
        cost_estimate=pl.CostEstimate(flops=18 * 2 * B**3, bytes_accessed=6 << 20, transcendentals=0),
    )(place, fresh, decay, *arrays)


def cut_kernel(place, cotangents, activations, *rest):
    outs, sem = rest[:-1], rest[-1]
    copies = []

    def copy(src, dst):
        copies.append(pltpu.make_async_copy(src, dst, sem.at[len(copies)]))
        copies[-1].start()

    for k, out in zip((2, 1, 3, 0), outs[0::2]):
        t = lax.rem(place[0] + k, 4)
        copy(cotangents.at[:, pl.ds(pl.multiple_of(t * 4 * B, 4 * B), 2 * B)], out.at[:, : 2 * B])
        copy(activations, out.at[:, 2 * B :])
    for k, out in zip((2, 1, 3, 0), outs[1::2]):
        t = lax.rem(place[1] + k, 4)
        for j in range(4):
            start = pl.multiple_of(t * (B // 2) + (4 * j + 2) * B, B // 2)
            copy(cotangents.at[:, pl.ds(start, B // 2)], out.at[:, j * (B // 2) : (j + 1) * (B // 2)])
        copy(activations, out.at[:, 2 * B :])
    for c in copies:
        c.wait()


def cut(place, cotangents, activations):
    free = pl.BlockSpec(memory_space=pl.ANY)
    return pl.pallas_call(
        cut_kernel,
        name="cut",
        out_shape=(jax.ShapeDtypeStruct((TOKENS, WIDE), jnp.bfloat16),) * 8,
        in_specs=[pl.BlockSpec(memory_space=pltpu.SMEM), free, free],
        out_specs=(free,) * 8,
        scratch_shapes=[pltpu.SemaphoreType.DMA((28,))],
        cost_estimate=pl.CostEstimate(flops=0, bytes_accessed=6 << 20, transcendentals=0),
    )(place, cotangents, activations)


def product_kernel(core, p0, p1, p2, p3, keep, send):
    parts = (p0, p1, p2, p3)
    right = jnp.concatenate([p[:, 2 * B :] for p in parts], axis=0)
    for out, side in ((send, 1 - core[0]), (keep, core[0])):
        left = jnp.concatenate(
            [
                jnp.concatenate(
                    [p[:, pl.ds(pl.multiple_of((2 * g + side) * ROWS, ROWS), ROWS)] for g in range(4)], axis=1
                )
                for p in parts
            ],
            axis=0,
        )
        out[...] = dot(left, right, (0, 0)).reshape(4, ROWS, B).astype(out.dtype)


def product(core, parts):
    vmem = pl.BlockSpec(memory_space=pltpu.VMEM)
    return pl.pallas_call(
        product_kernel,
        name="product",
        out_shape=(
            jax.ShapeDtypeStruct((4, ROWS, B), jnp.float32),
            jax.ShapeDtypeStruct((4, ROWS, B), SEND),
        ),
        in_specs=[pl.BlockSpec(memory_space=pltpu.SMEM)] + [vmem] * 4,
        out_specs=(vmem,) * 2,
        compiler_params=pltpu.CompilerParams(vmem_limit_bytes=24 << 20),
        cost_estimate=pl.CostEstimate(flops=4 * B**3, bytes_accessed=3 << 20, transcendentals=0),
    )(core, *parts)


def core_sum_kernel(place, keep, came, own, *sends):
    for k, out in zip((0, 2, 1, 3), (own,) + sends):
        t = lax.rem(place[0] + k, 4)
        out[...] = (keep[t] + came[t].astype(jnp.float32)).astype(out.dtype)


def core_sum(place, keep, came):
    vmem = pl.BlockSpec(memory_space=pltpu.VMEM)
    return pl.pallas_call(
        core_sum_kernel,
        name="core_sum",
        out_shape=(jax.ShapeDtypeStruct((ROWS, B), jnp.float32),) + (jax.ShapeDtypeStruct((ROWS, B), SEND),) * 3,
        in_specs=[pl.BlockSpec(memory_space=pltpu.SMEM)] + [vmem] * 2,
        out_specs=(vmem,) * 4,
        cost_estimate=pl.CostEstimate(flops=4 * ROWS * B, bytes_accessed=2 << 20, transcendentals=0),
    )(place, keep, came)


def per_device(activations, cotangents, statistics, roots, ages, refresh):
    x, y = lax.axis_index(X), lax.axis_index("y")
    x_hi, x_lo, z_hi, z_lo = (lax.axis_index(a) for a in ("x_hi", "x_lo", "z_hi", "z_lo"))
    core = lax.axis_index("core")

    def scalars(*values):
        return jnp.stack(values).astype(jnp.int32)

    pieces = cut(scalars(y, x), cotangents, activations)
    y_parts, x_parts = [pieces[6]], [pieces[7]]
    for i, k in enumerate((2, 1, 3)):
        y_parts.append(shift(pieces[2 * i], "y", k))
        x_parts.append(shift(pieces[2 * i + 1], X, k))
    stats_core, right_core = partner(statistics, "core"), partner(roots[1], "core")

    y_keep, y_send = product(scalars(core), y_parts)
    y_came = partner(y_send, "core")
    x_keep, x_send = product(scalars(core), x_parts)
    x_came = partner(x_send, "core")
    y_total, *y_sends = core_sum(scalars(x), y_keep, y_came)
    x_total, *x_sends = core_sum(scalars(y), x_keep, x_came)
    for i, k in enumerate((2, 1, 3)):
        y_total += shift(y_sends[i], X, k).astype(jnp.float32)
        x_total += shift(x_sends[i], "y", k).astype(jnp.float32)

    keep = jnp.where(z_hi == 0, y_total, x_total)
    send = jnp.where(z_hi == 0, x_total, y_total).astype(SEND)
    keep, send, statistics, right = lax.optimization_barrier((keep, send, statistics, roots[1]))
    part = rounded(keep + swap_z(send, 7).astype(jnp.float32))
    stats_x, right_x = partner(statistics, "x_lo"), partner(right, "x_lo")
    part = rounded(part.astype(jnp.float32) + swap_z(part, 1).astype(jnp.float32))
    part = rounded(part.astype(jnp.float32) + swap_z(part, 2).astype(jnp.float32))
    part_x, part_core = partner(part, "x_lo"), partner(part, "core")
    grads = (part, part_x, part_core, partner(part_x, "core"))
    stats = (statistics, stats_x, stats_core, partner(stats_x, "core"))
    rights = (right, right_x, right_core, partner(right_x, "core"))

    block = y * 4 + z_hi * 2 + x_hi
    ages_here = lax.dynamic_slice_in_dim(ages, 2 * block, 2, 0)
    fresh = lax.dynamic_slice_in_dim(refresh, 2 * block, 2, 0)
    decay = decay_base ** ages_here.astype(jnp.float32)
    return finish(scalars(x_lo, core), fresh, decay, *grads, *stats, *rights, roots[0])


def solution(mesh):
    split = Mesh(mesh.devices.reshape(4, 4, 2, 2, 2, 2), EVERY)
    placed = (P(EVERY, None), P(EVERY, None), P(None, SHARD, None), P(None, SHARD, None), P(), P())
    return jax.shard_map(
        per_device,
        mesh=split,
        in_specs=placed,
        out_specs=(P(SHARD, None), P(None, SHARD, None), P(None, SHARD, None)),
        check_vma=False,
    )
```

time: 117 us -> 192 us (1.64)
  Pallas kernels: 8.43 us -> 112 us
  starting transfers between devices: 51.3 us -> 35.4 us
  local copies, waits for them, and re-layouts: 14.1 us -> 5.7 us
  waiting for transfers between devices: 28.5 us -> 35.8 us
  other arithmetic: 9.19 us -> 1.94 us
  matrix products: 3.43 us -> 0 us
    pallas_call x0 -> x5, Pallas kernels: none -> 103 us  [the longest x1 97.3 us: cut(): pl.pallas_call(cut_kernel, name='cut', out_shape=(jax.ShapeDtypeStruct((T...]
    ppermute x7 -> x3, waiting for transfers between devices: 3.01 us -> 15.3 us  [swap_z(): return lax.ppermute(x, Z, [(spot[i], spot[i ^ bits]) for i in range(8)])]
    ppermute x7 -> x3, starting transfers between devices: 15 us -> 6.49 us  [swap_z(): return lax.ppermute(x, Z, [(spot[i], spot[i ^ bits]) for i in range(8)])]
    ppermute x11, starting transfers between devices: 16.5 us -> 8.41 us  [partner(): return lax.ppermute(x, axis, [(i, i ^ bits) for i in range(n)])]
    unnamed x22, local copies, waits for them, and re-layouts: 10.3 us -> 5.61 us
    dot_general x2 -> x0, matrix products: 3.43 us -> none  [dot(): return lax.dot_general(a, b, dims, preferred_element_type=jnp.float32)]
    ppermute x12, waiting for transfers between devices: 20.5 us -> 17.4 us  [shift(): return lax.ppermute(x, axis, [(i, (i + by) % n) for i in range(n)])]
    add x2 -> x0, other arithmetic: 3.18 us -> none  [core_sum(): return pick(halves, core) + partner(pick(halves, 1 - core), 'core')]
  transfers between devices with their start and end apart: 30 -> 26, of which waited for: 10 -> 10; matrix products, arithmetic and copies ran while one was open for 13% -> 0% of each run, Pallas kernels for 0% -> 3%
where the time goes in v2:
time: 192 us; the launch traced here: 191 us
  Pallas kernels  112 us (58%)
  waiting for transfers between devices  35.8 us (19%)
  starting transfers between devices  35.4 us (18%)
  local copies, waits for them, and re-layouts  5.7 us (3%)
  other arithmetic  1.94 us (1%)
    pallas_call x1, Pallas kernels, cut(): pl.pallas_call(cut_kernel, name='cut', out_shape=(jax.ShapeDtypeStruct((T...  97.3 us
    ppermute x12, starting transfers between devices, shift(): return lax.ppermute(x, axis, [(i, (i + by) % n) for i in range(n)])  20.5 us
    ppermute x12, waiting for transfers between devices, shift(): return lax.ppermute(x, axis, [(i, (i + by) % n) for i in range(n)])  17.4 us
    ppermute x3, waiting for transfers between devices, swap_z(): return lax.ppermute(x, Z, [(spot[i], spot[i ^ bits]) for i in range(8)])  15.3 us
    pallas_call x1, Pallas kernels, finish(): pl.pallas_call(finish_kernel, name='finish', out_shape=(jax.ShapeDtypeStr...  8.42 us
    ppermute x11, starting transfers between devices, partner(): return lax.ppermute(x, axis, [(i, i ^ bits) for i in range(n)])  8.41 us
    ppermute x3, starting transfers between devices, swap_z(): return lax.ppermute(x, Z, [(spot[i], spot[i ^ bits]) for i in range(8)])  6.49 us
    unnamed x22, local copies, waits for them, and re-layouts  5.61 us
  transfers between devices with their start and end apart: 26, of which 10 were waited for; matrix products, arithmetic and copies ran while one was open for 0% of the time, Pallas kernels for 3%

profile of v2, /device:TPU:1, one launch (start us, length us, event | category | flops | bytes accessed | tf_op | source)
XLA Modules:
  0.0 191.4 jit_solution(8622623416269899796)
XLA Ops:
  1.2 97.3 %cut.1 = (bf16[128,1536]{1,0:T(8,128)(2,1)}, bf16[128,1536]{1,0:T(8,128)(2,1)}, bf16[128,1536]{1,0:T(8,128)(2,1)}, bf16[128,1536]{1,0:T(8,128)(2,1)}, bf16[128,1...) custom-call(s32[2]{0:T(128)} %pad_add_fusion.1.place, ...), custom_call_target="tpu_custom_call" | custom-call | bytes 6291456 | tf_op jit(solution)/shard_map/cut/pallas_call | solution.py:163
  98.5 3.7 %collective-permute-start.7 = (bf16[128,1536]{1,0:T(8,128)(2,1)}, bf16[128,1536]{1,0:T(8,128)(2,1)S(1)}, u32[]{:S(2)}, u32[]{:S(2)}) collective-permute-start(bf16[128,1536]{1,0:T(8,128)(2,1)} %get-tuple-element.38), channel_id=1, source_target_pairs={{0,4},{2,6},{4,0},{6,2},{1,5},{3,7},{5,1},{7,3},{8,12},{10,14},{12... | collective-permute-start | bytes 1179656 | tf_op jit(solution)/shard_map/ppermute | solution.py:28
  102.5 2.4 %collective-permute-start.9 = (bf16[128,1536]{1,0:T(8,128)(2,1)}, bf16[128,1536]{1,0:T(8,128)(2,1)S(1)}, u32[]{:S(2)}, u32[]{:S(2)}) collective-permute-start(bf16[128,1536]{1,0:T(8,128)(2,1)} %get-tuple-element.40), channel_id=1, source_target_pairs={{0,6},{2,0},{4,2},{6,4},{1,7},{3,1},{5,3},{7,5},{8,14},{10,8},{12,... | collective-permute-start | bytes 1179656 | tf_op jit(solution)/shard_map/ppermute | solution.py:28
  104.9 2.9 %collective-permute-start = (bf16[128,1536]{1,0:T(8,128)(2,1)}, bf16[128,1536]{1,0:T(8,128)(2,1)S(1)}, u32[]{:S(2)}, u32[]{:S(2)}) collective-permute-start(bf16[128,1536]{1,0:T(8,128)(2,1)} %get-tuple-element.28), channel_id=1, source_target_pairs={{0,32},{16,48},{32,0},{48,16},{1,33},{17,49},{33,1},{49,17},{2,34}... | collective-permute-start | bytes 1179656 | tf_op jit(solution)/shard_map/ppermute | solution.py:28
  108.2 2.2 %collective-permute-done.7.p1 = bf16[128,1536]{1,0:T(8,128)(2,1)S(1)} collective-permute-done((bf16[128,1536]{1,0:T(8,128)(2,1)}, bf16[128,1536]{1,0:T(8,128)(2,1)S(1)}, u32[]{:S(2)}, u32[]{:S(2)}) %collective-permute-start.7) | collective-permute-done | bytes 393248 | tf_op jit(solution)/shard_map/ppermute | solution.py:28
  110.4 3.5 %collective-permute-start.2 = (bf16[128,1536]{1,0:T(8,128)(2,1)}, bf16[128,1536]{1,0:T(8,128)(2,1)S(1)}, u32[]{:S(2)}, u32[]{:S(2)}) collective-permute-start(bf16[128,1536]{1,0:T(8,128)(2,1)} %get-tuple-element.30), channel_id=1, source_target_pairs={{0,48},{16,0},{32,16},{48,32},{1,49},{17,1},{33,17},{49,33},{2,50}... | collective-permute-start | bytes 1179656 | tf_op jit(solution)/shard_map/ppermute | solution.py:28
  113.9 6.5 %collective-permute-done.8.p2 = bf16[128,1536]{1,0:T(8,128)(2,1)S(1)} collective-permute-done((bf16[128,1536]{1,0:T(8,128)(2,1)}, bf16[128,1536]{1,0:T(8,128)(2,1)S(1)}, u32[]{:S(2)}, u32[]{:S(2)}) %collective-permute-start.8) | collective-permute-done | bytes 393248 | tf_op jit(solution)/shard_map/ppermute | solution.py:28
  124.0 2.1 %collective-permute-done.1.p2 = bf16[128,1536]{1,0:T(8,128)(2,1)S(1)} collective-permute-done((bf16[128,1536]{1,0:T(8,128)(2,1)}, bf16[128,1536]{1,0:T(8,128)(2,1)S(1)}, u32[]{:S(2)}, u32[]{:S(2)}) %collective-permute-start.1) | collective-permute-done | bytes 393248 | tf_op jit(solution)/shard_map/ppermute | solution.py:28
  130.5 2.3 %core_sum.3 = (f32[128,512]{1,0:T(8,128)}, bf16[128,512]{1,0:T(8,128)(2,1)}, bf16[128,512]{1,0:T(8,128)(2,1)}, bf16[128,512]{1,0:T(8,128)(2,1)}) custom-call(s32[1]{0:T(128)} %bitcast.3.place, f32[4,128,512]{2,1,0:T(8,128)} %copy-done.1, bf16[4,128,512]{2,1,0:T(8,128)(2,1)} %copy-done.6), custom_call_target="tpu_custom_call" | custom-call | flops 262144 | bytes 2097152 | tf_op jit(solution)/shard_map/core_sum/pallas_call | solution.py:214
  132.8 1.8 collective-permute-start.11
  135.8 1.5 collective-permute-start.13
  138.1 2.2 %core_sum.2 = (f32[128,512]{1,0:T(8,128)}, bf16[128,512]{1,0:T(8,128)(2,1)}, bf16[128,512]{1,0:T(8,128)(2,1)}, bf16[128,512]{1,0:T(8,128)(2,1)}) custom-call(s32[1]{0:T(128)} %bitcast.2.place, f32[4,128,512]{2,1,0:T(8,128)} %copy-done, bf16[4,128,512]{2,1,0:T(8,128)(2,1)} %copy-done.5), custom_call_target="tpu_custom_call" | custom-call | flops 262144 | bytes 2097152 | tf_op jit(solution)/shard_map/core_sum/pallas_call | solution.py:214
  141.5 1.6 collective-permute-start.6
  143.2 3.2 %collective-permute-done.4 = bf16[128,512]{1,0:T(8,128)(2,1)S(1)} collective-permute-done((bf16[128,512]{1,0:T(8,128)(2,1)}, bf16[128,512]{1,0:T(8,128)(2,1)S(1)}, u32[]{:S(2)}, u32[]{:S(2)}) %collective-permute-start.4) | collective-permute-done | bytes 131104 | tf_op jit(solution)/shard_map/ppermute | solution.py:28
  146.3 3.4 %collective-permute-done.5 = bf16[128,512]{1,0:T(8,128)(2,1)S(1)} collective-permute-done((bf16[128,512]{1,0:T(8,128)(2,1)}, bf16[128,512]{1,0:T(8,128)(2,1)S(1)}, u32[]{:S(2)}, u32[]{:S(2)}) %collective-permute-start.5) | collective-permute-done | bytes 131104 | tf_op jit(solution)/shard_map/ppermute | solution.py:28
  150.9 5.7 %collective-permute-start.14 = (bf16[128,512]{1,0:T(8,128)(2,1)S(1)}, bf16[128,512]{1,0:T(8,128)(2,1)S(1)}, u32[]{:S(2)}, u32[]{:S(2)}) collective-permute-start(bf16[128,512]{1,0:T(8,128)(2,1)S(1)} %get-tuple-element.48), channel_id=1, source_target_pairs={{0,200},{64,136},{128,72},{192,8},{8,192},{72,128},{136,64},{200,0... | collective-permute-start | bytes 393224 | tf_op jit(solution)/shard_map/ppermute | solution.py:33
  156.6 6.3 %collective-permute-done.14 = bf16[128,512]{1,0:T(8,128)(2,1)S(1)} collective-permute-done((bf16[128,512]{1,0:T(8,128)(2,1)S(1)}, bf16[128,512]{1,0:T(8,128)(2,1)S(1)}, u32[]{:S(2)}, u32[]{:S(2)}) %collective-permute-start.14) | collective-permute-done | bytes 131104 | tf_op jit(solution)/shard_map/ppermute | solution.py:33
  163.0 4.1 %collective-permute-done.15 = bf16[128,512]{1,0:T(8,128)(2,1)S(1)} collective-permute-done((bf16[128,512]{1,0:T(8,128)(2,1)S(1)}, bf16[128,512]{1,0:T(8,128)(2,1)S(1)}, u32[]{:S(2)}, u32[]{:S(2)}) %collective-permute-start.15) | collective-permute-done | bytes 131104 | tf_op jit(solution)/shard_map/ppermute | solution.py:33
  167.9 1.8 collective-permute-start.24
  170.9 4.8 %collective-permute-done.16 = bf16[128,512]{1,0:T(8,128)(2,1)S(1)} collective-permute-done((bf16[128,512]{1,0:T(8,128)(2,1)S(1)}, bf16[128,512]{1,0:T(8,128)(2,1)S(1)}, u32[]{:S(2)}, u32[]{:S(2)}) %collective-permute-start.16) | collective-permute-done | bytes 131104 | tf_op jit(solution)/shard_map/ppermute | solution.py:33
  175.9 1.2 collective-permute-start.25
  177.2 2.4 %collective-permute-done.17.g1 = bf16[128,512]{1,0:T(8,128)(2,1)S(1)} collective-permute-done((bf16[128,512]{1,0:T(8,128)(2,1)S(1)}, bf16[128,512]{1,0:T(8,128)(2,1)S(1)}, u32[]{:S(2)}, u32[]{:S(2)}) %collective-permute-start.17) | collective-permute-done | bytes 131104 | tf_op jit(solution)/shard_map/ppermute | solution.py:38
  179.7 2.3 %collective-permute-start.19 = (bf16[128,512]{1,0:T(8,128)(2,1)S(1)}, bf16[128,512]{1,0:T(8,128)(2,1)S(1)}, u32[]{:S(2)}, u32[]{:S(2)}) collective-permute-start(bf16[128,512]{1,0:T(8,128)(2,1)S(1)} %collective-permute-done.17.g1), channel_id=1, source_target_pairs={{0,1},{1,0},{2,3},{3,2},{4,5},{5,4},{6,7},{7,6},{8,9},{9,8},{10,11... | collective-permute-start | bytes 393224 | tf_op jit(solution)/shard_map/ppermute | solution.py:38
  182.9 8.4 %finish.1 = (bf16[128,512]{1,0:T(8,128)(2,1)}, f32[2,128,512]{2,1,0:T(8,128)}, bf16[2,128,512]{2,1,0:T(8,128)(2,1)}) custom-call(s32[2]{0:T(128)S(1)} %pad_add_fusion.place, s32[2]{0:T(128)S(1)} %dynamic_slice.6.fresh, f32[2]{0:T(128)S(1)} %convert_power_fusion.decay, bf16[128,512]{1,0:T(8,128)(2,1)S(1)} %add_convert_fusion.g0, ...), custom_call_target="tpu_custom_call" | custom-call | flops 4831838208 | bytes 6291456 | tf_op jit(solution)/shard_map/finish/pallas_call | solution.py:118
  (65 shorter events, 16.9 us)
Async XLA Ops:
  98.5 11.9 %collective-permute-start.7 = (bf16[128,1536]{1,0:T(8,128)(2,1)}, bf16[128,1536]{1,0:T(8,128)(2,1)S(1)}, u32[]{:S(2)}, u32[]{:S(2)}) collective-permute-start(bf16[128,1536]{1,0:T(8,128)(2,1)} %get-tuple-element.38), channel_id=1, source_target_pairs={{0,4},{2,6},{4,0},{6,2},{1,5},{3,7},{5,1},{7,3},{8,12},{10,14},{12... | collective-permute-start | bytes 1179656 | tf_op jit(solution)/shard_map/ppermute | solution.py:28
  102.2 18.2 %collective-permute-start.8 = (bf16[128,1536]{1,0:T(8,128)(2,1)}, bf16[128,1536]{1,0:T(8,128)(2,1)S(1)}, u32[]{:S(2)}, u32[]{:S(2)}) collective-permute-start(bf16[128,1536]{1,0:T(8,128)(2,1)} %get-tuple-element.39), channel_id=1, source_target_pairs={{0,2},{2,4},{4,6},{6,0},{1,3},{3,5},{5,7},{7,1},{8,10},{10,12},{12... | collective-permute-start | bytes 1179656 | tf_op jit(solution)/shard_map/ppermute | solution.py:28
  102.5 17.9 %collective-permute-start.9 = (bf16[128,1536]{1,0:T(8,128)(2,1)}, bf16[128,1536]{1,0:T(8,128)(2,1)S(1)}, u32[]{:S(2)}, u32[]{:S(2)}) collective-permute-start(bf16[128,1536]{1,0:T(8,128)(2,1)} %get-tuple-element.40), channel_id=1, source_target_pairs={{0,6},{2,0},{4,2},{6,4},{1,7},{3,1},{5,3},{7,5},{8,14},{10,8},{12,... | collective-permute-start | bytes 1179656 | tf_op jit(solution)/shard_map/ppermute | solution.py:28
  104.9 19.1 %collective-permute-start = (bf16[128,1536]{1,0:T(8,128)(2,1)}, bf16[128,1536]{1,0:T(8,128)(2,1)S(1)}, u32[]{:S(2)}, u32[]{:S(2)}) collective-permute-start(bf16[128,1536]{1,0:T(8,128)(2,1)} %get-tuple-element.28), channel_id=1, source_target_pairs={{0,32},{16,48},{32,0},{48,16},{1,33},{17,49},{33,1},{49,17},{2,34}... | collective-permute-start | bytes 1179656 | tf_op jit(solution)/shard_map/ppermute | solution.py:28
  107.8 18.3 %collective-permute-start.1 = (bf16[128,1536]{1,0:T(8,128)(2,1)}, bf16[128,1536]{1,0:T(8,128)(2,1)S(1)}, u32[]{:S(2)}, u32[]{:S(2)}) collective-permute-start(bf16[128,1536]{1,0:T(8,128)(2,1)} %get-tuple-element.29), channel_id=1, source_target_pairs={{0,16},{16,32},{32,48},{48,0},{1,17},{17,33},{33,49},{49,1},{2,18}... | collective-permute-start | bytes 1179656 | tf_op jit(solution)/shard_map/ppermute | solution.py:28
  110.4 15.7 %collective-permute-start.2 = (bf16[128,1536]{1,0:T(8,128)(2,1)}, bf16[128,1536]{1,0:T(8,128)(2,1)S(1)}, u32[]{:S(2)}, u32[]{:S(2)}) collective-permute-start(bf16[128,1536]{1,0:T(8,128)(2,1)} %get-tuple-element.30), channel_id=1, source_target_pairs={{0,48},{16,0},{32,16},{48,32},{1,49},{17,1},{33,17},{49,33},{2,50}... | collective-permute-start | bytes 1179656 | tf_op jit(solution)/shard_map/ppermute | solution.py:28
  123.2 6.5 %collective-permute-start.10 = (bf16[4,128,512]{2,1,0:T(8,128)(2,1)S(1)}, bf16[4,128,512]{2,1,0:T(8,128)(2,1)S(1)}, u32[]{:S(2)}, u32[]{:S(2)}) collective-permute-start(bf16[4,128,512]{2,1,0:T(8,128)(2,1)S(1)} %get-tuple-element.42), channel_id=1, source_target_pairs={{0,1},{1,0},{2,3},{3,2},{4,5},{5,4},{6,7},{7,6},{8,9},{9,8},{10,11... | collective-permute-start | bytes 1572872 | tf_op jit(solution)/shard_map/ppermute | solution.py:38
  128.8 8.4 %collective-permute-start.3 = (bf16[4,128,512]{2,1,0:T(8,128)(2,1)S(1)}, bf16[4,128,512]{2,1,0:T(8,128)(2,1)S(1)}, u32[]{:S(2)}, u32[]{:S(2)}) collective-permute-start(bf16[4,128,512]{2,1,0:T(8,128)(2,1)S(1)} %get-tuple-element.32), channel_id=1, source_target_pairs={{0,1},{1,0},{2,3},{3,2},{4,5},{5,4},{6,7},{7,6},{8,9},{9,8},{10,11... | collective-permute-start | bytes 1572872 | tf_op jit(solution)/shard_map/ppermute | solution.py:38
  132.8 8.8 %collective-permute-start.11 = (bf16[128,512]{1,0:T(8,128)(2,1)}, bf16[128,512]{1,0:T(8,128)(2,1)S(1)}, u32[]{:S(2)}, u32[]{:S(2)}) collective-permute-start(bf16[128,512]{1,0:T(8,128)(2,1)} %get-tuple-element.44), channel_id=1, source_target_pairs={{0,32},{16,48},{32,0},{48,16},{1,33},{17,49},{33,1},{49,17},{2,34}... | collective-permute-start | bytes 393224 | tf_op jit(solution)/shard_map/ppermute | solution.py:28
  134.6 8.6 %collective-permute-start.12 = (bf16[128,512]{1,0:T(8,128)(2,1)}, bf16[128,512]{1,0:T(8,128)(2,1)S(1)}, u32[]{:S(2)}, u32[]{:S(2)}) collective-permute-start(bf16[128,512]{1,0:T(8,128)(2,1)} %get-tuple-element.45), channel_id=1, source_target_pairs={{0,16},{16,32},{32,48},{48,0},{1,17},{17,33},{33,49},{49,1},{2,18}... | collective-permute-start | bytes 393224 | tf_op jit(solution)/shard_map/ppermute | solution.py:28
  135.8 7.4 %collective-permute-start.13 = (bf16[128,512]{1,0:T(8,128)(2,1)}, bf16[128,512]{1,0:T(8,128)(2,1)S(1)}, u32[]{:S(2)}, u32[]{:S(2)}) collective-permute-start(bf16[128,512]{1,0:T(8,128)(2,1)} %get-tuple-element.46), channel_id=1, source_target_pairs={{0,48},{16,0},{32,16},{48,32},{1,49},{17,1},{33,17},{49,33},{2,50}... | collective-permute-start | bytes 393224 | tf_op jit(solution)/shard_map/ppermute | solution.py:28
  140.3 6.0 %collective-permute-start.4 = (bf16[128,512]{1,0:T(8,128)(2,1)}, bf16[128,512]{1,0:T(8,128)(2,1)S(1)}, u32[]{:S(2)}, u32[]{:S(2)}) collective-permute-start(bf16[128,512]{1,0:T(8,128)(2,1)} %get-tuple-element.34), channel_id=1, source_target_pairs={{0,4},{2,6},{4,0},{6,2},{1,5},{3,7},{5,1},{7,3},{8,12},{10,14},{12... | collective-permute-start | bytes 393224 | tf_op jit(solution)/shard_map/ppermute | solution.py:28
  140.4 9.4 %collective-permute-start.5 = (bf16[128,512]{1,0:T(8,128)(2,1)}, bf16[128,512]{1,0:T(8,128)(2,1)S(1)}, u32[]{:S(2)}, u32[]{:S(2)}) collective-permute-start(bf16[128,512]{1,0:T(8,128)(2,1)} %get-tuple-element.35), channel_id=1, source_target_pairs={{0,2},{2,4},{4,6},{6,0},{1,3},{3,5},{5,7},{7,1},{8,10},{10,12},{12... | collective-permute-start | bytes 393224 | tf_op jit(solution)/shard_map/ppermute | solution.py:28
  141.5 8.2 %collective-permute-start.6 = (bf16[128,512]{1,0:T(8,128)(2,1)}, bf16[128,512]{1,0:T(8,128)(2,1)S(1)}, u32[]{:S(2)}, u32[]{:S(2)}) collective-permute-start(bf16[128,512]{1,0:T(8,128)(2,1)} %get-tuple-element.36), channel_id=1, source_target_pairs={{0,6},{2,0},{4,2},{6,4},{1,7},{3,1},{5,3},{7,5},{8,14},{10,8},{12,... | collective-permute-start | bytes 393224 | tf_op jit(solution)/shard_map/ppermute | solution.py:28
  150.9 12.0 %collective-permute-start.14 = (bf16[128,512]{1,0:T(8,128)(2,1)S(1)}, bf16[128,512]{1,0:T(8,128)(2,1)S(1)}, u32[]{:S(2)}, u32[]{:S(2)}) collective-permute-start(bf16[128,512]{1,0:T(8,128)(2,1)S(1)} %get-tuple-element.48), channel_id=1, source_target_pairs={{0,200},{64,136},{128,72},{192,8},{8,192},{72,128},{136,64},{200,0... | collective-permute-start | bytes 393224 | tf_op jit(solution)/shard_map/ppermute | solution.py:33
  156.6 13.2 %collective-permute-start.20 = (f32[2,128,512]{2,1,0:T(8,128)S(1)}, f32[2,128,512]{2,1,0:T(8,128)S(1)}, u32[]{:S(2)}, u32[]{:S(2)}) collective-permute-start(f32[2,128,512]{2,1,0:T(8,128)S(1)} %copy-done.2), channel_id=1, source_target_pairs={{0,2},{2,0},{1,3},{3,1},{4,6},{6,4},{5,7},{7,5},{8,10},{10,8},{9,1... | collective-permute-start | bytes 1572872 | tf_op jit(solution)/shard_map/ppermute | solution.py:38
  162.9 4.2 %collective-permute-start.15 = (bf16[128,512]{1,0:T(8,128)(2,1)S(1)}, bf16[128,512]{1,0:T(8,128)(2,1)S(1)}, u32[]{:S(2)}, u32[]{:S(2)}) collective-permute-start(bf16[128,512]{1,0:T(8,128)(2,1)S(1)} %add_convert_fusion.2), channel_id=1, source_target_pairs={{0,64},{64,0},{128,192},{192,128},{8,72},{72,8},{136,200},{200,136... | collective-permute-start | bytes 393224 | tf_op jit(solution)/shard_map/ppermute | solution.py:33
  167.2 8.6 %collective-permute-start.16 = (bf16[128,512]{1,0:T(8,128)(2,1)S(1)}, bf16[128,512]{1,0:T(8,128)(2,1)S(1)}, u32[]{:S(2)}, u32[]{:S(2)}) collective-permute-start(bf16[128,512]{1,0:T(8,128)(2,1)S(1)} %add_convert_fusion.1), channel_id=1, source_target_pairs={{0,128},{64,192},{128,0},{192,64},{8,136},{72,200},{136,8},{200,72... | collective-permute-start | bytes 393224 | tf_op jit(solution)/shard_map/ppermute | solution.py:33
  167.9 9.2 %collective-permute-start.24 = (bf16[128,512]{1,0:T(8,128)(2,1)S(1)}, bf16[128,512]{1,0:T(8,128)(2,1)S(1)}, u32[]{:S(2)}, u32[]{:S(2)}) collective-permute-start(bf16[128,512]{1,0:T(8,128)(2,1)S(1)} %get-tuple-element.50.r0), channel_id=1, source_target_pairs={{0,1},{1,0},{2,3},{3,2},{4,5},{5,4},{6,7},{7,6},{8,9},{9,8},{10,11... | collective-permute-start | bytes 393224 | tf_op jit(solution)/shard_map/ppermute | solution.py:38
  169.7 12.5 %collective-permute-start.21 = (f32[2,128,512]{2,1,0:T(8,128)S(1)}, f32[2,128,512]{2,1,0:T(8,128)S(1)}, u32[]{:S(2)}, u32[]{:S(2)}) collective-permute-start(f32[2,128,512]{2,1,0:T(8,128)S(1)} %copy-done.2), channel_id=1, source_target_pairs={{0,1},{1,0},{2,3},{3,2},{4,5},{5,4},{6,7},{7,6},{8,9},{9,8},{10,11... | collective-permute-start | bytes 1572872 | tf_op jit(solution)/shard_map/ppermute | solution.py:38
  169.7 6.1 %collective-permute-start.23 = (bf16[128,512]{1,0:T(8,128)(2,1)S(1)}, bf16[128,512]{1,0:T(8,128)(2,1)S(1)}, u32[]{:S(2)}, u32[]{:S(2)}) collective-permute-start(bf16[128,512]{1,0:T(8,128)(2,1)S(1)} %get-tuple-element.50.r0), channel_id=1, source_target_pairs={{0,2},{2,0},{1,3},{3,1},{4,6},{6,4},{5,7},{7,5},{8,10},{10,8},{9,1... | collective-permute-start | bytes 393224 | tf_op jit(solution)/shard_map/ppermute | solution.py:38
  169.7 13.2 %collective-permute-start.22 = (f32[2,128,512]{2,1,0:T(8,128)S(1)}, f32[2,128,512]{2,1,0:T(8,128)S(1)}, u32[]{:S(2)}, u32[]{:S(2)}) collective-permute-start(f32[2,128,512]{2,1,0:T(8,128)S(1)} %collective-permute-done.20.s1), channel_id=1, source_target_pairs={{0,1},{1,0},{2,3},{3,2},{4,5},{5,4},{6,7},{7,6},{8,9},{9,8},{10,11... | collective-permute-start | bytes 1572872 | tf_op jit(solution)/shard_map/ppermute | solution.py:38
  175.9 6.3 %collective-permute-start.25 = (bf16[128,512]{1,0:T(8,128)(2,1)S(1)}, bf16[128,512]{1,0:T(8,128)(2,1)S(1)}, u32[]{:S(2)}, u32[]{:S(2)}) collective-permute-start(bf16[128,512]{1,0:T(8,128)(2,1)S(1)} %collective-permute-done.23.r1), channel_id=1, source_target_pairs={{0,1},{1,0},{2,3},{3,2},{4,5},{5,4},{6,7},{7,6},{8,9},{9,8},{10,11... | collective-permute-start | bytes 393224 | tf_op jit(solution)/shard_map/ppermute | solution.py:38
  177.1 5.1 %collective-permute-start.18 = (bf16[128,512]{1,0:T(8,128)(2,1)S(1)}, bf16[128,512]{1,0:T(8,128)(2,1)S(1)}, u32[]{:S(2)}, u32[]{:S(2)}) collective-permute-start(bf16[128,512]{1,0:T(8,128)(2,1)S(1)} %add_convert_fusion.g0), channel_id=1, source_target_pairs={{0,1},{1,0},{2,3},{3,2},{4,5},{5,4},{6,7},{7,6},{8,9},{9,8},{10,11... | collective-permute-start | bytes 393224 | tf_op jit(solution)/shard_map/ppermute | solution.py:38
  (13 other events, 153.0 us)

commit v3 on v2

--- a/solution.py
+++ b/solution.py
@@ -131,42 +131,34 @@
             pltpu.VMEM((B, B), jnp.bfloat16),
             pltpu.VMEM((3, B, B), jnp.float32),
         ],
-        compiler_params=pltpu.CompilerParams(vmem_limit_bytes=40 << 20),
+        compiler_params=pltpu.CompilerParams(vmem_limit_bytes=14 << 20),
         cost_estimate=pl.CostEstimate(flops=18 * 2 * B**3, bytes_accessed=6 << 20, transcendentals=0),
     )(place, fresh, decay, *arrays)
 
 
-def cut_kernel(place, cotangents, activations, *rest):
-    outs, sem = rest[:-1], rest[-1]
-    copies = []
-
-    def copy(src, dst):
-        copies.append(pltpu.make_async_copy(src, dst, sem.at[len(copies)]))
-        copies[-1].start()
-
-    for k, out in zip((2, 1, 3, 0), outs[0::2]):
+def cut_kernel(place, cotangents, activations, *outs):
+    for i, k in enumerate((2, 1, 3, 0)):
         t = lax.rem(place[0] + k, 4)
-        copy(cotangents.at[:, pl.ds(pl.multiple_of(t * 4 * B, 4 * B), 2 * B)], out.at[:, : 2 * B])
-        copy(activations, out.at[:, 2 * B :])
-    for k, out in zip((2, 1, 3, 0), outs[1::2]):
+        out = outs[2 * i]
+        out[:, : 2 * B] = cotangents[:, pl.ds(pl.multiple_of(t * 4 * B, 4 * B), 2 * B)]
+        out[:, 2 * B :] = activations[...]
         t = lax.rem(place[1] + k, 4)
+        out = outs[2 * i + 1]
         for j in range(4):
             start = pl.multiple_of(t * (B // 2) + (4 * j + 2) * B, B // 2)
-            copy(cotangents.at[:, pl.ds(start, B // 2)], out.at[:, j * (B // 2) : (j + 1) * (B // 2)])
-        copy(activations, out.at[:, 2 * B :])
-    for c in copies:
-        c.wait()
+            out[:, j * (B // 2) : (j + 1) * (B // 2)] = cotangents[:, pl.ds(start, B // 2)]
+        out[:, 2 * B :] = activations[...]
 
 
 def cut(place, cotangents, activations):
-    free = pl.BlockSpec(memory_space=pl.ANY)
+    vmem = pl.BlockSpec(memory_space=pltpu.VMEM)
     return pl.pallas_call(
         cut_kernel,
         name="cut",
         out_shape=(jax.ShapeDtypeStruct((TOKENS, WIDE), jnp.bfloat16),) * 8,
-        in_specs=[pl.BlockSpec(memory_space=pltpu.SMEM), free, free],
-        out_specs=(free,) * 8,
-        scratch_shapes=[pltpu.SemaphoreType.DMA((28,))],
+        in_specs=[pl.BlockSpec(memory_space=pltpu.SMEM), vmem, vmem],
+        out_specs=(vmem,) * 8,
+        compiler_params=pltpu.CompilerParams(vmem_limit_bytes=1 << 20),
         cost_estimate=pl.CostEstimate(flops=0, bytes_accessed=6 << 20, transcendentals=0),
     )(place, cotangents, activations)
 
@@ -198,7 +190,7 @@
         ),
         in_specs=[pl.BlockSpec(memory_space=pltpu.SMEM)] + [vmem] * 4,
         out_specs=(vmem,) * 2,
-        compiler_params=pltpu.CompilerParams(vmem_limit_bytes=24 << 20),
+        compiler_params=pltpu.CompilerParams(vmem_limit_bytes=8 << 20),
         cost_estimate=pl.CostEstimate(flops=4 * B**3, bytes_accessed=3 << 20, transcendentals=0),
     )(core, *parts)
 
@@ -217,6 +209,7 @@
         out_shape=(jax.ShapeDtypeStruct((ROWS, B), jnp.float32),) + (jax.ShapeDtypeStruct((ROWS, B), SEND),) * 3,
         in_specs=[pl.BlockSpec(memory_space=pltpu.SMEM)] + [vmem] * 2,
         out_specs=(vmem,) * 4,
+        compiler_params=pltpu.CompilerParams(vmem_limit_bytes=1 << 20),
         cost_estimate=pl.CostEstimate(flops=4 * ROWS * B, bytes_accessed=2 << 20, transcendentals=0),
     )(place, keep, came)
 

time: 192 us -> 90.7 us (0.47)
  Pallas kernels: 112 us -> 13.9 us
    pallas_call x1, Pallas kernels: 97.3 us -> 1.67 us  [cut(): pl.pallas_call(cut_kernel, name='cut', out_shape=(jax.ShapeDtypeStruct((T...]
    pallas_call x2, Pallas kernels: 4.53 us -> 0.18 us  [core_sum(): pl.pallas_call(core_sum_kernel, name='core_sum', out_shape=(jax.ShapeDtyp...]
    pallas_call x2, Pallas kernels: 1.48 us -> 3.62 us  [product(): pl.pallas_call(product_kernel, name='product', out_shape=(jax.ShapeDtypeS...]
    unnamed x22 -> x16, local copies, waits for them, and re-layouts: 5.61 us -> 4.27 us
  transfers between devices with their start and end apart: 26 -> 26, of which waited for: 10 -> 12; matrix products, arithmetic and copies ran while one was open for 0% -> 0% of each run, Pallas kernels for 3% -> 4%
where the time goes in v3:
time: 90.7 us; the launch traced here: 90.5 us
  starting transfers between devices  35.7 us (39%)
  waiting for transfers between devices  34.4 us (38%)
  Pallas kernels  13.9 us (15%)
  local copies, waits for them, and re-layouts  4.36 us (5%)
  other arithmetic  1.37 us (2%)
    ppermute x12, starting transfers between devices, shift(): return lax.ppermute(x, axis, [(i, (i + by) % n) for i in range(n)])  20.4 us
    ppermute x12, waiting for transfers between devices, shift(): return lax.ppermute(x, axis, [(i, (i + by) % n) for i in range(n)])  16.1 us
    ppermute x3, waiting for transfers between devices, swap_z(): return lax.ppermute(x, Z, [(spot[i], spot[i ^ bits]) for i in range(8)])  15.1 us
    ppermute x11, starting transfers between devices, partner(): return lax.ppermute(x, axis, [(i, i ^ bits) for i in range(n)])  8.71 us
    pallas_call x1, Pallas kernels, finish(): pl.pallas_call(finish_kernel, name='finish', out_shape=(jax.ShapeDtypeStr...  8.43 us
    ppermute x3, starting transfers between devices, swap_z(): return lax.ppermute(x, Z, [(spot[i], spot[i ^ bits]) for i in range(8)])  6.52 us
    unnamed x16, local copies, waits for them, and re-layouts  4.27 us
    pallas_call x2, Pallas kernels, product(): pl.pallas_call(product_kernel, name='product', out_shape=(jax.ShapeDtypeS...  3.62 us
  transfers between devices with their start and end apart: 26, of which 12 were waited for; matrix products, arithmetic and copies ran while one was open for 0% of the time, Pallas kernels for 4%

profile of v3, /device:TPU:1, one launch (start us, length us, event | category | flops | bytes accessed | tf_op | source)
XLA Modules:
  0.0 90.5 jit_solution(7828557771695359805)
XLA Ops:
  0.7 1.6 %copy-done = bf16[128,8192]{1,0:T(8,128)(2,1)S(1)} copy-done((bf16[128,8192]{1,0:T(8,128)(2,1)S(1)}, bf16[128,8192]{1,0:T(8,128)(2,1)}, u32[]{:S(2)}) %copy-start) | copy-done | bytes 2097176
  3.2 1.7 %cut.1 = (bf16[128,1536]{1,0:T(8,128)(2,1)S(1)}, bf16[128,1536]{1,0:T(8,128)(2,1)S(1)}, bf16[128,1536]{1,0:T(8,128)(2,1)S(1)}, bf16[128,1536]{1,0:T(8,128)(2,1)}...) custom-call(s32[2]{0:T(128)S(1)} %pad_add_fusion.1.place, ...), custom_call_target="tpu_custom_call" | custom-call | bytes 6291456 | tf_op jit(solution)/shard_map/cut/pallas_call | solution.py:155
  4.9 3.6 %collective-permute-start.7 = (bf16[128,1536]{1,0:T(8,128)(2,1)S(1)}, bf16[128,1536]{1,0:T(8,128)(2,1)S(1)}, u32[]{:S(2)}, u32[]{:S(2)}) collective-permute-start(bf16[128,1536]{1,0:T(8,128)(2,1)S(1)} %get-tuple-element.38), channel_id=1, source_target_pairs={{0,4},{2,6},{4,0},{6,2},{1,5},{3,7},{5,1},{7,3},{8,12},{10,14},{12... | collective-permute-start | bytes 1179656 | tf_op jit(solution)/shard_map/ppermute | solution.py:28
  8.8 2.4 %collective-permute-start.9 = (bf16[128,1536]{1,0:T(8,128)(2,1)}, bf16[128,1536]{1,0:T(8,128)(2,1)}, u32[]{:S(2)}, u32[]{:S(2)}) collective-permute-start(bf16[128,1536]{1,0:T(8,128)(2,1)} %get-tuple-element.40), channel_id=1, source_target_pairs={{0,6},{2,0},{4,2},{6,4},{1,7},{3,1},{5,3},{7,5},{8,14},{10,8},{12,... | collective-permute-start | bytes 1179656 | tf_op jit(solution)/shard_map/ppermute | solution.py:28
  11.1 2.9 %collective-permute-start = (bf16[128,1536]{1,0:T(8,128)(2,1)S(1)}, bf16[128,1536]{1,0:T(8,128)(2,1)S(1)}, u32[]{:S(2)}, u32[]{:S(2)}) collective-permute-start(bf16[128,1536]{1,0:T(8,128)(2,1)S(1)} %get-tuple-element.28), channel_id=1, source_target_pairs={{0,32},{16,48},{32,0},{48,16},{1,33},{17,49},{33,1},{49,17},{2,34}... | collective-permute-start | bytes 1179656 | tf_op jit(solution)/shard_map/ppermute | solution.py:28
  14.5 1.9 %collective-permute-done.7.p1 = bf16[128,1536]{1,0:T(8,128)(2,1)S(1)} collective-permute-done((bf16[128,1536]{1,0:T(8,128)(2,1)S(1)}, bf16[128,1536]{1,0:T(8,128)(2,1)S(1)}, u32[]{:S(2)}, u32[]{:S(2)}) %collective-permute-start.7) | collective-permute-done | bytes 393248 | tf_op jit(solution)/shard_map/ppermute | solution.py:28
  17.1 3.7 %collective-permute-start.2 = (bf16[128,1536]{1,0:T(8,128)(2,1)S(1)}, bf16[128,1536]{1,0:T(8,128)(2,1)}, u32[]{:S(2)}, u32[]{:S(2)}) collective-permute-start(bf16[128,1536]{1,0:T(8,128)(2,1)S(1)} %get-tuple-element.30), channel_id=1, source_target_pairs={{0,48},{16,0},{32,16},{48,32},{1,49},{17,1},{33,17},{49,33},{2,50}... | collective-permute-start | bytes 1179656 | tf_op jit(solution)/shard_map/ppermute | solution.py:28
  20.7 5.8 %collective-permute-done.8.p2 = bf16[128,1536]{1,0:T(8,128)(2,1)} collective-permute-done((bf16[128,1536]{1,0:T(8,128)(2,1)}, bf16[128,1536]{1,0:T(8,128)(2,1)}, u32[]{:S(2)}, u32[]{:S(2)}) %collective-permute-start.8) | collective-permute-done | bytes 393248 | tf_op jit(solution)/shard_map/ppermute | solution.py:28
  27.6 1.8 %product.3 = (f32[4,128,512]{2,1,0:T(8,128)S(1)}, bf16[4,128,512]{2,1,0:T(8,128)(2,1)S(1)}) custom-call(s32[1]{0:T(128)} %bitcast.1.core, bf16[128,1536]{1,0:T(8,128)(2,1)S(1)} %get-tuple-element.37.p0, bf16[128,1536]{1,0:T(8,128)(2,1)S(1)} %copy-done.4, bf16[128,1536]{1,0:T(8,128)(2,1)} %collective-permute-done.8.p2, ...), custom_call_target="tpu_custom_call" | custom-call | flops 536870912 | bytes 3145728 | tf_op jit(solution)/shard_map/product/pallas_call | solution.py:184
  30.4 1.8 %collective-permute-done.1.p2 = bf16[128,1536]{1,0:T(8,128)(2,1)S(1)} collective-permute-done((bf16[128,1536]{1,0:T(8,128)(2,1)S(1)}, bf16[128,1536]{1,0:T(8,128)(2,1)S(1)}, u32[]{:S(2)}, u32[]{:S(2)}) %collective-permute-start.1) | collective-permute-done | bytes 393248 | tf_op jit(solution)/shard_map/ppermute | solution.py:28
  32.1 1.8 %product.2 = (f32[4,128,512]{2,1,0:T(8,128)S(1)}, bf16[4,128,512]{2,1,0:T(8,128)(2,1)S(1)}) custom-call(s32[1]{0:T(128)} %bitcast.1.core, bf16[128,1536]{1,0:T(8,128)(2,1)S(1)} %get-tuple-element.27.p0, bf16[128,1536]{1,0:T(8,128)(2,1)S(1)} %collective-permute-done.p1, bf16[128,1536]{1,0:T(8,128)(2,1)S(1)} %collective-permute-done.1.p2, ...), custom_call_target="tpu_custom_call" | custom-call | flops 536870912 | bytes 3145728 | tf_op jit(solution)/shard_map/product/pallas_call | solution.py:184
  35.0 1.8 %collective-permute-start.11 = (bf16[128,512]{1,0:T(8,128)(2,1)S(1)}, bf16[128,512]{1,0:T(8,128)(2,1)}, u32[]{:S(2)}, u32[]{:S(2)}) collective-permute-start(bf16[128,512]{1,0:T(8,128)(2,1)S(1)} %get-tuple-element.44), channel_id=1, source_target_pairs={{0,32},{16,48},{32,0},{48,16},{1,33},{17,49},{33,1},{49,17},{2,34}... | collective-permute-start | bytes 393224 | tf_op jit(solution)/shard_map/ppermute | solution.py:28
  36.8 1.4 %collective-permute-start.12 = (bf16[128,512]{1,0:T(8,128)(2,1)S(1)}, bf16[128,512]{1,0:T(8,128)(2,1)S(1)}, u32[]{:S(2)}, u32[]{:S(2)}) collective-permute-start(bf16[128,512]{1,0:T(8,128)(2,1)S(1)} %get-tuple-element.45), channel_id=1, source_target_pairs={{0,16},{16,32},{32,48},{48,0},{1,17},{17,33},{33,49},{49,1},{2,18}... | collective-permute-start | bytes 393224 | tf_op jit(solution)/shard_map/ppermute | solution.py:28
  38.2 1.3 %collective-permute-start.13 = (bf16[128,512]{1,0:T(8,128)(2,1)S(1)}, bf16[128,512]{1,0:T(8,128)(2,1)S(1)}, u32[]{:S(2)}, u32[]{:S(2)}) collective-permute-start(bf16[128,512]{1,0:T(8,128)(2,1)S(1)} %get-tuple-element.46), channel_id=1, source_target_pairs={{0,48},{16,0},{32,16},{48,32},{1,49},{17,1},{33,17},{49,33},{2,50}... | collective-permute-start | bytes 393224 | tf_op jit(solution)/shard_map/ppermute | solution.py:28
  43.0 1.9 %collective-permute-done.12 = bf16[128,512]{1,0:T(8,128)(2,1)S(1)} collective-permute-done((bf16[128,512]{1,0:T(8,128)(2,1)S(1)}, bf16[128,512]{1,0:T(8,128)(2,1)S(1)}, u32[]{:S(2)}, u32[]{:S(2)}) %collective-permute-start.12) | collective-permute-done | bytes 131104 | tf_op jit(solution)/shard_map/ppermute | solution.py:28
  45.3 3.7 %collective-permute-done.5 = bf16[128,512]{1,0:T(8,128)(2,1)S(1)} collective-permute-done((bf16[128,512]{1,0:T(8,128)(2,1)S(1)}, bf16[128,512]{1,0:T(8,128)(2,1)S(1)}, u32[]{:S(2)}, u32[]{:S(2)}) %collective-permute-start.5) | collective-permute-done | bytes 131104 | tf_op jit(solution)/shard_map/ppermute | solution.py:28
  50.1 5.7 %collective-permute-start.14 = (bf16[128,512]{1,0:T(8,128)(2,1)S(1)}, bf16[128,512]{1,0:T(8,128)(2,1)S(1)}, u32[]{:S(2)}, u32[]{:S(2)}) collective-permute-start(bf16[128,512]{1,0:T(8,128)(2,1)S(1)} %get-tuple-element.48), channel_id=1, source_target_pairs={{0,200},{64,136},{128,72},{192,8},{8,192},{72,128},{136,64},{200,0... | collective-permute-start | bytes 393224 | tf_op jit(solution)/shard_map/ppermute | solution.py:33
  55.7 6.3 %collective-permute-done.14 = bf16[128,512]{1,0:T(8,128)(2,1)S(1)} collective-permute-done((bf16[128,512]{1,0:T(8,128)(2,1)S(1)}, bf16[128,512]{1,0:T(8,128)(2,1)S(1)}, u32[]{:S(2)}, u32[]{:S(2)}) %collective-permute-start.14) | collective-permute-done | bytes 131104 | tf_op jit(solution)/shard_map/ppermute | solution.py:33
  62.2 4.1 %collective-permute-done.15 = bf16[128,512]{1,0:T(8,128)(2,1)S(1)} collective-permute-done((bf16[128,512]{1,0:T(8,128)(2,1)S(1)}, bf16[128,512]{1,0:T(8,128)(2,1)S(1)}, u32[]{:S(2)}, u32[]{:S(2)}) %collective-permute-start.15) | collective-permute-done | bytes 131104 | tf_op jit(solution)/shard_map/ppermute | solution.py:33
  67.1 1.8 %collective-permute-start.24 = (bf16[128,512]{1,0:T(8,128)(2,1)S(1)}, bf16[128,512]{1,0:T(8,128)(2,1)S(1)}, u32[]{:S(2)}, u32[]{:S(2)}) collective-permute-start(bf16[128,512]{1,0:T(8,128)(2,1)S(1)} %get-tuple-element.50.r0), channel_id=1, source_target_pairs={{0,1},{1,0},{2,3},{3,2},{4,5},{5,4},{6,7},{7,6},{8,9},{9,8},{10,11... | collective-permute-start | bytes 393224 | tf_op jit(solution)/shard_map/ppermute | solution.py:38
  70.1 4.8 %collective-permute-done.16 = bf16[128,512]{1,0:T(8,128)(2,1)S(1)} collective-permute-done((bf16[128,512]{1,0:T(8,128)(2,1)S(1)}, bf16[128,512]{1,0:T(8,128)(2,1)S(1)}, u32[]{:S(2)}, u32[]{:S(2)}) %collective-permute-start.16) | collective-permute-done | bytes 131104 | tf_op jit(solution)/shard_map/ppermute | solution.py:33
  76.3 2.4 %collective-permute-done.17.g1 = bf16[128,512]{1,0:T(8,128)(2,1)S(1)} collective-permute-done((bf16[128,512]{1,0:T(8,128)(2,1)S(1)}, bf16[128,512]{1,0:T(8,128)(2,1)S(1)}, u32[]{:S(2)}, u32[]{:S(2)}) %collective-permute-start.17) | collective-permute-done | bytes 131104 | tf_op jit(solution)/shard_map/ppermute | solution.py:38
  78.8 2.3 %collective-permute-start.19 = (bf16[128,512]{1,0:T(8,128)(2,1)S(1)}, bf16[128,512]{1,0:T(8,128)(2,1)S(1)}, u32[]{:S(2)}, u32[]{:S(2)}) collective-permute-start(bf16[128,512]{1,0:T(8,128)(2,1)S(1)} %collective-permute-done.17.g1), channel_id=1, source_target_pairs={{0,1},{1,0},{2,3},{3,2},{4,5},{5,4},{6,7},{7,6},{8,9},{9,8},{10,11... | collective-permute-start | bytes 393224 | tf_op jit(solution)/shard_map/ppermute | solution.py:38
  82.1 8.4 %finish.1 = (bf16[128,512]{1,0:T(8,128)(2,1)}, f32[2,128,512]{2,1,0:T(8,128)}, bf16[2,128,512]{2,1,0:T(8,128)(2,1)}) custom-call(s32[2]{0:T(128)S(1)} %pad_add_fusion.place, s32[2]{0:T(128)S(1)} %dynamic_slice.6.fresh, f32[2]{0:T(128)S(1)} %convert_power_fusion.decay, bf16[128,512]{1,0:T(8,128)(2,1)S(1)} %add_convert_fusion.g0, ...), custom_call_target="tpu_custom_call" | custom-call | flops 4831838208 | bytes 6291456 | tf_op jit(solution)/shard_map/finish/pallas_call | solution.py:118
  (59 shorter events, 15.1 us)
Async XLA Ops:
  4.9 11.4 %collective-permute-start.7 = (bf16[128,1536]{1,0:T(8,128)(2,1)S(1)}, bf16[128,1536]{1,0:T(8,128)(2,1)S(1)}, u32[]{:S(2)}, u32[]{:S(2)}) collective-permute-start(bf16[128,1536]{1,0:T(8,128)(2,1)S(1)} %get-tuple-element.38), channel_id=1, source_target_pairs={{0,4},{2,6},{4,0},{6,2},{1,5},{3,7},{5,1},{7,3},{8,12},{10,14},{12... | collective-permute-start | bytes 1179656 | tf_op jit(solution)/shard_map/ppermute | solution.py:28
  8.5 18.1 %collective-permute-start.8 = (bf16[128,1536]{1,0:T(8,128)(2,1)}, bf16[128,1536]{1,0:T(8,128)(2,1)}, u32[]{:S(2)}, u32[]{:S(2)}) collective-permute-start(bf16[128,1536]{1,0:T(8,128)(2,1)} %get-tuple-element.39), channel_id=1, source_target_pairs={{0,2},{2,4},{4,6},{6,0},{1,3},{3,5},{5,7},{7,1},{8,10},{10,12},{12... | collective-permute-start | bytes 1179656 | tf_op jit(solution)/shard_map/ppermute | solution.py:28
  8.8 17.8 %collective-permute-start.9 = (bf16[128,1536]{1,0:T(8,128)(2,1)}, bf16[128,1536]{1,0:T(8,128)(2,1)}, u32[]{:S(2)}, u32[]{:S(2)}) collective-permute-start(bf16[128,1536]{1,0:T(8,128)(2,1)} %get-tuple-element.40), channel_id=1, source_target_pairs={{0,6},{2,0},{4,2},{6,4},{1,7},{3,1},{5,3},{7,5},{8,14},{10,8},{12,... | collective-permute-start | bytes 1179656 | tf_op jit(solution)/shard_map/ppermute | solution.py:28
  11.1 19.2 %collective-permute-start = (bf16[128,1536]{1,0:T(8,128)(2,1)S(1)}, bf16[128,1536]{1,0:T(8,128)(2,1)S(1)}, u32[]{:S(2)}, u32[]{:S(2)}) collective-permute-start(bf16[128,1536]{1,0:T(8,128)(2,1)S(1)} %get-tuple-element.28), channel_id=1, source_target_pairs={{0,32},{16,48},{32,0},{48,16},{1,33},{17,49},{33,1},{49,17},{2,34}... | collective-permute-start | bytes 1179656 | tf_op jit(solution)/shard_map/ppermute | solution.py:28
  14.1 18.1 %collective-permute-start.1 = (bf16[128,1536]{1,0:T(8,128)(2,1)S(1)}, bf16[128,1536]{1,0:T(8,128)(2,1)S(1)}, u32[]{:S(2)}, u32[]{:S(2)}) collective-permute-start(bf16[128,1536]{1,0:T(8,128)(2,1)S(1)} %get-tuple-element.29), channel_id=1, source_target_pairs={{0,16},{16,32},{32,48},{48,0},{1,17},{17,33},{33,49},{49,1},{2,18}... | collective-permute-start | bytes 1179656 | tf_op jit(solution)/shard_map/ppermute | solution.py:28
  17.1 15.0 %collective-permute-start.2 = (bf16[128,1536]{1,0:T(8,128)(2,1)S(1)}, bf16[128,1536]{1,0:T(8,128)(2,1)}, u32[]{:S(2)}, u32[]{:S(2)}) collective-permute-start(bf16[128,1536]{1,0:T(8,128)(2,1)S(1)} %get-tuple-element.30), channel_id=1, source_target_pairs={{0,48},{16,0},{32,16},{48,32},{1,49},{17,1},{33,17},{49,33},{2,50}... | collective-permute-start | bytes 1179656 | tf_op jit(solution)/shard_map/ppermute | solution.py:28
  29.4 5.5 %collective-permute-start.10 = (bf16[4,128,512]{2,1,0:T(8,128)(2,1)S(1)}, bf16[4,128,512]{2,1,0:T(8,128)(2,1)S(1)}, u32[]{:S(2)}, u32[]{:S(2)}) collective-permute-start(bf16[4,128,512]{2,1,0:T(8,128)(2,1)S(1)} %get-tuple-element.42), channel_id=1, source_target_pairs={{0,1},{1,0},{2,3},{3,2},{4,5},{5,4},{6,7},{7,6},{8,9},{9,8},{10,11... | collective-permute-start | bytes 1572872 | tf_op jit(solution)/shard_map/ppermute | solution.py:38
  33.9 5.6 %collective-permute-start.3 = (bf16[4,128,512]{2,1,0:T(8,128)(2,1)S(1)}, bf16[4,128,512]{2,1,0:T(8,128)(2,1)S(1)}, u32[]{:S(2)}, u32[]{:S(2)}) collective-permute-start(bf16[4,128,512]{2,1,0:T(8,128)(2,1)S(1)} %get-tuple-element.32), channel_id=1, source_target_pairs={{0,1},{1,0},{2,3},{3,2},{4,5},{5,4},{6,7},{7,6},{8,9},{9,8},{10,11... | collective-permute-start | bytes 1572872 | tf_op jit(solution)/shard_map/ppermute | solution.py:38
  35.0 6.8 %collective-permute-start.11 = (bf16[128,512]{1,0:T(8,128)(2,1)S(1)}, bf16[128,512]{1,0:T(8,128)(2,1)}, u32[]{:S(2)}, u32[]{:S(2)}) collective-permute-start(bf16[128,512]{1,0:T(8,128)(2,1)S(1)} %get-tuple-element.44), channel_id=1, source_target_pairs={{0,32},{16,48},{32,0},{48,16},{1,33},{17,49},{33,1},{49,17},{2,34}... | collective-permute-start | bytes 393224 | tf_op jit(solution)/shard_map/ppermute | solution.py:28
  36.8 8.1 %collective-permute-start.12 = (bf16[128,512]{1,0:T(8,128)(2,1)S(1)}, bf16[128,512]{1,0:T(8,128)(2,1)S(1)}, u32[]{:S(2)}, u32[]{:S(2)}) collective-permute-start(bf16[128,512]{1,0:T(8,128)(2,1)S(1)} %get-tuple-element.45), channel_id=1, source_target_pairs={{0,16},{16,32},{32,48},{48,0},{1,17},{17,33},{33,49},{49,1},{2,18}... | collective-permute-start | bytes 393224 | tf_op jit(solution)/shard_map/ppermute | solution.py:28
  38.2 6.7 %collective-permute-start.13 = (bf16[128,512]{1,0:T(8,128)(2,1)S(1)}, bf16[128,512]{1,0:T(8,128)(2,1)S(1)}, u32[]{:S(2)}, u32[]{:S(2)}) collective-permute-start(bf16[128,512]{1,0:T(8,128)(2,1)S(1)} %get-tuple-element.46), channel_id=1, source_target_pairs={{0,48},{16,0},{32,16},{48,32},{1,49},{17,1},{33,17},{49,33},{2,50}... | collective-permute-start | bytes 393224 | tf_op jit(solution)/shard_map/ppermute | solution.py:28
  39.6 5.7 %collective-permute-start.4 = (bf16[128,512]{1,0:T(8,128)(2,1)S(1)}, bf16[128,512]{1,0:T(8,128)(2,1)S(1)}, u32[]{:S(2)}, u32[]{:S(2)}) collective-permute-start(bf16[128,512]{1,0:T(8,128)(2,1)S(1)} %get-tuple-element.34), channel_id=1, source_target_pairs={{0,4},{2,6},{4,0},{6,2},{1,5},{3,7},{5,1},{7,3},{8,12},{10,14},{12... | collective-permute-start | bytes 393224 | tf_op jit(solution)/shard_map/ppermute | solution.py:28
  40.3 8.7 %collective-permute-start.5 = (bf16[128,512]{1,0:T(8,128)(2,1)S(1)}, bf16[128,512]{1,0:T(8,128)(2,1)S(1)}, u32[]{:S(2)}, u32[]{:S(2)}) collective-permute-start(bf16[128,512]{1,0:T(8,128)(2,1)S(1)} %get-tuple-element.35), channel_id=1, source_target_pairs={{0,2},{2,4},{4,6},{6,0},{1,3},{3,5},{5,7},{7,1},{8,10},{10,12},{12... | collective-permute-start | bytes 393224 | tf_op jit(solution)/shard_map/ppermute | solution.py:28
  41.8 7.2 %collective-permute-start.6 = (bf16[128,512]{1,0:T(8,128)(2,1)S(1)}, bf16[128,512]{1,0:T(8,128)(2,1)S(1)}, u32[]{:S(2)}, u32[]{:S(2)}) collective-permute-start(bf16[128,512]{1,0:T(8,128)(2,1)S(1)} %get-tuple-element.36), channel_id=1, source_target_pairs={{0,6},{2,0},{4,2},{6,4},{1,7},{3,1},{5,3},{7,5},{8,14},{10,8},{12,... | collective-permute-start | bytes 393224 | tf_op jit(solution)/shard_map/ppermute | solution.py:28
  50.1 12.0 %collective-permute-start.14 = (bf16[128,512]{1,0:T(8,128)(2,1)S(1)}, bf16[128,512]{1,0:T(8,128)(2,1)S(1)}, u32[]{:S(2)}, u32[]{:S(2)}) collective-permute-start(bf16[128,512]{1,0:T(8,128)(2,1)S(1)} %get-tuple-element.48), channel_id=1, source_target_pairs={{0,200},{64,136},{128,72},{192,8},{8,192},{72,128},{136,64},{200,0... | collective-permute-start | bytes 393224 | tf_op jit(solution)/shard_map/ppermute | solution.py:33
  55.7 13.2 %collective-permute-start.20 = (f32[2,128,512]{2,1,0:T(8,128)S(1)}, f32[2,128,512]{2,1,0:T(8,128)S(1)}, u32[]{:S(2)}, u32[]{:S(2)}) collective-permute-start(f32[2,128,512]{2,1,0:T(8,128)S(1)} %copy-done.2), channel_id=1, source_target_pairs={{0,2},{2,0},{1,3},{3,1},{4,6},{6,4},{5,7},{7,5},{8,10},{10,8},{9,1... | collective-permute-start | bytes 1572872 | tf_op jit(solution)/shard_map/ppermute | solution.py:38
  62.1 4.2 %collective-permute-start.15 = (bf16[128,512]{1,0:T(8,128)(2,1)S(1)}, bf16[128,512]{1,0:T(8,128)(2,1)S(1)}, u32[]{:S(2)}, u32[]{:S(2)}) collective-permute-start(bf16[128,512]{1,0:T(8,128)(2,1)S(1)} %add_convert_fusion.2), channel_id=1, source_target_pairs={{0,64},{64,0},{128,192},{192,128},{8,72},{72,8},{136,200},{200,136... | collective-permute-start | bytes 393224 | tf_op jit(solution)/shard_map/ppermute | solution.py:33
  66.3 8.5 %collective-permute-start.16 = (bf16[128,512]{1,0:T(8,128)(2,1)S(1)}, bf16[128,512]{1,0:T(8,128)(2,1)S(1)}, u32[]{:S(2)}, u32[]{:S(2)}) collective-permute-start(bf16[128,512]{1,0:T(8,128)(2,1)S(1)} %add_convert_fusion.1), channel_id=1, source_target_pairs={{0,128},{64,192},{128,0},{192,64},{8,136},{72,200},{136,8},{200,72... | collective-permute-start | bytes 393224 | tf_op jit(solution)/shard_map/ppermute | solution.py:33
  67.1 9.2 %collective-permute-start.24 = (bf16[128,512]{1,0:T(8,128)(2,1)S(1)}, bf16[128,512]{1,0:T(8,128)(2,1)S(1)}, u32[]{:S(2)}, u32[]{:S(2)}) collective-permute-start(bf16[128,512]{1,0:T(8,128)(2,1)S(1)} %get-tuple-element.50.r0), channel_id=1, source_target_pairs={{0,1},{1,0},{2,3},{3,2},{4,5},{5,4},{6,7},{7,6},{8,9},{9,8},{10,11... | collective-permute-start | bytes 393224 | tf_op jit(solution)/shard_map/ppermute | solution.py:38
  68.9 12.4 %collective-permute-start.21 = (f32[2,128,512]{2,1,0:T(8,128)S(1)}, f32[2,128,512]{2,1,0:T(8,128)S(1)}, u32[]{:S(2)}, u32[]{:S(2)}) collective-permute-start(f32[2,128,512]{2,1,0:T(8,128)S(1)} %copy-done.2), channel_id=1, source_target_pairs={{0,1},{1,0},{2,3},{3,2},{4,5},{5,4},{6,7},{7,6},{8,9},{9,8},{10,11... | collective-permute-start | bytes 1572872 | tf_op jit(solution)/shard_map/ppermute | solution.py:38
  68.9 6.1 %collective-permute-start.23 = (bf16[128,512]{1,0:T(8,128)(2,1)S(1)}, bf16[128,512]{1,0:T(8,128)(2,1)S(1)}, u32[]{:S(2)}, u32[]{:S(2)}) collective-permute-start(bf16[128,512]{1,0:T(8,128)(2,1)S(1)} %get-tuple-element.50.r0), channel_id=1, source_target_pairs={{0,2},{2,0},{1,3},{3,1},{4,6},{6,4},{5,7},{7,5},{8,10},{10,8},{9,1... | collective-permute-start | bytes 393224 | tf_op jit(solution)/shard_map/ppermute | solution.py:38
  68.9 13.1 %collective-permute-start.22 = (f32[2,128,512]{2,1,0:T(8,128)S(1)}, f32[2,128,512]{2,1,0:T(8,128)S(1)}, u32[]{:S(2)}, u32[]{:S(2)}) collective-permute-start(f32[2,128,512]{2,1,0:T(8,128)S(1)} %collective-permute-done.20.s1), channel_id=1, source_target_pairs={{0,1},{1,0},{2,3},{3,2},{4,5},{5,4},{6,7},{7,6},{8,9},{9,8},{10,11... | collective-permute-start | bytes 1572872 | tf_op jit(solution)/shard_map/ppermute | solution.py:38
  75.0 6.3 %collective-permute-start.25 = (bf16[128,512]{1,0:T(8,128)(2,1)S(1)}, bf16[128,512]{1,0:T(8,128)(2,1)S(1)}, u32[]{:S(2)}, u32[]{:S(2)}) collective-permute-start(bf16[128,512]{1,0:T(8,128)(2,1)S(1)} %collective-permute-done.23.r1), channel_id=1, source_target_pairs={{0,1},{1,0},{2,3},{3,2},{4,5},{5,4},{6,7},{7,6},{8,9},{9,8},{10,11... | collective-permute-start | bytes 393224 | tf_op jit(solution)/shard_map/ppermute | solution.py:38
  76.2 5.1 %collective-permute-start.18 = (bf16[128,512]{1,0:T(8,128)(2,1)S(1)}, bf16[128,512]{1,0:T(8,128)(2,1)S(1)}, u32[]{:S(2)}, u32[]{:S(2)}) collective-permute-start(bf16[128,512]{1,0:T(8,128)(2,1)S(1)} %add_convert_fusion.g0), channel_id=1, source_target_pairs={{0,1},{1,0},{2,3},{3,2},{4,5},{5,4},{6,7},{7,6},{8,9},{9,8},{10,11... | collective-permute-start | bytes 393224 | tf_op jit(solution)/shard_map/ppermute | solution.py:38
  (10 other events, 126.1 us)

commit v4 on v2

v4 whole, which is shorter than its diff:
```python
import functools
import math

import jax
import jax.numpy as jnp
from jax import lax
from jax.experimental import pallas as pl
from jax.experimental.pallas import tpu as pltpu
from jax.sharding import Mesh
from jax.sharding import PartitionSpec as P

X = ("x_hi", "x_lo")
Z = ("z_lo", "z_hi")
SHARD = ("y", "z_hi", "x_hi", "x_lo", "core")
EVERY = ("z_lo",) + SHARD

B = 512
ROWS = 128
TOKENS = 128
WIDE = 3 * B
SEND = jnp.bfloat16
VMEM = pl.BlockSpec(memory_space=pltpu.VMEM)

decay_base = 0.9
tiny_term = 1e-06


def shift(x, axis, by):
    n = lax.axis_size(axis)
    return lax.ppermute(x, axis, [(i, (i + by) % n) for i in range(n)])


def swap_z(x, bits):
    spot = [(i % 4) * 2 + i // 4 for i in range(8)]
    return lax.ppermute(x, Z, [(spot[i], spot[i ^ bits]) for i in range(8)])


def partner(x, axis, bits=1):
    n = lax.axis_size(axis)
    return lax.ppermute(x, axis, [(i, i ^ bits) for i in range(n)])


def dot(a, b, contract=(1, 0)):
    dims = (((contract[0],), (contract[1],)), ((), ()))
    return lax.dot_general(a, b, dims, preferred_element_type=jnp.float32)


def narrow(x):
    return x.astype(jnp.bfloat16)


def rounded(x):
    return lax.optimization_barrier(narrow(x))


def finish_kernel(decays, refresh, g0, g1, g2, g3, old_stats, old_right, left_old,
                  update, new_stats, new_roots, grad, full, right, work):
    at = places()
    quarter = at["x_lo"] * 2 + at["core"]
    own = quarter_rows(at, 0, 0)
    factor = 2 * (at["y"] * 4 + at["z_hi"] * 2 + at["x_hi"])
    decay = (decays[factor], decays[factor + 1])
    fresh = (refresh[factor], refresh[factor + 1])
    for a in range(2):
        for b in range(2):
            grad[quarter_rows(at, a, b), :] = (g0, g1, g2, g3)[2 * b + a][...]
    g = grad[...]

    def refresh_stats(layer, gram):
        old = old_stats[layer]
        d = decay[layer]
        a = jnp.where(fresh[layer] == 1, d * old + (1.0 - d) * gram, old)
        full[layer] = a
        new_stats[layer] = full[layer, own, :]
        total = jnp.sum(jnp.sum(a * a, axis=0, keepdims=True), axis=1, keepdims=True)
        scaling = 2.5 / jnp.sqrt(total + tiny_term)
        return scaling * a, jnp.sqrt(jnp.sqrt(scaling))

    def advance(m):
        mb = narrow(m)
        u = narrow(dot(mb, mb) * 0.0625 - 0.625 * m)
        w = dot(u, mb)
        return 2.44140625 * m + 3.125 * w + dot(u, narrow(w))

    def root_of(m, m_rows, m2, m2_rows, m3, m3_rows, row0, scale):
        y = dot(narrow(m_rows), narrow(m2)) * 0.0625 - 0.3125 * (m_rows + m2_rows)
        r = lax.broadcasted_iota(jnp.int32, m_rows.shape, 0) + row0
        c = lax.broadcasted_iota(jnp.int32, m_rows.shape, 1)
        out = jnp.where(r == c, 1.953125, 0.0) + 1.25 * y - 0.390625 * m3_rows
        out = out - 0.25 * dot(narrow(y), narrow(m3))
        return narrow(scale * out)

    m, scale = refresh_stats(1, dot(g, g, (0, 0)))
    m2 = advance(m)
    m3 = advance(m2)
    root = root_of(m, m, m2, m2, m3, m3, 0, scale)
    root = jnp.where(fresh[1] == 1, root, old_right[...])
    right[...] = root
    new_roots[1] = right[own, :]
    mixed = narrow(dot(g, root))

    m, scale = refresh_stats(0, dot(g, g, (1, 1)))
    work[0] = m
    m2 = advance(m)
    work[1] = m2
    m3 = advance(m2)
    work[2] = m3
    rows = root_of(m, work[0, own, :], m2, work[1, own, :], m3, work[2, own, :], quarter * ROWS, scale)
    rows = jnp.where(fresh[0] == 1, rows, left_old[...])
    new_roots[0] = rows
    update[...] = narrow(dot(rows, mixed) * math.sqrt(B))


def finish(decays, refresh, *arrays):
    smem = pl.BlockSpec(memory_space=pltpu.SMEM)
    return pl.pallas_call(
        finish_kernel,
        name="finish",
        out_shape=(
            jax.ShapeDtypeStruct((ROWS, B), jnp.bfloat16),
            jax.ShapeDtypeStruct((2, ROWS, B), jnp.float32),
            jax.ShapeDtypeStruct((2, ROWS, B), jnp.bfloat16),
        ),
        in_specs=[smem] * 2 + [VMEM] * 7,
        out_specs=(VMEM,) * 3,
        scratch_shapes=[
            pltpu.VMEM((B, B), jnp.bfloat16),
            pltpu.VMEM((2, B, B), jnp.float32),
            pltpu.VMEM((B, B), jnp.bfloat16),
            pltpu.VMEM((3, B, B), jnp.float32),
        ],
        compiler_params=pltpu.CompilerParams(vmem_limit_bytes=16 << 20),
        cost_estimate=pl.CostEstimate(flops=18 * 2 * B**3, bytes_accessed=6 << 20, transcendentals=0),
    )(decays, refresh, *arrays)


def places():
    return {name: lax.axis_index(name) for name in EVERY}


def cut_kernel(cotangents, activations, *rest):
    outs, sem = rest[:-1], rest[-1]
    at = places()
    copies = []

    def copy(src, dst):
        copies.append(pltpu.make_async_copy(src, dst, sem.at[len(copies)]))
        copies[-1].start()

    for i, k in enumerate((2, 1, 3, 0)):
        t = lax.rem(at["y"] + k, 4)
        copy(cotangents.at[:, pl.ds(pl.multiple_of(t * 4 * B, 4 * B), 2 * B)], outs[2 * i].at[:, : 2 * B])
        copy(activations, outs[2 * i].at[:, 2 * B :])
        t = lax.rem(at["x_hi"] * 2 + at["x_lo"] + k, 4)
        for j in range(4):
            start = pl.multiple_of(t * (B // 2) + (4 * j + 2) * B, B // 2)
            here = slice(j * (B // 2), (j + 1) * (B // 2))
            copy(cotangents.at[:, pl.ds(start, B // 2)], outs[2 * i + 1].at[:, here])
        copy(activations, outs[2 * i + 1].at[:, 2 * B :])
    for c in copies:
        c.wait()


def cut(cotangents, activations):
    free = pl.BlockSpec(memory_space=pltpu.HBM)
    return pl.pallas_call(
        cut_kernel,
        name="cut",
        out_shape=(jax.ShapeDtypeStruct((TOKENS, WIDE), jnp.bfloat16),) * 8,
        in_specs=[free, free],
        out_specs=(VMEM,) * 8,
        scratch_shapes=[pltpu.SemaphoreType.DMA((28,))],
        compiler_params=pltpu.CompilerParams(vmem_limit_bytes=4 << 20),
        cost_estimate=pl.CostEstimate(flops=0, bytes_accessed=6 << 20, transcendentals=0),
    )(cotangents, activations)


def product_kernel(p0, p1, p2, p3, keep, send):
    parts = (p0, p1, p2, p3)
    right = jnp.concatenate([p[:, 2 * B :] for p in parts], axis=0)
    core = lax.axis_index("core")
    for out, side in ((send, 1 - core), (keep, core)):
        left = jnp.concatenate(
            [
                jnp.concatenate(
                    [p[:, pl.ds(pl.multiple_of((2 * g + side) * ROWS, ROWS), ROWS)] for g in range(4)], axis=1
                )
                for p in parts
            ],
            axis=0,
        )
        out[...] = dot(left, right, (0, 0)).reshape(4, ROWS, B).astype(out.dtype)


def product(parts):
    return pl.pallas_call(
        product_kernel,
        name="product",
        out_shape=(
            jax.ShapeDtypeStruct((4, ROWS, B), jnp.float32),
            jax.ShapeDtypeStruct((4, ROWS, B), SEND),
        ),
        in_specs=[VMEM] * 4,
        out_specs=(VMEM,) * 2,
        compiler_params=pltpu.CompilerParams(vmem_limit_bytes=8 << 20),
        cost_estimate=pl.CostEstimate(flops=4 * B**3, bytes_accessed=3 << 20, transcendentals=0),
    )(*parts)


def core_sum_kernel(along_x, keep, came, own, *sends):
    at = places()
    me = at["x_hi"] * 2 + at["x_lo"] if along_x else at["y"]
    for k, out in zip((0, 2, 1, 3), (own,) + sends):
        t = lax.rem(me + k, 4)
        out[...] = (keep[t] + came[t].astype(jnp.float32)).astype(out.dtype)


def core_sum(along_x, keep, came):
    return pl.pallas_call(
        functools.partial(core_sum_kernel, along_x),
        name="core_sum",
        out_shape=(jax.ShapeDtypeStruct((ROWS, B), jnp.float32),) + (jax.ShapeDtypeStruct((ROWS, B), SEND),) * 3,
        in_specs=[VMEM] * 2,
        out_specs=(VMEM,) * 4,
        compiler_params=pltpu.CompilerParams(vmem_limit_bytes=1 << 20),
        cost_estimate=pl.CostEstimate(flops=4 * ROWS * B, bytes_accessed=2 << 20, transcendentals=0),
    )(keep, came)


def plane_sum_kernel(y0, y1, y2, y3, x0, x1, x2, x3, keep, send):
    def total(parts):
        first, second, third = (p[...].astype(jnp.float32) for p in parts[1:])
        return parts[0][...] + first + second + third

    low = lax.axis_index("z_hi") == 0

    @pl.when(low)
    def _():
        keep[...] = total((y0, y1, y2, y3))
        send[...] = total((x0, x1, x2, x3)).astype(SEND)

    @pl.when(jnp.logical_not(low))
    def _():
        keep[...] = total((x0, x1, x2, x3))
        send[...] = total((y0, y1, y2, y3)).astype(SEND)


def plane_sum(y_parts, x_parts):
    return pl.pallas_call(
        plane_sum_kernel,
        name="plane_sum",
        out_shape=(jax.ShapeDtypeStruct((ROWS, B), jnp.float32), jax.ShapeDtypeStruct((ROWS, B), SEND)),
        in_specs=[VMEM] * 8,
        out_specs=(VMEM,) * 2,
        compiler_params=pltpu.CompilerParams(vmem_limit_bytes=2 << 20),
        cost_estimate=pl.CostEstimate(flops=8 * ROWS * B, bytes_accessed=2 << 20, transcendentals=0),
    )(*y_parts, *x_parts)


def quarter_rows(at, a, b):
    top = ((at["x_lo"] ^ a) * 2 + (at["core"] ^ b)) * ROWS
    return pl.ds(pl.multiple_of(top, ROWS), ROWS)


def assemble_kernel(own, p0, p1, p2, p3, full, right):
    at = places()
    for a in range(2):
        for b in range(2):
            pack = (p0, p1, p2, p3)[2 * b + a]
            here = quarter_rows(at, a, b)
            right[here, :] = pack[2]
            for layer in range(2):
                full[layer, here, :] = pack[layer].astype(jnp.float32) if a + b else own[layer]


def assemble(own, packs):
    return pl.pallas_call(
        assemble_kernel,
        name="assemble",
        out_shape=(jax.ShapeDtypeStruct((2, B, B), jnp.float32), jax.ShapeDtypeStruct((B, B), jnp.bfloat16)),
        in_specs=[VMEM] * 5,
        out_specs=(VMEM,) * 2,
        compiler_params=pltpu.CompilerParams(vmem_limit_bytes=1 << 20),
        cost_estimate=pl.CostEstimate(flops=0, bytes_accessed=4 << 20, transcendentals=0),
    )(own, *packs)


def per_device(activations, cotangents, statistics, roots, ages, refresh):
    decays = decay_base ** ages.astype(jnp.float32)
    pieces = cut(cotangents, activations)
    y_parts, x_parts = [pieces[6]], [pieces[7]]
    for i, k in enumerate((2, 1, 3)):
        y_parts.append(shift(pieces[2 * i], "y", k))
        x_parts.append(shift(pieces[2 * i + 1], X, k))
    pack = jnp.concatenate([narrow(statistics), roots[1:]], axis=0)
    pack_core = partner(pack, "core")

    y_keep, y_send = product(y_parts)
    y_came = partner(y_send, "core")
    x_keep, x_send = product(x_parts)
    x_came = partner(x_send, "core")
    y_own, *y_sends = core_sum(True, y_keep, y_came)
    x_own, *x_sends = core_sum(False, x_keep, x_came)
    y_sums, x_sums = [y_own], [x_own]
    for i, k in enumerate((2, 1, 3)):
        y_sums.append(shift(y_sends[i], X, k))
        x_sums.append(shift(x_sends[i], "y", k))

    keep, send = plane_sum(y_sums, x_sums)
    keep, send, pack = lax.optimization_barrier((keep, send, pack))
    part = rounded(keep + swap_z(send, 7).astype(jnp.float32))
    pack_x = partner(pack, "x_lo")
    part = rounded(part.astype(jnp.float32) + swap_z(part, 1).astype(jnp.float32))
    part = rounded(part.astype(jnp.float32) + swap_z(part, 2).astype(jnp.float32))
    part_x, part_core = partner(part, "x_lo"), partner(part, "core")
    grads = (part, part_x, part_core, partner(part_x, "core"))
    full, right = assemble(statistics, (pack, pack_x, pack_core, partner(pack_x, "core")))
    return finish(decays, refresh, *grads, full, right, roots[0])


def solution(mesh):
    split = Mesh(mesh.devices.reshape(4, 4, 2, 2, 2, 2), EVERY)
    placed = (P(EVERY, None), P(EVERY, None), P(None, SHARD, None), P(None, SHARD, None), P(), P())
    return jax.shard_map(
        per_device,
        mesh=split,
        in_specs=placed,
        out_specs=(P(SHARD, None), P(None, SHARD, None), P(None, SHARD, None)),
        check_vma=False,
    )
```

time: 192 us -> 87.5 us (0.46)
  Pallas kernels: 112 us -> 11 us
  local copies, waits for them, and re-layouts: 5.7 us -> 2.53 us
    pallas_call x1, Pallas kernels: 97.3 us -> 0.67 us  [cut(): pl.pallas_call(cut_kernel, name='cut', out_shape=(jax.ShapeDtypeStruct((T...]
    ppermute x3, waiting for transfers between devices: 15.3 us -> 10.5 us  [swap_z(): return lax.ppermute(x, Z, [(spot[i], spot[i ^ bits]) for i in range(8)])]
    pallas_call x2 -> x4, Pallas kernels: 4.53 us -> 0.52 us  [the longest x2 0.22 us: core_sum(): pl.pallas_call(functools.partial(core_sum_kernel, along_x), name='core_su...]
    unnamed x22 -> x12, local copies, waits for them, and re-layouts: 5.61 us -> 2.51 us
    ppermute x11 -> x8, waiting for transfers between devices: 3.2 us -> 6.08 us  [partner(): return lax.ppermute(x, axis, [(i, i ^ bits) for i in range(n)])]
    ppermute x12, waiting for transfers between devices: 17.4 us -> 20.1 us  [shift(): return lax.ppermute(x, axis, [(i, (i + by) % n) for i in range(n)])]
    ppermute x11 -> x8, starting transfers between devices: 8.41 us -> 9.79 us  [partner(): return lax.ppermute(x, axis, [(i, i ^ bits) for i in range(n)])]
  transfers between devices with their start and end apart: 26 -> 23, of which waited for: 10 -> 13; matrix products, arithmetic and copies ran while one was open for 0% -> 0% of each run, Pallas kernels for 3% -> 2%
where the time goes in v4:
time: 87.5 us; the launch traced here: 87.3 us
  waiting for transfers between devices  36.7 us (42%)
  starting transfers between devices  36.1 us (41%)
  Pallas kernels  11 us (13%)
  local copies, waits for them, and re-layouts  2.53 us (3%)
    ppermute x12, waiting for transfers between devices, shift(): return lax.ppermute(x, axis, [(i, (i + by) % n) for i in range(n)])  20.1 us
    ppermute x12, starting transfers between devices, shift(): return lax.ppermute(x, axis, [(i, (i + by) % n) for i in range(n)])  19.4 us
    ppermute x3, waiting for transfers between devices, swap_z(): return lax.ppermute(x, Z, [(spot[i], spot[i ^ bits]) for i in range(8)])  10.5 us
    ppermute x8, starting transfers between devices, partner(): return lax.ppermute(x, axis, [(i, i ^ bits) for i in range(n)])  9.79 us
    pallas_call x1, Pallas kernels, finish(): pl.pallas_call(finish_kernel, name='finish', out_shape=(jax.ShapeDtypeStr...  8.31 us
    ppermute x3, starting transfers between devices, swap_z(): return lax.ppermute(x, Z, [(spot[i], spot[i ^ bits]) for i in range(8)])  6.99 us
    ppermute x8, waiting for transfers between devices, partner(): return lax.ppermute(x, axis, [(i, i ^ bits) for i in range(n)])  6.08 us
    unnamed x12, local copies, waits for them, and re-layouts  2.51 us
  transfers between devices with their start and end apart: 23, of which 13 were waited for; matrix products, arithmetic and copies ran while one was open for 0% of the time, Pallas kernels for 2%

profile of v4, /device:TPU:1, one launch (start us, length us, event | category | flops | bytes accessed | tf_op | source)
XLA Modules:
  0.0 87.3 jit_solution(4703654263755558433)
XLA Ops:
  0.6 1.6 %copy-done = bf16[128,8192]{1,0:T(8,128)(2,1)S(1)} copy-done((bf16[128,8192]{1,0:T(8,128)(2,1)S(1)}, bf16[128,8192]{1,0:T(8,128)(2,1)}, u32[]{:S(2)}) %copy-start) | copy-done | bytes 2097176
  3.8 3.7 %collective-permute-start.7 = (bf16[128,1536]{1,0:T(8,128)(2,1)S(1)}, bf16[128,1536]{1,0:T(8,128)(2,1)S(1)}, u32[]{:S(2)}, u32[]{:S(2)}) collective-permute-start(bf16[128,1536]{1,0:T(8,128)(2,1)S(1)} %get-tuple-element.41), channel_id=1, source_target_pairs={{0,4},{2,6},{4,0},{6,2},{1,5},{3,7},{5,1},{7,3},{8,12},{10,14},{12... | collective-permute-start | bytes 1179656 | tf_op jit(solution)/shard_map/ppermute | solution.py:30
  7.8 2.4 %collective-permute-start.9 = (bf16[128,1536]{1,0:T(8,128)(2,1)S(1)}, bf16[128,1536]{1,0:T(8,128)(2,1)S(1)}, u32[]{:S(2)}, u32[]{:S(2)}) collective-permute-start(bf16[128,1536]{1,0:T(8,128)(2,1)S(1)} %get-tuple-element.43), channel_id=1, source_target_pairs={{0,6},{2,0},{4,2},{6,4},{1,7},{3,1},{5,3},{7,5},{8,14},{10,8},{12,... | collective-permute-start | bytes 1179656 | tf_op jit(solution)/shard_map/ppermute | solution.py:30
  10.1 2.9 %collective-permute-start = (bf16[128,1536]{1,0:T(8,128)(2,1)S(1)}, bf16[128,1536]{1,0:T(8,128)(2,1)S(1)}, u32[]{:S(2)}, u32[]{:S(2)}) collective-permute-start(bf16[128,1536]{1,0:T(8,128)(2,1)S(1)} %get-tuple-element.31), channel_id=1, source_target_pairs={{0,32},{16,48},{32,0},{48,16},{1,33},{17,49},{33,1},{49,17},{2,34}... | collective-permute-start | bytes 1179656 | tf_op jit(solution)/shard_map/ppermute | solution.py:30
  13.5 1.9 %collective-permute-done.7.p1 = bf16[128,1536]{1,0:T(8,128)(2,1)S(1)} collective-permute-done((bf16[128,1536]{1,0:T(8,128)(2,1)S(1)}, bf16[128,1536]{1,0:T(8,128)(2,1)S(1)}, u32[]{:S(2)}, u32[]{:S(2)}) %collective-permute-start.7) | collective-permute-done | bytes 393248 | tf_op jit(solution)/shard_map/ppermute | solution.py:30
  15.3 3.6 %collective-permute-start.2 = (bf16[128,1536]{1,0:T(8,128)(2,1)S(1)}, bf16[128,1536]{1,0:T(8,128)(2,1)S(1)}, u32[]{:S(2)}, u32[]{:S(2)}) collective-permute-start(bf16[128,1536]{1,0:T(8,128)(2,1)S(1)} %get-tuple-element.33), channel_id=1, source_target_pairs={{0,48},{16,0},{32,16},{48,32},{1,49},{17,1},{33,17},{49,33},{2,50}... | collective-permute-start | bytes 1179656 | tf_op jit(solution)/shard_map/ppermute | solution.py:30
  19.0 6.5 %collective-permute-done.8.p2 = bf16[128,1536]{1,0:T(8,128)(2,1)S(1)} collective-permute-done((bf16[128,1536]{1,0:T(8,128)(2,1)S(1)}, bf16[128,1536]{1,0:T(8,128)(2,1)S(1)}, u32[]{:S(2)}, u32[]{:S(2)}) %collective-permute-start.8) | collective-permute-done | bytes 393248 | tf_op jit(solution)/shard_map/ppermute | solution.py:30
  27.1 4.0 %collective-permute-done.1.p2 = bf16[128,1536]{1,0:T(8,128)(2,1)S(1)} collective-permute-done((bf16[128,1536]{1,0:T(8,128)(2,1)S(1)}, bf16[128,1536]{1,0:T(8,128)(2,1)S(1)}, u32[]{:S(2)}, u32[]{:S(2)}) %collective-permute-start.1) | collective-permute-done | bytes 393248 | tf_op jit(solution)/shard_map/ppermute | solution.py:30
  32.9 1.9 %collective-permute-start.11 = (bf16[128,512]{1,0:T(8,128)(2,1)S(1)}, bf16[128,512]{1,0:T(8,128)(2,1)S(1)}, u32[]{:S(2)}, u32[]{:S(2)}) collective-permute-start(bf16[128,512]{1,0:T(8,128)(2,1)S(1)} %get-tuple-element.47), channel_id=1, source_target_pairs={{0,32},{16,48},{32,0},{48,16},{1,33},{17,49},{33,1},{49,17},{2,34}... | collective-permute-start | bytes 393224 | tf_op jit(solution)/shard_map/ppermute | solution.py:30
  34.8 1.2 %collective-permute-start.12 = (bf16[128,512]{1,0:T(8,128)(2,1)S(1)}, bf16[128,512]{1,0:T(8,128)(2,1)S(1)}, u32[]{:S(2)}, u32[]{:S(2)}) collective-permute-start(bf16[128,512]{1,0:T(8,128)(2,1)S(1)} %get-tuple-element.48), channel_id=1, source_target_pairs={{0,16},{16,32},{32,48},{48,0},{1,17},{17,33},{33,49},{49,1},{2,18}... | collective-permute-start | bytes 393224 | tf_op jit(solution)/shard_map/ppermute | solution.py:30
  36.0 1.5 %collective-permute-start.13 = (bf16[128,512]{1,0:T(8,128)(2,1)S(1)}, bf16[128,512]{1,0:T(8,128)(2,1)S(1)}, u32[]{:S(2)}, u32[]{:S(2)}) collective-permute-start(bf16[128,512]{1,0:T(8,128)(2,1)S(1)} %get-tuple-element.49), channel_id=1, source_target_pairs={{0,48},{16,0},{32,16},{48,32},{1,49},{17,1},{33,17},{49,33},{2,50}... | collective-permute-start | bytes 393224 | tf_op jit(solution)/shard_map/ppermute | solution.py:30
  38.3 1.4 %collective-permute-done.11.x1 = bf16[128,512]{1,0:T(8,128)(2,1)S(1)} collective-permute-done((bf16[128,512]{1,0:T(8,128)(2,1)S(1)}, bf16[128,512]{1,0:T(8,128)(2,1)S(1)}, u32[]{:S(2)}, u32[]{:S(2)}) %collective-permute-start.11) | collective-permute-done | bytes 131104 | tf_op jit(solution)/shard_map/ppermute | solution.py:30
  40.6 2.2 %collective-permute-done.12.x2 = bf16[128,512]{1,0:T(8,128)(2,1)S(1)} collective-permute-done((bf16[128,512]{1,0:T(8,128)(2,1)S(1)}, bf16[128,512]{1,0:T(8,128)(2,1)S(1)}, u32[]{:S(2)}, u32[]{:S(2)}) %collective-permute-start.12) | collective-permute-done | bytes 131104 | tf_op jit(solution)/shard_map/ppermute | solution.py:30
  43.4 3.6 %collective-permute-done.5.y2 = bf16[128,512]{1,0:T(8,128)(2,1)S(1)} collective-permute-done((bf16[128,512]{1,0:T(8,128)(2,1)S(1)}, bf16[128,512]{1,0:T(8,128)(2,1)S(1)}, u32[]{:S(2)}, u32[]{:S(2)}) %collective-permute-start.5) | collective-permute-done | bytes 131104 | tf_op jit(solution)/shard_map/ppermute | solution.py:30
  47.1 5.6 %collective-permute-start.14 = (bf16[128,512]{1,0:T(8,128)(2,1)S(1)}, bf16[128,512]{1,0:T(8,128)(2,1)S(1)}, u32[]{:S(2)}, u32[]{:S(2)}) collective-permute-start(bf16[128,512]{1,0:T(8,128)(2,1)S(1)} %get-tuple-element.53), channel_id=1, source_target_pairs={{0,200},{64,136},{128,72},{192,8},{8,192},{72,128},{136,64},{200,0... | collective-permute-start | bytes 393224 | tf_op jit(solution)/shard_map/ppermute | solution.py:35
  52.8 6.3 %collective-permute-done.14 = bf16[128,512]{1,0:T(8,128)(2,1)S(1)} collective-permute-done((bf16[128,512]{1,0:T(8,128)(2,1)S(1)}, bf16[128,512]{1,0:T(8,128)(2,1)S(1)}, u32[]{:S(2)}, u32[]{:S(2)}) %collective-permute-start.14) | collective-permute-done | bytes 131104 | tf_op jit(solution)/shard_map/ppermute | solution.py:35
  59.5 3.7 %collective-permute-done.15 = bf16[128,512]{1,0:T(8,128)(2,1)S(1)} collective-permute-done((bf16[128,512]{1,0:T(8,128)(2,1)S(1)}, bf16[128,512]{1,0:T(8,128)(2,1)S(1)}, u32[]{:S(2)}, u32[]{:S(2)}) %collective-permute-start.15) | collective-permute-done | bytes 131104 | tf_op jit(solution)/shard_map/ppermute | solution.py:35
  64.3 1.8 %collective-permute-start.21 = (bf16[3,128,512]{2,1,0:T(8,128)(2,1)S(1)}, bf16[3,128,512]{2,1,0:T(8,128)(2,1)S(1)}, u32[]{:S(2)}, u32[]{:S(2)}) collective-permute-start(bf16[3,128,512]{2,1,0:T(8,128)(2,1)S(1)} %pad_maximum_fusion.p0), channel_id=1, source_target_pairs={{0,1},{1,0},{2,3},{3,2},{4,5},{5,4},{6,7},{7,6},{8,9},{9,8},{10,11... | collective-permute-start | bytes 1179656 | tf_op jit(solution)/shard_map/ppermute | solution.py:40
  66.1 3.0 %collective-permute-done.20.p1 = bf16[3,128,512]{2,1,0:T(8,128)(2,1)S(1)} collective-permute-done((bf16[3,128,512]{2,1,0:T(8,128)(2,1)S(1)}, bf16[3,128,512]{2,1,0:T(8,128)(2,1)S(1)}, u32[]{:S(2)}, u32[]{:S(2)}) %collective-permute-start.20) | collective-permute-done | bytes 393248 | tf_op jit(solution)/shard_map/ppermute | solution.py:40
  69.2 1.8 %collective-permute-start.22 = (bf16[3,128,512]{2,1,0:T(8,128)(2,1)S(1)}, bf16[3,128,512]{2,1,0:T(8,128)(2,1)S(1)}, u32[]{:S(2)}, u32[]{:S(2)}) collective-permute-start(bf16[3,128,512]{2,1,0:T(8,128)(2,1)S(1)} %collective-permute-done.20.p1), channel_id=1, source_target_pairs={{0,1},{1,0},{2,3},{3,2},{4,5},{5,4},{6,7},{7,6},{8,9},{9,8},{10,11... | collective-permute-start | bytes 1179656 | tf_op jit(solution)/shard_map/ppermute | solution.py:40
  71.7 1.5 %collective-permute-start.18 = (bf16[128,512]{1,0:T(8,128)(2,1)S(1)}, bf16[128,512]{1,0:T(8,128)(2,1)S(1)}, u32[]{:S(2)}, u32[]{:S(2)}) collective-permute-start(bf16[128,512]{1,0:T(8,128)(2,1)S(1)} %add_convert_fusion.g0), channel_id=1, source_target_pairs={{0,1},{1,0},{2,3},{3,2},{4,5},{5,4},{6,7},{7,6},{8,9},{9,8},{10,11... | collective-permute-start | bytes 393224 | tf_op jit(solution)/shard_map/ppermute | solution.py:40
  73.2 2.3 %collective-permute-done.17.g1 = bf16[128,512]{1,0:T(8,128)(2,1)S(1)} collective-permute-done((bf16[128,512]{1,0:T(8,128)(2,1)S(1)}, bf16[128,512]{1,0:T(8,128)(2,1)S(1)}, u32[]{:S(2)}, u32[]{:S(2)}) %collective-permute-start.17) | collective-permute-done | bytes 131104 | tf_op jit(solution)/shard_map/ppermute | solution.py:40
  75.5 2.6 %collective-permute-start.19 = (bf16[128,512]{1,0:T(8,128)(2,1)S(1)}, bf16[128,512]{1,0:T(8,128)(2,1)S(1)}, u32[]{:S(2)}, u32[]{:S(2)}) collective-permute-start(bf16[128,512]{1,0:T(8,128)(2,1)S(1)} %collective-permute-done.17.g1), channel_id=1, source_target_pairs={{0,1},{1,0},{2,3},{3,2},{4,5},{5,4},{6,7},{7,6},{8,9},{9,8},{10,11... | collective-permute-start | bytes 393224 | tf_op jit(solution)/shard_map/ppermute | solution.py:40
  79.0 8.3 %finish.1 = (bf16[128,512]{1,0:T(8,128)(2,1)}, f32[2,128,512]{2,1,0:T(8,128)}, bf16[2,128,512]{2,1,0:T(8,128)(2,1)}) custom-call(f32[32]{0:T(128)S(1)} %convert_power_fusion.decays, s32[32]{0:T(128)S(1)} %copy-done.3, bf16[128,512]{1,0:T(8,128)(2,1)S(1)} %add_convert_fusion.g0, bf16[128,512]{1,0:T(8,128)(2,1)S(1)} %collective-permute-done.17.g1, ...), custom_call_target="tpu_custom_call" | custom-call | flops 4831838208 | bytes 6291456 | tf_op jit(solution)/shard_map/finish/pallas_call | solution.py:116
  (49 shorter events, 11.3 us)
Async XLA Ops:
  3.8 11.5 %collective-permute-start.7 = (bf16[128,1536]{1,0:T(8,128)(2,1)S(1)}, bf16[128,1536]{1,0:T(8,128)(2,1)S(1)}, u32[]{:S(2)}, u32[]{:S(2)}) collective-permute-start(bf16[128,1536]{1,0:T(8,128)(2,1)S(1)} %get-tuple-element.41), channel_id=1, source_target_pairs={{0,4},{2,6},{4,0},{6,2},{1,5},{3,7},{5,1},{7,3},{8,12},{10,14},{12... | collective-permute-start | bytes 1179656 | tf_op jit(solution)/shard_map/ppermute | solution.py:30
  7.5 18.0 %collective-permute-start.8 = (bf16[128,1536]{1,0:T(8,128)(2,1)S(1)}, bf16[128,1536]{1,0:T(8,128)(2,1)S(1)}, u32[]{:S(2)}, u32[]{:S(2)}) collective-permute-start(bf16[128,1536]{1,0:T(8,128)(2,1)S(1)} %get-tuple-element.42), channel_id=1, source_target_pairs={{0,2},{2,4},{4,6},{6,0},{1,3},{3,5},{5,7},{7,1},{8,10},{10,12},{12... | collective-permute-start | bytes 1179656 | tf_op jit(solution)/shard_map/ppermute | solution.py:30
  7.8 17.7 %collective-permute-start.9 = (bf16[128,1536]{1,0:T(8,128)(2,1)S(1)}, bf16[128,1536]{1,0:T(8,128)(2,1)S(1)}, u32[]{:S(2)}, u32[]{:S(2)}) collective-permute-start(bf16[128,1536]{1,0:T(8,128)(2,1)S(1)} %get-tuple-element.43), channel_id=1, source_target_pairs={{0,6},{2,0},{4,2},{6,4},{1,7},{3,1},{5,3},{7,5},{8,14},{10,8},{12,... | collective-permute-start | bytes 1179656 | tf_op jit(solution)/shard_map/ppermute | solution.py:30
  10.1 17.0 %collective-permute-start = (bf16[128,1536]{1,0:T(8,128)(2,1)S(1)}, bf16[128,1536]{1,0:T(8,128)(2,1)S(1)}, u32[]{:S(2)}, u32[]{:S(2)}) collective-permute-start(bf16[128,1536]{1,0:T(8,128)(2,1)S(1)} %get-tuple-element.31), channel_id=1, source_target_pairs={{0,32},{16,48},{32,0},{48,16},{1,33},{17,49},{33,1},{49,17},{2,34}... | collective-permute-start | bytes 1179656 | tf_op jit(solution)/shard_map/ppermute | solution.py:30
  13.1 18.1 %collective-permute-start.1 = (bf16[128,1536]{1,0:T(8,128)(2,1)S(1)}, bf16[128,1536]{1,0:T(8,128)(2,1)S(1)}, u32[]{:S(2)}, u32[]{:S(2)}) collective-permute-start(bf16[128,1536]{1,0:T(8,128)(2,1)S(1)} %get-tuple-element.32), channel_id=1, source_target_pairs={{0,16},{16,32},{32,48},{48,0},{1,17},{17,33},{33,49},{49,1},{2,18}... | collective-permute-start | bytes 1179656 | tf_op jit(solution)/shard_map/ppermute | solution.py:30
  15.3 15.8 %collective-permute-start.2 = (bf16[128,1536]{1,0:T(8,128)(2,1)S(1)}, bf16[128,1536]{1,0:T(8,128)(2,1)S(1)}, u32[]{:S(2)}, u32[]{:S(2)}) collective-permute-start(bf16[128,1536]{1,0:T(8,128)(2,1)S(1)} %get-tuple-element.33), channel_id=1, source_target_pairs={{0,48},{16,0},{32,16},{48,32},{1,49},{17,1},{33,17},{49,33},{2,50}... | collective-permute-start | bytes 1179656 | tf_op jit(solution)/shard_map/ppermute | solution.py:30
  26.2 6.6 %collective-permute-start.10 = (bf16[4,128,512]{2,1,0:T(8,128)(2,1)S(1)}, bf16[4,128,512]{2,1,0:T(8,128)(2,1)S(1)}, u32[]{:S(2)}, u32[]{:S(2)}) collective-permute-start(bf16[4,128,512]{2,1,0:T(8,128)(2,1)S(1)} %get-tuple-element.45), channel_id=1, source_target_pairs={{0,1},{1,0},{2,3},{3,2},{4,5},{5,4},{6,7},{7,6},{8,9},{9,8},{10,11... | collective-permute-start | bytes 1572872 | tf_op jit(solution)/shard_map/ppermute | solution.py:40
  31.9 5.6 %collective-permute-start.3 = (bf16[4,128,512]{2,1,0:T(8,128)(2,1)S(1)}, bf16[4,128,512]{2,1,0:T(8,128)(2,1)S(1)}, u32[]{:S(2)}, u32[]{:S(2)}) collective-permute-start(bf16[4,128,512]{2,1,0:T(8,128)(2,1)S(1)} %get-tuple-element.35), channel_id=1, source_target_pairs={{0,1},{1,0},{2,3},{3,2},{4,5},{5,4},{6,7},{7,6},{8,9},{9,8},{10,11... | collective-permute-start | bytes 1572872 | tf_op jit(solution)/shard_map/ppermute | solution.py:40
  32.9 6.7 %collective-permute-start.11 = (bf16[128,512]{1,0:T(8,128)(2,1)S(1)}, bf16[128,512]{1,0:T(8,128)(2,1)S(1)}, u32[]{:S(2)}, u32[]{:S(2)}) collective-permute-start(bf16[128,512]{1,0:T(8,128)(2,1)S(1)} %get-tuple-element.47), channel_id=1, source_target_pairs={{0,32},{16,48},{32,0},{48,16},{1,33},{17,49},{33,1},{49,17},{2,34}... | collective-permute-start | bytes 393224 | tf_op jit(solution)/shard_map/ppermute | solution.py:30
  34.8 8.0 %collective-permute-start.12 = (bf16[128,512]{1,0:T(8,128)(2,1)S(1)}, bf16[128,512]{1,0:T(8,128)(2,1)S(1)}, u32[]{:S(2)}, u32[]{:S(2)}) collective-permute-start(bf16[128,512]{1,0:T(8,128)(2,1)S(1)} %get-tuple-element.48), channel_id=1, source_target_pairs={{0,16},{16,32},{32,48},{48,0},{1,17},{17,33},{33,49},{49,1},{2,18}... | collective-permute-start | bytes 393224 | tf_op jit(solution)/shard_map/ppermute | solution.py:30
  36.0 6.8 %collective-permute-start.13 = (bf16[128,512]{1,0:T(8,128)(2,1)S(1)}, bf16[128,512]{1,0:T(8,128)(2,1)S(1)}, u32[]{:S(2)}, u32[]{:S(2)}) collective-permute-start(bf16[128,512]{1,0:T(8,128)(2,1)S(1)} %get-tuple-element.49), channel_id=1, source_target_pairs={{0,48},{16,0},{32,16},{48,32},{1,49},{17,1},{33,17},{49,33},{2,50}... | collective-permute-start | bytes 393224 | tf_op jit(solution)/shard_map/ppermute | solution.py:30
  37.6 5.8 %collective-permute-start.4 = (bf16[128,512]{1,0:T(8,128)(2,1)S(1)}, bf16[128,512]{1,0:T(8,128)(2,1)S(1)}, u32[]{:S(2)}, u32[]{:S(2)}) collective-permute-start(bf16[128,512]{1,0:T(8,128)(2,1)S(1)} %get-tuple-element.37), channel_id=1, source_target_pairs={{0,4},{2,6},{4,0},{6,2},{1,5},{3,7},{5,1},{7,3},{8,12},{10,14},{12... | collective-permute-start | bytes 393224 | tf_op jit(solution)/shard_map/ppermute | solution.py:30
  37.7 9.3 %collective-permute-start.5 = (bf16[128,512]{1,0:T(8,128)(2,1)S(1)}, bf16[128,512]{1,0:T(8,128)(2,1)S(1)}, u32[]{:S(2)}, u32[]{:S(2)}) collective-permute-start(bf16[128,512]{1,0:T(8,128)(2,1)S(1)} %get-tuple-element.38), channel_id=1, source_target_pairs={{0,2},{2,4},{4,6},{6,0},{1,3},{3,5},{5,7},{7,1},{8,10},{10,12},{12... | collective-permute-start | bytes 393224 | tf_op jit(solution)/shard_map/ppermute | solution.py:30
  39.6 7.4 %collective-permute-start.6 = (bf16[128,512]{1,0:T(8,128)(2,1)S(1)}, bf16[128,512]{1,0:T(8,128)(2,1)S(1)}, u32[]{:S(2)}, u32[]{:S(2)}) collective-permute-start(bf16[128,512]{1,0:T(8,128)(2,1)S(1)} %get-tuple-element.39), channel_id=1, source_target_pairs={{0,6},{2,0},{4,2},{6,4},{1,7},{3,1},{5,3},{7,5},{8,14},{10,8},{12,... | collective-permute-start | bytes 393224 | tf_op jit(solution)/shard_map/ppermute | solution.py:30
  40.5 37.6 %copy-start.5 = (s32[32]{0:T(128)S(1)}, s32[32]{0:T(128)}, u32[]{:S(2)}) copy-start(s32[32]{0:T(128)} %param.10) | copy-start | bytes 388
  47.1 12.0 %collective-permute-start.14 = (bf16[128,512]{1,0:T(8,128)(2,1)S(1)}, bf16[128,512]{1,0:T(8,128)(2,1)S(1)}, u32[]{:S(2)}, u32[]{:S(2)}) collective-permute-start(bf16[128,512]{1,0:T(8,128)(2,1)S(1)} %get-tuple-element.53), channel_id=1, source_target_pairs={{0,200},{64,136},{128,72},{192,8},{8,192},{72,128},{136,64},{200,0... | collective-permute-start | bytes 393224 | tf_op jit(solution)/shard_map/ppermute | solution.py:35
  59.1 4.1 %collective-permute-start.15 = (bf16[128,512]{1,0:T(8,128)(2,1)S(1)}, bf16[128,512]{1,0:T(8,128)(2,1)S(1)}, u32[]{:S(2)}, u32[]{:S(2)}) collective-permute-start(bf16[128,512]{1,0:T(8,128)(2,1)S(1)} %add_convert_fusion.2), channel_id=1, source_target_pairs={{0,64},{64,0},{128,192},{192,128},{8,72},{72,8},{136,200},{200,136... | collective-permute-start | bytes 393224 | tf_op jit(solution)/shard_map/ppermute | solution.py:35
  59.4 9.8 %collective-permute-start.20 = (bf16[3,128,512]{2,1,0:T(8,128)(2,1)S(1)}, bf16[3,128,512]{2,1,0:T(8,128)(2,1)S(1)}, u32[]{:S(2)}, u32[]{:S(2)}) collective-permute-start(bf16[3,128,512]{2,1,0:T(8,128)(2,1)S(1)} %pad_maximum_fusion.p0), channel_id=1, source_target_pairs={{0,2},{2,0},{1,3},{3,1},{4,6},{6,4},{5,7},{7,5},{8,10},{10,8},{9,1... | collective-permute-start | bytes 1179656 | tf_op jit(solution)/shard_map/ppermute | solution.py:40
  63.2 8.3 %collective-permute-start.16 = (bf16[128,512]{1,0:T(8,128)(2,1)S(1)}, bf16[128,512]{1,0:T(8,128)(2,1)S(1)}, u32[]{:S(2)}, u32[]{:S(2)}) collective-permute-start(bf16[128,512]{1,0:T(8,128)(2,1)S(1)} %add_convert_fusion.1), channel_id=1, source_target_pairs={{0,128},{64,192},{128,0},{192,64},{8,136},{72,200},{136,8},{200,72... | collective-permute-start | bytes 393224 | tf_op jit(solution)/shard_map/ppermute | solution.py:35
  64.3 13.7 %collective-permute-start.21 = (bf16[3,128,512]{2,1,0:T(8,128)(2,1)S(1)}, bf16[3,128,512]{2,1,0:T(8,128)(2,1)S(1)}, u32[]{:S(2)}, u32[]{:S(2)}) collective-permute-start(bf16[3,128,512]{2,1,0:T(8,128)(2,1)S(1)} %pad_maximum_fusion.p0), channel_id=1, source_target_pairs={{0,1},{1,0},{2,3},{3,2},{4,5},{5,4},{6,7},{7,6},{8,9},{9,8},{10,11... | collective-permute-start | bytes 1179656 | tf_op jit(solution)/shard_map/ppermute | solution.py:40
  69.2 8.9 %collective-permute-start.22 = (bf16[3,128,512]{2,1,0:T(8,128)(2,1)S(1)}, bf16[3,128,512]{2,1,0:T(8,128)(2,1)S(1)}, u32[]{:S(2)}, u32[]{:S(2)}) collective-permute-start(bf16[3,128,512]{2,1,0:T(8,128)(2,1)S(1)} %collective-permute-done.20.p1), channel_id=1, source_target_pairs={{0,1},{1,0},{2,3},{3,2},{4,5},{5,4},{6,7},{7,6},{8,9},{9,8},{10,11... | collective-permute-start | bytes 1179656 | tf_op jit(solution)/shard_map/ppermute | solution.py:40
  71.6 3.9 %collective-permute-start.17 = (bf16[128,512]{1,0:T(8,128)(2,1)S(1)}, bf16[128,512]{1,0:T(8,128)(2,1)S(1)}, u32[]{:S(2)}, u32[]{:S(2)}) collective-permute-start(bf16[128,512]{1,0:T(8,128)(2,1)S(1)} %add_convert_fusion.g0), channel_id=1, source_target_pairs={{0,2},{2,0},{1,3},{3,1},{4,6},{6,4},{5,7},{7,5},{8,10},{10,8},{9,1... | collective-permute-start | bytes 393224 | tf_op jit(solution)/shard_map/ppermute | solution.py:40
  71.7 6.6 %collective-permute-start.18 = (bf16[128,512]{1,0:T(8,128)(2,1)S(1)}, bf16[128,512]{1,0:T(8,128)(2,1)S(1)}, u32[]{:S(2)}, u32[]{:S(2)}) collective-permute-start(bf16[128,512]{1,0:T(8,128)(2,1)S(1)} %add_convert_fusion.g0), channel_id=1, source_target_pairs={{0,1},{1,0},{2,3},{3,2},{4,5},{5,4},{6,7},{7,6},{8,9},{9,8},{10,11... | collective-permute-start | bytes 393224 | tf_op jit(solution)/shard_map/ppermute | solution.py:40
  75.5 3.6 %collective-permute-start.19 = (bf16[128,512]{1,0:T(8,128)(2,1)S(1)}, bf16[128,512]{1,0:T(8,128)(2,1)S(1)}, u32[]{:S(2)}, u32[]{:S(2)}) collective-permute-start(bf16[128,512]{1,0:T(8,128)(2,1)S(1)} %collective-permute-done.17.g1), channel_id=1, source_target_pairs={{0,1},{1,0},{2,3},{3,2},{4,5},{5,4},{6,7},{7,6},{8,9},{9,8},{10,11... | collective-permute-start | bytes 393224 | tf_op jit(solution)/shard_map/ppermute | solution.py:40
  (5 other events, 52.5 us)

commit v5 on v4

--- a/solution.py
+++ b/solution.py
@@ -76,39 +76,48 @@
         scaling = 2.5 / jnp.sqrt(total + tiny_term)
         return scaling * a, jnp.sqrt(jnp.sqrt(scaling))
 
+    def both(f, *pairs):
+        return f(*(p[0] for p in pairs)), f(*(p[1] for p in pairs))
+
     def advance(m):
-        mb = narrow(m)
-        u = narrow(dot(mb, mb) * 0.0625 - 0.625 * m)
-        w = dot(u, mb)
-        return 2.44140625 * m + 3.125 * w + dot(u, narrow(w))
-
-    def root_of(m, m_rows, m2, m2_rows, m3, m3_rows, row0, scale):
-        y = dot(narrow(m_rows), narrow(m2)) * 0.0625 - 0.3125 * (m_rows + m2_rows)
-        r = lax.broadcasted_iota(jnp.int32, m_rows.shape, 0) + row0
-        c = lax.broadcasted_iota(jnp.int32, m_rows.shape, 1)
-        out = jnp.where(r == c, 1.953125, 0.0) + 1.25 * y - 0.390625 * m3_rows
-        out = out - 0.25 * dot(narrow(y), narrow(m3))
-        return narrow(scale * out)
-
-    m, scale = refresh_stats(1, dot(g, g, (0, 0)))
-    m2 = advance(m)
-    m3 = advance(m2)
-    root = root_of(m, m, m2, m2, m3, m3, 0, scale)
-    root = jnp.where(fresh[1] == 1, root, old_right[...])
+        mb = both(narrow, m)
+        square = both(dot, mb, mb)
+        u = both(lambda s, v: narrow(s * 0.0625 - 0.625 * v), square, m)
+        w = both(dot, u, mb)
+        wb = both(narrow, w)
+        last = both(dot, u, wb)
+        return both(lambda v, w, t: 2.44140625 * v + 3.125 * w + t, m, w, last), mb
+
+    def spread(shape, row0):
+        r = lax.broadcasted_iota(jnp.int32, shape, 0) + row0
+        c = lax.broadcasted_iota(jnp.int32, shape, 1)
+        return jnp.where(r == c, 1.953125, 0.0)
+
+    grams = (dot(g, g, (1, 1)), dot(g, g, (0, 0)))
+    m, scale = zip(refresh_stats(0, grams[0]), refresh_stats(1, grams[1]))
+    work[0] = m[0]
+    m2, mb = advance(m)
+    work[1] = m2[0]
+    m3, m2b = advance(m2)
+    work[2] = m3[0]
+    m3b = both(narrow, m3)
+    rows = [work[i, own, :] for i in range(3)]
+    first = (rows[0], m[1]), (rows[1], m2[1]), (rows[2], m3[1])
+    product = dot(narrow(rows[0]), m2b[0]), dot(mb[1], m2b[1])
+    y = both(lambda p, v, v2: p * 0.0625 - 0.3125 * (v + v2), product, first[0], first[1])
+    product = both(dot, both(narrow, y), m3b)
+    diagonal = spread((ROWS, B), quarter * ROWS), spread((B, B), 0)
+    out = both(
+        lambda e, v, v3, p, s: narrow(s * (e + 1.25 * v - 0.390625 * v3 - 0.25 * p)),
+        diagonal, y, first[2], product, scale,
+    )
+    root = jnp.where(fresh[1] == 1, out[1], old_right[...])
+    mixed = narrow(dot(g, root))
     right[...] = root
     new_roots[1] = right[own, :]
-    mixed = narrow(dot(g, root))
-
-    m, scale = refresh_stats(0, dot(g, g, (1, 1)))
-    work[0] = m
-    m2 = advance(m)
-    work[1] = m2
-    m3 = advance(m2)
-    work[2] = m3
-    rows = root_of(m, work[0, own, :], m2, work[1, own, :], m3, work[2, own, :], quarter * ROWS, scale)
-    rows = jnp.where(fresh[0] == 1, rows, left_old[...])
-    new_roots[0] = rows
-    update[...] = narrow(dot(rows, mixed) * math.sqrt(B))
+    left = jnp.where(fresh[0] == 1, out[0], left_old[...])
+    new_roots[0] = left
+    update[...] = narrow(dot(left, mixed) * math.sqrt(B))
 
 
 def finish(decays, refresh, *arrays):
@@ -139,7 +148,7 @@
 
 
 def cut_kernel(cotangents, activations, *rest):
-    outs, sem = rest[:-1], rest[-1]
+    outs, held, sem = rest[:-2], rest[-2], rest[-1]
     at = places()
     copies = []
 
@@ -147,29 +156,33 @@
         copies.append(pltpu.make_async_copy(src, dst, sem.at[len(copies)]))
         copies[-1].start()
 
+    copy(activations, held)
     for i, k in enumerate((2, 1, 3, 0)):
         t = lax.rem(at["y"] + k, 4)
         copy(cotangents.at[:, pl.ds(pl.multiple_of(t * 4 * B, 4 * B), 2 * B)], outs[2 * i].at[:, : 2 * B])
-        copy(activations, outs[2 * i].at[:, 2 * B :])
         t = lax.rem(at["x_hi"] * 2 + at["x_lo"] + k, 4)
         for j in range(4):
             start = pl.multiple_of(t * (B // 2) + (4 * j + 2) * B, B // 2)
             here = slice(j * (B // 2), (j + 1) * (B // 2))
             copy(cotangents.at[:, pl.ds(start, B // 2)], outs[2 * i + 1].at[:, here])
-        copy(activations, outs[2 * i + 1].at[:, 2 * B :])
-    for c in copies:
+    copies[0].wait()
+    for out in outs:
+        out[:, 2 * B :] = held[...]
+    for c in copies[1:]:
         c.wait()
 
 
 def cut(cotangents, activations):
     free = pl.BlockSpec(memory_space=pltpu.HBM)
+    cotangents = pltpu.with_memory_space_constraint(cotangents, pltpu.HBM)
+    activations = pltpu.with_memory_space_constraint(activations, pltpu.HBM)
     return pl.pallas_call(
         cut_kernel,
         name="cut",
         out_shape=(jax.ShapeDtypeStruct((TOKENS, WIDE), jnp.bfloat16),) * 8,
         in_specs=[free, free],
         out_specs=(VMEM,) * 8,
-        scratch_shapes=[pltpu.SemaphoreType.DMA((28,))],
+        scratch_shapes=[pltpu.VMEM((TOKENS, B), jnp.bfloat16), pltpu.SemaphoreType.DMA((21,))],
         compiler_params=pltpu.CompilerParams(vmem_limit_bytes=4 << 20),
         cost_estimate=pl.CostEstimate(flops=0, bytes_accessed=6 << 20, transcendentals=0),
     )(cotangents, activations)
@@ -292,8 +305,6 @@
     for i, k in enumerate((2, 1, 3)):
         y_parts.append(shift(pieces[2 * i], "y", k))
         x_parts.append(shift(pieces[2 * i + 1], X, k))
-    pack = jnp.concatenate([narrow(statistics), roots[1:]], axis=0)
-    pack_core = partner(pack, "core")
 
     y_keep, y_send = product(y_parts)
     y_came = partner(y_send, "core")
@@ -307,10 +318,13 @@
         x_sums.append(shift(x_sends[i], "y", k))
 
     keep, send = plane_sum(y_sums, x_sums)
+    pack = jnp.concatenate([narrow(statistics), roots[1:]], axis=0)
     keep, send, pack = lax.optimization_barrier((keep, send, pack))
     part = rounded(keep + swap_z(send, 7).astype(jnp.float32))
     pack_x = partner(pack, "x_lo")
+    part, pack_core = lax.optimization_barrier((part, partner(pack, "core")))
     part = rounded(part.astype(jnp.float32) + swap_z(part, 1).astype(jnp.float32))
+    part, pack_x = lax.optimization_barrier((part, pack_x))
     part = rounded(part.astype(jnp.float32) + swap_z(part, 2).astype(jnp.float32))
     part_x, part_core = partner(part, "x_lo"), partner(part, "core")
     grads = (part, part_x, part_core, partner(part_x, "core"))

time: 87.5 us -> 86.3 us (0.986)
  waiting for transfers between devices: 36.7 us -> 39.7 us
  local copies, waits for them, and re-layouts: 2.53 us -> 0.04 us
  starting transfers between devices: 36.1 us -> 34.3 us
    ppermute x3, waiting for transfers between devices: 10.5 us -> 16.3 us  [swap_z(): return lax.ppermute(x, Z, [(spot[i], spot[i ^ bits]) for i in range(8)])]
    ppermute x8, waiting for transfers between devices: 6.08 us -> 3.32 us  [partner(): return lax.ppermute(x, axis, [(i, i ^ bits) for i in range(n)])]
    unnamed x12 -> x8, local copies, waits for them, and re-layouts: 2.51 us -> 0.02 us
    ppermute x8, starting transfers between devices: 9.79 us -> 8.01 us  [partner(): return lax.ppermute(x, axis, [(i, i ^ bits) for i in range(n)])]
    pallas_call x1, Pallas kernels: 0.67 us -> 1.75 us  [cut(): pl.pallas_call(cut_kernel, name='cut', out_shape=(jax.ShapeDtypeStruct((T...]
    pallas_call x1, Pallas kernels: 8.31 us -> 7.39 us  [finish(): pl.pallas_call(finish_kernel, name='finish', out_shape=(jax.ShapeDtypeStr...]
  transfers between devices with their start and end apart: 23 -> 23, of which waited for: 13 -> 12; matrix products, arithmetic and copies ran while one was open for 0% -> 0% of each run, Pallas kernels for 2% -> 2%
where the time goes in v5:
time: 86.3 us; the launch traced here: 86.2 us
  waiting for transfers between devices  39.7 us (46%)
  starting transfers between devices  34.3 us (40%)
  Pallas kernels  11.2 us (13%)
    ppermute x12, waiting for transfers between devices, shift(): return lax.ppermute(x, axis, [(i, (i + by) % n) for i in range(n)])  20.1 us
    ppermute x12, starting transfers between devices, shift(): return lax.ppermute(x, axis, [(i, (i + by) % n) for i in range(n)])  19.3 us
    ppermute x3, waiting for transfers between devices, swap_z(): return lax.ppermute(x, Z, [(spot[i], spot[i ^ bits]) for i in range(8)])  16.3 us
    ppermute x8, starting transfers between devices, partner(): return lax.ppermute(x, axis, [(i, i ^ bits) for i in range(n)])  8.01 us
    pallas_call x1, Pallas kernels, finish(): pl.pallas_call(finish_kernel, name='finish', out_shape=(jax.ShapeDtypeStr...  7.39 us
    ppermute x3, starting transfers between devices, swap_z(): return lax.ppermute(x, Z, [(spot[i], spot[i ^ bits]) for i in range(8)])  6.94 us
    ppermute x8, waiting for transfers between devices, partner(): return lax.ppermute(x, axis, [(i, i ^ bits) for i in range(n)])  3.32 us
    pallas_call x1, Pallas kernels, cut(): pl.pallas_call(cut_kernel, name='cut', out_shape=(jax.ShapeDtypeStruct((T...  1.75 us
  transfers between devices with their start and end apart: 23, of which 12 were waited for; matrix products, arithmetic and copies ran while one was open for 0% of the time, Pallas kernels for 2%

profile of v5, /device:TPU:1, one launch (start us, length us, event | category | flops | bytes accessed | tf_op | source)
XLA Modules:
  0.0 86.2 jit_solution(17860833777728440596)
XLA Ops:
  0.6 1.8 %cut.1 = (bf16[128,1536]{1,0:T(8,128)(2,1)S(1)}, bf16[128,1536]{1,0:T(8,128)(2,1)S(1)}, bf16[128,1536]{1,0:T(8,128)(2,1)S(1)}, bf16[128,1536]{1,0:T(8,128)(2,1)S...) custom-call(bf16[128,8192]{1,0:T(8,128)(2,1)} %cotangents.1, ...), custom_call_target="tpu_custom_call" | custom-call | bytes 6291456 | tf_op jit(solution)/shard_map/cut/pallas_call | solution.py:179
  2.4 3.7 %collective-permute-start.7 = (bf16[128,1536]{1,0:T(8,128)(2,1)S(1)}, bf16[128,1536]{1,0:T(8,128)(2,1)S(1)}, u32[]{:S(2)}, u32[]{:S(2)}) collective-permute-start(bf16[128,1536]{1,0:T(8,128)(2,1)S(1)} %get-tuple-element.45), channel_id=1, source_target_pairs={{0,4},{2,6},{4,0},{6,2},{1,5},{3,7},{5,1},{7,3},{8,12},{10,14},{12... | collective-permute-start | bytes 1179656 | tf_op jit(solution)/shard_map/ppermute | solution.py:30
  6.4 2.4 %collective-permute-start.9 = (bf16[128,1536]{1,0:T(8,128)(2,1)S(1)}, bf16[128,1536]{1,0:T(8,128)(2,1)S(1)}, u32[]{:S(2)}, u32[]{:S(2)}) collective-permute-start(bf16[128,1536]{1,0:T(8,128)(2,1)S(1)} %get-tuple-element.47), channel_id=1, source_target_pairs={{0,6},{2,0},{4,2},{6,4},{1,7},{3,1},{5,3},{7,5},{8,14},{10,8},{12,... | collective-permute-start | bytes 1179656 | tf_op jit(solution)/shard_map/ppermute | solution.py:30
  8.7 2.9 %collective-permute-start = (bf16[128,1536]{1,0:T(8,128)(2,1)S(1)}, bf16[128,1536]{1,0:T(8,128)(2,1)S(1)}, u32[]{:S(2)}, u32[]{:S(2)}) collective-permute-start(bf16[128,1536]{1,0:T(8,128)(2,1)S(1)} %get-tuple-element.35), channel_id=1, source_target_pairs={{0,32},{16,48},{32,0},{48,16},{1,33},{17,49},{33,1},{49,17},{2,34}... | collective-permute-start | bytes 1179656 | tf_op jit(solution)/shard_map/ppermute | solution.py:30
  12.0 1.9 %collective-permute-done.7.p1 = bf16[128,1536]{1,0:T(8,128)(2,1)S(1)} collective-permute-done((bf16[128,1536]{1,0:T(8,128)(2,1)S(1)}, bf16[128,1536]{1,0:T(8,128)(2,1)S(1)}, u32[]{:S(2)}, u32[]{:S(2)}) %collective-permute-start.7) | collective-permute-done | bytes 393248 | tf_op jit(solution)/shard_map/ppermute | solution.py:30
  13.9 3.6 %collective-permute-start.2 = (bf16[128,1536]{1,0:T(8,128)(2,1)S(1)}, bf16[128,1536]{1,0:T(8,128)(2,1)S(1)}, u32[]{:S(2)}, u32[]{:S(2)}) collective-permute-start(bf16[128,1536]{1,0:T(8,128)(2,1)S(1)} %get-tuple-element.37), channel_id=1, source_target_pairs={{0,48},{16,0},{32,16},{48,32},{1,49},{17,1},{33,17},{49,33},{2,50}... | collective-permute-start | bytes 1179656 | tf_op jit(solution)/shard_map/ppermute | solution.py:30
  17.6 6.5 %collective-permute-done.8.p2 = bf16[128,1536]{1,0:T(8,128)(2,1)S(1)} collective-permute-done((bf16[128,1536]{1,0:T(8,128)(2,1)S(1)}, bf16[128,1536]{1,0:T(8,128)(2,1)S(1)}, u32[]{:S(2)}, u32[]{:S(2)}) %collective-permute-start.8) | collective-permute-done | bytes 393248 | tf_op jit(solution)/shard_map/ppermute | solution.py:30
  25.7 4.0 %collective-permute-done.1.p2 = bf16[128,1536]{1,0:T(8,128)(2,1)S(1)} collective-permute-done((bf16[128,1536]{1,0:T(8,128)(2,1)S(1)}, bf16[128,1536]{1,0:T(8,128)(2,1)S(1)}, u32[]{:S(2)}, u32[]{:S(2)}) %collective-permute-start.1) | collective-permute-done | bytes 393248 | tf_op jit(solution)/shard_map/ppermute | solution.py:30
  31.5 1.9 %collective-permute-start.11 = (bf16[128,512]{1,0:T(8,128)(2,1)S(1)}, bf16[128,512]{1,0:T(8,128)(2,1)S(1)}, u32[]{:S(2)}, u32[]{:S(2)}) collective-permute-start(bf16[128,512]{1,0:T(8,128)(2,1)S(1)} %get-tuple-element.51), channel_id=1, source_target_pairs={{0,32},{16,48},{32,0},{48,16},{1,33},{17,49},{33,1},{49,17},{2,34}... | collective-permute-start | bytes 393224 | tf_op jit(solution)/shard_map/ppermute | solution.py:30
  33.4 1.2 %collective-permute-start.12 = (bf16[128,512]{1,0:T(8,128)(2,1)S(1)}, bf16[128,512]{1,0:T(8,128)(2,1)S(1)}, u32[]{:S(2)}, u32[]{:S(2)}) collective-permute-start(bf16[128,512]{1,0:T(8,128)(2,1)S(1)} %get-tuple-element.52), channel_id=1, source_target_pairs={{0,16},{16,32},{32,48},{48,0},{1,17},{17,33},{33,49},{49,1},{2,18}... | collective-permute-start | bytes 393224 | tf_op jit(solution)/shard_map/ppermute | solution.py:30
  34.6 1.5 %collective-permute-start.13 = (bf16[128,512]{1,0:T(8,128)(2,1)S(1)}, bf16[128,512]{1,0:T(8,128)(2,1)S(1)}, u32[]{:S(2)}, u32[]{:S(2)}) collective-permute-start(bf16[128,512]{1,0:T(8,128)(2,1)S(1)} %get-tuple-element.53), channel_id=1, source_target_pairs={{0,48},{16,0},{32,16},{48,32},{1,49},{17,1},{33,17},{49,33},{2,50}... | collective-permute-start | bytes 393224 | tf_op jit(solution)/shard_map/ppermute | solution.py:30
  36.8 1.4 %collective-permute-done.11.x1 = bf16[128,512]{1,0:T(8,128)(2,1)S(1)} collective-permute-done((bf16[128,512]{1,0:T(8,128)(2,1)S(1)}, bf16[128,512]{1,0:T(8,128)(2,1)S(1)}, u32[]{:S(2)}, u32[]{:S(2)}) %collective-permute-start.11) | collective-permute-done | bytes 131104 | tf_op jit(solution)/shard_map/ppermute | solution.py:30
  39.2 2.2 %collective-permute-done.12.x2 = bf16[128,512]{1,0:T(8,128)(2,1)S(1)} collective-permute-done((bf16[128,512]{1,0:T(8,128)(2,1)S(1)}, bf16[128,512]{1,0:T(8,128)(2,1)S(1)}, u32[]{:S(2)}, u32[]{:S(2)}) %collective-permute-start.12) | collective-permute-done | bytes 131104 | tf_op jit(solution)/shard_map/ppermute | solution.py:30
  42.0 3.6 %collective-permute-done.5.y2 = bf16[128,512]{1,0:T(8,128)(2,1)S(1)} collective-permute-done((bf16[128,512]{1,0:T(8,128)(2,1)S(1)}, bf16[128,512]{1,0:T(8,128)(2,1)S(1)}, u32[]{:S(2)}, u32[]{:S(2)}) %collective-permute-start.5) | collective-permute-done | bytes 131104 | tf_op jit(solution)/shard_map/ppermute | solution.py:30
  46.5 5.6 %collective-permute-start.14 = (bf16[128,512]{1,0:T(8,128)(2,1)S(1)}, bf16[128,512]{1,0:T(8,128)(2,1)S(1)}, u32[]{:S(2)}, u32[]{:S(2)}) collective-permute-start(bf16[128,512]{1,0:T(8,128)(2,1)S(1)} %get-tuple-element.57), channel_id=1, source_target_pairs={{0,200},{64,136},{128,72},{192,8},{8,192},{72,128},{136,64},{200,0... | collective-permute-start | bytes 393224 | tf_op jit(solution)/shard_map/ppermute | solution.py:35
  52.1 6.5 %collective-permute-done.14 = bf16[128,512]{1,0:T(8,128)(2,1)S(1)} collective-permute-done((bf16[128,512]{1,0:T(8,128)(2,1)S(1)}, bf16[128,512]{1,0:T(8,128)(2,1)S(1)}, u32[]{:S(2)}, u32[]{:S(2)}) %collective-permute-start.14) | collective-permute-done | bytes 131104 | tf_op jit(solution)/shard_map/ppermute | solution.py:35
  58.7 4.2 %collective-permute-done.16 = bf16[128,512]{1,0:T(8,128)(2,1)S(1)} collective-permute-done((bf16[128,512]{1,0:T(8,128)(2,1)S(1)}, bf16[128,512]{1,0:T(8,128)(2,1)S(1)}, u32[]{:S(2)}, u32[]{:S(2)}) %collective-permute-start.16) | collective-permute-done | bytes 131104 | tf_op jit(solution)/shard_map/ppermute | solution.py:35
  63.0 1.3 %collective-permute-start.18 = (bf16[128,512]{1,0:T(8,128)(2,1)S(1)}, bf16[128,512]{1,0:T(8,128)(2,1)S(1)}, u32[]{:S(2)}, u32[]{:S(2)}) collective-permute-start(bf16[128,512]{1,0:T(8,128)(2,1)S(1)} %add_convert_fusion.1), channel_id=1, source_target_pairs={{0,128},{64,192},{128,0},{192,64},{8,136},{72,200},{136,8},{200,72... | collective-permute-start | bytes 393224 | tf_op jit(solution)/shard_map/ppermute | solution.py:35
  64.3 1.7 %collective-permute-start.22 = (bf16[3,128,512]{2,1,0:T(8,128)(2,1)S(1)}, bf16[3,128,512]{2,1,0:T(8,128)(2,1)S(1)}, u32[]{:S(2)}, u32[]{:S(2)}) collective-permute-start(bf16[3,128,512]{2,1,0:T(8,128)(2,1)S(1)} %collective-permute-done.17.p1), channel_id=1, source_target_pairs={{0,1},{1,0},{2,3},{3,2},{4,5},{5,4},{6,7},{7,6},{8,9},{9,8},{10,11... | collective-permute-start | bytes 1179656 | tf_op jit(solution)/shard_map/ppermute | solution.py:40
  65.9 5.6 %collective-permute-done.18 = bf16[128,512]{1,0:T(8,128)(2,1)S(1)} collective-permute-done((bf16[128,512]{1,0:T(8,128)(2,1)S(1)}, bf16[128,512]{1,0:T(8,128)(2,1)S(1)}, u32[]{:S(2)}, u32[]{:S(2)}) %collective-permute-start.18) | collective-permute-done | bytes 131104 | tf_op jit(solution)/shard_map/ppermute | solution.py:35
  71.6 1.3 %collective-permute-start.20 = (bf16[128,512]{1,0:T(8,128)(2,1)S(1)}, bf16[128,512]{1,0:T(8,128)(2,1)S(1)}, u32[]{:S(2)}, u32[]{:S(2)}) collective-permute-start(bf16[128,512]{1,0:T(8,128)(2,1)S(1)} %add_convert_fusion.g0), channel_id=1, source_target_pairs={{0,1},{1,0},{2,3},{3,2},{4,5},{5,4},{6,7},{7,6},{8,9},{9,8},{10,11... | collective-permute-start | bytes 393224 | tf_op jit(solution)/shard_map/ppermute | solution.py:40
  72.9 2.5 %collective-permute-done.19.g1 = bf16[128,512]{1,0:T(8,128)(2,1)S(1)} collective-permute-done((bf16[128,512]{1,0:T(8,128)(2,1)S(1)}, bf16[128,512]{1,0:T(8,128)(2,1)S(1)}, u32[]{:S(2)}, u32[]{:S(2)}) %collective-permute-start.19) | collective-permute-done | bytes 131104 | tf_op jit(solution)/shard_map/ppermute | solution.py:40
  75.5 2.3 %collective-permute-start.21 = (bf16[128,512]{1,0:T(8,128)(2,1)S(1)}, bf16[128,512]{1,0:T(8,128)(2,1)S(1)}, u32[]{:S(2)}, u32[]{:S(2)}) collective-permute-start(bf16[128,512]{1,0:T(8,128)(2,1)S(1)} %collective-permute-done.19.g1), channel_id=1, source_target_pairs={{0,1},{1,0},{2,3},{3,2},{4,5},{5,4},{6,7},{7,6},{8,9},{9,8},{10,11... | collective-permute-start | bytes 393224 | tf_op jit(solution)/shard_map/ppermute | solution.py:40
  78.8 7.4 %finish.1 = (bf16[128,512]{1,0:T(8,128)(2,1)}, f32[2,128,512]{2,1,0:T(8,128)}, bf16[2,128,512]{2,1,0:T(8,128)(2,1)}) custom-call(f32[32]{0:T(128)S(1)} %convert_power_fusion.decays, s32[32]{0:T(128)S(1)} %copy-done.1, bf16[128,512]{1,0:T(8,128)(2,1)S(1)} %add_convert_fusion.g0, bf16[128,512]{1,0:T(8,128)(2,1)S(1)} %collective-permute-done.19.g1, ...), custom_call_target="tpu_custom_call" | custom-call | flops 4831838208 | bytes 6291456 | tf_op jit(solution)/shard_map/finish/pallas_call | solution.py:125
  (45 shorter events, 8.6 us)
Async XLA Ops:
  2.4 11.5 %collective-permute-start.7 = (bf16[128,1536]{1,0:T(8,128)(2,1)S(1)}, bf16[128,1536]{1,0:T(8,128)(2,1)S(1)}, u32[]{:S(2)}, u32[]{:S(2)}) collective-permute-start(bf16[128,1536]{1,0:T(8,128)(2,1)S(1)} %get-tuple-element.45), channel_id=1, source_target_pairs={{0,4},{2,6},{4,0},{6,2},{1,5},{3,7},{5,1},{7,3},{8,12},{10,14},{12... | collective-permute-start | bytes 1179656 | tf_op jit(solution)/shard_map/ppermute | solution.py:30
  6.1 18.0 %collective-permute-start.8 = (bf16[128,1536]{1,0:T(8,128)(2,1)S(1)}, bf16[128,1536]{1,0:T(8,128)(2,1)S(1)}, u32[]{:S(2)}, u32[]{:S(2)}) collective-permute-start(bf16[128,1536]{1,0:T(8,128)(2,1)S(1)} %get-tuple-element.46), channel_id=1, source_target_pairs={{0,2},{2,4},{4,6},{6,0},{1,3},{3,5},{5,7},{7,1},{8,10},{10,12},{12... | collective-permute-start | bytes 1179656 | tf_op jit(solution)/shard_map/ppermute | solution.py:30
  6.4 17.7 %collective-permute-start.9 = (bf16[128,1536]{1,0:T(8,128)(2,1)S(1)}, bf16[128,1536]{1,0:T(8,128)(2,1)S(1)}, u32[]{:S(2)}, u32[]{:S(2)}) collective-permute-start(bf16[128,1536]{1,0:T(8,128)(2,1)S(1)} %get-tuple-element.47), channel_id=1, source_target_pairs={{0,6},{2,0},{4,2},{6,4},{1,7},{3,1},{5,3},{7,5},{8,14},{10,8},{12,... | collective-permute-start | bytes 1179656 | tf_op jit(solution)/shard_map/ppermute | solution.py:30
  8.7 17.0 %collective-permute-start = (bf16[128,1536]{1,0:T(8,128)(2,1)S(1)}, bf16[128,1536]{1,0:T(8,128)(2,1)S(1)}, u32[]{:S(2)}, u32[]{:S(2)}) collective-permute-start(bf16[128,1536]{1,0:T(8,128)(2,1)S(1)} %get-tuple-element.35), channel_id=1, source_target_pairs={{0,32},{16,48},{32,0},{48,16},{1,33},{17,49},{33,1},{49,17},{2,34}... | collective-permute-start | bytes 1179656 | tf_op jit(solution)/shard_map/ppermute | solution.py:30
  11.6 18.1 %collective-permute-start.1 = (bf16[128,1536]{1,0:T(8,128)(2,1)S(1)}, bf16[128,1536]{1,0:T(8,128)(2,1)S(1)}, u32[]{:S(2)}, u32[]{:S(2)}) collective-permute-start(bf16[128,1536]{1,0:T(8,128)(2,1)S(1)} %get-tuple-element.36), channel_id=1, source_target_pairs={{0,16},{16,32},{32,48},{48,0},{1,17},{17,33},{33,49},{49,1},{2,18}... | collective-permute-start | bytes 1179656 | tf_op jit(solution)/shard_map/ppermute | solution.py:30
  13.9 15.8 %collective-permute-start.2 = (bf16[128,1536]{1,0:T(8,128)(2,1)S(1)}, bf16[128,1536]{1,0:T(8,128)(2,1)S(1)}, u32[]{:S(2)}, u32[]{:S(2)}) collective-permute-start(bf16[128,1536]{1,0:T(8,128)(2,1)S(1)} %get-tuple-element.37), channel_id=1, source_target_pairs={{0,48},{16,0},{32,16},{48,32},{1,49},{17,1},{33,17},{49,33},{2,50}... | collective-permute-start | bytes 1179656 | tf_op jit(solution)/shard_map/ppermute | solution.py:30
  24.8 6.6 %collective-permute-start.10 = (bf16[4,128,512]{2,1,0:T(8,128)(2,1)S(1)}, bf16[4,128,512]{2,1,0:T(8,128)(2,1)S(1)}, u32[]{:S(2)}, u32[]{:S(2)}) collective-permute-start(bf16[4,128,512]{2,1,0:T(8,128)(2,1)S(1)} %get-tuple-element.49), channel_id=1, source_target_pairs={{0,1},{1,0},{2,3},{3,2},{4,5},{5,4},{6,7},{7,6},{8,9},{9,8},{10,11... | collective-permute-start | bytes 1572872 | tf_op jit(solution)/shard_map/ppermute | solution.py:40
  30.5 5.6 %collective-permute-start.3 = (bf16[4,128,512]{2,1,0:T(8,128)(2,1)S(1)}, bf16[4,128,512]{2,1,0:T(8,128)(2,1)S(1)}, u32[]{:S(2)}, u32[]{:S(2)}) collective-permute-start(bf16[4,128,512]{2,1,0:T(8,128)(2,1)S(1)} %get-tuple-element.39), channel_id=1, source_target_pairs={{0,1},{1,0},{2,3},{3,2},{4,5},{5,4},{6,7},{7,6},{8,9},{9,8},{10,11... | collective-permute-start | bytes 1572872 | tf_op jit(solution)/shard_map/ppermute | solution.py:40
  31.5 6.7 %collective-permute-start.11 = (bf16[128,512]{1,0:T(8,128)(2,1)S(1)}, bf16[128,512]{1,0:T(8,128)(2,1)S(1)}, u32[]{:S(2)}, u32[]{:S(2)}) collective-permute-start(bf16[128,512]{1,0:T(8,128)(2,1)S(1)} %get-tuple-element.51), channel_id=1, source_target_pairs={{0,32},{16,48},{32,0},{48,16},{1,33},{17,49},{33,1},{49,17},{2,34}... | collective-permute-start | bytes 393224 | tf_op jit(solution)/shard_map/ppermute | solution.py:30
  33.4 8.0 %collective-permute-start.12 = (bf16[128,512]{1,0:T(8,128)(2,1)S(1)}, bf16[128,512]{1,0:T(8,128)(2,1)S(1)}, u32[]{:S(2)}, u32[]{:S(2)}) collective-permute-start(bf16[128,512]{1,0:T(8,128)(2,1)S(1)} %get-tuple-element.52), channel_id=1, source_target_pairs={{0,16},{16,32},{32,48},{48,0},{1,17},{17,33},{33,49},{49,1},{2,18}... | collective-permute-start | bytes 393224 | tf_op jit(solution)/shard_map/ppermute | solution.py:30
  34.6 6.8 %collective-permute-start.13 = (bf16[128,512]{1,0:T(8,128)(2,1)S(1)}, bf16[128,512]{1,0:T(8,128)(2,1)S(1)}, u32[]{:S(2)}, u32[]{:S(2)}) collective-permute-start(bf16[128,512]{1,0:T(8,128)(2,1)S(1)} %get-tuple-element.53), channel_id=1, source_target_pairs={{0,48},{16,0},{32,16},{48,32},{1,49},{17,1},{33,17},{49,33},{2,50}... | collective-permute-start | bytes 393224 | tf_op jit(solution)/shard_map/ppermute | solution.py:30
  36.2 5.8 %collective-permute-start.4 = (bf16[128,512]{1,0:T(8,128)(2,1)S(1)}, bf16[128,512]{1,0:T(8,128)(2,1)S(1)}, u32[]{:S(2)}, u32[]{:S(2)}) collective-permute-start(bf16[128,512]{1,0:T(8,128)(2,1)S(1)} %get-tuple-element.41), channel_id=1, source_target_pairs={{0,4},{2,6},{4,0},{6,2},{1,5},{3,7},{5,1},{7,3},{8,12},{10,14},{12... | collective-permute-start | bytes 393224 | tf_op jit(solution)/shard_map/ppermute | solution.py:30
  36.3 9.3 %collective-permute-start.5 = (bf16[128,512]{1,0:T(8,128)(2,1)S(1)}, bf16[128,512]{1,0:T(8,128)(2,1)S(1)}, u32[]{:S(2)}, u32[]{:S(2)}) collective-permute-start(bf16[128,512]{1,0:T(8,128)(2,1)S(1)} %get-tuple-element.42), channel_id=1, source_target_pairs={{0,2},{2,4},{4,6},{6,0},{1,3},{3,5},{5,7},{7,1},{8,10},{10,12},{12... | collective-permute-start | bytes 393224 | tf_op jit(solution)/shard_map/ppermute | solution.py:30
  38.2 7.4 %collective-permute-start.6 = (bf16[128,512]{1,0:T(8,128)(2,1)S(1)}, bf16[128,512]{1,0:T(8,128)(2,1)S(1)}, u32[]{:S(2)}, u32[]{:S(2)}) collective-permute-start(bf16[128,512]{1,0:T(8,128)(2,1)S(1)} %get-tuple-element.43), channel_id=1, source_target_pairs={{0,6},{2,0},{4,2},{6,4},{1,7},{3,1},{5,3},{7,5},{8,14},{10,8},{12,... | collective-permute-start | bytes 393224 | tf_op jit(solution)/shard_map/ppermute | solution.py:30
  39.1 38.7 %copy-start.3 = (s32[32]{0:T(128)S(1)}, s32[32]{0:T(128)}, u32[]{:S(2)}) copy-start(s32[32]{0:T(128)} %param.10) | copy-start | bytes 388
  45.7 12.9 %collective-permute-start.15 = (bf16[3,128,512]{2,1,0:T(8,128)(2,1)S(1)}, bf16[3,128,512]{2,1,0:T(8,128)(2,1)S(1)}, u32[]{:S(2)}, u32[]{:S(2)}) collective-permute-start(bf16[3,128,512]{2,1,0:T(8,128)(2,1)S(1)} %pad_maximum_fusion.p0), channel_id=1, source_target_pairs={{0,1},{1,0},{2,3},{3,2},{4,5},{5,4},{6,7},{7,6},{8,9},{9,8},{10,11... | collective-permute-start | bytes 1179656 | tf_op jit(solution)/shard_map/ppermute | solution.py:40
  46.5 12.1 %collective-permute-start.14 = (bf16[128,512]{1,0:T(8,128)(2,1)S(1)}, bf16[128,512]{1,0:T(8,128)(2,1)S(1)}, u32[]{:S(2)}, u32[]{:S(2)}) collective-permute-start(bf16[128,512]{1,0:T(8,128)(2,1)S(1)} %get-tuple-element.57), channel_id=1, source_target_pairs={{0,200},{64,136},{128,72},{192,8},{8,192},{72,128},{136,64},{200,0... | collective-permute-start | bytes 393224 | tf_op jit(solution)/shard_map/ppermute | solution.py:35
  52.1 10.9 %collective-permute-start.17 = (bf16[3,128,512]{2,1,0:T(8,128)(2,1)S(1)}, bf16[3,128,512]{2,1,0:T(8,128)(2,1)S(1)}, u32[]{:S(2)}, u32[]{:S(2)}) collective-permute-start(bf16[3,128,512]{2,1,0:T(8,128)(2,1)S(1)} %pad_maximum_fusion.p0), channel_id=1, source_target_pairs={{0,2},{2,0},{1,3},{3,1},{4,6},{6,4},{5,7},{7,5},{8,10},{10,8},{9,1... | collective-permute-start | bytes 1179656 | tf_op jit(solution)/shard_map/ppermute | solution.py:40
  58.6 4.3 %collective-permute-start.16 = (bf16[128,512]{1,0:T(8,128)(2,1)S(1)}, bf16[128,512]{1,0:T(8,128)(2,1)S(1)}, u32[]{:S(2)}, u32[]{:S(2)}) collective-permute-start(bf16[128,512]{1,0:T(8,128)(2,1)S(1)} %add_convert_fusion.2), channel_id=1, source_target_pairs={{0,64},{64,0},{128,192},{192,128},{8,72},{72,8},{136,200},{200,136... | collective-permute-start | bytes 393224 | tf_op jit(solution)/shard_map/ppermute | solution.py:35
  63.0 8.5 %collective-permute-start.18 = (bf16[128,512]{1,0:T(8,128)(2,1)S(1)}, bf16[128,512]{1,0:T(8,128)(2,1)S(1)}, u32[]{:S(2)}, u32[]{:S(2)}) collective-permute-start(bf16[128,512]{1,0:T(8,128)(2,1)S(1)} %add_convert_fusion.1), channel_id=1, source_target_pairs={{0,128},{64,192},{128,0},{192,64},{8,136},{72,200},{136,8},{200,72... | collective-permute-start | bytes 393224 | tf_op jit(solution)/shard_map/ppermute | solution.py:35
  64.3 13.5 %collective-permute-start.22 = (bf16[3,128,512]{2,1,0:T(8,128)(2,1)S(1)}, bf16[3,128,512]{2,1,0:T(8,128)(2,1)S(1)}, u32[]{:S(2)}, u32[]{:S(2)}) collective-permute-start(bf16[3,128,512]{2,1,0:T(8,128)(2,1)S(1)} %collective-permute-done.17.p1), channel_id=1, source_target_pairs={{0,1},{1,0},{2,3},{3,2},{4,5},{5,4},{6,7},{7,6},{8,9},{9,8},{10,11... | collective-permute-start | bytes 1179656 | tf_op jit(solution)/shard_map/ppermute | solution.py:40
  71.5 3.9 %collective-permute-start.19 = (bf16[128,512]{1,0:T(8,128)(2,1)S(1)}, bf16[128,512]{1,0:T(8,128)(2,1)S(1)}, u32[]{:S(2)}, u32[]{:S(2)}) collective-permute-start(bf16[128,512]{1,0:T(8,128)(2,1)S(1)} %add_convert_fusion.g0), channel_id=1, source_target_pairs={{0,2},{2,0},{1,3},{3,1},{4,6},{6,4},{5,7},{7,5},{8,10},{10,8},{9,1... | collective-permute-start | bytes 393224 | tf_op jit(solution)/shard_map/ppermute | solution.py:40
  71.6 6.3 %collective-permute-start.20 = (bf16[128,512]{1,0:T(8,128)(2,1)S(1)}, bf16[128,512]{1,0:T(8,128)(2,1)S(1)}, u32[]{:S(2)}, u32[]{:S(2)}) collective-permute-start(bf16[128,512]{1,0:T(8,128)(2,1)S(1)} %add_convert_fusion.g0), channel_id=1, source_target_pairs={{0,1},{1,0},{2,3},{3,2},{4,5},{5,4},{6,7},{7,6},{8,9},{9,8},{10,11... | collective-permute-start | bytes 393224 | tf_op jit(solution)/shard_map/ppermute | solution.py:40
  75.5 3.3 %collective-permute-start.21 = (bf16[128,512]{1,0:T(8,128)(2,1)S(1)}, bf16[128,512]{1,0:T(8,128)(2,1)S(1)}, u32[]{:S(2)}, u32[]{:S(2)}) collective-permute-start(bf16[128,512]{1,0:T(8,128)(2,1)S(1)} %collective-permute-done.19.g1), channel_id=1, source_target_pairs={{0,1},{1,0},{2,3},{3,2},{4,5},{5,4},{6,7},{7,6},{8,9},{9,8},{10,11... | collective-permute-start | bytes 393224 | tf_op jit(solution)/shard_map/ppermute | solution.py:40
  (3 other events, 51.1 us)

commit v6 on v5

--- a/solution.py
+++ b/solution.py
@@ -17,6 +17,8 @@
 B = 512
 ROWS = 128
 TOKENS = 128
+HALF = B // 2
+ORDER = (2, 1, 3, 0)
 WIDE = 3 * B
 SEND = jnp.bfloat16
 VMEM = pl.BlockSpec(memory_space=pltpu.VMEM)
@@ -25,14 +27,35 @@
 tiny_term = 1e-06
 
 
-def shift(x, axis, by):
-    n = lax.axis_size(axis)
-    return lax.ppermute(x, axis, [(i, (i + by) % n) for i in range(n)])
+def shift(x, along_y, by):
+    pairs = []
+    for y in range(4):
+        for x_at in range(4):
+            for core in range(2):
+                moves_y = (core == 0) == along_y
+                to = ((y + by) % 4, x_at) if moves_y else (y, (x_at + by) % 4)
+                pairs.append(((y * 4 + x_at) * 2 + core, (to[0] * 4 + to[1]) * 2 + core))
+    return lax.ppermute(x, ("y",) + X + ("core",), pairs)
+
+
+def ring_spot(z, core=None):
+    spot = (z % 4) * 2 + z // 4
+    return spot if core is None else spot * 2 + core
 
 
 def swap_z(x, bits):
-    spot = [(i % 4) * 2 + i // 4 for i in range(8)]
-    return lax.ppermute(x, Z, [(spot[i], spot[i ^ bits]) for i in range(8)])
+    return lax.ppermute(x, Z, [(ring_spot(z), ring_spot(z ^ bits)) for z in range(8)])
+
+
+def mirror(near, far):
+    first, second = [], []
+    for z in range(8):
+        stays = z // 4
+        first.append((ring_spot(z, stays), ring_spot(z, 1 - stays)))
+        first.append((ring_spot(z, 1 - stays), ring_spot(7 - z, 1 - stays)))
+        second.append((ring_spot(z, 1 - stays), ring_spot(7 - z, stays)))
+    axes = Z + ("core",)
+    return lax.ppermute(near, axes, first), lax.ppermute(far, axes, second)
 
 
 def partner(x, axis, bits=1):
@@ -148,8 +171,9 @@
 
 
 def cut_kernel(cotangents, activations, *rest):
-    outs, held, sem = rest[:-2], rest[-2], rest[-1]
+    outs, other, held, sem = rest[:4], rest[4], rest[5], rest[6]
     at = places()
+    spot = (at["y"], at["x_hi"] * 2 + at["x_lo"])
     copies = []
 
     def copy(src, dst):
@@ -157,16 +181,18 @@
         copies[-1].start()
 
     copy(activations, held)
-    for i, k in enumerate((2, 1, 3, 0)):
-        t = lax.rem(at["y"] + k, 4)
-        copy(cotangents.at[:, pl.ds(pl.multiple_of(t * 4 * B, 4 * B), 2 * B)], outs[2 * i].at[:, : 2 * B])
-        t = lax.rem(at["x_hi"] * 2 + at["x_lo"] + k, 4)
+    pieces = [(at["core"], out) for out in outs] + [(1 - at["core"], other.at[i]) for i in range(4)]
+    for (core, out), k in zip(pieces, ORDER * 2):
         for j in range(4):
-            start = pl.multiple_of(t * (B // 2) + (4 * j + 2) * B, B // 2)
-            here = slice(j * (B // 2), (j + 1) * (B // 2))
-            copy(cotangents.at[:, pl.ds(start, B // 2)], outs[2 * i + 1].at[:, here])
+            start = jnp.where(
+                core == 0,
+                lax.rem(spot[0] + k, 4) * (4 * B) + j * HALF,
+                lax.rem(spot[1] + k, 4) * HALF + (4 * j + 2) * B,
+            )
+            columns = pl.ds(pl.multiple_of(start, HALF), HALF)
+            copy(cotangents.at[:, columns], out.at[:, j * HALF : (j + 1) * HALF])
     copies[0].wait()
-    for out in outs:
+    for core, out in pieces:
         out[:, 2 * B :] = held[...]
     for c in copies[1:]:
         c.wait()
@@ -179,95 +205,120 @@
     return pl.pallas_call(
         cut_kernel,
         name="cut",
-        out_shape=(jax.ShapeDtypeStruct((TOKENS, WIDE), jnp.bfloat16),) * 8,
+        out_shape=(jax.ShapeDtypeStruct((TOKENS, WIDE), jnp.bfloat16),) * 4
+        + (jax.ShapeDtypeStruct((4, TOKENS, WIDE), jnp.bfloat16),),
         in_specs=[free, free],
-        out_specs=(VMEM,) * 8,
-        scratch_shapes=[pltpu.VMEM((TOKENS, B), jnp.bfloat16), pltpu.SemaphoreType.DMA((21,))],
+        out_specs=(VMEM,) * 5,
+        scratch_shapes=[pltpu.VMEM((TOKENS, B), jnp.bfloat16), pltpu.SemaphoreType.DMA((33,))],
         compiler_params=pltpu.CompilerParams(vmem_limit_bytes=4 << 20),
         cost_estimate=pl.CostEstimate(flops=0, bytes_accessed=6 << 20, transcendentals=0),
     )(cotangents, activations)
 
 
-def product_kernel(p0, p1, p2, p3, keep, send):
-    parts = (p0, p1, p2, p3)
+def split_kernel(pieces, *outs):
+    for i, out in enumerate(outs):
+        out[...] = pieces[i]
+
+
+def split(pieces):
+    return pl.pallas_call(
+        split_kernel,
+        name="split",
+        out_shape=(jax.ShapeDtypeStruct((TOKENS, WIDE), jnp.bfloat16),) * 4,
+        in_specs=[VMEM],
+        out_specs=(VMEM,) * 4,
+        compiler_params=pltpu.CompilerParams(vmem_limit_bytes=1 << 20),
+        cost_estimate=pl.CostEstimate(flops=0, bytes_accessed=3 << 20, transcendentals=0),
+    )(pieces)
+
+
+def product_kernel(*refs):
+    parts, outs = refs[:8], refs[8:]
+    at = places()
+    me = jnp.where(at["core"] == 0, at["x_hi"] * 2 + at["x_lo"], at["y"])
     right = jnp.concatenate([p[:, 2 * B :] for p in parts], axis=0)
-    core = lax.axis_index("core")
-    for out, side in ((send, 1 - core), (keep, core)):
-        left = jnp.concatenate(
-            [
-                jnp.concatenate(
-                    [p[:, pl.ds(pl.multiple_of((2 * g + side) * ROWS, ROWS), ROWS)] for g in range(4)], axis=1
-                )
-                for p in parts
-            ],
-            axis=0,
-        )
-        out[...] = dot(left, right, (0, 0)).reshape(4, ROWS, B).astype(out.dtype)
+    for k, out in zip(ORDER, outs):
+        columns = pl.ds(pl.multiple_of(lax.rem(me + k, 4) * HALF, HALF), HALF)
+        left = jnp.concatenate([p[:, columns] for p in parts], axis=0)
+        out[...] = dot(left, right, (0, 0)).astype(out.dtype)
 
 
 def product(parts):
     return pl.pallas_call(
         product_kernel,
         name="product",
+        out_shape=(jax.ShapeDtypeStruct((HALF, B), SEND),) * 3 + (jax.ShapeDtypeStruct((HALF, B), jnp.float32),),
+        in_specs=[VMEM] * 8,
+        out_specs=(VMEM,) * 4,
+        compiler_params=pltpu.CompilerParams(vmem_limit_bytes=8 << 20),
+        cost_estimate=pl.CostEstimate(flops=8 * B**3, bytes_accessed=5 << 20, transcendentals=0),
+    )(*parts)
+
+
+def plane_sum_kernel(first, second, third, own, keep, near, far):
+    total = own[...]
+    for part in (first, second, third):
+        total += part[...].astype(jnp.float32)
+    core = lax.axis_index("core")
+    stays = core == lax.axis_index("z_hi")
+
+    @pl.when(core == 0)
+    def _():
+        keep[...] = total[:ROWS]
+        far[...] = total[ROWS:].astype(SEND)
+
+    @pl.when(core == 1)
+    def _():
+        keep[...] = total[ROWS:]
+        far[...] = total[:ROWS].astype(SEND)
+
+    @pl.when(stays)
+    def _():
+        near[...] = far[...]
+
+    @pl.when(jnp.logical_not(stays))
+    def _():
+        near[...] = keep[...].astype(SEND)
+
+
+def plane_sum(parts):
+    return pl.pallas_call(
+        plane_sum_kernel,
+        name="plane_sum",
         out_shape=(
-            jax.ShapeDtypeStruct((4, ROWS, B), jnp.float32),
-            jax.ShapeDtypeStruct((4, ROWS, B), SEND),
+            jax.ShapeDtypeStruct((ROWS, B), jnp.float32),
+            jax.ShapeDtypeStruct((ROWS, B), SEND),
+            jax.ShapeDtypeStruct((ROWS, B), SEND),
         ),
         in_specs=[VMEM] * 4,
-        out_specs=(VMEM,) * 2,
-        compiler_params=pltpu.CompilerParams(vmem_limit_bytes=8 << 20),
-        cost_estimate=pl.CostEstimate(flops=4 * B**3, bytes_accessed=3 << 20, transcendentals=0),
-    )(*parts)
-
-
-def core_sum_kernel(along_x, keep, came, own, *sends):
-    at = places()
-    me = at["x_hi"] * 2 + at["x_lo"] if along_x else at["y"]
-    for k, out in zip((0, 2, 1, 3), (own,) + sends):
-        t = lax.rem(me + k, 4)
-        out[...] = (keep[t] + came[t].astype(jnp.float32)).astype(out.dtype)
-
-
-def core_sum(along_x, keep, came):
-    return pl.pallas_call(
-        functools.partial(core_sum_kernel, along_x),
-        name="core_sum",
-        out_shape=(jax.ShapeDtypeStruct((ROWS, B), jnp.float32),) + (jax.ShapeDtypeStruct((ROWS, B), SEND),) * 3,
-        in_specs=[VMEM] * 2,
-        out_specs=(VMEM,) * 4,
-        compiler_params=pltpu.CompilerParams(vmem_limit_bytes=1 << 20),
-        cost_estimate=pl.CostEstimate(flops=4 * ROWS * B, bytes_accessed=2 << 20, transcendentals=0),
-    )(keep, came)
-
-
-def plane_sum_kernel(y0, y1, y2, y3, x0, x1, x2, x3, keep, send):
-    def total(parts):
-        first, second, third = (p[...].astype(jnp.float32) for p in parts[1:])
-        return parts[0][...] + first + second + third
-
-    low = lax.axis_index("z_hi") == 0
-
-    @pl.when(low)
-    def _():
-        keep[...] = total((y0, y1, y2, y3))
-        send[...] = total((x0, x1, x2, x3)).astype(SEND)
-
-    @pl.when(jnp.logical_not(low))
-    def _():
-        keep[...] = total((x0, x1, x2, x3))
-        send[...] = total((y0, y1, y2, y3)).astype(SEND)
-
-
-def plane_sum(y_parts, x_parts):
-    return pl.pallas_call(
-        plane_sum_kernel,
-        name="plane_sum",
-        out_shape=(jax.ShapeDtypeStruct((ROWS, B), jnp.float32), jax.ShapeDtypeStruct((ROWS, B), SEND)),
-        in_specs=[VMEM] * 8,
-        out_specs=(VMEM,) * 2,
+        out_specs=(VMEM,) * 3,
         compiler_params=pltpu.CompilerParams(vmem_limit_bytes=2 << 20),
         cost_estimate=pl.CostEstimate(flops=8 * ROWS * B, bytes_accessed=2 << 20, transcendentals=0),
-    )(*y_parts, *x_parts)
+    )(*parts)
+
+
+def mirror_sum_kernel(keep, near, far, out):
+    stays = lax.axis_index("core") == lax.axis_index("z_hi")
+
+    @pl.when(stays)
+    def _():
+        out[...] = narrow(keep[...] + near[...].astype(jnp.float32))
+
+    @pl.when(jnp.logical_not(stays))
+    def _():
+        out[...] = narrow(far[...].astype(jnp.float32) + near[...].astype(jnp.float32))
+
+
+def mirror_sum(keep, near, far):
+    return pl.pallas_call(
+        mirror_sum_kernel,
+        name="mirror_sum",
+        out_shape=jax.ShapeDtypeStruct((ROWS, B), jnp.bfloat16),
+        in_specs=[VMEM] * 3,
+        out_specs=VMEM,
+        compiler_params=pltpu.CompilerParams(vmem_limit_bytes=1 << 20),
+        cost_estimate=pl.CostEstimate(flops=2 * ROWS * B, bytes_accessed=1 << 19, transcendentals=0),
+    )(keep, near, far)
 
 
 def quarter_rows(at, a, b):
@@ -300,27 +351,16 @@
 
 def per_device(activations, cotangents, statistics, roots, ages, refresh):
     decays = decay_base ** ages.astype(jnp.float32)
-    pieces = cut(cotangents, activations)
-    y_parts, x_parts = [pieces[6]], [pieces[7]]
-    for i, k in enumerate((2, 1, 3)):
-        y_parts.append(shift(pieces[2 * i], "y", k))
-        x_parts.append(shift(pieces[2 * i + 1], X, k))
-
-    y_keep, y_send = product(y_parts)
-    y_came = partner(y_send, "core")
-    x_keep, x_send = product(x_parts)
-    x_came = partner(x_send, "core")
-    y_own, *y_sends = core_sum(True, y_keep, y_came)
-    x_own, *x_sends = core_sum(False, x_keep, x_came)
-    y_sums, x_sums = [y_own], [x_own]
-    for i, k in enumerate((2, 1, 3)):
-        y_sums.append(shift(y_sends[i], X, k))
-        x_sums.append(shift(x_sends[i], "y", k))
-
-    keep, send = plane_sum(y_sums, x_sums)
+    *pieces, other = cut(cotangents, activations)
+    parts = [pieces[3]] + [shift(pieces[i], True, ORDER[i]) for i in range(3)]
+    pieces = split(partner(other, "core"))
+    parts += [pieces[3]] + [shift(pieces[i], True, ORDER[i]) for i in range(3)]
+
+    *sends, own = product(parts)
+    keep, near, far = plane_sum([shift(sends[i], False, ORDER[i]) for i in range(3)] + [own])
     pack = jnp.concatenate([narrow(statistics), roots[1:]], axis=0)
-    keep, send, pack = lax.optimization_barrier((keep, send, pack))
-    part = rounded(keep + swap_z(send, 7).astype(jnp.float32))
+    keep, near, far, pack = lax.optimization_barrier((keep, near, far, pack))
+    part = mirror_sum(keep, *mirror(near, far))
     pack_x = partner(pack, "x_lo")
     part, pack_core = lax.optimization_barrier((part, partner(pack, "core")))
     part = rounded(part.astype(jnp.float32) + swap_z(part, 1).astype(jnp.float32))

time: 86.3 us -> 78.9 us (0.914)
  starting transfers between devices: 34.3 us -> 30 us
  waiting for transfers between devices: 39.7 us -> 36.6 us
    ppermute x15 -> x13, starting transfers between devices: 26.3 us -> 22.2 us  [the longest x9 9.3 us: shift(): return lax.ppermute(x, ('y',) + X + ('core',), pairs)]
    ppermute x15 -> x13, waiting for transfers between devices: 36.4 us -> 32.8 us  [the longest x9 21.4 us: shift(): return lax.ppermute(x, ('y',) + X + ('core',), pairs)]
    ppermute x8 -> x7, waiting for transfers between devices: 3.32 us -> 3.74 us  [partner(): return lax.ppermute(x, axis, [(i, i ^ bits) for i in range(n)])]
    ppermute x8 -> x7, starting transfers between devices: 8.01 us -> 7.8 us  [partner(): return lax.ppermute(x, axis, [(i, i ^ bits) for i in range(n)])]
  transfers between devices with their start and end apart: 23 -> 20, of which waited for: 12 -> 11; matrix products, arithmetic and copies ran while one was open for 0% -> 0% of each run, Pallas kernels for 2% -> 0%
where the time goes in v6:
time: 78.9 us; the launch traced here: 78.7 us
  waiting for transfers between devices  36.6 us (46%)
  starting transfers between devices  30 us (38%)
  Pallas kernels  11.2 us (14%)
    ppermute x9, waiting for transfers between devices, shift(): return lax.ppermute(x, ('y',) + X + ('core',), pairs)  21.4 us
    ppermute x9, starting transfers between devices, shift(): return lax.ppermute(x, ('y',) + X + ('core',), pairs)  9.3 us
    ppermute x7, starting transfers between devices, partner(): return lax.ppermute(x, axis, [(i, i ^ bits) for i in range(n)])  7.8 us
    pallas_call x1, Pallas kernels, finish(): pl.pallas_call(finish_kernel, name='finish', out_shape=(jax.ShapeDtypeStr...  7.39 us
    ppermute x2, waiting for transfers between devices, swap_z(): lax.ppermute(x, Z, [(ring_spot(z), ring_spot(z ^ bits)) for z in range(8)])  7.09 us
    ppermute x2, starting transfers between devices, swap_z(): lax.ppermute(x, Z, [(ring_spot(z), ring_spot(z ^ bits)) for z in range(8)])  6.68 us
    ppermute x2, starting transfers between devices, mirror(): return (lax.ppermute(near, axes, first), lax.ppermute(far, axes, second))  6.22 us
    ppermute x2, waiting for transfers between devices, mirror(): return (lax.ppermute(near, axes, first), lax.ppermute(far, axes, second))  4.29 us
  transfers between devices with their start and end apart: 20, of which 11 were waited for; matrix products, arithmetic and copies ran while one was open for 0% of the time, Pallas kernels for 0%

profile of v6, /device:TPU:1, one launch (start us, length us, event | category | flops | bytes accessed | tf_op | source)
XLA Modules:
  0.0 78.7 jit_solution(9567468547882411409)
XLA Ops:
  0.6 2.0 %cut.1 = (bf16[128,1536]{1,0:T(8,128)(2,1)S(1)}, bf16[128,1536]{1,0:T(8,128)(2,1)S(1)}, bf16[128,1536]{1,0:T(8,128)(2,1)S(1)}, bf16[128,1536]{1,0:T(8,128)(2,1)S(1)}, bf16[4,128,1536]{2,1,0:T(8,128)(2,1)S(1)}) custom-call(bf16[128,8192]{1,0:T(8,128)(2,1)} %cotangents.1, bf16[128,512]{1,0:T(8,128)(2,1)} %activations.1), custom_call_target="tpu_custom_call" | custom-call | bytes 6291456 | tf_op jit(solution)/shard_map/cut/pallas_call | solution.py:205
  2.6 3.3 %collective-permute-start.3 = (bf16[4,128,1536]{2,1,0:T(8,128)(2,1)S(1)}, bf16[4,128,1536]{2,1,0:T(8,128)(2,1)S(1)}, u32[]{:S(2)}, u32[]{:S(2)}) collective-permute-start(bf16[4,128,1536]{2,1,0:T(8,128)(2,1)S(1)} %get-tuple-element.33), channel_id=1, source_target_pairs={{0,1},{1,0},{2,3},{3,2},{4,5},{5,4},{6,7},{7,6},{8,9},{9,8},{10,11... | collective-permute-start | bytes 4718600 | tf_op jit(solution)/shard_map/ppermute | solution.py:63
  7.3 2.4 %collective-permute-start.2 = (bf16[128,1536]{1,0:T(8,128)(2,1)S(1)}, bf16[128,1536]{1,0:T(8,128)(2,1)S(1)}, u32[]{:S(2)}, u32[]{:S(2)}) collective-permute-start(bf16[128,1536]{1,0:T(8,128)(2,1)S(1)} %get-tuple-element.32), channel_id=1, source_target_pairs={{0,48},{1,7},{2,50},{3,1},{4,52},{5,3},{6,54},{7,5},{16,0},{17,23}... | collective-permute-start | bytes 1179656 | tf_op jit(solution)/shard_map/ppermute | solution.py:38
  10.6 3.8 %collective-permute-done.refs_1_ = bf16[128,1536]{1,0:T(8,128)(2,1)S(1)} collective-permute-done((bf16[128,1536]{1,0:T(8,128)(2,1)S(1)}, bf16[128,1536]{1,0:T(8,128)(2,1)S(1)}, u32[]{:S(2)}, u32[]{:S(2)}) %collective-permute-start) | collective-permute-done | bytes 393248 | tf_op jit(solution)/shard_map/ppermute | solution.py:38
  15.2 3.4 %collective-permute-done.1.refs_2_ = bf16[128,1536]{1,0:T(8,128)(2,1)S(1)} collective-permute-done((bf16[128,1536]{1,0:T(8,128)(2,1)S(1)}, bf16[128,1536]{1,0:T(8,128)(2,1)S(1)}, u32[]{:S(2)}, u32[]{:S(2)}) %collective-permute-start.1) | collective-permute-done | bytes 393248 | tf_op jit(solution)/shard_map/ppermute | solution.py:38
  18.6 4.3 %collective-permute-done.4.refs_5_ = bf16[128,1536]{1,0:T(8,128)(2,1)S(1)} collective-permute-done((bf16[128,1536]{1,0:T(8,128)(2,1)S(1)}, bf16[128,1536]{1,0:T(8,128)(2,1)S(1)}, u32[]{:S(2)}, u32[]{:S(2)}) %collective-permute-start.4) | collective-permute-done | bytes 393248 | tf_op jit(solution)/shard_map/ppermute | solution.py:38
  22.9 4.1 %collective-permute-done.5.refs_6_ = bf16[128,1536]{1,0:T(8,128)(2,1)S(1)} collective-permute-done((bf16[128,1536]{1,0:T(8,128)(2,1)S(1)}, bf16[128,1536]{1,0:T(8,128)(2,1)S(1)}, u32[]{:S(2)}, u32[]{:S(2)}) %collective-permute-start.5) | collective-permute-done | bytes 393248 | tf_op jit(solution)/shard_map/ppermute | solution.py:38
  27.0 1.3 %product.1 = (bf16[256,512]{1,0:T(8,128)(2,1)S(1)}, bf16[256,512]{1,0:T(8,128)(2,1)S(1)}, bf16[256,512]{1,0:T(8,128)(2,1)S(1)}, f32[256,512]{1,0:T(8,128)S(1)}) custom-call(bf16[128,1536]{1,0:T(8,128)(2,1)S(1)} %get-tuple-element.29.refs_0_, bf16[128,1536]{1,0:T(8,128)(2,1)S(1)} %collective-permute-done.refs_1_, ...), custom_call_target="tpu_custom_call" | custom-call | flops 1073741824 | bytes 5242880 | tf_op jit(solution)/shard_map/product/pallas_call | solution.py:247
  28.3 1.4 %collective-permute-start.7 = (bf16[256,512]{1,0:T(8,128)(2,1)S(1)}, bf16[256,512]{1,0:T(8,128)(2,1)S(1)}, u32[]{:S(2)}, u32[]{:S(2)}) collective-permute-start(bf16[256,512]{1,0:T(8,128)(2,1)S(1)} %get-tuple-element.38), channel_id=1, source_target_pairs={{0,4},{1,33},{2,6},{3,35},{4,0},{5,37},{6,2},{7,39},{16,20},{17,49... | collective-permute-start | bytes 786440 | tf_op jit(solution)/shard_map/ppermute | solution.py:38
  30.1 2.3 %collective-permute-start.9 = (bf16[256,512]{1,0:T(8,128)(2,1)S(1)}, bf16[256,512]{1,0:T(8,128)(2,1)S(1)}, u32[]{:S(2)}, u32[]{:S(2)}) collective-permute-start(bf16[256,512]{1,0:T(8,128)(2,1)S(1)} %get-tuple-element.40), channel_id=1, source_target_pairs={{0,6},{1,49},{2,0},{3,51},{4,2},{5,53},{6,4},{7,55},{16,22},{17,1}... | collective-permute-start | bytes 786440 | tf_op jit(solution)/shard_map/ppermute | solution.py:38
  32.5 3.0 %collective-permute-done.7.first = bf16[256,512]{1,0:T(8,128)(2,1)S(1)} collective-permute-done((bf16[256,512]{1,0:T(8,128)(2,1)S(1)}, bf16[256,512]{1,0:T(8,128)(2,1)S(1)}, u32[]{:S(2)}, u32[]{:S(2)}) %collective-permute-start.7) | collective-permute-done | bytes 262176 | tf_op jit(solution)/shard_map/ppermute | solution.py:38
  35.5 2.8 %collective-permute-done.8.second = bf16[256,512]{1,0:T(8,128)(2,1)S(1)} collective-permute-done((bf16[256,512]{1,0:T(8,128)(2,1)S(1)}, bf16[256,512]{1,0:T(8,128)(2,1)S(1)}, u32[]{:S(2)}, u32[]{:S(2)}) %collective-permute-start.8) | collective-permute-done | bytes 262176 | tf_op jit(solution)/shard_map/ppermute | solution.py:38
  38.5 1.9 %collective-permute-start.12 = (bf16[3,128,512]{2,1,0:T(8,128)(2,1)S(1)}, bf16[3,128,512]{2,1,0:T(8,128)(2,1)S(1)}, u32[]{:S(2)}, u32[]{:S(2)}) collective-permute-start(bf16[3,128,512]{2,1,0:T(8,128)(2,1)S(1)} %pad_maximum_fusion.p0), channel_id=1, source_target_pairs={{0,1},{1,0},{2,3},{3,2},{4,5},{5,4},{6,7},{7,6},{8,9},{9,8},{10,11... | collective-permute-start | bytes 1179656 | tf_op jit(solution)/shard_map/ppermute | solution.py:63
  40.4 4.3 %collective-permute-start.10 = (bf16[128,512]{1,0:T(8,128)(2,1)S(1)}, bf16[128,512]{1,0:T(8,128)(2,1)S(1)}, u32[]{:S(2)}, u32[]{:S(2)}) collective-permute-start(bf16[128,512]{1,0:T(8,128)(2,1)S(1)} %get-tuple-element.46), channel_id=1, source_target_pairs={{0,1},{1,201},{64,65},{65,137},{128,129},{129,73},{192,193},{193,9... | collective-permute-start | bytes 393224 | tf_op jit(solution)/shard_map/ppermute | solution.py:58
  44.7 1.9 %collective-permute-start.11 = (bf16[128,512]{1,0:T(8,128)(2,1)S(1)}, bf16[128,512]{1,0:T(8,128)(2,1)S(1)}, u32[]{:S(2)}, u32[]{:S(2)}) collective-permute-start(bf16[128,512]{1,0:T(8,128)(2,1)S(1)} %get-tuple-element.47), channel_id=1, source_target_pairs={{1,200},{65,136},{129,72},{193,8},{8,193},{72,129},{136,65},{200,1... | collective-permute-start | bytes 393224 | tf_op jit(solution)/shard_map/ppermute | solution.py:58
  46.6 1.3 %collective-permute-start.14 = (bf16[3,128,512]{2,1,0:T(8,128)(2,1)S(1)}, bf16[3,128,512]{2,1,0:T(8,128)(2,1)S(1)}, u32[]{:S(2)}, u32[]{:S(2)}) collective-permute-start(bf16[3,128,512]{2,1,0:T(8,128)(2,1)S(1)} %pad_maximum_fusion.p0), channel_id=1, source_target_pairs={{0,2},{2,0},{1,3},{3,1},{4,6},{6,4},{5,7},{7,5},{8,10},{10,8},{9,1... | collective-permute-start | bytes 1179656 | tf_op jit(solution)/shard_map/ppermute | solution.py:63
  47.9 4.3 %collective-permute-done.11.far = bf16[128,512]{1,0:T(8,128)(2,1)S(1)} collective-permute-done((bf16[128,512]{1,0:T(8,128)(2,1)S(1)}, bf16[128,512]{1,0:T(8,128)(2,1)S(1)}, u32[]{:S(2)}, u32[]{:S(2)}) %collective-permute-start.11) | collective-permute-done | bytes 131104 | tf_op jit(solution)/shard_map/ppermute | solution.py:58
  52.2 4.8 %collective-permute-start.13 = (bf16[128,512]{1,0:T(8,128)(2,1)S(1)}, bf16[128,512]{1,0:T(8,128)(2,1)S(1)}, u32[]{:S(2)}, u32[]{:S(2)}) collective-permute-start(bf16[128,512]{1,0:T(8,128)(2,1)S(1)} %mirror_sum.1), channel_id=1, source_target_pairs={{0,64},{64,0},{128,192},{192,128},{8,72},{72,8},{136,200},{200,136... | collective-permute-start | bytes 393224 | tf_op jit(solution)/shard_map/ppermute | solution.py:47
  57.0 2.8 %collective-permute-done.13 = bf16[128,512]{1,0:T(8,128)(2,1)S(1)} collective-permute-done((bf16[128,512]{1,0:T(8,128)(2,1)S(1)}, bf16[128,512]{1,0:T(8,128)(2,1)S(1)}, u32[]{:S(2)}, u32[]{:S(2)}) %collective-permute-start.13) | collective-permute-done | bytes 131104 | tf_op jit(solution)/shard_map/ppermute | solution.py:47
  59.8 1.9 %collective-permute-start.15 = (bf16[128,512]{1,0:T(8,128)(2,1)S(1)}, bf16[128,512]{1,0:T(8,128)(2,1)S(1)}, u32[]{:S(2)}, u32[]{:S(2)}) collective-permute-start(bf16[128,512]{1,0:T(8,128)(2,1)S(1)} %add_convert_fusion.1), channel_id=1, source_target_pairs={{0,128},{64,192},{128,0},{192,64},{8,136},{72,200},{136,8},{200,72... | collective-permute-start | bytes 393224 | tf_op jit(solution)/shard_map/ppermute | solution.py:47
  61.8 4.3 %collective-permute-done.15 = bf16[128,512]{1,0:T(8,128)(2,1)S(1)} collective-permute-done((bf16[128,512]{1,0:T(8,128)(2,1)S(1)}, bf16[128,512]{1,0:T(8,128)(2,1)S(1)}, u32[]{:S(2)}, u32[]{:S(2)}) %collective-permute-start.15) | collective-permute-done | bytes 131104 | tf_op jit(solution)/shard_map/ppermute | solution.py:47
  66.1 1.3 %collective-permute-start.16 = (bf16[128,512]{1,0:T(8,128)(2,1)S(1)}, bf16[128,512]{1,0:T(8,128)(2,1)S(1)}, u32[]{:S(2)}, u32[]{:S(2)}) collective-permute-start(bf16[128,512]{1,0:T(8,128)(2,1)S(1)} %add_convert_fusion.g0), channel_id=1, source_target_pairs={{0,2},{2,0},{1,3},{3,1},{4,6},{6,4},{5,7},{7,5},{8,10},{10,8},{9,1... | collective-permute-start | bytes 393224 | tf_op jit(solution)/shard_map/ppermute | solution.py:63
  67.4 2.6 %collective-permute-done.16.g1 = bf16[128,512]{1,0:T(8,128)(2,1)S(1)} collective-permute-done((bf16[128,512]{1,0:T(8,128)(2,1)S(1)}, bf16[128,512]{1,0:T(8,128)(2,1)S(1)}, u32[]{:S(2)}, u32[]{:S(2)}) %collective-permute-start.16) | collective-permute-done | bytes 131104 | tf_op jit(solution)/shard_map/ppermute | solution.py:63
  71.3 7.4 %finish.1 = (bf16[128,512]{1,0:T(8,128)(2,1)}, f32[2,128,512]{2,1,0:T(8,128)}, bf16[2,128,512]{2,1,0:T(8,128)(2,1)}) custom-call(f32[32]{0:T(128)S(1)} %convert_power_fusion.decays, s32[32]{0:T(128)S(1)} %copy-done.1, bf16[128,512]{1,0:T(8,128)(2,1)S(1)} %add_convert_fusion.g0, bf16[128,512]{1,0:T(8,128)(2,1)S(1)} %collective-permute-done.16.g1, ...), custom_call_target="tpu_custom_call" | custom-call | flops 4831838208 | bytes 6291456 | tf_op jit(solution)/shard_map/finish/pallas_call | solution.py:148
  (37 shorter events, 5.1 us)
Async XLA Ops:
  0.6 14.5 %copy-start = (f32[2,128,512]{2,1,0:T(8,128)S(1)}, f32[2,128,512]{2,1,0:T(8,128)}, u32[]{:S(2)}) copy-start(f32[2,128,512]{2,1,0:T(8,128)} %own.1) | copy-start | bytes 1572868
  2.6 7.0 %collective-permute-start.3 = (bf16[4,128,1536]{2,1,0:T(8,128)(2,1)S(1)}, bf16[4,128,1536]{2,1,0:T(8,128)(2,1)S(1)}, u32[]{:S(2)}, u32[]{:S(2)}) collective-permute-start(bf16[4,128,1536]{2,1,0:T(8,128)(2,1)S(1)} %get-tuple-element.33), channel_id=1, source_target_pairs={{0,1},{1,0},{2,3},{3,2},{4,5},{5,4},{6,7},{7,6},{8,9},{9,8},{10,11... | collective-permute-start | bytes 4718600 | tf_op jit(solution)/shard_map/ppermute | solution.py:63
  5.9 8.5 %collective-permute-start = (bf16[128,1536]{1,0:T(8,128)(2,1)S(1)}, bf16[128,1536]{1,0:T(8,128)(2,1)S(1)}, u32[]{:S(2)}, u32[]{:S(2)}) collective-permute-start(bf16[128,1536]{1,0:T(8,128)(2,1)S(1)} %get-tuple-element.30), channel_id=1, source_target_pairs={{0,32},{1,5},{2,34},{3,7},{4,36},{5,1},{6,38},{7,3},{16,48},{17,21... | collective-permute-start | bytes 1179656 | tf_op jit(solution)/shard_map/ppermute | solution.py:38
  7.0 11.6 %collective-permute-start.1 = (bf16[128,1536]{1,0:T(8,128)(2,1)S(1)}, bf16[128,1536]{1,0:T(8,128)(2,1)S(1)}, u32[]{:S(2)}, u32[]{:S(2)}) collective-permute-start(bf16[128,1536]{1,0:T(8,128)(2,1)S(1)} %get-tuple-element.31), channel_id=1, source_target_pairs={{0,16},{1,3},{2,18},{3,5},{4,20},{5,7},{6,22},{7,1},{16,32},{17,19... | collective-permute-start | bytes 1179656 | tf_op jit(solution)/shard_map/ppermute | solution.py:38
  7.3 11.3 %collective-permute-start.2 = (bf16[128,1536]{1,0:T(8,128)(2,1)S(1)}, bf16[128,1536]{1,0:T(8,128)(2,1)S(1)}, u32[]{:S(2)}, u32[]{:S(2)}) collective-permute-start(bf16[128,1536]{1,0:T(8,128)(2,1)S(1)} %get-tuple-element.32), channel_id=1, source_target_pairs={{0,48},{1,7},{2,50},{3,1},{4,52},{5,3},{6,54},{7,5},{16,0},{17,23}... | collective-permute-start | bytes 1179656 | tf_op jit(solution)/shard_map/ppermute | solution.py:38
  9.7 13.1 %collective-permute-start.4 = (bf16[128,1536]{1,0:T(8,128)(2,1)S(1)}, bf16[128,1536]{1,0:T(8,128)(2,1)S(1)}, u32[]{:S(2)}, u32[]{:S(2)}) collective-permute-start(bf16[128,1536]{1,0:T(8,128)(2,1)S(1)} %get-tuple-element.35), channel_id=1, source_target_pairs={{0,32},{1,5},{2,34},{3,7},{4,36},{5,1},{6,38},{7,3},{16,48},{17,21... | collective-permute-start | bytes 1179656 | tf_op jit(solution)/shard_map/ppermute | solution.py:38
  10.6 16.4 %collective-permute-start.5 = (bf16[128,1536]{1,0:T(8,128)(2,1)S(1)}, bf16[128,1536]{1,0:T(8,128)(2,1)S(1)}, u32[]{:S(2)}, u32[]{:S(2)}) collective-permute-start(bf16[128,1536]{1,0:T(8,128)(2,1)S(1)} %get-tuple-element.36), channel_id=1, source_target_pairs={{0,16},{1,3},{2,18},{3,5},{4,20},{5,7},{6,22},{7,1},{16,32},{17,19... | collective-permute-start | bytes 1179656 | tf_op jit(solution)/shard_map/ppermute | solution.py:38
  14.4 12.6 %collective-permute-start.6 = (bf16[128,1536]{1,0:T(8,128)(2,1)S(1)}, bf16[128,1536]{1,0:T(8,128)(2,1)S(1)}, u32[]{:S(2)}, u32[]{:S(2)}) collective-permute-start(bf16[128,1536]{1,0:T(8,128)(2,1)S(1)} %get-tuple-element.37), channel_id=1, source_target_pairs={{0,48},{1,7},{2,50},{3,1},{4,52},{5,3},{6,54},{7,5},{16,0},{17,23}... | collective-permute-start | bytes 1179656 | tf_op jit(solution)/shard_map/ppermute | solution.py:38
  15.2 17.2 %copy-start.2 = (bf16[2,128,512]{2,1,0:T(8,128)(2,1)S(1)}, bf16[2,128,512]{2,1,0:T(8,128)(2,1)}, u32[]{:S(2)}) copy-start(bf16[2,128,512]{2,1,0:T(8,128)(2,1)} %param.9) | copy-start | bytes 786436
  28.3 41.7 %copy-start.3 = (s32[32]{0:T(128)S(1)}, s32[32]{0:T(128)}, u32[]{:S(2)}) copy-start(s32[32]{0:T(128)} %param.10) | copy-start | bytes 388
  28.3 7.1 %collective-permute-start.7 = (bf16[256,512]{1,0:T(8,128)(2,1)S(1)}, bf16[256,512]{1,0:T(8,128)(2,1)S(1)}, u32[]{:S(2)}, u32[]{:S(2)}) collective-permute-start(bf16[256,512]{1,0:T(8,128)(2,1)S(1)} %get-tuple-element.38), channel_id=1, source_target_pairs={{0,4},{1,33},{2,6},{3,35},{4,0},{5,37},{6,2},{7,39},{16,20},{17,49... | collective-permute-start | bytes 786440 | tf_op jit(solution)/shard_map/ppermute | solution.py:38
  29.7 8.5 %collective-permute-start.8 = (bf16[256,512]{1,0:T(8,128)(2,1)S(1)}, bf16[256,512]{1,0:T(8,128)(2,1)S(1)}, u32[]{:S(2)}, u32[]{:S(2)}) collective-permute-start(bf16[256,512]{1,0:T(8,128)(2,1)S(1)} %get-tuple-element.39), channel_id=1, source_target_pairs={{0,2},{1,17},{2,4},{3,19},{4,6},{5,21},{6,0},{7,23},{16,18},{17,33... | collective-permute-start | bytes 786440 | tf_op jit(solution)/shard_map/ppermute | solution.py:38
  30.1 8.1 %collective-permute-start.9 = (bf16[256,512]{1,0:T(8,128)(2,1)S(1)}, bf16[256,512]{1,0:T(8,128)(2,1)S(1)}, u32[]{:S(2)}, u32[]{:S(2)}) collective-permute-start(bf16[256,512]{1,0:T(8,128)(2,1)S(1)} %get-tuple-element.40), channel_id=1, source_target_pairs={{0,6},{1,49},{2,0},{3,51},{4,2},{5,53},{6,4},{7,55},{16,22},{17,1}... | collective-permute-start | bytes 786440 | tf_op jit(solution)/shard_map/ppermute | solution.py:38
  38.5 32.9 %copy-start.1 = (s32[32]{0:T(128)S(1)}, s32[32]{0:T(128)}, u32[]{:S(2)}) copy-start(s32[32]{0:T(128)} %refresh.1) | copy-start | bytes 388
  38.5 13.7 %collective-permute-start.12 = (bf16[3,128,512]{2,1,0:T(8,128)(2,1)S(1)}, bf16[3,128,512]{2,1,0:T(8,128)(2,1)S(1)}, u32[]{:S(2)}, u32[]{:S(2)}) collective-permute-start(bf16[3,128,512]{2,1,0:T(8,128)(2,1)S(1)} %pad_maximum_fusion.p0), channel_id=1, source_target_pairs={{0,1},{1,0},{2,3},{3,2},{4,5},{5,4},{6,7},{7,6},{8,9},{9,8},{10,11... | collective-permute-start | bytes 1179656 | tf_op jit(solution)/shard_map/ppermute | solution.py:63
  40.4 7.5 %collective-permute-start.10 = (bf16[128,512]{1,0:T(8,128)(2,1)S(1)}, bf16[128,512]{1,0:T(8,128)(2,1)S(1)}, u32[]{:S(2)}, u32[]{:S(2)}) collective-permute-start(bf16[128,512]{1,0:T(8,128)(2,1)S(1)} %get-tuple-element.46), channel_id=1, source_target_pairs={{0,1},{1,201},{64,65},{65,137},{128,129},{129,73},{192,193},{193,9... | collective-permute-start | bytes 393224 | tf_op jit(solution)/shard_map/ppermute | solution.py:58
  44.7 7.5 %collective-permute-start.11 = (bf16[128,512]{1,0:T(8,128)(2,1)S(1)}, bf16[128,512]{1,0:T(8,128)(2,1)S(1)}, u32[]{:S(2)}, u32[]{:S(2)}) collective-permute-start(bf16[128,512]{1,0:T(8,128)(2,1)S(1)} %get-tuple-element.47), channel_id=1, source_target_pairs={{1,200},{65,136},{129,72},{193,8},{8,193},{72,129},{136,65},{200,1... | collective-permute-start | bytes 393224 | tf_op jit(solution)/shard_map/ppermute | solution.py:58
  46.6 13.2 %collective-permute-start.14 = (bf16[3,128,512]{2,1,0:T(8,128)(2,1)S(1)}, bf16[3,128,512]{2,1,0:T(8,128)(2,1)S(1)}, u32[]{:S(2)}, u32[]{:S(2)}) collective-permute-start(bf16[3,128,512]{2,1,0:T(8,128)(2,1)S(1)} %pad_maximum_fusion.p0), channel_id=1, source_target_pairs={{0,2},{2,0},{1,3},{3,1},{4,6},{6,4},{5,7},{7,5},{8,10},{10,8},{9,1... | collective-permute-start | bytes 1179656 | tf_op jit(solution)/shard_map/ppermute | solution.py:63
  52.2 7.6 %collective-permute-start.13 = (bf16[128,512]{1,0:T(8,128)(2,1)S(1)}, bf16[128,512]{1,0:T(8,128)(2,1)S(1)}, u32[]{:S(2)}, u32[]{:S(2)}) collective-permute-start(bf16[128,512]{1,0:T(8,128)(2,1)S(1)} %mirror_sum.1), channel_id=1, source_target_pairs={{0,64},{64,0},{128,192},{192,128},{8,72},{72,8},{136,200},{200,136... | collective-permute-start | bytes 393224 | tf_op jit(solution)/shard_map/ppermute | solution.py:47
  59.8 6.2 %collective-permute-start.15 = (bf16[128,512]{1,0:T(8,128)(2,1)S(1)}, bf16[128,512]{1,0:T(8,128)(2,1)S(1)}, u32[]{:S(2)}, u32[]{:S(2)}) collective-permute-start(bf16[128,512]{1,0:T(8,128)(2,1)S(1)} %add_convert_fusion.1), channel_id=1, source_target_pairs={{0,128},{64,192},{128,0},{192,64},{8,136},{72,200},{136,8},{200,72... | collective-permute-start | bytes 393224 | tf_op jit(solution)/shard_map/ppermute | solution.py:47
  61.7 8.3 %collective-permute-start.19 = (bf16[3,128,512]{2,1,0:T(8,128)(2,1)S(1)}, bf16[3,128,512]{2,1,0:T(8,128)(2,1)S(1)}, u32[]{:S(2)}, u32[]{:S(2)}) collective-permute-start(bf16[3,128,512]{2,1,0:T(8,128)(2,1)S(1)} %collective-permute-done.14.p1), channel_id=1, source_target_pairs={{0,1},{1,0},{2,3},{3,2},{4,5},{5,4},{6,7},{7,6},{8,9},{9,8},{10,11... | collective-permute-start | bytes 1179656 | tf_op jit(solution)/shard_map/ppermute | solution.py:63
  66.1 3.9 %collective-permute-start.16 = (bf16[128,512]{1,0:T(8,128)(2,1)S(1)}, bf16[128,512]{1,0:T(8,128)(2,1)S(1)}, u32[]{:S(2)}, u32[]{:S(2)}) collective-permute-start(bf16[128,512]{1,0:T(8,128)(2,1)S(1)} %add_convert_fusion.g0), channel_id=1, source_target_pairs={{0,2},{2,0},{1,3},{3,1},{4,6},{6,4},{5,7},{7,5},{8,10},{10,8},{9,1... | collective-permute-start | bytes 393224 | tf_op jit(solution)/shard_map/ppermute | solution.py:63
  67.4 2.8 %collective-permute-start.17 = (bf16[128,512]{1,0:T(8,128)(2,1)S(1)}, bf16[128,512]{1,0:T(8,128)(2,1)S(1)}, u32[]{:S(2)}, u32[]{:S(2)}) collective-permute-start(bf16[128,512]{1,0:T(8,128)(2,1)S(1)} %add_convert_fusion.g0), channel_id=1, source_target_pairs={{0,1},{1,0},{2,3},{3,2},{4,5},{5,4},{6,7},{7,6},{8,9},{9,8},{10,11... | collective-permute-start | bytes 393224 | tf_op jit(solution)/shard_map/ppermute | solution.py:63
  70.0 1.3 %collective-permute-start.18 = (bf16[128,512]{1,0:T(8,128)(2,1)S(1)}, bf16[128,512]{1,0:T(8,128)(2,1)S(1)}, u32[]{:S(2)}, u32[]{:S(2)}) collective-permute-start(bf16[128,512]{1,0:T(8,128)(2,1)S(1)} %collective-permute-done.16.g1), channel_id=1, source_target_pairs={{0,1},{1,0},{2,3},{3,2},{4,5},{5,4},{6,7},{7,6},{8,9},{9,8},{10,11... | collective-permute-start | bytes 393224 | tf_op jit(solution)/shard_map/ppermute | solution.py:63

commit v7 on v6

--- a/solution.py
+++ b/solution.py
@@ -77,7 +77,7 @@
 
 
 def finish_kernel(decays, refresh, g0, g1, g2, g3, old_stats, old_right, left_old,
-                  update, new_stats, new_roots, grad, full, right, work):
+                  update, new_stats, new_roots, grad, full, right, left, result, work, sem):
     at = places()
     quarter = at["x_lo"] * 2 + at["core"]
     own = quarter_rows(at, 0, 0)
@@ -88,13 +88,18 @@
         for b in range(2):
             grad[quarter_rows(at, a, b), :] = (g0, g1, g2, g3)[2 * b + a][...]
     g = grad[...]
+    writes = []
+
+    def write(i, src, dst):
+        writes.append(pltpu.make_async_copy(src, dst, sem.at[i]))
+        writes[-1].start()
 
     def refresh_stats(layer, gram):
         old = old_stats[layer]
         d = decay[layer]
         a = jnp.where(fresh[layer] == 1, d * old + (1.0 - d) * gram, old)
         full[layer] = a
-        new_stats[layer] = full[layer, own, :]
+        write(layer, full.at[layer, own, :], new_stats.at[layer])
         total = jnp.sum(jnp.sum(a * a, axis=0, keepdims=True), axis=1, keepdims=True)
         scaling = 2.5 / jnp.sqrt(total + tiny_term)
         return scaling * a, jnp.sqrt(jnp.sqrt(scaling))
@@ -134,13 +139,15 @@
         lambda e, v, v3, p, s: narrow(s * (e + 1.25 * v - 0.390625 * v3 - 0.25 * p)),
         diagonal, y, first[2], product, scale,
     )
-    root = jnp.where(fresh[1] == 1, out[1], old_right[...])
-    mixed = narrow(dot(g, root))
-    right[...] = root
-    new_roots[1] = right[own, :]
-    left = jnp.where(fresh[0] == 1, out[0], left_old[...])
-    new_roots[0] = left
-    update[...] = narrow(dot(left, mixed) * math.sqrt(B))
+    left[...] = jnp.where(fresh[0] == 1, out[0], left_old[...])
+    write(2, left, new_roots.at[0])
+    right[...] = jnp.where(fresh[1] == 1, out[1], old_right[...])
+    write(3, right.at[own, :], new_roots.at[1])
+    mixed = narrow(dot(g, right[...]))
+    result[...] = narrow(dot(left[...], mixed) * math.sqrt(B))
+    write(4, result, update)
+    for w in writes:
+        w.wait()
 
 
 def finish(decays, refresh, *arrays):
@@ -154,12 +161,15 @@
             jax.ShapeDtypeStruct((2, ROWS, B), jnp.bfloat16),
         ),
         in_specs=[smem] * 2 + [VMEM] * 7,
-        out_specs=(VMEM,) * 3,
+        out_specs=(pl.BlockSpec(memory_space=pltpu.HBM),) * 3,
         scratch_shapes=[
             pltpu.VMEM((B, B), jnp.bfloat16),
             pltpu.VMEM((2, B, B), jnp.float32),
             pltpu.VMEM((B, B), jnp.bfloat16),
+            pltpu.VMEM((ROWS, B), jnp.bfloat16),
+            pltpu.VMEM((ROWS, B), jnp.bfloat16),
             pltpu.VMEM((3, B, B), jnp.float32),
+            pltpu.SemaphoreType.DMA((5,)),
         ],
         compiler_params=pltpu.CompilerParams(vmem_limit_bytes=16 << 20),
         cost_estimate=pl.CostEstimate(flops=18 * 2 * B**3, bytes_accessed=6 << 20, transcendentals=0),
@@ -232,27 +242,31 @@
     )(pieces)
 
 
-def product_kernel(*refs):
-    parts, outs = refs[:8], refs[8:]
+def product_kernel(count, *refs):
+    parts, before, outs = refs[:count], refs[count:-4], refs[-4:]
     at = places()
     me = jnp.where(at["core"] == 0, at["x_hi"] * 2 + at["x_lo"], at["y"])
     right = jnp.concatenate([p[:, 2 * B :] for p in parts], axis=0)
-    for k, out in zip(ORDER, outs):
-        columns = pl.ds(pl.multiple_of(lax.rem(me + k, 4) * HALF, HALF), HALF)
+    for i, out in enumerate(outs):
+        columns = pl.ds(pl.multiple_of(lax.rem(me + ORDER[i], 4) * HALF, HALF), HALF)
         left = jnp.concatenate([p[:, columns] for p in parts], axis=0)
-        out[...] = dot(left, right, (0, 0)).astype(out.dtype)
-
-
-def product(parts):
-    return pl.pallas_call(
-        product_kernel,
+        total = dot(left, right, (0, 0))
+        if before:
+            total += before[i][...]
+        out[...] = total.astype(out.dtype)
+
+
+def product(parts, before=()):
+    send = SEND if before else jnp.float32
+    return pl.pallas_call(
+        functools.partial(product_kernel, len(parts)),
         name="product",
-        out_shape=(jax.ShapeDtypeStruct((HALF, B), SEND),) * 3 + (jax.ShapeDtypeStruct((HALF, B), jnp.float32),),
-        in_specs=[VMEM] * 8,
+        out_shape=(jax.ShapeDtypeStruct((HALF, B), send),) * 3 + (jax.ShapeDtypeStruct((HALF, B), jnp.float32),),
+        in_specs=[VMEM] * (len(parts) + len(before)),
         out_specs=(VMEM,) * 4,
         compiler_params=pltpu.CompilerParams(vmem_limit_bytes=8 << 20),
-        cost_estimate=pl.CostEstimate(flops=8 * B**3, bytes_accessed=5 << 20, transcendentals=0),
-    )(*parts)
+        cost_estimate=pl.CostEstimate(flops=len(parts) * B**3, bytes_accessed=4 << 20, transcendentals=0),
+    )(*parts, *before)
 
 
 def plane_sum_kernel(first, second, third, own, keep, near, far):
@@ -351,18 +365,20 @@
 
 def per_device(activations, cotangents, statistics, roots, ages, refresh):
     decays = decay_base ** ages.astype(jnp.float32)
-    *pieces, other = cut(cotangents, activations)
-    parts = [pieces[3]] + [shift(pieces[i], True, ORDER[i]) for i in range(3)]
+    *own_pieces, other = cut(cotangents, activations)
+    own_came = [shift(own_pieces[i], True, ORDER[i]) for i in range(3)]
     pieces = split(partner(other, "core"))
-    parts += [pieces[3]] + [shift(pieces[i], True, ORDER[i]) for i in range(3)]
-
-    *sends, own = product(parts)
-    keep, near, far = plane_sum([shift(sends[i], False, ORDER[i]) for i in range(3)] + [own])
+    came = [shift(pieces[i], True, ORDER[i]) for i in range(3)]
+
+    early = product([own_pieces[3], pieces[3]] + own_came)
+    *sends, own = product(came, early)
+    came = [shift(sends[i], False, ORDER[i]) for i in range(3)]
     pack = jnp.concatenate([narrow(statistics), roots[1:]], axis=0)
+    own, pack_core = lax.optimization_barrier((own, partner(pack, "core")))
+    keep, near, far = plane_sum(came + [own])
     keep, near, far, pack = lax.optimization_barrier((keep, near, far, pack))
     part = mirror_sum(keep, *mirror(near, far))
     pack_x = partner(pack, "x_lo")
-    part, pack_core = lax.optimization_barrier((part, partner(pack, "core")))
     part = rounded(part.astype(jnp.float32) + swap_z(part, 1).astype(jnp.float32))
     part, pack_x = lax.optimization_barrier((part, pack_x))
     part = rounded(part.astype(jnp.float32) + swap_z(part, 2).astype(jnp.float32))

time: 78.9 us -> 76.5 us (0.970)
  waiting for transfers between devices: 36.6 us -> 32.4 us
  starting transfers between devices: 30 us -> 31.2 us
    ppermute x9, waiting for transfers between devices: 21.4 us -> 19.5 us  [shift(): return lax.ppermute(x, ('y',) + X + ('core',), pairs)]
    ppermute x2, starting transfers between devices: 6.22 us -> 8.01 us  [mirror(): return (lax.ppermute(near, axes, first), lax.ppermute(far, axes, second))]
    ppermute x2, waiting for transfers between devices: 4.29 us -> 2.58 us  [mirror(): return (lax.ppermute(near, axes, first), lax.ppermute(far, axes, second))]
    ppermute x7, starting transfers between devices: 7.8 us -> 6.86 us  [partner(): return lax.ppermute(x, axis, [(i, i ^ bits) for i in range(n)])]
    pallas_call x1 -> x2, Pallas kernels: 1.29 us -> 1.78 us  [product(): pl.pallas_call(functools.partial(product_kernel, len(parts)), name='produ...]
  transfers between devices with their start and end apart: 20 -> 20, of which waited for: 11 -> 11; matrix products, arithmetic and copies ran while one was open for 0% -> 0% of each run, Pallas kernels for 0% -> 3%
where the time goes in v7:
time: 76.5 us; the launch traced here: 76.4 us
  waiting for transfers between devices  32.4 us (42%)
  starting transfers between devices  31.2 us (41%)
  Pallas kernels  11.6 us (15%)
  between operations  0.95 us (1%)
    ppermute x9, waiting for transfers between devices, shift(): return lax.ppermute(x, ('y',) + X + ('core',), pairs)  19.5 us
    ppermute x9, starting transfers between devices, shift(): return lax.ppermute(x, ('y',) + X + ('core',), pairs)  9.31 us
    ppermute x2, starting transfers between devices, mirror(): return (lax.ppermute(near, axes, first), lax.ppermute(far, axes, second))  8.01 us
    pallas_call x1, Pallas kernels, finish(): pl.pallas_call(finish_kernel, name='finish', out_shape=(jax.ShapeDtypeStr...  7.32 us
    ppermute x2, starting transfers between devices, swap_z(): lax.ppermute(x, Z, [(ring_spot(z), ring_spot(z ^ bits)) for z in range(8)])  7.01 us
    ppermute x7, starting transfers between devices, partner(): return lax.ppermute(x, axis, [(i, i ^ bits) for i in range(n)])  6.86 us
    ppermute x2, waiting for transfers between devices, swap_z(): lax.ppermute(x, Z, [(ring_spot(z), ring_spot(z ^ bits)) for z in range(8)])  6.65 us
    ppermute x7, waiting for transfers between devices, partner(): return lax.ppermute(x, axis, [(i, i ^ bits) for i in range(n)])  3.75 us
  transfers between devices with their start and end apart: 20, of which 11 were waited for; matrix products, arithmetic and copies ran while one was open for 0% of the time, Pallas kernels for 3%

profile of v7, /device:TPU:1, one launch (start us, length us, event | category | flops | bytes accessed | tf_op | source)
XLA Modules:
  0.0 76.4 jit_solution(14584660036788271432)
XLA Ops:
  0.7 2.0 %cut.1 = (bf16[128,1536]{1,0:T(8,128)(2,1)S(1)}, bf16[128,1536]{1,0:T(8,128)(2,1)S(1)}, bf16[128,1536]{1,0:T(8,128)(2,1)S(1)}, bf16[128,1536]{1,0:T(8,128)(2,1)S(1)}, bf16[4,128,1536]{2,1,0:T(8,128)(2,1)S(1)}) custom-call(bf16[128,8192]{1,0:T(8,128)(2,1)} %cotangents.1, bf16[128,512]{1,0:T(8,128)(2,1)} %activations.1), custom_call_target="tpu_custom_call" | custom-call | bytes 6291456 | tf_op jit(solution)/shard_map/cut/pallas_call | solution.py:215
  2.6 3.3 %collective-permute-start = (bf16[4,128,1536]{2,1,0:T(8,128)(2,1)S(1)}, bf16[4,128,1536]{2,1,0:T(8,128)(2,1)S(1)}, u32[]{:S(2)}, u32[]{:S(2)}) collective-permute-start(bf16[4,128,1536]{2,1,0:T(8,128)(2,1)S(1)} %get-tuple-element.33), channel_id=1, source_target_pairs={{0,1},{1,0},{2,3},{3,2},{4,5},{5,4},{6,7},{7,6},{8,9},{9,8},{10,11... | collective-permute-start | bytes 4718600 | tf_op jit(solution)/shard_map/ppermute | solution.py:63
  7.3 2.4 %collective-permute-start.6 = (bf16[128,1536]{1,0:T(8,128)(2,1)S(1)}, bf16[128,1536]{1,0:T(8,128)(2,1)S(1)}, u32[]{:S(2)}, u32[]{:S(2)}) collective-permute-start(bf16[128,1536]{1,0:T(8,128)(2,1)S(1)} %get-tuple-element.41), channel_id=1, source_target_pairs={{0,48},{1,7},{2,50},{3,1},{4,52},{5,3},{6,54},{7,5},{16,0},{17,23}... | collective-permute-start | bytes 1179656 | tf_op jit(solution)/shard_map/ppermute | solution.py:38
  10.7 3.8 %collective-permute-done.4.refs_2_ = bf16[128,1536]{1,0:T(8,128)(2,1)S(1)} collective-permute-done((bf16[128,1536]{1,0:T(8,128)(2,1)S(1)}, bf16[128,1536]{1,0:T(8,128)(2,1)S(1)}, u32[]{:S(2)}, u32[]{:S(2)}) %collective-permute-start.4) | collective-permute-done | bytes 393248 | tf_op jit(solution)/shard_map/ppermute | solution.py:38
  15.2 3.4 %collective-permute-done.5.refs_3_ = bf16[128,1536]{1,0:T(8,128)(2,1)S(1)} collective-permute-done((bf16[128,1536]{1,0:T(8,128)(2,1)S(1)}, bf16[128,1536]{1,0:T(8,128)(2,1)S(1)}, u32[]{:S(2)}, u32[]{:S(2)}) %collective-permute-start.5) | collective-permute-done | bytes 393248 | tf_op jit(solution)/shard_map/ppermute | solution.py:38
  19.6 1.0 %product.2 = (f32[256,512]{1,0:T(8,128)S(1)}, f32[256,512]{1,0:T(8,128)S(1)}, f32[256,512]{1,0:T(8,128)S(1)}, f32[256,512]{1,0:T(8,128)S(1)}) custom-call(bf16[128,1536]{1,0:T(8,128)(2,1)S(1)} %get-tuple-element.37.refs_0_, bf16[128,1536]{1,0:T(8,128)(2,1)S(1)} %get-tuple-element.38.refs_1_, bf16[128,1536]{1,0:T(8,128)(2,1)S(1)} %collective-permute-done.4.refs_2_, ...), custom_call_target="tpu_custom_call" | custom-call | flops 671088640 | bytes 4194304 | tf_op jit(solution)/shard_map/product/pallas_call | solution.py:261
  20.6 2.3 %collective-permute-done.1.refs_0_ = bf16[128,1536]{1,0:T(8,128)(2,1)S(1)} collective-permute-done((bf16[128,1536]{1,0:T(8,128)(2,1)S(1)}, bf16[128,1536]{1,0:T(8,128)(2,1)S(1)}, u32[]{:S(2)}, u32[]{:S(2)}) %collective-permute-start.1) | collective-permute-done | bytes 393248 | tf_op jit(solution)/shard_map/ppermute | solution.py:38
  22.9 4.1 %collective-permute-done.2.refs_1_ = bf16[128,1536]{1,0:T(8,128)(2,1)S(1)} collective-permute-done((bf16[128,1536]{1,0:T(8,128)(2,1)S(1)}, bf16[128,1536]{1,0:T(8,128)(2,1)S(1)}, u32[]{:S(2)}, u32[]{:S(2)}) %collective-permute-start.2) | collective-permute-done | bytes 393248 | tf_op jit(solution)/shard_map/ppermute | solution.py:38
  27.8 1.4 %collective-permute-start.7 = (bf16[256,512]{1,0:T(8,128)(2,1)S(1)}, bf16[256,512]{1,0:T(8,128)(2,1)S(1)}, u32[]{:S(2)}, u32[]{:S(2)}) collective-permute-start(bf16[256,512]{1,0:T(8,128)(2,1)S(1)} %get-tuple-element.46), channel_id=1, source_target_pairs={{0,4},{1,33},{2,6},{3,35},{4,0},{5,37},{6,2},{7,39},{16,20},{17,49... | collective-permute-start | bytes 786440 | tf_op jit(solution)/shard_map/ppermute | solution.py:38
  29.6 2.3 %collective-permute-start.9 = (bf16[256,512]{1,0:T(8,128)(2,1)S(1)}, bf16[256,512]{1,0:T(8,128)(2,1)S(1)}, u32[]{:S(2)}, u32[]{:S(2)}) collective-permute-start(bf16[256,512]{1,0:T(8,128)(2,1)S(1)} %get-tuple-element.48), channel_id=1, source_target_pairs={{0,6},{1,49},{2,0},{3,51},{4,2},{5,53},{6,4},{7,55},{16,22},{17,1}... | collective-permute-start | bytes 786440 | tf_op jit(solution)/shard_map/ppermute | solution.py:38
  31.9 3.1 %collective-permute-done.7.first = bf16[256,512]{1,0:T(8,128)(2,1)S(1)} collective-permute-done((bf16[256,512]{1,0:T(8,128)(2,1)S(1)}, bf16[256,512]{1,0:T(8,128)(2,1)S(1)}, u32[]{:S(2)}, u32[]{:S(2)}) %collective-permute-start.7) | collective-permute-done | bytes 262176 | tf_op jit(solution)/shard_map/ppermute | solution.py:38
  35.0 2.8 %collective-permute-done.8.second = bf16[256,512]{1,0:T(8,128)(2,1)S(1)} collective-permute-done((bf16[256,512]{1,0:T(8,128)(2,1)S(1)}, bf16[256,512]{1,0:T(8,128)(2,1)S(1)}, u32[]{:S(2)}, u32[]{:S(2)}) %collective-permute-start.8) | collective-permute-done | bytes 262176 | tf_op jit(solution)/shard_map/ppermute | solution.py:38
  38.0 4.4 %collective-permute-start.11 = (bf16[128,512]{1,0:T(8,128)(2,1)S(1)}, bf16[128,512]{1,0:T(8,128)(2,1)S(1)}, u32[]{:S(2)}, u32[]{:S(2)}) collective-permute-start(bf16[128,512]{1,0:T(8,128)(2,1)S(1)} %get-tuple-element.55), channel_id=1, source_target_pairs={{0,1},{1,201},{64,65},{65,137},{128,129},{129,73},{192,193},{193,9... | collective-permute-start | bytes 393224 | tf_op jit(solution)/shard_map/ppermute | solution.py:58
  42.4 3.6 %collective-permute-start.12 = (bf16[128,512]{1,0:T(8,128)(2,1)S(1)}, bf16[128,512]{1,0:T(8,128)(2,1)S(1)}, u32[]{:S(2)}, u32[]{:S(2)}) collective-permute-start(bf16[128,512]{1,0:T(8,128)(2,1)S(1)} %get-tuple-element.56), channel_id=1, source_target_pairs={{1,200},{65,136},{129,72},{193,8},{8,193},{72,129},{136,65},{200,1... | collective-permute-start | bytes 393224 | tf_op jit(solution)/shard_map/ppermute | solution.py:58
  46.0 1.3 %collective-permute-start.14 = (bf16[3,128,512]{2,1,0:T(8,128)(2,1)S(1)}, bf16[3,128,512]{2,1,0:T(8,128)(2,1)S(1)}, u32[]{:S(2)}, u32[]{:S(2)}) collective-permute-start(bf16[3,128,512]{2,1,0:T(8,128)(2,1)S(1)} %pad_maximum_fusion.p0), channel_id=1, source_target_pairs={{0,2},{2,0},{1,3},{3,1},{4,6},{6,4},{5,7},{7,5},{8,10},{10,8},{9,1... | collective-permute-start | bytes 1179656 | tf_op jit(solution)/shard_map/ppermute | solution.py:63
  47.3 2.6 %collective-permute-done.12.far = bf16[128,512]{1,0:T(8,128)(2,1)S(1)} collective-permute-done((bf16[128,512]{1,0:T(8,128)(2,1)S(1)}, bf16[128,512]{1,0:T(8,128)(2,1)S(1)}, u32[]{:S(2)}, u32[]{:S(2)}) %collective-permute-start.12) | collective-permute-done | bytes 131104 | tf_op jit(solution)/shard_map/ppermute | solution.py:58
  49.9 4.8 %collective-permute-start.13 = (bf16[128,512]{1,0:T(8,128)(2,1)S(1)}, bf16[128,512]{1,0:T(8,128)(2,1)S(1)}, u32[]{:S(2)}, u32[]{:S(2)}) collective-permute-start(bf16[128,512]{1,0:T(8,128)(2,1)S(1)} %mirror_sum.1), channel_id=1, source_target_pairs={{0,64},{64,0},{128,192},{192,128},{8,72},{72,8},{136,200},{200,136... | collective-permute-start | bytes 393224 | tf_op jit(solution)/shard_map/ppermute | solution.py:47
  54.7 2.4 %collective-permute-done.13 = bf16[128,512]{1,0:T(8,128)(2,1)S(1)} collective-permute-done((bf16[128,512]{1,0:T(8,128)(2,1)S(1)}, bf16[128,512]{1,0:T(8,128)(2,1)S(1)}, u32[]{:S(2)}, u32[]{:S(2)}) %collective-permute-start.13) | collective-permute-done | bytes 131104 | tf_op jit(solution)/shard_map/ppermute | solution.py:47
  57.1 2.2 %collective-permute-start.15 = (bf16[128,512]{1,0:T(8,128)(2,1)S(1)}, bf16[128,512]{1,0:T(8,128)(2,1)S(1)}, u32[]{:S(2)}, u32[]{:S(2)}) collective-permute-start(bf16[128,512]{1,0:T(8,128)(2,1)S(1)} %add_convert_fusion.1), channel_id=1, source_target_pairs={{0,128},{64,192},{128,0},{192,64},{8,136},{72,200},{136,8},{200,72... | collective-permute-start | bytes 393224 | tf_op jit(solution)/shard_map/ppermute | solution.py:47
  59.3 4.3 %collective-permute-done.15 = bf16[128,512]{1,0:T(8,128)(2,1)S(1)} collective-permute-done((bf16[128,512]{1,0:T(8,128)(2,1)S(1)}, bf16[128,512]{1,0:T(8,128)(2,1)S(1)}, u32[]{:S(2)}, u32[]{:S(2)}) %collective-permute-start.15) | collective-permute-done | bytes 131104 | tf_op jit(solution)/shard_map/ppermute | solution.py:47
  63.6 1.3 %collective-permute-start.16 = (bf16[128,512]{1,0:T(8,128)(2,1)S(1)}, bf16[128,512]{1,0:T(8,128)(2,1)S(1)}, u32[]{:S(2)}, u32[]{:S(2)}) collective-permute-start(bf16[128,512]{1,0:T(8,128)(2,1)S(1)} %add_convert_fusion.g0), channel_id=1, source_target_pairs={{0,2},{2,0},{1,3},{3,1},{4,6},{6,4},{5,7},{7,5},{8,10},{10,8},{9,1... | collective-permute-start | bytes 393224 | tf_op jit(solution)/shard_map/ppermute | solution.py:63
  64.9 2.6 %collective-permute-done.16.g1 = bf16[128,512]{1,0:T(8,128)(2,1)S(1)} collective-permute-done((bf16[128,512]{1,0:T(8,128)(2,1)S(1)}, bf16[128,512]{1,0:T(8,128)(2,1)S(1)}, u32[]{:S(2)}, u32[]{:S(2)}) %collective-permute-start.16) | collective-permute-done | bytes 131104 | tf_op jit(solution)/shard_map/ppermute | solution.py:63
  67.8 1.1 %collective-permute-done.18.g3 = bf16[128,512]{1,0:T(8,128)(2,1)S(1)} collective-permute-done((bf16[128,512]{1,0:T(8,128)(2,1)S(1)}, bf16[128,512]{1,0:T(8,128)(2,1)S(1)}, u32[]{:S(2)}, u32[]{:S(2)}) %collective-permute-start.18) | collective-permute-done | bytes 131104 | tf_op jit(solution)/shard_map/ppermute | solution.py:63
  68.9 7.3 %finish.1 = (bf16[128,512]{1,0:T(8,128)(2,1)}, f32[2,128,512]{2,1,0:T(8,128)}, bf16[2,128,512]{2,1,0:T(8,128)(2,1)}) custom-call(f32[32]{0:T(128)S(1)} %convert_power_fusion.decays, s32[32]{0:T(128)S(1)} %copy-done.1, bf16[128,512]{1,0:T(8,128)(2,1)S(1)} %add_convert_fusion.g0, bf16[128,512]{1,0:T(8,128)(2,1)S(1)} %collective-permute-done.16.g1, ...), custom_call_target="tpu_custom_call" | custom-call | flops 4831838208 | bytes 6291456 | tf_op jit(solution)/shard_map/finish/pallas_call | solution.py:155
  (38 shorter events, 5.7 us)
Async XLA Ops:
  0.6 9.0 %copy-start = (f32[2,128,512]{2,1,0:T(8,128)S(1)}, f32[2,128,512]{2,1,0:T(8,128)}, u32[]{:S(2)}) copy-start(f32[2,128,512]{2,1,0:T(8,128)} %own.1) | copy-start | bytes 1572868
  0.6 14.5 %copy-start.2 = (bf16[2,128,512]{2,1,0:T(8,128)(2,1)S(1)}, bf16[2,128,512]{2,1,0:T(8,128)(2,1)}, u32[]{:S(2)}) copy-start(bf16[2,128,512]{2,1,0:T(8,128)(2,1)} %param.9) | copy-start | bytes 786436
  2.6 7.1 %collective-permute-start = (bf16[4,128,1536]{2,1,0:T(8,128)(2,1)S(1)}, bf16[4,128,1536]{2,1,0:T(8,128)(2,1)S(1)}, u32[]{:S(2)}, u32[]{:S(2)}) collective-permute-start(bf16[4,128,1536]{2,1,0:T(8,128)(2,1)S(1)} %get-tuple-element.33), channel_id=1, source_target_pairs={{0,1},{1,0},{2,3},{3,2},{4,5},{5,4},{6,7},{7,6},{8,9},{9,8},{10,11... | collective-permute-start | bytes 4718600 | tf_op jit(solution)/shard_map/ppermute | solution.py:63
  6.0 8.5 %collective-permute-start.4 = (bf16[128,1536]{1,0:T(8,128)(2,1)S(1)}, bf16[128,1536]{1,0:T(8,128)(2,1)S(1)}, u32[]{:S(2)}, u32[]{:S(2)}) collective-permute-start(bf16[128,1536]{1,0:T(8,128)(2,1)S(1)} %get-tuple-element.39), channel_id=1, source_target_pairs={{0,32},{1,5},{2,34},{3,7},{4,36},{5,1},{6,38},{7,3},{16,48},{17,21... | collective-permute-start | bytes 1179656 | tf_op jit(solution)/shard_map/ppermute | solution.py:38
  7.0 11.6 %collective-permute-start.5 = (bf16[128,1536]{1,0:T(8,128)(2,1)S(1)}, bf16[128,1536]{1,0:T(8,128)(2,1)S(1)}, u32[]{:S(2)}, u32[]{:S(2)}) collective-permute-start(bf16[128,1536]{1,0:T(8,128)(2,1)S(1)} %get-tuple-element.40), channel_id=1, source_target_pairs={{0,16},{1,3},{2,18},{3,5},{4,20},{5,7},{6,22},{7,1},{16,32},{17,19... | collective-permute-start | bytes 1179656 | tf_op jit(solution)/shard_map/ppermute | solution.py:38
  7.3 12.3 %collective-permute-start.6 = (bf16[128,1536]{1,0:T(8,128)(2,1)S(1)}, bf16[128,1536]{1,0:T(8,128)(2,1)S(1)}, u32[]{:S(2)}, u32[]{:S(2)}) collective-permute-start(bf16[128,1536]{1,0:T(8,128)(2,1)S(1)} %get-tuple-element.41), channel_id=1, source_target_pairs={{0,48},{1,7},{2,50},{3,1},{4,52},{5,3},{6,54},{7,5},{16,0},{17,23}... | collective-permute-start | bytes 1179656 | tf_op jit(solution)/shard_map/ppermute | solution.py:38
  9.8 13.1 %collective-permute-start.1 = (bf16[128,1536]{1,0:T(8,128)(2,1)S(1)}, bf16[128,1536]{1,0:T(8,128)(2,1)S(1)}, u32[]{:S(2)}, u32[]{:S(2)}) collective-permute-start(bf16[128,1536]{1,0:T(8,128)(2,1)S(1)} %get-tuple-element.34), channel_id=1, source_target_pairs={{0,32},{1,5},{2,34},{3,7},{4,36},{5,1},{6,38},{7,3},{16,48},{17,21... | collective-permute-start | bytes 1179656 | tf_op jit(solution)/shard_map/ppermute | solution.py:38
  10.7 16.4 %collective-permute-start.2 = (bf16[128,1536]{1,0:T(8,128)(2,1)S(1)}, bf16[128,1536]{1,0:T(8,128)(2,1)S(1)}, u32[]{:S(2)}, u32[]{:S(2)}) collective-permute-start(bf16[128,1536]{1,0:T(8,128)(2,1)S(1)} %get-tuple-element.35), channel_id=1, source_target_pairs={{0,16},{1,3},{2,18},{3,5},{4,20},{5,7},{6,22},{7,1},{16,32},{17,19... | collective-permute-start | bytes 1179656 | tf_op jit(solution)/shard_map/ppermute | solution.py:38
  14.4 12.6 %collective-permute-start.3 = (bf16[128,1536]{1,0:T(8,128)(2,1)S(1)}, bf16[128,1536]{1,0:T(8,128)(2,1)S(1)}, u32[]{:S(2)}, u32[]{:S(2)}) collective-permute-start(bf16[128,1536]{1,0:T(8,128)(2,1)S(1)} %get-tuple-element.36), channel_id=1, source_target_pairs={{0,48},{1,7},{2,50},{3,1},{4,52},{5,3},{6,54},{7,5},{16,0},{17,23}... | collective-permute-start | bytes 1179656 | tf_op jit(solution)/shard_map/ppermute | solution.py:38
  18.6 13.3 %collective-permute-start.10 = (bf16[3,128,512]{2,1,0:T(8,128)(2,1)S(1)}, bf16[3,128,512]{2,1,0:T(8,128)(2,1)S(1)}, u32[]{:S(2)}, u32[]{:S(2)}) collective-permute-start(bf16[3,128,512]{2,1,0:T(8,128)(2,1)S(1)} %pad_maximum_fusion.p0), channel_id=1, source_target_pairs={{0,1},{1,0},{2,3},{3,2},{4,5},{5,4},{6,7},{7,6},{8,9},{9,8},{10,11... | collective-permute-start | bytes 1179656 | tf_op jit(solution)/shard_map/ppermute | solution.py:63
  27.8 39.7 %copy-start.3 = (s32[32]{0:T(128)S(1)}, s32[32]{0:T(128)}, u32[]{:S(2)}) copy-start(s32[32]{0:T(128)} %param.10) | copy-start | bytes 388
  27.8 7.1 %collective-permute-start.7 = (bf16[256,512]{1,0:T(8,128)(2,1)S(1)}, bf16[256,512]{1,0:T(8,128)(2,1)S(1)}, u32[]{:S(2)}, u32[]{:S(2)}) collective-permute-start(bf16[256,512]{1,0:T(8,128)(2,1)S(1)} %get-tuple-element.46), channel_id=1, source_target_pairs={{0,4},{1,33},{2,6},{3,35},{4,0},{5,37},{6,2},{7,39},{16,20},{17,49... | collective-permute-start | bytes 786440 | tf_op jit(solution)/shard_map/ppermute | solution.py:38
  29.2 8.5 %collective-permute-start.8 = (bf16[256,512]{1,0:T(8,128)(2,1)S(1)}, bf16[256,512]{1,0:T(8,128)(2,1)S(1)}, u32[]{:S(2)}, u32[]{:S(2)}) collective-permute-start(bf16[256,512]{1,0:T(8,128)(2,1)S(1)} %get-tuple-element.47), channel_id=1, source_target_pairs={{0,2},{1,17},{2,4},{3,19},{4,6},{5,21},{6,0},{7,23},{16,18},{17,33... | collective-permute-start | bytes 786440 | tf_op jit(solution)/shard_map/ppermute | solution.py:38
  29.6 8.1 %collective-permute-start.9 = (bf16[256,512]{1,0:T(8,128)(2,1)S(1)}, bf16[256,512]{1,0:T(8,128)(2,1)S(1)}, u32[]{:S(2)}, u32[]{:S(2)}) collective-permute-start(bf16[256,512]{1,0:T(8,128)(2,1)S(1)} %get-tuple-element.48), channel_id=1, source_target_pairs={{0,6},{1,49},{2,0},{3,51},{4,2},{5,53},{6,4},{7,55},{16,22},{17,1}... | collective-permute-start | bytes 786440 | tf_op jit(solution)/shard_map/ppermute | solution.py:38
  38.0 30.9 %copy-start.1 = (s32[32]{0:T(128)S(1)}, s32[32]{0:T(128)}, u32[]{:S(2)}) copy-start(s32[32]{0:T(128)} %refresh.1) | copy-start | bytes 388
  38.0 9.3 %collective-permute-start.11 = (bf16[128,512]{1,0:T(8,128)(2,1)S(1)}, bf16[128,512]{1,0:T(8,128)(2,1)S(1)}, u32[]{:S(2)}, u32[]{:S(2)}) collective-permute-start(bf16[128,512]{1,0:T(8,128)(2,1)S(1)} %get-tuple-element.55), channel_id=1, source_target_pairs={{0,1},{1,201},{64,65},{65,137},{128,129},{129,73},{192,193},{193,9... | collective-permute-start | bytes 393224 | tf_op jit(solution)/shard_map/ppermute | solution.py:58
  42.4 7.5 %collective-permute-start.12 = (bf16[128,512]{1,0:T(8,128)(2,1)S(1)}, bf16[128,512]{1,0:T(8,128)(2,1)S(1)}, u32[]{:S(2)}, u32[]{:S(2)}) collective-permute-start(bf16[128,512]{1,0:T(8,128)(2,1)S(1)} %get-tuple-element.56), channel_id=1, source_target_pairs={{1,200},{65,136},{129,72},{193,8},{8,193},{72,129},{136,65},{200,1... | collective-permute-start | bytes 393224 | tf_op jit(solution)/shard_map/ppermute | solution.py:58
  46.0 11.1 %collective-permute-start.14 = (bf16[3,128,512]{2,1,0:T(8,128)(2,1)S(1)}, bf16[3,128,512]{2,1,0:T(8,128)(2,1)S(1)}, u32[]{:S(2)}, u32[]{:S(2)}) collective-permute-start(bf16[3,128,512]{2,1,0:T(8,128)(2,1)S(1)} %pad_maximum_fusion.p0), channel_id=1, source_target_pairs={{0,2},{2,0},{1,3},{3,1},{4,6},{6,4},{5,7},{7,5},{8,10},{10,8},{9,1... | collective-permute-start | bytes 1179656 | tf_op jit(solution)/shard_map/ppermute | solution.py:63
  49.9 7.2 %collective-permute-start.13 = (bf16[128,512]{1,0:T(8,128)(2,1)S(1)}, bf16[128,512]{1,0:T(8,128)(2,1)S(1)}, u32[]{:S(2)}, u32[]{:S(2)}) collective-permute-start(bf16[128,512]{1,0:T(8,128)(2,1)S(1)} %mirror_sum.1), channel_id=1, source_target_pairs={{0,64},{64,0},{128,192},{192,128},{8,72},{72,8},{136,200},{200,136... | collective-permute-start | bytes 393224 | tf_op jit(solution)/shard_map/ppermute | solution.py:47
  57.1 6.5 %collective-permute-start.15 = (bf16[128,512]{1,0:T(8,128)(2,1)S(1)}, bf16[128,512]{1,0:T(8,128)(2,1)S(1)}, u32[]{:S(2)}, u32[]{:S(2)}) collective-permute-start(bf16[128,512]{1,0:T(8,128)(2,1)S(1)} %add_convert_fusion.1), channel_id=1, source_target_pairs={{0,128},{64,192},{128,0},{192,64},{8,136},{72,200},{136,8},{200,72... | collective-permute-start | bytes 393224 | tf_op jit(solution)/shard_map/ppermute | solution.py:47
  59.3 8.3 %collective-permute-start.19 = (bf16[3,128,512]{2,1,0:T(8,128)(2,1)S(1)}, bf16[3,128,512]{2,1,0:T(8,128)(2,1)S(1)}, u32[]{:S(2)}, u32[]{:S(2)}) collective-permute-start(bf16[3,128,512]{2,1,0:T(8,128)(2,1)S(1)} %collective-permute-done.14.p1), channel_id=1, source_target_pairs={{0,1},{1,0},{2,3},{3,2},{4,5},{5,4},{6,7},{7,6},{8,9},{9,8},{10,11... | collective-permute-start | bytes 1179656 | tf_op jit(solution)/shard_map/ppermute | solution.py:63
  63.6 3.9 %collective-permute-start.16 = (bf16[128,512]{1,0:T(8,128)(2,1)S(1)}, bf16[128,512]{1,0:T(8,128)(2,1)S(1)}, u32[]{:S(2)}, u32[]{:S(2)}) collective-permute-start(bf16[128,512]{1,0:T(8,128)(2,1)S(1)} %add_convert_fusion.g0), channel_id=1, source_target_pairs={{0,2},{2,0},{1,3},{3,1},{4,6},{6,4},{5,7},{7,5},{8,10},{10,8},{9,1... | collective-permute-start | bytes 393224 | tf_op jit(solution)/shard_map/ppermute | solution.py:63
  64.9 2.8 %collective-permute-start.17 = (bf16[128,512]{1,0:T(8,128)(2,1)S(1)}, bf16[128,512]{1,0:T(8,128)(2,1)S(1)}, u32[]{:S(2)}, u32[]{:S(2)}) collective-permute-start(bf16[128,512]{1,0:T(8,128)(2,1)S(1)} %add_convert_fusion.g0), channel_id=1, source_target_pairs={{0,1},{1,0},{2,3},{3,2},{4,5},{5,4},{6,7},{7,6},{8,9},{9,8},{10,11... | collective-permute-start | bytes 393224 | tf_op jit(solution)/shard_map/ppermute | solution.py:63
  67.5 1.3 %collective-permute-start.18 = (bf16[128,512]{1,0:T(8,128)(2,1)S(1)}, bf16[128,512]{1,0:T(8,128)(2,1)S(1)}, u32[]{:S(2)}, u32[]{:S(2)}) collective-permute-start(bf16[128,512]{1,0:T(8,128)(2,1)S(1)} %collective-permute-done.16.g1), channel_id=1, source_target_pairs={{0,1},{1,0},{2,3},{3,2},{4,5},{5,4},{6,7},{7,6},{8,9},{9,8},{10,11... | collective-permute-start | bytes 393224 | tf_op jit(solution)/shard_map/ppermute | solution.py:63

commit v8 on v7

--- a/solution.py
+++ b/solution.py
@@ -17,6 +17,7 @@
 B = 512
 ROWS = 128
 TOKENS = 128
+PART = 64
 HALF = B // 2
 ORDER = (2, 1, 3, 0)
 WIDE = 3 * B
@@ -51,11 +52,17 @@
     first, second = [], []
     for z in range(8):
         stays = z // 4
+        across = (6 + 2 * (z % 2) - z) % 8
         first.append((ring_spot(z, stays), ring_spot(z, 1 - stays)))
-        first.append((ring_spot(z, 1 - stays), ring_spot(7 - z, 1 - stays)))
-        second.append((ring_spot(z, 1 - stays), ring_spot(7 - z, stays)))
+        first.append((ring_spot(z, 1 - stays), ring_spot(across, 1 - stays)))
+        second.append((ring_spot(z, 1 - stays), ring_spot(across, stays)))
     axes = Z + ("core",)
     return lax.ppermute(near, axes, first), lax.ppermute(far, axes, second)
+
+
+def diagonal(x):
+    pairs = [(z * 2 + a, (z ^ 1) * 2 + 1 - a) for z in range(4) for a in range(2)]
+    return lax.ppermute(x, ("z_lo", "x_lo"), pairs)
 
 
 def partner(x, axis, bits=1):
@@ -76,7 +83,7 @@
     return lax.optimization_barrier(narrow(x))
 
 
-def finish_kernel(decays, refresh, g0, g1, g2, g3, old_stats, old_right, left_old,
+def finish_kernel(decays, refresh, g_own, g_core, old_stats, old_right, left_old,
                   update, new_stats, new_roots, grad, full, right, left, result, work, sem):
     at = places()
     quarter = at["x_lo"] * 2 + at["core"]
@@ -84,9 +91,11 @@
     factor = 2 * (at["y"] * 4 + at["z_hi"] * 2 + at["x_hi"])
     decay = (decays[factor], decays[factor + 1])
     fresh = (refresh[factor], refresh[factor + 1])
-    for a in range(2):
-        for b in range(2):
-            grad[quarter_rows(at, a, b), :] = (g0, g1, g2, g3)[2 * b + a][...]
+    side = lax.rem(at["z_lo"], 2)
+    for i in range(4):
+        for b, pieces in enumerate((g_own, g_core)):
+            top = ((at["x_lo"] ^ (i // 2)) * 2 + (at["core"] ^ b)) * ROWS + (side ^ (i % 2)) * PART
+            grad[pl.ds(pl.multiple_of(top, PART), PART), :] = pieces[i]
     g = grad[...]
     writes = []
 
@@ -160,7 +169,7 @@
             jax.ShapeDtypeStruct((2, ROWS, B), jnp.float32),
             jax.ShapeDtypeStruct((2, ROWS, B), jnp.bfloat16),
         ),
-        in_specs=[smem] * 2 + [VMEM] * 7,
+        in_specs=[smem] * 2 + [VMEM] * 5,
         out_specs=(pl.BlockSpec(memory_space=pltpu.HBM),) * 3,
         scratch_shapes=[
             pltpu.VMEM((B, B), jnp.bfloat16),
@@ -269,30 +278,17 @@
     )(*parts, *before)
 
 
-def plane_sum_kernel(first, second, third, own, keep, near, far):
-    total = own[...]
+def plane_sum_kernel(first, second, third, own, keep, send, total):
+    t = own[...]
     for part in (first, second, third):
-        total += part[...].astype(jnp.float32)
-    core = lax.axis_index("core")
-    stays = core == lax.axis_index("z_hi")
-
-    @pl.when(core == 0)
-    def _():
-        keep[...] = total[:ROWS]
-        far[...] = total[ROWS:].astype(SEND)
-
-    @pl.when(core == 1)
-    def _():
-        keep[...] = total[ROWS:]
-        far[...] = total[:ROWS].astype(SEND)
-
-    @pl.when(stays)
-    def _():
-        near[...] = far[...]
-
-    @pl.when(jnp.logical_not(stays))
-    def _():
-        near[...] = keep[...].astype(SEND)
+        t += part[...].astype(jnp.float32)
+    total[...] = t
+    side = lax.rem(lax.axis_index("z_lo"), 2)
+    for i in range(2):
+        here = pl.ds(pl.multiple_of(i * ROWS + side * PART, PART), PART)
+        there = pl.ds(pl.multiple_of(i * ROWS + (1 - side) * PART, PART), PART)
+        keep[i] = total[here, :]
+        send[i] = total[there, :].astype(SEND)
 
 
 def plane_sum(parts):
@@ -300,39 +296,89 @@
         plane_sum_kernel,
         name="plane_sum",
         out_shape=(
-            jax.ShapeDtypeStruct((ROWS, B), jnp.float32),
-            jax.ShapeDtypeStruct((ROWS, B), SEND),
-            jax.ShapeDtypeStruct((ROWS, B), SEND),
+            jax.ShapeDtypeStruct((2, PART, B), jnp.float32),
+            jax.ShapeDtypeStruct((2, PART, B), SEND),
         ),
         in_specs=[VMEM] * 4,
-        out_specs=(VMEM,) * 3,
+        out_specs=(VMEM,) * 2,
+        scratch_shapes=[pltpu.VMEM((HALF, B), jnp.float32)],
         compiler_params=pltpu.CompilerParams(vmem_limit_bytes=2 << 20),
         cost_estimate=pl.CostEstimate(flops=8 * ROWS * B, bytes_accessed=2 << 20, transcendentals=0),
     )(*parts)
 
 
-def mirror_sum_kernel(keep, near, far, out):
-    stays = lax.axis_index("core") == lax.axis_index("z_hi")
+def pair_sum_kernel(keep, came, base, near, far):
+    core = lax.axis_index("core")
+    mine = keep[core] + came[core].astype(jnp.float32)
+    other = (keep[1 - core] + came[1 - core].astype(jnp.float32)).astype(SEND)
+    base[...] = mine
+    far[...] = other
+    stays = core == lax.axis_index("z_hi")
 
     @pl.when(stays)
     def _():
-        out[...] = narrow(keep[...] + near[...].astype(jnp.float32))
+        near[...] = other
+
+    @pl.when(jnp.logical_not(stays))
+    def _():
+        near[...] = mine.astype(SEND)
+
+
+def pair_sum(keep, came):
+    return pl.pallas_call(
+        pair_sum_kernel,
+        name="pair_sum",
+        out_shape=(
+            jax.ShapeDtypeStruct((PART, B), jnp.float32),
+            jax.ShapeDtypeStruct((PART, B), SEND),
+            jax.ShapeDtypeStruct((PART, B), SEND),
+        ),
+        in_specs=[VMEM] * 2,
+        out_specs=(VMEM,) * 3,
+        compiler_params=pltpu.CompilerParams(vmem_limit_bytes=1 << 20),
+        cost_estimate=pl.CostEstimate(flops=2 * ROWS * B, bytes_accessed=1 << 20, transcendentals=0),
+    )(keep, came)
+
+
+def mirror_sum_kernel(base, near, far, out):
+    stays = lax.axis_index("core") == lax.axis_index("z_hi")
+
+    @pl.when(stays)
+    def _():
+        out[...] = narrow(base[...] + near[...].astype(jnp.float32))
 
     @pl.when(jnp.logical_not(stays))
     def _():
         out[...] = narrow(far[...].astype(jnp.float32) + near[...].astype(jnp.float32))
 
 
-def mirror_sum(keep, near, far):
+def mirror_sum(base, near, far):
     return pl.pallas_call(
         mirror_sum_kernel,
         name="mirror_sum",
-        out_shape=jax.ShapeDtypeStruct((ROWS, B), jnp.bfloat16),
+        out_shape=jax.ShapeDtypeStruct((PART, B), jnp.bfloat16),
         in_specs=[VMEM] * 3,
         out_specs=VMEM,
         compiler_params=pltpu.CompilerParams(vmem_limit_bytes=1 << 20),
-        cost_estimate=pl.CostEstimate(flops=2 * ROWS * B, bytes_accessed=1 << 19, transcendentals=0),
-    )(keep, near, far)
+        cost_estimate=pl.CostEstimate(flops=2 * PART * B, bytes_accessed=1 << 19, transcendentals=0),
+    )(base, near, far)
+
+
+def stack_kernel(*refs):
+    for i, ref in enumerate(refs[:-1]):
+        refs[-1][i] = ref[...]
+
+
+def stack(parts):
+    return pl.pallas_call(
+        stack_kernel,
+        name="stack",
+        out_shape=jax.ShapeDtypeStruct((len(parts),) + parts[0].shape, parts[0].dtype),
+        in_specs=[VMEM] * len(parts),
+        out_specs=VMEM,
+        compiler_params=pltpu.CompilerParams(vmem_limit_bytes=1 << 20),
+        cost_estimate=pl.CostEstimate(flops=0, bytes_accessed=1 << 19, transcendentals=0),
+    )(*parts)
 
 
 def quarter_rows(at, a, b):
@@ -375,15 +421,14 @@
     came = [shift(sends[i], False, ORDER[i]) for i in range(3)]
     pack = jnp.concatenate([narrow(statistics), roots[1:]], axis=0)
     own, pack_core = lax.optimization_barrier((own, partner(pack, "core")))
-    keep, near, far = plane_sum(came + [own])
-    keep, near, far, pack = lax.optimization_barrier((keep, near, far, pack))
-    part = mirror_sum(keep, *mirror(near, far))
+    keep, send = plane_sum(came + [own])
+    keep, send, pack = lax.optimization_barrier((keep, send, pack))
+    base, near, far = pair_sum(keep, swap_z(send, 1))
     pack_x = partner(pack, "x_lo")
-    part = rounded(part.astype(jnp.float32) + swap_z(part, 1).astype(jnp.float32))
-    part, pack_x = lax.optimization_barrier((part, pack_x))
+    part, pack_x = lax.optimization_barrier((mirror_sum(base, *mirror(near, far)), pack_x))
     part = rounded(part.astype(jnp.float32) + swap_z(part, 2).astype(jnp.float32))
-    part_x, part_core = partner(part, "x_lo"), partner(part, "core")
-    grads = (part, part_x, part_core, partner(part_x, "core"))
+    grad = stack((part, swap_z(part, 1), partner(part, "x_lo"), diagonal(part)))
+    grads = (grad, partner(grad, "core"))
     full, right = assemble(statistics, (pack, pack_x, pack_core, partner(pack_x, "core")))
     return finish(decays, refresh, *grads, full, right, roots[0])
 

time: 76.5 us -> 76 us (level)
    ppermute x2, starting transfers between devices: 8.01 us -> 11 us  [mirror(): return (lax.ppermute(near, axes, first), lax.ppermute(far, axes, second))]
    ppermute x2 -> x3, starting transfers between devices: 7.01 us -> 4.84 us  [swap_z(): lax.ppermute(x, Z, [(ring_spot(z), ring_spot(z ^ bits)) for z in range(8)])]
    ppermute x7 -> x6, starting transfers between devices: 6.86 us -> 4.92 us  [partner(): return lax.ppermute(x, axis, [(i, i ^ bits) for i in range(n)])]
    ppermute x2 -> x3, waiting for transfers between devices: 6.65 us -> 5.16 us  [swap_z(): lax.ppermute(x, Z, [(ring_spot(z), ring_spot(z ^ bits)) for z in range(8)])]
    ppermute x0 -> x1, starting transfers between devices: none -> 1.31 us  [diagonal(): return lax.ppermute(x, ('z_lo', 'x_lo'), pairs)]
    ppermute x7 -> x6, waiting for transfers between devices: 3.75 us -> 4.15 us  [partner(): return lax.ppermute(x, axis, [(i, i ^ bits) for i in range(n)])]
  transfers between devices with their start and end apart: 20 -> 21, of which waited for: 11 -> 12; matrix products, arithmetic and copies ran while one was open for 0% -> 0% of each run, Pallas kernels for 3% -> 3%
where the time goes in v8:
time: 76 us; the launch traced here: 75.9 us
  waiting for transfers between devices  31.8 us (42%)
  starting transfers between devices  31.4 us (41%)
  Pallas kernels  11.7 us (15%)
  between operations  0.96 us (1%)
    ppermute x9, waiting for transfers between devices, shift(): return lax.ppermute(x, ('y',) + X + ('core',), pairs)  19.4 us
    ppermute x2, starting transfers between devices, mirror(): return (lax.ppermute(near, axes, first), lax.ppermute(far, axes, second))  11 us
    ppermute x9, starting transfers between devices, shift(): return lax.ppermute(x, ('y',) + X + ('core',), pairs)  9.31 us
    pallas_call x1, Pallas kernels, finish(): pl.pallas_call(finish_kernel, name='finish', out_shape=(jax.ShapeDtypeStr...  7.32 us
    ppermute x3, waiting for transfers between devices, swap_z(): lax.ppermute(x, Z, [(ring_spot(z), ring_spot(z ^ bits)) for z in range(8)])  5.16 us
    ppermute x6, starting transfers between devices, partner(): return lax.ppermute(x, axis, [(i, i ^ bits) for i in range(n)])  4.92 us
    ppermute x3, starting transfers between devices, swap_z(): lax.ppermute(x, Z, [(ring_spot(z), ring_spot(z ^ bits)) for z in range(8)])  4.84 us
    ppermute x6, waiting for transfers between devices, partner(): return lax.ppermute(x, axis, [(i, i ^ bits) for i in range(n)])  4.15 us
  transfers between devices with their start and end apart: 21, of which 12 were waited for; matrix products, arithmetic and copies ran while one was open for 0% of the time, Pallas kernels for 3%

profile of v8, /device:TPU:1, one launch (start us, length us, event | category | flops | bytes accessed | tf_op | source)
XLA Modules:
  0.0 75.9 jit_solution(11157627359071194403)
XLA Ops:
  0.7 2.0 %cut.1 = (bf16[128,1536]{1,0:T(8,128)(2,1)S(1)}, bf16[128,1536]{1,0:T(8,128)(2,1)S(1)}, bf16[128,1536]{1,0:T(8,128)(2,1)S(1)}, bf16[128,1536]{1,0:T(8,128)(2,1)S(1)}, bf16[4,128,1536]{2,1,0:T(8,128)(2,1)S(1)}) custom-call(bf16[128,8192]{1,0:T(8,128)(2,1)} %cotangents.1, bf16[128,512]{1,0:T(8,128)(2,1)} %activations.1), custom_call_target="tpu_custom_call" | custom-call | bytes 6291456 | tf_op jit(solution)/shard_map/cut/pallas_call | solution.py:224
  2.6 3.3 %collective-permute-start = (bf16[4,128,1536]{2,1,0:T(8,128)(2,1)S(1)}, bf16[4,128,1536]{2,1,0:T(8,128)(2,1)S(1)}, u32[]{:S(2)}, u32[]{:S(2)}) collective-permute-start(bf16[4,128,1536]{2,1,0:T(8,128)(2,1)S(1)} %get-tuple-element.34), channel_id=1, source_target_pairs={{0,1},{1,0},{2,3},{3,2},{4,5},{5,4},{6,7},{7,6},{8,9},{9,8},{10,11... | collective-permute-start | bytes 4718600 | tf_op jit(solution)/shard_map/ppermute | solution.py:70
  6.0 1.0 %collective-permute-start.4 = (bf16[128,1536]{1,0:T(8,128)(2,1)S(1)}, bf16[128,1536]{1,0:T(8,128)(2,1)S(1)}, u32[]{:S(2)}, u32[]{:S(2)}) collective-permute-start(bf16[128,1536]{1,0:T(8,128)(2,1)S(1)} %get-tuple-element.40), channel_id=1, source_target_pairs={{0,32},{1,5},{2,34},{3,7},{4,36},{5,1},{6,38},{7,3},{16,48},{17,21... | collective-permute-start | bytes 1179656 | tf_op jit(solution)/shard_map/ppermute | solution.py:39
  7.3 2.4 %collective-permute-start.6 = (bf16[128,1536]{1,0:T(8,128)(2,1)S(1)}, bf16[128,1536]{1,0:T(8,128)(2,1)S(1)}, u32[]{:S(2)}, u32[]{:S(2)}) collective-permute-start(bf16[128,1536]{1,0:T(8,128)(2,1)S(1)} %get-tuple-element.42), channel_id=1, source_target_pairs={{0,48},{1,7},{2,50},{3,1},{4,52},{5,3},{6,54},{7,5},{16,0},{17,23}... | collective-permute-start | bytes 1179656 | tf_op jit(solution)/shard_map/ppermute | solution.py:39
  10.7 3.8 %collective-permute-done.4.refs_2_ = bf16[128,1536]{1,0:T(8,128)(2,1)S(1)} collective-permute-done((bf16[128,1536]{1,0:T(8,128)(2,1)S(1)}, bf16[128,1536]{1,0:T(8,128)(2,1)S(1)}, u32[]{:S(2)}, u32[]{:S(2)}) %collective-permute-start.4) | collective-permute-done | bytes 393248 | tf_op jit(solution)/shard_map/ppermute | solution.py:39
  15.2 3.4 %collective-permute-done.5.refs_3_ = bf16[128,1536]{1,0:T(8,128)(2,1)S(1)} collective-permute-done((bf16[128,1536]{1,0:T(8,128)(2,1)S(1)}, bf16[128,1536]{1,0:T(8,128)(2,1)S(1)}, u32[]{:S(2)}, u32[]{:S(2)}) %collective-permute-start.5) | collective-permute-done | bytes 393248 | tf_op jit(solution)/shard_map/ppermute | solution.py:39
  19.6 1.0 %product.2 = (f32[256,512]{1,0:T(8,128)S(1)}, f32[256,512]{1,0:T(8,128)S(1)}, f32[256,512]{1,0:T(8,128)S(1)}, f32[256,512]{1,0:T(8,128)S(1)}) custom-call(bf16[128,1536]{1,0:T(8,128)(2,1)S(1)} %get-tuple-element.38.refs_0_, bf16[128,1536]{1,0:T(8,128)(2,1)S(1)} %get-tuple-element.39.refs_1_, bf16[128,1536]{1,0:T(8,128)(2,1)S(1)} %collective-permute-done.4.refs_2_, ...), custom_call_target="tpu_custom_call" | custom-call | flops 671088640 | bytes 4194304 | tf_op jit(solution)/shard_map/product/pallas_call | solution.py:270
  20.6 2.3 %collective-permute-done.1.refs_0_ = bf16[128,1536]{1,0:T(8,128)(2,1)S(1)} collective-permute-done((bf16[128,1536]{1,0:T(8,128)(2,1)S(1)}, bf16[128,1536]{1,0:T(8,128)(2,1)S(1)}, u32[]{:S(2)}, u32[]{:S(2)}) %collective-permute-start.1) | collective-permute-done | bytes 393248 | tf_op jit(solution)/shard_map/ppermute | solution.py:39
  22.9 4.1 %collective-permute-done.2.refs_1_ = bf16[128,1536]{1,0:T(8,128)(2,1)S(1)} collective-permute-done((bf16[128,1536]{1,0:T(8,128)(2,1)S(1)}, bf16[128,1536]{1,0:T(8,128)(2,1)S(1)}, u32[]{:S(2)}, u32[]{:S(2)}) %collective-permute-start.2) | collective-permute-done | bytes 393248 | tf_op jit(solution)/shard_map/ppermute | solution.py:39
  27.8 1.4 %collective-permute-start.7 = (bf16[256,512]{1,0:T(8,128)(2,1)S(1)}, bf16[256,512]{1,0:T(8,128)(2,1)S(1)}, u32[]{:S(2)}, u32[]{:S(2)}) collective-permute-start(bf16[256,512]{1,0:T(8,128)(2,1)S(1)} %get-tuple-element.47), channel_id=1, source_target_pairs={{0,4},{1,33},{2,6},{3,35},{4,0},{5,37},{6,2},{7,39},{16,20},{17,49... | collective-permute-start | bytes 786440 | tf_op jit(solution)/shard_map/ppermute | solution.py:39
  29.6 2.3 %collective-permute-start.9 = (bf16[256,512]{1,0:T(8,128)(2,1)S(1)}, bf16[256,512]{1,0:T(8,128)(2,1)S(1)}, u32[]{:S(2)}, u32[]{:S(2)}) collective-permute-start(bf16[256,512]{1,0:T(8,128)(2,1)S(1)} %get-tuple-element.49), channel_id=1, source_target_pairs={{0,6},{1,49},{2,0},{3,51},{4,2},{5,53},{6,4},{7,55},{16,22},{17,1}... | collective-permute-start | bytes 786440 | tf_op jit(solution)/shard_map/ppermute | solution.py:39
  31.9 3.1 %collective-permute-done.7.first = bf16[256,512]{1,0:T(8,128)(2,1)S(1)} collective-permute-done((bf16[256,512]{1,0:T(8,128)(2,1)S(1)}, bf16[256,512]{1,0:T(8,128)(2,1)S(1)}, u32[]{:S(2)}, u32[]{:S(2)}) %collective-permute-start.7) | collective-permute-done | bytes 262176 | tf_op jit(solution)/shard_map/ppermute | solution.py:39
  35.0 2.8 %collective-permute-done.8.second = bf16[256,512]{1,0:T(8,128)(2,1)S(1)} collective-permute-done((bf16[256,512]{1,0:T(8,128)(2,1)S(1)}, bf16[256,512]{1,0:T(8,128)(2,1)S(1)}, u32[]{:S(2)}, u32[]{:S(2)}) %collective-permute-start.8) | collective-permute-done | bytes 262176 | tf_op jit(solution)/shard_map/ppermute | solution.py:39
  38.1 1.6 %collective-permute-start.11 = (bf16[2,64,512]{2,1,0:T(8,128)(2,1)S(1)}, bf16[2,64,512]{2,1,0:T(8,128)(2,1)S(1)}, u32[]{:S(2)}, u32[]{:S(2)}) collective-permute-start(bf16[2,64,512]{2,1,0:T(8,128)(2,1)S(1)} %get-tuple-element.55), channel_id=1, source_target_pairs={{0,64},{64,0},{128,192},{192,128},{8,72},{72,8},{136,200},{200,136... | collective-permute-start | bytes 393224 | tf_op jit(solution)/shard_map/ppermute | solution.py:48
  39.6 2.4 %collective-permute-done.11.came = bf16[2,64,512]{2,1,0:T(8,128)(2,1)S(1)} collective-permute-done((bf16[2,64,512]{2,1,0:T(8,128)(2,1)S(1)}, bf16[2,64,512]{2,1,0:T(8,128)(2,1)S(1)}, u32[]{:S(2)}, u32[]{:S(2)}) %collective-permute-start.11) | collective-permute-done | bytes 131104 | tf_op jit(solution)/shard_map/ppermute | solution.py:48
  42.0 6.2 %collective-permute-start.12 = (bf16[64,512]{1,0:T(8,128)(2,1)S(1)}, bf16[64,512]{1,0:T(8,128)(2,1)S(1)}, u32[]{:S(2)}, u32[]{:S(2)}) collective-permute-start(bf16[64,512]{1,0:T(8,128)(2,1)S(1)} %get-tuple-element.57), channel_id=1, source_target_pairs={{0,1},{1,137},{64,65},{65,201},{128,129},{129,9},{192,193},{193,73... | collective-permute-start | bytes 196616 | tf_op jit(solution)/shard_map/ppermute | solution.py:60
  48.2 4.7 %collective-permute-start.13 = (bf16[64,512]{1,0:T(8,128)(2,1)S(1)}, bf16[64,512]{1,0:T(8,128)(2,1)S(1)}, u32[]{:S(2)}, u32[]{:S(2)}) collective-permute-start(bf16[64,512]{1,0:T(8,128)(2,1)S(1)} %get-tuple-element.58), channel_id=1, source_target_pairs={{1,136},{65,200},{129,8},{193,72},{8,129},{72,193},{136,1},{200,65... | collective-permute-start | bytes 196616 | tf_op jit(solution)/shard_map/ppermute | solution.py:60
  53.0 3.0 %collective-permute-done.13.far = bf16[64,512]{1,0:T(8,128)(2,1)S(1)} collective-permute-done((bf16[64,512]{1,0:T(8,128)(2,1)S(1)}, bf16[64,512]{1,0:T(8,128)(2,1)S(1)}, u32[]{:S(2)}, u32[]{:S(2)}) %collective-permute-start.13) | collective-permute-done | bytes 65568 | tf_op jit(solution)/shard_map/ppermute | solution.py:60
  56.1 1.9 %collective-permute-start.15 = (bf16[64,512]{1,0:T(8,128)(2,1)S(1)}, bf16[64,512]{1,0:T(8,128)(2,1)S(1)}, u32[]{:S(2)}, u32[]{:S(2)}) collective-permute-start(bf16[64,512]{1,0:T(8,128)(2,1)S(1)} %mirror_sum.1), channel_id=1, source_target_pairs={{0,128},{64,192},{128,0},{192,64},{8,136},{72,200},{136,8},{200,72... | collective-permute-start | bytes 196616 | tf_op jit(solution)/shard_map/ppermute | solution.py:48
  57.9 2.2 %collective-permute-done.15 = bf16[64,512]{1,0:T(8,128)(2,1)S(1)} collective-permute-done((bf16[64,512]{1,0:T(8,128)(2,1)S(1)}, bf16[64,512]{1,0:T(8,128)(2,1)S(1)}, u32[]{:S(2)}, u32[]{:S(2)}) %collective-permute-start.15) | collective-permute-done | bytes 65568 | tf_op jit(solution)/shard_map/ppermute | solution.py:48
  60.2 1.4 %collective-permute-start.16 = (bf16[64,512]{1,0:T(8,128)(2,1)S(1)}, bf16[64,512]{1,0:T(8,128)(2,1)S(1)}, u32[]{:S(2)}, u32[]{:S(2)}) collective-permute-start(bf16[64,512]{1,0:T(8,128)(2,1)S(1)} %add_convert_fusion.refs_0_), channel_id=1, source_target_pairs={{0,64},{64,0},{128,192},{192,128},{8,72},{72,8},{136,200},{200,136... | collective-permute-start | bytes 196616 | tf_op jit(solution)/shard_map/ppermute | solution.py:48
  61.6 1.3 %collective-permute-start.18 = (bf16[64,512]{1,0:T(8,128)(2,1)S(1)}, bf16[64,512]{1,0:T(8,128)(2,1)S(1)}, u32[]{:S(2)}, u32[]{:S(2)}) collective-permute-start(bf16[64,512]{1,0:T(8,128)(2,1)S(1)} %add_convert_fusion.refs_0_), channel_id=1, source_target_pairs={{0,66},{2,64},{64,2},{66,0},{128,194},{130,192},{192,130},{194,128... | collective-permute-start | bytes 196616 | tf_op jit(solution)/shard_map/ppermute | solution.py:65
  63.5 3.2 %collective-permute-done.17.refs_2_ = bf16[64,512]{1,0:T(8,128)(2,1)S(1)} collective-permute-done((bf16[64,512]{1,0:T(8,128)(2,1)S(1)}, bf16[64,512]{1,0:T(8,128)(2,1)S(1)}, u32[]{:S(2)}, u32[]{:S(2)}) %collective-permute-start.17) | collective-permute-done | bytes 65568 | tf_op jit(solution)/shard_map/ppermute | solution.py:70
  68.4 7.3 %finish.1 = (bf16[128,512]{1,0:T(8,128)(2,1)}, f32[2,128,512]{2,1,0:T(8,128)}, bf16[2,128,512]{2,1,0:T(8,128)(2,1)}) custom-call(f32[32]{0:T(128)S(1)} %convert_power_fusion.decays, s32[32]{0:T(128)S(1)} %copy-done.1, bf16[4,64,512]{2,1,0:T(8,128)(2,1)S(1)} %stack.1.g_own, bf16[4,64,512]{2,1,0:T(8,128)(2,1)S(1)} %collective-permute-done.19.g_core, ...), custom_call_target="tpu_custom_call" | custom-call | flops 4831838208 | bytes 6291456 | tf_op jit(solution)/shard_map/finish/pallas_call | solution.py:164
  (41 shorter events, 6.9 us)
Async XLA Ops:
  0.6 14.5 %copy-start.2 = (bf16[2,128,512]{2,1,0:T(8,128)(2,1)S(1)}, bf16[2,128,512]{2,1,0:T(8,128)(2,1)}, u32[]{:S(2)}) copy-start(bf16[2,128,512]{2,1,0:T(8,128)(2,1)} %param.9) | copy-start | bytes 786436
  2.6 7.1 %collective-permute-start = (bf16[4,128,1536]{2,1,0:T(8,128)(2,1)S(1)}, bf16[4,128,1536]{2,1,0:T(8,128)(2,1)S(1)}, u32[]{:S(2)}, u32[]{:S(2)}) collective-permute-start(bf16[4,128,1536]{2,1,0:T(8,128)(2,1)S(1)} %get-tuple-element.34), channel_id=1, source_target_pairs={{0,1},{1,0},{2,3},{3,2},{4,5},{5,4},{6,7},{7,6},{8,9},{9,8},{10,11... | collective-permute-start | bytes 4718600 | tf_op jit(solution)/shard_map/ppermute | solution.py:70
  6.0 8.5 %collective-permute-start.4 = (bf16[128,1536]{1,0:T(8,128)(2,1)S(1)}, bf16[128,1536]{1,0:T(8,128)(2,1)S(1)}, u32[]{:S(2)}, u32[]{:S(2)}) collective-permute-start(bf16[128,1536]{1,0:T(8,128)(2,1)S(1)} %get-tuple-element.40), channel_id=1, source_target_pairs={{0,32},{1,5},{2,34},{3,7},{4,36},{5,1},{6,38},{7,3},{16,48},{17,21... | collective-permute-start | bytes 1179656 | tf_op jit(solution)/shard_map/ppermute | solution.py:39
  7.0 11.6 %collective-permute-start.5 = (bf16[128,1536]{1,0:T(8,128)(2,1)S(1)}, bf16[128,1536]{1,0:T(8,128)(2,1)S(1)}, u32[]{:S(2)}, u32[]{:S(2)}) collective-permute-start(bf16[128,1536]{1,0:T(8,128)(2,1)S(1)} %get-tuple-element.41), channel_id=1, source_target_pairs={{0,16},{1,3},{2,18},{3,5},{4,20},{5,7},{6,22},{7,1},{16,32},{17,19... | collective-permute-start | bytes 1179656 | tf_op jit(solution)/shard_map/ppermute | solution.py:39
  7.3 12.3 %collective-permute-start.6 = (bf16[128,1536]{1,0:T(8,128)(2,1)S(1)}, bf16[128,1536]{1,0:T(8,128)(2,1)S(1)}, u32[]{:S(2)}, u32[]{:S(2)}) collective-permute-start(bf16[128,1536]{1,0:T(8,128)(2,1)S(1)} %get-tuple-element.42), channel_id=1, source_target_pairs={{0,48},{1,7},{2,50},{3,1},{4,52},{5,3},{6,54},{7,5},{16,0},{17,23}... | collective-permute-start | bytes 1179656 | tf_op jit(solution)/shard_map/ppermute | solution.py:39
  9.8 13.1 %collective-permute-start.1 = (bf16[128,1536]{1,0:T(8,128)(2,1)S(1)}, bf16[128,1536]{1,0:T(8,128)(2,1)S(1)}, u32[]{:S(2)}, u32[]{:S(2)}) collective-permute-start(bf16[128,1536]{1,0:T(8,128)(2,1)S(1)} %get-tuple-element.35), channel_id=1, source_target_pairs={{0,32},{1,5},{2,34},{3,7},{4,36},{5,1},{6,38},{7,3},{16,48},{17,21... | collective-permute-start | bytes 1179656 | tf_op jit(solution)/shard_map/ppermute | solution.py:39
  10.7 16.4 %collective-permute-start.2 = (bf16[128,1536]{1,0:T(8,128)(2,1)S(1)}, bf16[128,1536]{1,0:T(8,128)(2,1)S(1)}, u32[]{:S(2)}, u32[]{:S(2)}) collective-permute-start(bf16[128,1536]{1,0:T(8,128)(2,1)S(1)} %get-tuple-element.36), channel_id=1, source_target_pairs={{0,16},{1,3},{2,18},{3,5},{4,20},{5,7},{6,22},{7,1},{16,32},{17,19... | collective-permute-start | bytes 1179656 | tf_op jit(solution)/shard_map/ppermute | solution.py:39
  14.4 12.6 %collective-permute-start.3 = (bf16[128,1536]{1,0:T(8,128)(2,1)S(1)}, bf16[128,1536]{1,0:T(8,128)(2,1)S(1)}, u32[]{:S(2)}, u32[]{:S(2)}) collective-permute-start(bf16[128,1536]{1,0:T(8,128)(2,1)S(1)} %get-tuple-element.37), channel_id=1, source_target_pairs={{0,48},{1,7},{2,50},{3,1},{4,52},{5,3},{6,54},{7,5},{16,0},{17,23}... | collective-permute-start | bytes 1179656 | tf_op jit(solution)/shard_map/ppermute | solution.py:39
  18.6 13.3 %collective-permute-start.10 = (bf16[3,128,512]{2,1,0:T(8,128)(2,1)S(1)}, bf16[3,128,512]{2,1,0:T(8,128)(2,1)S(1)}, u32[]{:S(2)}, u32[]{:S(2)}) collective-permute-start(bf16[3,128,512]{2,1,0:T(8,128)(2,1)S(1)} %pad_maximum_fusion.p0), channel_id=1, source_target_pairs={{0,1},{1,0},{2,3},{3,2},{4,5},{5,4},{6,7},{7,6},{8,9},{9,8},{10,11... | collective-permute-start | bytes 1179656 | tf_op jit(solution)/shard_map/ppermute | solution.py:70
  27.8 39.4 %copy-start.3 = (s32[32]{0:T(128)S(1)}, s32[32]{0:T(128)}, u32[]{:S(2)}) copy-start(s32[32]{0:T(128)} %param.10) | copy-start | bytes 388
  27.8 7.1 %collective-permute-start.7 = (bf16[256,512]{1,0:T(8,128)(2,1)S(1)}, bf16[256,512]{1,0:T(8,128)(2,1)S(1)}, u32[]{:S(2)}, u32[]{:S(2)}) collective-permute-start(bf16[256,512]{1,0:T(8,128)(2,1)S(1)} %get-tuple-element.47), channel_id=1, source_target_pairs={{0,4},{1,33},{2,6},{3,35},{4,0},{5,37},{6,2},{7,39},{16,20},{17,49... | collective-permute-start | bytes 786440 | tf_op jit(solution)/shard_map/ppermute | solution.py:39
  29.2 8.5 %collective-permute-start.8 = (bf16[256,512]{1,0:T(8,128)(2,1)S(1)}, bf16[256,512]{1,0:T(8,128)(2,1)S(1)}, u32[]{:S(2)}, u32[]{:S(2)}) collective-permute-start(bf16[256,512]{1,0:T(8,128)(2,1)S(1)} %get-tuple-element.48), channel_id=1, source_target_pairs={{0,2},{1,17},{2,4},{3,19},{4,6},{5,21},{6,0},{7,23},{16,18},{17,33... | collective-permute-start | bytes 786440 | tf_op jit(solution)/shard_map/ppermute | solution.py:39
  29.6 8.1 %collective-permute-start.9 = (bf16[256,512]{1,0:T(8,128)(2,1)S(1)}, bf16[256,512]{1,0:T(8,128)(2,1)S(1)}, u32[]{:S(2)}, u32[]{:S(2)}) collective-permute-start(bf16[256,512]{1,0:T(8,128)(2,1)S(1)} %get-tuple-element.49), channel_id=1, source_target_pairs={{0,6},{1,49},{2,0},{3,51},{4,2},{5,53},{6,4},{7,55},{16,22},{17,1}... | collective-permute-start | bytes 786440 | tf_op jit(solution)/shard_map/ppermute | solution.py:39
  37.9 30.5 %copy-start.1 = (s32[32]{0:T(128)S(1)}, s32[32]{0:T(128)}, u32[]{:S(2)}) copy-start(s32[32]{0:T(128)} %refresh.1) | copy-start | bytes 388
  38.0 18.1 %collective-permute-start.14 = (bf16[3,128,512]{2,1,0:T(8,128)(2,1)S(1)}, bf16[3,128,512]{2,1,0:T(8,128)(2,1)S(1)}, u32[]{:S(2)}, u32[]{:S(2)}) collective-permute-start(bf16[3,128,512]{2,1,0:T(8,128)(2,1)S(1)} %pad_maximum_fusion.p0), channel_id=1, source_target_pairs={{0,2},{2,0},{1,3},{3,1},{4,6},{6,4},{5,7},{7,5},{8,10},{10,8},{9,1... | collective-permute-start | bytes 1179656 | tf_op jit(solution)/shard_map/ppermute | solution.py:70
  38.1 3.9 %collective-permute-start.11 = (bf16[2,64,512]{2,1,0:T(8,128)(2,1)S(1)}, bf16[2,64,512]{2,1,0:T(8,128)(2,1)S(1)}, u32[]{:S(2)}, u32[]{:S(2)}) collective-permute-start(bf16[2,64,512]{2,1,0:T(8,128)(2,1)S(1)} %get-tuple-element.55), channel_id=1, source_target_pairs={{0,64},{64,0},{128,192},{192,128},{8,72},{72,8},{136,200},{200,136... | collective-permute-start | bytes 393224 | tf_op jit(solution)/shard_map/ppermute | solution.py:48
  42.0 11.0 %collective-permute-start.12 = (bf16[64,512]{1,0:T(8,128)(2,1)S(1)}, bf16[64,512]{1,0:T(8,128)(2,1)S(1)}, u32[]{:S(2)}, u32[]{:S(2)}) collective-permute-start(bf16[64,512]{1,0:T(8,128)(2,1)S(1)} %get-tuple-element.57), channel_id=1, source_target_pairs={{0,1},{1,137},{64,65},{65,201},{128,129},{129,9},{192,193},{193,73... | collective-permute-start | bytes 196616 | tf_op jit(solution)/shard_map/ppermute | solution.py:60
  48.2 7.8 %collective-permute-start.13 = (bf16[64,512]{1,0:T(8,128)(2,1)S(1)}, bf16[64,512]{1,0:T(8,128)(2,1)S(1)}, u32[]{:S(2)}, u32[]{:S(2)}) collective-permute-start(bf16[64,512]{1,0:T(8,128)(2,1)S(1)} %get-tuple-element.58), channel_id=1, source_target_pairs={{1,136},{65,200},{129,8},{193,72},{8,129},{72,193},{136,1},{200,65... | collective-permute-start | bytes 196616 | tf_op jit(solution)/shard_map/ppermute | solution.py:60
  56.1 4.1 %collective-permute-start.15 = (bf16[64,512]{1,0:T(8,128)(2,1)S(1)}, bf16[64,512]{1,0:T(8,128)(2,1)S(1)}, u32[]{:S(2)}, u32[]{:S(2)}) collective-permute-start(bf16[64,512]{1,0:T(8,128)(2,1)S(1)} %mirror_sum.1), channel_id=1, source_target_pairs={{0,128},{64,192},{128,0},{192,64},{8,136},{72,200},{136,8},{200,72... | collective-permute-start | bytes 196616 | tf_op jit(solution)/shard_map/ppermute | solution.py:48
  57.9 9.3 %collective-permute-start.20 = (bf16[3,128,512]{2,1,0:T(8,128)(2,1)S(1)}, bf16[3,128,512]{2,1,0:T(8,128)(2,1)S(1)}, u32[]{:S(2)}, u32[]{:S(2)}) collective-permute-start(bf16[3,128,512]{2,1,0:T(8,128)(2,1)S(1)} %collective-permute-done.14.p1), channel_id=1, source_target_pairs={{0,1},{1,0},{2,3},{3,2},{4,5},{5,4},{6,7},{7,6},{8,9},{9,8},{10,11... | collective-permute-start | bytes 1179656 | tf_op jit(solution)/shard_map/ppermute | solution.py:70
  60.2 3.3 %collective-permute-start.16 = (bf16[64,512]{1,0:T(8,128)(2,1)S(1)}, bf16[64,512]{1,0:T(8,128)(2,1)S(1)}, u32[]{:S(2)}, u32[]{:S(2)}) collective-permute-start(bf16[64,512]{1,0:T(8,128)(2,1)S(1)} %add_convert_fusion.refs_0_), channel_id=1, source_target_pairs={{0,64},{64,0},{128,192},{192,128},{8,72},{72,8},{136,200},{200,136... | collective-permute-start | bytes 196616 | tf_op jit(solution)/shard_map/ppermute | solution.py:48
  61.6 5.1 %collective-permute-start.17 = (bf16[64,512]{1,0:T(8,128)(2,1)S(1)}, bf16[64,512]{1,0:T(8,128)(2,1)S(1)}, u32[]{:S(2)}, u32[]{:S(2)}) collective-permute-start(bf16[64,512]{1,0:T(8,128)(2,1)S(1)} %add_convert_fusion.refs_0_), channel_id=1, source_target_pairs={{0,2},{2,0},{1,3},{3,1},{4,6},{6,4},{5,7},{7,5},{8,10},{10,8},{9,1... | collective-permute-start | bytes 196616 | tf_op jit(solution)/shard_map/ppermute | solution.py:70
  61.6 5.1 %collective-permute-start.18 = (bf16[64,512]{1,0:T(8,128)(2,1)S(1)}, bf16[64,512]{1,0:T(8,128)(2,1)S(1)}, u32[]{:S(2)}, u32[]{:S(2)}) collective-permute-start(bf16[64,512]{1,0:T(8,128)(2,1)S(1)} %add_convert_fusion.refs_0_), channel_id=1, source_target_pairs={{0,66},{2,64},{64,2},{66,0},{128,194},{130,192},{192,130},{194,128... | collective-permute-start | bytes 196616 | tf_op jit(solution)/shard_map/ppermute | solution.py:65
  66.7 1.7 %collective-permute-start.19 = (bf16[4,64,512]{2,1,0:T(8,128)(2,1)S(1)}, bf16[4,64,512]{2,1,0:T(8,128)(2,1)S(1)}, u32[]{:S(2)}, u32[]{:S(2)}) collective-permute-start(bf16[4,64,512]{2,1,0:T(8,128)(2,1)S(1)} %stack.1.g_own), channel_id=1, source_target_pairs={{0,1},{1,0},{2,3},{3,2},{4,5},{5,4},{6,7},{7,6},{8,9},{9,8},{10,11... | collective-permute-start | bytes 786440 | tf_op jit(solution)/shard_map/ppermute | solution.py:70
  (1 other events, 9.0 us)

commit v9 on v8

--- a/solution.py
+++ b/solution.py
@@ -39,25 +39,16 @@
     return lax.ppermute(x, ("y",) + X + ("core",), pairs)
 
 
-def ring_spot(z, core=None):
-    spot = (z % 4) * 2 + z // 4
-    return spot if core is None else spot * 2 + core
+def ring_spot(z):
+    return (z % 4) * 2 + z // 4
 
 
 def swap_z(x, bits):
     return lax.ppermute(x, Z, [(ring_spot(z), ring_spot(z ^ bits)) for z in range(8)])
 
 
-def mirror(near, far):
-    first, second = [], []
-    for z in range(8):
-        stays = z // 4
-        across = (6 + 2 * (z % 2) - z) % 8
-        first.append((ring_spot(z, stays), ring_spot(z, 1 - stays)))
-        first.append((ring_spot(z, 1 - stays), ring_spot(across, 1 - stays)))
-        second.append((ring_spot(z, 1 - stays), ring_spot(across, stays)))
-    axes = Z + ("core",)
-    return lax.ppermute(near, axes, first), lax.ppermute(far, axes, second)
+def cross_z(x):
+    return lax.ppermute(x, Z, [(ring_spot(z), ring_spot((6 + 2 * (z % 2) - z) % 8)) for z in range(8)])
 
 
 def diagonal(x):
@@ -307,61 +298,48 @@
     )(*parts)
 
 
-def pair_sum_kernel(keep, came, base, near, far):
+def pair_sum_kernel(keep, came, mine, other):
     core = lax.axis_index("core")
-    mine = keep[core] + came[core].astype(jnp.float32)
-    other = (keep[1 - core] + came[1 - core].astype(jnp.float32)).astype(SEND)
-    base[...] = mine
-    far[...] = other
-    stays = core == lax.axis_index("z_hi")
-
-    @pl.when(stays)
-    def _():
-        near[...] = other
-
-    @pl.when(jnp.logical_not(stays))
-    def _():
-        near[...] = mine.astype(SEND)
+    mine[...] = keep[core] + came[core].astype(jnp.float32)
+    other[...] = (keep[1 - core] + came[1 - core].astype(jnp.float32)).astype(SEND)
 
 
 def pair_sum(keep, came):
     return pl.pallas_call(
         pair_sum_kernel,
         name="pair_sum",
-        out_shape=(
-            jax.ShapeDtypeStruct((PART, B), jnp.float32),
-            jax.ShapeDtypeStruct((PART, B), SEND),
-            jax.ShapeDtypeStruct((PART, B), SEND),
-        ),
+        out_shape=(jax.ShapeDtypeStruct((PART, B), jnp.float32), jax.ShapeDtypeStruct((PART, B), SEND)),
         in_specs=[VMEM] * 2,
-        out_specs=(VMEM,) * 3,
+        out_specs=(VMEM,) * 2,
         compiler_params=pltpu.CompilerParams(vmem_limit_bytes=1 << 20),
         cost_estimate=pl.CostEstimate(flops=2 * ROWS * B, bytes_accessed=1 << 20, transcendentals=0),
     )(keep, came)
 
 
-def mirror_sum_kernel(base, near, far, out):
+def choose_kernel(mine, came, stay, leave):
     stays = lax.axis_index("core") == lax.axis_index("z_hi")
 
     @pl.when(stays)
     def _():
-        out[...] = narrow(base[...] + near[...].astype(jnp.float32))
+        stay[...] = mine[...]
+        leave[...] = came[...]
 
     @pl.when(jnp.logical_not(stays))
     def _():
-        out[...] = narrow(far[...].astype(jnp.float32) + near[...].astype(jnp.float32))
-
-
-def mirror_sum(base, near, far):
-    return pl.pallas_call(
-        mirror_sum_kernel,
-        name="mirror_sum",
-        out_shape=jax.ShapeDtypeStruct((PART, B), jnp.bfloat16),
-        in_specs=[VMEM] * 3,
-        out_specs=VMEM,
+        stay[...] = came[...].astype(jnp.float32)
+        leave[...] = mine[...].astype(SEND)
+
+
+def choose(mine, came):
+    return pl.pallas_call(
+        choose_kernel,
+        name="choose",
+        out_shape=(jax.ShapeDtypeStruct((PART, B), jnp.float32), jax.ShapeDtypeStruct((PART, B), SEND)),
+        in_specs=[VMEM] * 2,
+        out_specs=(VMEM,) * 2,
         compiler_params=pltpu.CompilerParams(vmem_limit_bytes=1 << 20),
-        cost_estimate=pl.CostEstimate(flops=2 * PART * B, bytes_accessed=1 << 19, transcendentals=0),
-    )(base, near, far)
+        cost_estimate=pl.CostEstimate(flops=0, bytes_accessed=1 << 19, transcendentals=0),
+    )(mine, came)
 
 
 def stack_kernel(*refs):
@@ -422,11 +400,13 @@
     pack = jnp.concatenate([narrow(statistics), roots[1:]], axis=0)
     own, pack_core = lax.optimization_barrier((own, partner(pack, "core")))
     keep, send = plane_sum(came + [own])
-    keep, send, pack = lax.optimization_barrier((keep, send, pack))
-    base, near, far = pair_sum(keep, swap_z(send, 1))
+    mine, other = pair_sum(keep, swap_z(send, 1))
+    stay, leave = choose(mine, partner(other, "core"))
+    stay, leave, pack = lax.optimization_barrier((stay, leave, pack))
+    part = rounded(stay + cross_z(leave).astype(jnp.float32))
     pack_x = partner(pack, "x_lo")
-    part, pack_x = lax.optimization_barrier((mirror_sum(base, *mirror(near, far)), pack_x))
     part = rounded(part.astype(jnp.float32) + swap_z(part, 2).astype(jnp.float32))
+    part, pack_x = lax.optimization_barrier((part, pack_x))
     grad = stack((part, swap_z(part, 1), partner(part, "x_lo"), diagonal(part)))
     grads = (grad, partner(grad, "core"))
     full, right = assemble(statistics, (pack, pack_x, pack_core, partner(pack_x, "core")))

time: 76 us -> 78.8 us (1.037)
  waiting for transfers between devices: 31.8 us -> 34 us
    ppermute x6 -> x7, starting transfers between devices: 4.92 us -> 13 us  [partner(): return lax.ppermute(x, axis, [(i, i ^ bits) for i in range(n)])]
    ppermute x2 -> x1, starting transfers between devices: 11 us -> 4.84 us  [cross_z(): lax.ppermute(x, Z, [(ring_spot(z), ring_spot((6 + 2 * (z % 2) - z) % 8))...]
    ppermute x2 -> x1, waiting for transfers between devices: 3.02 us -> 0.99 us  [cross_z(): lax.ppermute(x, Z, [(ring_spot(z), ring_spot((6 + 2 * (z % 2) - z) % 8))...]
    ppermute x1, waiting for transfers between devices: 0.01 us -> 1.84 us  [diagonal(): return lax.ppermute(x, ('z_lo', 'x_lo'), pairs)]
    ppermute x6 -> x7, waiting for transfers between devices: 4.15 us -> 5.55 us  [partner(): return lax.ppermute(x, axis, [(i, i ^ bits) for i in range(n)])]
    ppermute x3, waiting for transfers between devices: 5.16 us -> 6.17 us  [swap_z(): lax.ppermute(x, Z, [(ring_spot(z), ring_spot(z ^ bits)) for z in range(8)])]
    ppermute x3, starting transfers between devices: 4.84 us -> 4.05 us  [swap_z(): lax.ppermute(x, Z, [(ring_spot(z), ring_spot(z ^ bits)) for z in range(8)])]
  transfers between devices with their start and end apart: 21 -> 21, of which waited for: 12 -> 15; matrix products, arithmetic and copies ran while one was open for 0% -> 0% of each run, Pallas kernels for 3% -> 3%
where the time goes in v9:
time: 78.8 us; the launch traced here: 78.7 us
  waiting for transfers between devices  34 us (43%)
  starting transfers between devices  31.9 us (40%)
  Pallas kernels  11.6 us (15%)
  between operations  0.93 us (1%)
    ppermute x9, waiting for transfers between devices, shift(): return lax.ppermute(x, ('y',) + X + ('core',), pairs)  19.5 us
    ppermute x7, starting transfers between devices, partner(): return lax.ppermute(x, axis, [(i, i ^ bits) for i in range(n)])  13 us
    ppermute x9, starting transfers between devices, shift(): return lax.ppermute(x, ('y',) + X + ('core',), pairs)  9.31 us
    pallas_call x1, Pallas kernels, finish(): pl.pallas_call(finish_kernel, name='finish', out_shape=(jax.ShapeDtypeStr...  7.33 us
    ppermute x3, waiting for transfers between devices, swap_z(): lax.ppermute(x, Z, [(ring_spot(z), ring_spot(z ^ bits)) for z in range(8)])  6.17 us
    ppermute x7, waiting for transfers between devices, partner(): return lax.ppermute(x, axis, [(i, i ^ bits) for i in range(n)])  5.55 us
    ppermute x1, starting transfers between devices, cross_z(): lax.ppermute(x, Z, [(ring_spot(z), ring_spot((6 + 2 * (z % 2) - z) % 8))...  4.84 us
    ppermute x3, starting transfers between devices, swap_z(): lax.ppermute(x, Z, [(ring_spot(z), ring_spot(z ^ bits)) for z in range(8)])  4.05 us
  transfers between devices with their start and end apart: 21, of which 15 were waited for; matrix products, arithmetic and copies ran while one was open for 0% of the time, Pallas kernels for 3%

profile of v9, /device:TPU:1, one launch (start us, length us, event | category | flops | bytes accessed | tf_op | source)
XLA Modules:
  0.0 78.7 jit_solution(2615768606002675020)
XLA Ops:
  0.7 2.0 %cut.1 = (bf16[128,1536]{1,0:T(8,128)(2,1)S(1)}, bf16[128,1536]{1,0:T(8,128)(2,1)S(1)}, bf16[128,1536]{1,0:T(8,128)(2,1)S(1)}, bf16[128,1536]{1,0:T(8,128)(2,1)S(1)}, bf16[4,128,1536]{2,1,0:T(8,128)(2,1)S(1)}) custom-call(bf16[128,8192]{1,0:T(8,128)(2,1)} %cotangents.1, bf16[128,512]{1,0:T(8,128)(2,1)} %activations.1), custom_call_target="tpu_custom_call" | custom-call | bytes 6291456 | tf_op jit(solution)/shard_map/cut/pallas_call | solution.py:215
  2.6 3.3 %collective-permute-start = (bf16[4,128,1536]{2,1,0:T(8,128)(2,1)S(1)}, bf16[4,128,1536]{2,1,0:T(8,128)(2,1)S(1)}, u32[]{:S(2)}, u32[]{:S(2)}) collective-permute-start(bf16[4,128,1536]{2,1,0:T(8,128)(2,1)S(1)} %get-tuple-element.35), channel_id=1, source_target_pairs={{0,1},{1,0},{2,3},{3,2},{4,5},{5,4},{6,7},{7,6},{8,9},{9,8},{10,11... | collective-permute-start | bytes 4718600 | tf_op jit(solution)/shard_map/ppermute | solution.py:61
  7.3 2.4 %collective-permute-start.6 = (bf16[128,1536]{1,0:T(8,128)(2,1)S(1)}, bf16[128,1536]{1,0:T(8,128)(2,1)S(1)}, u32[]{:S(2)}, u32[]{:S(2)}) collective-permute-start(bf16[128,1536]{1,0:T(8,128)(2,1)S(1)} %get-tuple-element.43), channel_id=1, source_target_pairs={{0,48},{1,7},{2,50},{3,1},{4,52},{5,3},{6,54},{7,5},{16,0},{17,23}... | collective-permute-start | bytes 1179656 | tf_op jit(solution)/shard_map/ppermute | solution.py:39
  10.7 3.8 %collective-permute-done.4.refs_2_ = bf16[128,1536]{1,0:T(8,128)(2,1)S(1)} collective-permute-done((bf16[128,1536]{1,0:T(8,128)(2,1)S(1)}, bf16[128,1536]{1,0:T(8,128)(2,1)S(1)}, u32[]{:S(2)}, u32[]{:S(2)}) %collective-permute-start.4) | collective-permute-done | bytes 393248 | tf_op jit(solution)/shard_map/ppermute | solution.py:39
  15.2 3.4 %collective-permute-done.5.refs_3_ = bf16[128,1536]{1,0:T(8,128)(2,1)S(1)} collective-permute-done((bf16[128,1536]{1,0:T(8,128)(2,1)S(1)}, bf16[128,1536]{1,0:T(8,128)(2,1)S(1)}, u32[]{:S(2)}, u32[]{:S(2)}) %collective-permute-start.5) | collective-permute-done | bytes 393248 | tf_op jit(solution)/shard_map/ppermute | solution.py:39
  20.6 2.3 %collective-permute-done.1.refs_0_ = bf16[128,1536]{1,0:T(8,128)(2,1)S(1)} collective-permute-done((bf16[128,1536]{1,0:T(8,128)(2,1)S(1)}, bf16[128,1536]{1,0:T(8,128)(2,1)S(1)}, u32[]{:S(2)}, u32[]{:S(2)}) %collective-permute-start.1) | collective-permute-done | bytes 393248 | tf_op jit(solution)/shard_map/ppermute | solution.py:39
  22.9 4.1 %collective-permute-done.2.refs_1_ = bf16[128,1536]{1,0:T(8,128)(2,1)S(1)} collective-permute-done((bf16[128,1536]{1,0:T(8,128)(2,1)S(1)}, bf16[128,1536]{1,0:T(8,128)(2,1)S(1)}, u32[]{:S(2)}, u32[]{:S(2)}) %collective-permute-start.2) | collective-permute-done | bytes 393248 | tf_op jit(solution)/shard_map/ppermute | solution.py:39
  27.8 1.4 %collective-permute-start.7 = (bf16[256,512]{1,0:T(8,128)(2,1)S(1)}, bf16[256,512]{1,0:T(8,128)(2,1)S(1)}, u32[]{:S(2)}, u32[]{:S(2)}) collective-permute-start(bf16[256,512]{1,0:T(8,128)(2,1)S(1)} %get-tuple-element.48), channel_id=1, source_target_pairs={{0,4},{1,33},{2,6},{3,35},{4,0},{5,37},{6,2},{7,39},{16,20},{17,49... | collective-permute-start | bytes 786440 | tf_op jit(solution)/shard_map/ppermute | solution.py:39
  29.6 2.3 %collective-permute-start.9 = (bf16[256,512]{1,0:T(8,128)(2,1)S(1)}, bf16[256,512]{1,0:T(8,128)(2,1)S(1)}, u32[]{:S(2)}, u32[]{:S(2)}) collective-permute-start(bf16[256,512]{1,0:T(8,128)(2,1)S(1)} %get-tuple-element.50), channel_id=1, source_target_pairs={{0,6},{1,49},{2,0},{3,51},{4,2},{5,53},{6,4},{7,55},{16,22},{17,1}... | collective-permute-start | bytes 786440 | tf_op jit(solution)/shard_map/ppermute | solution.py:39
  31.9 3.1 %collective-permute-done.7.first = bf16[256,512]{1,0:T(8,128)(2,1)S(1)} collective-permute-done((bf16[256,512]{1,0:T(8,128)(2,1)S(1)}, bf16[256,512]{1,0:T(8,128)(2,1)S(1)}, u32[]{:S(2)}, u32[]{:S(2)}) %collective-permute-start.7) | collective-permute-done | bytes 262176 | tf_op jit(solution)/shard_map/ppermute | solution.py:39
  35.0 2.8 %collective-permute-done.8.second = bf16[256,512]{1,0:T(8,128)(2,1)S(1)} collective-permute-done((bf16[256,512]{1,0:T(8,128)(2,1)S(1)}, bf16[256,512]{1,0:T(8,128)(2,1)S(1)}, u32[]{:S(2)}, u32[]{:S(2)}) %collective-permute-start.8) | collective-permute-done | bytes 262176 | tf_op jit(solution)/shard_map/ppermute | solution.py:39
  38.4 3.4 %collective-permute-done.11.came = bf16[2,64,512]{2,1,0:T(8,128)(2,1)S(1)} collective-permute-done((bf16[2,64,512]{2,1,0:T(8,128)(2,1)S(1)}, bf16[2,64,512]{2,1,0:T(8,128)(2,1)S(1)}, u32[]{:S(2)}, u32[]{:S(2)}) %collective-permute-start.11) | collective-permute-done | bytes 131104 | tf_op jit(solution)/shard_map/ppermute | solution.py:47
  41.9 3.0 %collective-permute-start.12 = (bf16[64,512]{1,0:T(8,128)(2,1)S(1)}, bf16[64,512]{1,0:T(8,128)(2,1)S(1)}, u32[]{:S(2)}, u32[]{:S(2)}) collective-permute-start(bf16[64,512]{1,0:T(8,128)(2,1)S(1)} %get-tuple-element.56), channel_id=1, source_target_pairs={{0,1},{1,0},{2,3},{3,2},{4,5},{5,4},{6,7},{7,6},{8,9},{9,8},{10,11... | collective-permute-start | bytes 196616 | tf_op jit(solution)/shard_map/ppermute | solution.py:61
  45.9 4.8 %collective-permute-start.13 = (bf16[64,512]{1,0:T(8,128)(2,1)S(1)}, bf16[64,512]{1,0:T(8,128)(2,1)S(1)}, u32[]{:S(2)}, u32[]{:S(2)}) collective-permute-start(bf16[64,512]{1,0:T(8,128)(2,1)S(1)} %get-tuple-element.60), channel_id=1, source_target_pairs={{0,136},{64,200},{128,8},{192,72},{8,128},{72,192},{136,0},{200,64... | collective-permute-start | bytes 196616 | tf_op jit(solution)/shard_map/ppermute | solution.py:51
  50.7 1.2 %collective-permute-start.15 = (bf16[3,128,512]{2,1,0:T(8,128)(2,1)S(1)}, bf16[3,128,512]{2,1,0:T(8,128)(2,1)S(1)}, u32[]{:S(2)}, u32[]{:S(2)}) collective-permute-start(bf16[3,128,512]{2,1,0:T(8,128)(2,1)S(1)} %pad_maximum_fusion.p0), channel_id=1, source_target_pairs={{0,2},{2,0},{1,3},{3,1},{4,6},{6,4},{5,7},{7,5},{8,10},{10,8},{9,1... | collective-permute-start | bytes 1179656 | tf_op jit(solution)/shard_map/ppermute | solution.py:61
  52.9 2.8 %collective-permute-start.14 = (bf16[64,512]{1,0:T(8,128)(2,1)S(1)}, bf16[64,512]{1,0:T(8,128)(2,1)S(1)}, u32[]{:S(2)}, u32[]{:S(2)}) collective-permute-start(bf16[64,512]{1,0:T(8,128)(2,1)S(1)} %add_convert_fusion.1), channel_id=1, source_target_pairs={{0,128},{64,192},{128,0},{192,64},{8,136},{72,200},{136,8},{200,72... | collective-permute-start | bytes 196616 | tf_op jit(solution)/shard_map/ppermute | solution.py:47
  55.8 1.7 %collective-permute-done.14 = bf16[64,512]{1,0:T(8,128)(2,1)S(1)} collective-permute-done((bf16[64,512]{1,0:T(8,128)(2,1)S(1)}, bf16[64,512]{1,0:T(8,128)(2,1)S(1)}, u32[]{:S(2)}, u32[]{:S(2)}) %collective-permute-start.14) | collective-permute-done | bytes 65568 | tf_op jit(solution)/shard_map/ppermute | solution.py:47
  57.4 3.3 %collective-permute-done.15.p1 = bf16[3,128,512]{2,1,0:T(8,128)(2,1)S(1)} collective-permute-done((bf16[3,128,512]{2,1,0:T(8,128)(2,1)S(1)}, bf16[3,128,512]{2,1,0:T(8,128)(2,1)S(1)}, u32[]{:S(2)}, u32[]{:S(2)}) %collective-permute-start.15) | collective-permute-done | bytes 393248 | tf_op jit(solution)/shard_map/ppermute | solution.py:61
  60.7 1.5 %collective-permute-start.20 = (bf16[3,128,512]{2,1,0:T(8,128)(2,1)S(1)}, bf16[3,128,512]{2,1,0:T(8,128)(2,1)S(1)}, u32[]{:S(2)}, u32[]{:S(2)}) collective-permute-start(bf16[3,128,512]{2,1,0:T(8,128)(2,1)S(1)} %collective-permute-done.15.p1), channel_id=1, source_target_pairs={{0,1},{1,0},{2,3},{3,2},{4,5},{5,4},{6,7},{7,6},{8,9},{9,8},{10,11... | collective-permute-start | bytes 1179656 | tf_op jit(solution)/shard_map/ppermute | solution.py:61
  63.0 1.2 %collective-permute-start.17 = (bf16[64,512]{1,0:T(8,128)(2,1)S(1)}, bf16[64,512]{1,0:T(8,128)(2,1)S(1)}, u32[]{:S(2)}, u32[]{:S(2)}) collective-permute-start(bf16[64,512]{1,0:T(8,128)(2,1)S(1)} %add_convert_fusion.refs_0_), channel_id=1, source_target_pairs={{0,2},{2,0},{1,3},{3,1},{4,6},{6,4},{5,7},{7,5},{8,10},{10,8},{9,1... | collective-permute-start | bytes 196616 | tf_op jit(solution)/shard_map/ppermute | solution.py:61
  64.9 1.1 %collective-permute-done.16.refs_1_ = bf16[64,512]{1,0:T(8,128)(2,1)S(1)} collective-permute-done((bf16[64,512]{1,0:T(8,128)(2,1)S(1)}, bf16[64,512]{1,0:T(8,128)(2,1)S(1)}, u32[]{:S(2)}, u32[]{:S(2)}) %collective-permute-start.16) | collective-permute-done | bytes 65568 | tf_op jit(solution)/shard_map/ppermute | solution.py:47
  66.3 1.8 %collective-permute-done.18.refs_3_ = bf16[64,512]{1,0:T(8,128)(2,1)S(1)} collective-permute-done((bf16[64,512]{1,0:T(8,128)(2,1)S(1)}, bf16[64,512]{1,0:T(8,128)(2,1)S(1)}, u32[]{:S(2)}, u32[]{:S(2)}) %collective-permute-start.18) | collective-permute-done | bytes 65568 | tf_op jit(solution)/shard_map/ppermute | solution.py:56
  68.2 1.8 %collective-permute-start.19 = (bf16[4,64,512]{2,1,0:T(8,128)(2,1)S(1)}, bf16[4,64,512]{2,1,0:T(8,128)(2,1)S(1)}, u32[]{:S(2)}, u32[]{:S(2)}) collective-permute-start(bf16[4,64,512]{2,1,0:T(8,128)(2,1)S(1)} %stack.1.g_own), channel_id=1, source_target_pairs={{0,1},{1,0},{2,3},{3,2},{4,5},{5,4},{6,7},{7,6},{8,9},{9,8},{10,11... | collective-permute-start | bytes 786440 | tf_op jit(solution)/shard_map/ppermute | solution.py:61
  71.2 7.3 %finish.1 = (bf16[128,512]{1,0:T(8,128)(2,1)}, f32[2,128,512]{2,1,0:T(8,128)}, bf16[2,128,512]{2,1,0:T(8,128)(2,1)}) custom-call(f32[32]{0:T(128)S(1)} %convert_power_fusion.decays, s32[32]{0:T(128)S(1)} %copy-done.1, bf16[4,64,512]{2,1,0:T(8,128)(2,1)S(1)} %stack.1.g_own, bf16[4,64,512]{2,1,0:T(8,128)(2,1)S(1)} %collective-permute-done.19.g_core, ...), custom_call_target="tpu_custom_call" | custom-call | flops 4831838208 | bytes 6291456 | tf_op jit(solution)/shard_map/finish/pallas_call | solution.py:155
  (42 shorter events, 11.9 us)
Async XLA Ops:
  0.6 14.5 %copy-start.2 = (bf16[2,128,512]{2,1,0:T(8,128)(2,1)S(1)}, bf16[2,128,512]{2,1,0:T(8,128)(2,1)}, u32[]{:S(2)}) copy-start(bf16[2,128,512]{2,1,0:T(8,128)(2,1)} %param.9) | copy-start | bytes 786436
  2.6 7.1 %collective-permute-start = (bf16[4,128,1536]{2,1,0:T(8,128)(2,1)S(1)}, bf16[4,128,1536]{2,1,0:T(8,128)(2,1)S(1)}, u32[]{:S(2)}, u32[]{:S(2)}) collective-permute-start(bf16[4,128,1536]{2,1,0:T(8,128)(2,1)S(1)} %get-tuple-element.35), channel_id=1, source_target_pairs={{0,1},{1,0},{2,3},{3,2},{4,5},{5,4},{6,7},{7,6},{8,9},{9,8},{10,11... | collective-permute-start | bytes 4718600 | tf_op jit(solution)/shard_map/ppermute | solution.py:61
  6.0 8.5 %collective-permute-start.4 = (bf16[128,1536]{1,0:T(8,128)(2,1)S(1)}, bf16[128,1536]{1,0:T(8,128)(2,1)S(1)}, u32[]{:S(2)}, u32[]{:S(2)}) collective-permute-start(bf16[128,1536]{1,0:T(8,128)(2,1)S(1)} %get-tuple-element.41), channel_id=1, source_target_pairs={{0,32},{1,5},{2,34},{3,7},{4,36},{5,1},{6,38},{7,3},{16,48},{17,21... | collective-permute-start | bytes 1179656 | tf_op jit(solution)/shard_map/ppermute | solution.py:39
  7.0 11.6 %collective-permute-start.5 = (bf16[128,1536]{1,0:T(8,128)(2,1)S(1)}, bf16[128,1536]{1,0:T(8,128)(2,1)S(1)}, u32[]{:S(2)}, u32[]{:S(2)}) collective-permute-start(bf16[128,1536]{1,0:T(8,128)(2,1)S(1)} %get-tuple-element.42), channel_id=1, source_target_pairs={{0,16},{1,3},{2,18},{3,5},{4,20},{5,7},{6,22},{7,1},{16,32},{17,19... | collective-permute-start | bytes 1179656 | tf_op jit(solution)/shard_map/ppermute | solution.py:39
  7.3 12.3 %collective-permute-start.6 = (bf16[128,1536]{1,0:T(8,128)(2,1)S(1)}, bf16[128,1536]{1,0:T(8,128)(2,1)S(1)}, u32[]{:S(2)}, u32[]{:S(2)}) collective-permute-start(bf16[128,1536]{1,0:T(8,128)(2,1)S(1)} %get-tuple-element.43), channel_id=1, source_target_pairs={{0,48},{1,7},{2,50},{3,1},{4,52},{5,3},{6,54},{7,5},{16,0},{17,23}... | collective-permute-start | bytes 1179656 | tf_op jit(solution)/shard_map/ppermute | solution.py:39
  9.8 13.1 %collective-permute-start.1 = (bf16[128,1536]{1,0:T(8,128)(2,1)S(1)}, bf16[128,1536]{1,0:T(8,128)(2,1)S(1)}, u32[]{:S(2)}, u32[]{:S(2)}) collective-permute-start(bf16[128,1536]{1,0:T(8,128)(2,1)S(1)} %get-tuple-element.36), channel_id=1, source_target_pairs={{0,32},{1,5},{2,34},{3,7},{4,36},{5,1},{6,38},{7,3},{16,48},{17,21... | collective-permute-start | bytes 1179656 | tf_op jit(solution)/shard_map/ppermute | solution.py:39
  10.7 16.4 %collective-permute-start.2 = (bf16[128,1536]{1,0:T(8,128)(2,1)S(1)}, bf16[128,1536]{1,0:T(8,128)(2,1)S(1)}, u32[]{:S(2)}, u32[]{:S(2)}) collective-permute-start(bf16[128,1536]{1,0:T(8,128)(2,1)S(1)} %get-tuple-element.37), channel_id=1, source_target_pairs={{0,16},{1,3},{2,18},{3,5},{4,20},{5,7},{6,22},{7,1},{16,32},{17,19... | collective-permute-start | bytes 1179656 | tf_op jit(solution)/shard_map/ppermute | solution.py:39
  14.4 12.6 %collective-permute-start.3 = (bf16[128,1536]{1,0:T(8,128)(2,1)S(1)}, bf16[128,1536]{1,0:T(8,128)(2,1)S(1)}, u32[]{:S(2)}, u32[]{:S(2)}) collective-permute-start(bf16[128,1536]{1,0:T(8,128)(2,1)S(1)} %get-tuple-element.38), channel_id=1, source_target_pairs={{0,48},{1,7},{2,50},{3,1},{4,52},{5,3},{6,54},{7,5},{16,0},{17,23}... | collective-permute-start | bytes 1179656 | tf_op jit(solution)/shard_map/ppermute | solution.py:39
  18.6 13.3 %collective-permute-start.10 = (bf16[3,128,512]{2,1,0:T(8,128)(2,1)S(1)}, bf16[3,128,512]{2,1,0:T(8,128)(2,1)S(1)}, u32[]{:S(2)}, u32[]{:S(2)}) collective-permute-start(bf16[3,128,512]{2,1,0:T(8,128)(2,1)S(1)} %pad_maximum_fusion.p0), channel_id=1, source_target_pairs={{0,1},{1,0},{2,3},{3,2},{4,5},{5,4},{6,7},{7,6},{8,9},{9,8},{10,11... | collective-permute-start | bytes 1179656 | tf_op jit(solution)/shard_map/ppermute | solution.py:61
  27.8 42.2 %copy-start.3 = (s32[32]{0:T(128)S(1)}, s32[32]{0:T(128)}, u32[]{:S(2)}) copy-start(s32[32]{0:T(128)} %param.10) | copy-start | bytes 388
  27.8 7.1 %collective-permute-start.7 = (bf16[256,512]{1,0:T(8,128)(2,1)S(1)}, bf16[256,512]{1,0:T(8,128)(2,1)S(1)}, u32[]{:S(2)}, u32[]{:S(2)}) collective-permute-start(bf16[256,512]{1,0:T(8,128)(2,1)S(1)} %get-tuple-element.48), channel_id=1, source_target_pairs={{0,4},{1,33},{2,6},{3,35},{4,0},{5,37},{6,2},{7,39},{16,20},{17,49... | collective-permute-start | bytes 786440 | tf_op jit(solution)/shard_map/ppermute | solution.py:39
  29.2 8.5 %collective-permute-start.8 = (bf16[256,512]{1,0:T(8,128)(2,1)S(1)}, bf16[256,512]{1,0:T(8,128)(2,1)S(1)}, u32[]{:S(2)}, u32[]{:S(2)}) collective-permute-start(bf16[256,512]{1,0:T(8,128)(2,1)S(1)} %get-tuple-element.49), channel_id=1, source_target_pairs={{0,2},{1,17},{2,4},{3,19},{4,6},{5,21},{6,0},{7,23},{16,18},{17,33... | collective-permute-start | bytes 786440 | tf_op jit(solution)/shard_map/ppermute | solution.py:39
  29.6 8.1 %collective-permute-start.9 = (bf16[256,512]{1,0:T(8,128)(2,1)S(1)}, bf16[256,512]{1,0:T(8,128)(2,1)S(1)}, u32[]{:S(2)}, u32[]{:S(2)}) collective-permute-start(bf16[256,512]{1,0:T(8,128)(2,1)S(1)} %get-tuple-element.50), channel_id=1, source_target_pairs={{0,6},{1,49},{2,0},{3,51},{4,2},{5,53},{6,4},{7,55},{16,22},{17,1}... | collective-permute-start | bytes 786440 | tf_op jit(solution)/shard_map/ppermute | solution.py:39
  37.9 33.2 %copy-start.1 = (s32[32]{0:T(128)S(1)}, s32[32]{0:T(128)}, u32[]{:S(2)}) copy-start(s32[32]{0:T(128)} %refresh.1) | copy-start | bytes 388
  38.0 3.9 %collective-permute-start.11 = (bf16[2,64,512]{2,1,0:T(8,128)(2,1)S(1)}, bf16[2,64,512]{2,1,0:T(8,128)(2,1)S(1)}, u32[]{:S(2)}, u32[]{:S(2)}) collective-permute-start(bf16[2,64,512]{2,1,0:T(8,128)(2,1)S(1)} %get-tuple-element.54), channel_id=1, source_target_pairs={{0,64},{64,0},{128,192},{192,128},{8,72},{72,8},{136,200},{200,136... | collective-permute-start | bytes 393224 | tf_op jit(solution)/shard_map/ppermute | solution.py:47
  41.9 3.9 %collective-permute-start.12 = (bf16[64,512]{1,0:T(8,128)(2,1)S(1)}, bf16[64,512]{1,0:T(8,128)(2,1)S(1)}, u32[]{:S(2)}, u32[]{:S(2)}) collective-permute-start(bf16[64,512]{1,0:T(8,128)(2,1)S(1)} %get-tuple-element.56), channel_id=1, source_target_pairs={{0,1},{1,0},{2,3},{3,2},{4,5},{5,4},{6,7},{7,6},{8,9},{9,8},{10,11... | collective-permute-start | bytes 196616 | tf_op jit(solution)/shard_map/ppermute | solution.py:61
  45.9 7.0 %collective-permute-start.13 = (bf16[64,512]{1,0:T(8,128)(2,1)S(1)}, bf16[64,512]{1,0:T(8,128)(2,1)S(1)}, u32[]{:S(2)}, u32[]{:S(2)}) collective-permute-start(bf16[64,512]{1,0:T(8,128)(2,1)S(1)} %get-tuple-element.60), channel_id=1, source_target_pairs={{0,136},{64,200},{128,8},{192,72},{8,128},{72,192},{136,0},{200,64... | collective-permute-start | bytes 196616 | tf_op jit(solution)/shard_map/ppermute | solution.py:51
  50.7 10.0 %collective-permute-start.15 = (bf16[3,128,512]{2,1,0:T(8,128)(2,1)S(1)}, bf16[3,128,512]{2,1,0:T(8,128)(2,1)S(1)}, u32[]{:S(2)}, u32[]{:S(2)}) collective-permute-start(bf16[3,128,512]{2,1,0:T(8,128)(2,1)S(1)} %pad_maximum_fusion.p0), channel_id=1, source_target_pairs={{0,2},{2,0},{1,3},{3,1},{4,6},{6,4},{5,7},{7,5},{8,10},{10,8},{9,1... | collective-permute-start | bytes 1179656 | tf_op jit(solution)/shard_map/ppermute | solution.py:61
  52.9 4.5 %collective-permute-start.14 = (bf16[64,512]{1,0:T(8,128)(2,1)S(1)}, bf16[64,512]{1,0:T(8,128)(2,1)S(1)}, u32[]{:S(2)}, u32[]{:S(2)}) collective-permute-start(bf16[64,512]{1,0:T(8,128)(2,1)S(1)} %add_convert_fusion.1), channel_id=1, source_target_pairs={{0,128},{64,192},{128,0},{192,64},{8,136},{72,200},{136,8},{200,72... | collective-permute-start | bytes 196616 | tf_op jit(solution)/shard_map/ppermute | solution.py:47
  60.7 9.3 %collective-permute-start.20 = (bf16[3,128,512]{2,1,0:T(8,128)(2,1)S(1)}, bf16[3,128,512]{2,1,0:T(8,128)(2,1)S(1)}, u32[]{:S(2)}, u32[]{:S(2)}) collective-permute-start(bf16[3,128,512]{2,1,0:T(8,128)(2,1)S(1)} %collective-permute-done.15.p1), channel_id=1, source_target_pairs={{0,1},{1,0},{2,3},{3,2},{4,5},{5,4},{6,7},{7,6},{8,9},{9,8},{10,11... | collective-permute-start | bytes 1179656 | tf_op jit(solution)/shard_map/ppermute | solution.py:61
  62.2 3.7 %collective-permute-start.16 = (bf16[64,512]{1,0:T(8,128)(2,1)S(1)}, bf16[64,512]{1,0:T(8,128)(2,1)S(1)}, u32[]{:S(2)}, u32[]{:S(2)}) collective-permute-start(bf16[64,512]{1,0:T(8,128)(2,1)S(1)} %add_convert_fusion.refs_0_), channel_id=1, source_target_pairs={{0,64},{64,0},{128,192},{192,128},{8,72},{72,8},{136,200},{200,136... | collective-permute-start | bytes 196616 | tf_op jit(solution)/shard_map/ppermute | solution.py:47
  63.0 3.4 %collective-permute-start.17 = (bf16[64,512]{1,0:T(8,128)(2,1)S(1)}, bf16[64,512]{1,0:T(8,128)(2,1)S(1)}, u32[]{:S(2)}, u32[]{:S(2)}) collective-permute-start(bf16[64,512]{1,0:T(8,128)(2,1)S(1)} %add_convert_fusion.refs_0_), channel_id=1, source_target_pairs={{0,2},{2,0},{1,3},{3,1},{4,6},{6,4},{5,7},{7,5},{8,10},{10,8},{9,1... | collective-permute-start | bytes 196616 | tf_op jit(solution)/shard_map/ppermute | solution.py:61
  64.2 4.0 %collective-permute-start.18 = (bf16[64,512]{1,0:T(8,128)(2,1)S(1)}, bf16[64,512]{1,0:T(8,128)(2,1)S(1)}, u32[]{:S(2)}, u32[]{:S(2)}) collective-permute-start(bf16[64,512]{1,0:T(8,128)(2,1)S(1)} %add_convert_fusion.refs_0_), channel_id=1, source_target_pairs={{0,66},{2,64},{64,2},{66,0},{128,194},{130,192},{192,130},{194,128... | collective-permute-start | bytes 196616 | tf_op jit(solution)/shard_map/ppermute | solution.py:56
  68.2 3.0 %collective-permute-start.19 = (bf16[4,64,512]{2,1,0:T(8,128)(2,1)S(1)}, bf16[4,64,512]{2,1,0:T(8,128)(2,1)S(1)}, u32[]{:S(2)}, u32[]{:S(2)}) collective-permute-start(bf16[4,64,512]{2,1,0:T(8,128)(2,1)S(1)} %stack.1.g_own), channel_id=1, source_target_pairs={{0,1},{1,0},{2,3},{3,2},{4,5},{5,4},{6,7},{7,6},{8,9},{9,8},{10,11... | collective-permute-start | bytes 786440 | tf_op jit(solution)/shard_map/ppermute | solution.py:61
  (1 other events, 9.0 us)

commit v10 on v7

--- a/solution.py
+++ b/solution.py
@@ -52,8 +52,9 @@
     for z in range(8):
         stays = z // 4
         first.append((ring_spot(z, stays), ring_spot(z, 1 - stays)))
-        first.append((ring_spot(z, 1 - stays), ring_spot(7 - z, 1 - stays)))
-        second.append((ring_spot(z, 1 - stays), ring_spot(7 - z, stays)))
+        across = (6 + 2 * (z % 2) - z) % 8
+        first.append((ring_spot(z, 1 - stays), ring_spot(across, 1 - stays)))
+        second.append((ring_spot(z, 1 - stays), ring_spot(across, stays)))
     axes = Z + ("core",)
     return lax.ppermute(near, axes, first), lax.ppermute(far, axes, second)
 
@@ -180,8 +181,8 @@
     return {name: lax.axis_index(name) for name in EVERY}
 
 
-def cut_kernel(cotangents, activations, *rest):
-    outs, other, held, sem = rest[:4], rest[4], rest[5], rest[6]
+def cut_kernel(order, cotangents, activations, *rest):
+    outs, other, held, sem = rest[: len(order)], rest[-3], rest[-2], rest[-1]
     at = places()
     spot = (at["y"], at["x_hi"] * 2 + at["x_lo"])
     copies = []
@@ -191,8 +192,8 @@
         copies[-1].start()
 
     copy(activations, held)
-    pieces = [(at["core"], out) for out in outs] + [(1 - at["core"], other.at[i]) for i in range(4)]
-    for (core, out), k in zip(pieces, ORDER * 2):
+    pieces = [(at["core"], out) for out in outs] + [(1 - at["core"], other.at[i]) for i in range(len(order))]
+    for (core, out), k in zip(pieces, order * 2):
         for j in range(4):
             start = jnp.where(
                 core == 0,
@@ -208,20 +209,21 @@
         c.wait()
 
 
-def cut(cotangents, activations):
+def cut(order, cotangents, activations):
     free = pl.BlockSpec(memory_space=pltpu.HBM)
     cotangents = pltpu.with_memory_space_constraint(cotangents, pltpu.HBM)
     activations = pltpu.with_memory_space_constraint(activations, pltpu.HBM)
-    return pl.pallas_call(
-        cut_kernel,
-        name="cut",
-        out_shape=(jax.ShapeDtypeStruct((TOKENS, WIDE), jnp.bfloat16),) * 4
-        + (jax.ShapeDtypeStruct((4, TOKENS, WIDE), jnp.bfloat16),),
+    n = len(order)
+    return pl.pallas_call(
+        functools.partial(cut_kernel, order),
+        name=f"cut_{n}",
+        out_shape=(jax.ShapeDtypeStruct((TOKENS, WIDE), jnp.bfloat16),) * n
+        + (jax.ShapeDtypeStruct((n, TOKENS, WIDE), jnp.bfloat16),),
         in_specs=[free, free],
-        out_specs=(VMEM,) * 5,
-        scratch_shapes=[pltpu.VMEM((TOKENS, B), jnp.bfloat16), pltpu.SemaphoreType.DMA((33,))],
+        out_specs=(VMEM,) * (n + 1),
+        scratch_shapes=[pltpu.VMEM((TOKENS, B), jnp.bfloat16), pltpu.SemaphoreType.DMA((8 * n + 1,))],
         compiler_params=pltpu.CompilerParams(vmem_limit_bytes=4 << 20),
-        cost_estimate=pl.CostEstimate(flops=0, bytes_accessed=6 << 20, transcendentals=0),
+        cost_estimate=pl.CostEstimate(flops=0, bytes_accessed=n << 20, transcendentals=0),
     )(cotangents, activations)
 
 
@@ -234,9 +236,9 @@
     return pl.pallas_call(
         split_kernel,
         name="split",
-        out_shape=(jax.ShapeDtypeStruct((TOKENS, WIDE), jnp.bfloat16),) * 4,
+        out_shape=(jax.ShapeDtypeStruct((TOKENS, WIDE), jnp.bfloat16),) * 3,
         in_specs=[VMEM],
-        out_specs=(VMEM,) * 4,
+        out_specs=(VMEM,) * 3,
         compiler_params=pltpu.CompilerParams(vmem_limit_bytes=1 << 20),
         cost_estimate=pl.CostEstimate(flops=0, bytes_accessed=3 << 20, transcendentals=0),
     )(pieces)
@@ -365,12 +367,13 @@
 
 def per_device(activations, cotangents, statistics, roots, ages, refresh):
     decays = decay_base ** ages.astype(jnp.float32)
-    *own_pieces, other = cut(cotangents, activations)
+    *own_pieces, other = cut(ORDER[:3], cotangents, activations)
+    here, here_other = cut(ORDER[3:], cotangents, activations)
     own_came = [shift(own_pieces[i], True, ORDER[i]) for i in range(3)]
     pieces = split(partner(other, "core"))
     came = [shift(pieces[i], True, ORDER[i]) for i in range(3)]
 
-    early = product([own_pieces[3], pieces[3]] + own_came)
+    early = product([here, partner(here_other, "core")[0]] + own_came)
     *sends, own = product(came, early)
     came = [shift(sends[i], False, ORDER[i]) for i in range(3)]
     pack = jnp.concatenate([narrow(statistics), roots[1:]], axis=0)

time: 76.5 us -> 80.5 us (1.052)
  the two profiles are of different devices: /device:TPU:1 before, /device:TPU:9 now
where the time goes in v10:
time: 80.5 us; the launch traced here: 80.3 us
  starting transfers between devices  36.2 us (45%)
  waiting for transfers between devices  30.4 us (38%)
  Pallas kernels  12.5 us (16%)
  between operations  1 us (1%)
    ppermute x9, starting transfers between devices, shift(): return lax.ppermute(x, ('y',) + X + ('core',), pairs)  13 us
    ppermute x9, waiting for transfers between devices, shift(): return lax.ppermute(x, ('y',) + X + ('core',), pairs)  12.9 us
    ppermute x2, starting transfers between devices, mirror(): return (lax.ppermute(near, axes, first), lax.ppermute(far, axes, second))  12.2 us
    ppermute x2, waiting for transfers between devices, swap_z(): lax.ppermute(x, Z, [(ring_spot(z), ring_spot(z ^ bits)) for z in range(8)])  10.8 us
    pallas_call x1, Pallas kernels, finish(): pl.pallas_call(finish_kernel, name='finish', out_shape=(jax.ShapeDtypeStr...  7.31 us
    ppermute x8, starting transfers between devices, partner(): return lax.ppermute(x, axis, [(i, i ^ bits) for i in range(n)])  7.24 us
    ppermute x2, starting transfers between devices, swap_z(): lax.ppermute(x, Z, [(ring_spot(z), ring_spot(z ^ bits)) for z in range(8)])  3.76 us
    ppermute x8, waiting for transfers between devices, partner(): return lax.ppermute(x, axis, [(i, i ^ bits) for i in range(n)])  3.47 us
  transfers between devices with their start and end apart: 21, of which 11 were waited for; matrix products, arithmetic and copies ran while one was open for 0% of the time, Pallas kernels for 4%

profile of v10, /device:TPU:9, one launch (start us, length us, event | category | flops | bytes accessed | tf_op | source)
XLA Modules:
  0.0 80.3 jit_solution(2661274609023161590)
XLA Ops:
  0.6 1.7 %cut_3.1 = (bf16[128,1536]{1,0:T(8,128)(2,1)S(1)}, bf16[128,1536]{1,0:T(8,128)(2,1)S(1)}, bf16[128,1536]{1,0:T(8,128)(2,1)S(1)}, bf16[3,128,1536]{2,1,0:T(8,128)(2,1)S(1)}) custom-call(bf16[128,8192]{1,0:T(8,128)(2,1)} %cotangents.3, bf16[128,512]{1,0:T(8,128)(2,1)} %activations.3), custom_call_target="tpu_custom_call" | custom-call | bytes 3145728 | tf_op jit(solution)/shard_map/cut_3/pallas_call | solution.py:217
  3.1 2.7 %collective-permute-start.5 = (bf16[128,1536]{1,0:T(8,128)(2,1)S(1)}, bf16[128,1536]{1,0:T(8,128)(2,1)S(1)}, u32[]{:S(2)}, u32[]{:S(2)}) collective-permute-start(bf16[128,1536]{1,0:T(8,128)(2,1)S(1)} %get-tuple-element.39), channel_id=1, source_target_pairs={{0,32},{1,5},{2,34},{3,7},{4,36},{5,1},{6,38},{7,3},{16,48},{17,21... | collective-permute-start | bytes 1179656 | tf_op jit(solution)/shard_map/ppermute | solution.py:38
  6.2 2.4 %collective-permute-start.7 = (bf16[128,1536]{1,0:T(8,128)(2,1)S(1)}, bf16[128,1536]{1,0:T(8,128)(2,1)S(1)}, u32[]{:S(2)}, u32[]{:S(2)}) collective-permute-start(bf16[128,1536]{1,0:T(8,128)(2,1)S(1)} %get-tuple-element.41), channel_id=1, source_target_pairs={{0,48},{1,7},{2,50},{3,1},{4,52},{5,3},{6,54},{7,5},{16,0},{17,23}... | collective-permute-start | bytes 1179656 | tf_op jit(solution)/shard_map/ppermute | solution.py:38
  8.6 1.2 %cut_1.1 = (bf16[128,1536]{1,0:T(8,128)(2,1)S(1)}, bf16[1,128,1536]{2,1,0:T(8,128)(2,1)S(1)}) custom-call(bf16[128,8192]{1,0:T(8,128)(2,1)} %cotangents.3, bf16[128,512]{1,0:T(8,128)(2,1)} %activations.3), custom_call_target="tpu_custom_call" | custom-call | bytes 1048576 | tf_op jit(solution)/shard_map/cut_1/pallas_call | solution.py:217
  10.0 1.8 %collective-permute-start.1 = (bf16[128,1536]{1,0:T(8,128)(2,1)S(1)}, bf16[128,1536]{1,0:T(8,128)(2,1)S(1)}, u32[]{:S(2)}, u32[]{:S(2)}) collective-permute-start(bf16[128,1536]{1,0:T(8,128)(2,1)S(1)} %get-tuple-element.34), channel_id=1, source_target_pairs={{0,32},{1,5},{2,34},{3,7},{4,36},{5,1},{6,38},{7,3},{16,48},{17,21... | collective-permute-start | bytes 1179656 | tf_op jit(solution)/shard_map/ppermute | solution.py:38
  12.8 2.7 %collective-permute-done.6.refs_3_ = bf16[128,1536]{1,0:T(8,128)(2,1)S(1)} collective-permute-done((bf16[128,1536]{1,0:T(8,128)(2,1)S(1)}, bf16[128,1536]{1,0:T(8,128)(2,1)S(1)}, u32[]{:S(2)}, u32[]{:S(2)}) %collective-permute-start.6) | collective-permute-done | bytes 393248 | tf_op jit(solution)/shard_map/ppermute | solution.py:38
  16.2 2.9 %collective-permute-start.11 = (bf16[3,128,512]{2,1,0:T(8,128)(2,1)S(1)}, bf16[3,128,512]{2,1,0:T(8,128)(2,1)S(1)}, u32[]{:S(2)}, u32[]{:S(2)}) collective-permute-start(bf16[3,128,512]{2,1,0:T(8,128)(2,1)S(1)} %pad_maximum_fusion.p0), channel_id=1, source_target_pairs={{0,1},{1,0},{2,3},{3,2},{4,5},{5,4},{6,7},{7,6},{8,9},{9,8},{10,11... | collective-permute-start | bytes 1179656 | tf_op jit(solution)/shard_map/ppermute | solution.py:64
  19.1 1.0 %product.2 = (f32[256,512]{1,0:T(8,128)S(1)}, f32[256,512]{1,0:T(8,128)S(1)}, f32[256,512]{1,0:T(8,128)S(1)}, f32[256,512]{1,0:T(8,128)S(1)}) custom-call(bf16[128,1536]{1,0:T(8,128)(2,1)S(1)} %get-tuple-element.37.refs_0_, bf16[128,1536]{1,0:T(8,128)(2,1)S(1)} %bitcast.3, bf16[128,1536]{1,0:T(8,128)(2,1)S(1)} %collective-permute-done.5.refs_2_, ...), custom_call_target="tpu_custom_call" | custom-call | flops 671088640 | bytes 4194304 | tf_op jit(solution)/shard_map/product/pallas_call | solution.py:263
  20.1 3.8 %collective-permute-done.2.refs_1_ = bf16[128,1536]{1,0:T(8,128)(2,1)S(1)} collective-permute-done((bf16[128,1536]{1,0:T(8,128)(2,1)S(1)}, bf16[128,1536]{1,0:T(8,128)(2,1)S(1)}, u32[]{:S(2)}, u32[]{:S(2)}) %collective-permute-start.2) | collective-permute-done | bytes 393248 | tf_op jit(solution)/shard_map/ppermute | solution.py:38
  25.1 1.9 %collective-permute-start.10 = (bf16[256,512]{1,0:T(8,128)(2,1)S(1)}, bf16[256,512]{1,0:T(8,128)(2,1)S(1)}, u32[]{:S(2)}, u32[]{:S(2)}) collective-permute-start(bf16[256,512]{1,0:T(8,128)(2,1)S(1)} %get-tuple-element.48), channel_id=1, source_target_pairs={{0,6},{1,49},{2,0},{3,51},{4,2},{5,53},{6,4},{7,55},{16,22},{17,1}... | collective-permute-start | bytes 786440 | tf_op jit(solution)/shard_map/ppermute | solution.py:38
  27.7 1.6 %collective-permute-start.9 = (bf16[256,512]{1,0:T(8,128)(2,1)S(1)}, bf16[256,512]{1,0:T(8,128)(2,1)S(1)}, u32[]{:S(2)}, u32[]{:S(2)}) collective-permute-start(bf16[256,512]{1,0:T(8,128)(2,1)S(1)} %get-tuple-element.47), channel_id=1, source_target_pairs={{0,2},{1,17},{2,4},{3,19},{4,6},{5,21},{6,0},{7,23},{16,18},{17,33... | collective-permute-start | bytes 786440 | tf_op jit(solution)/shard_map/ppermute | solution.py:38
  29.3 1.4 %collective-permute-done.10.third = bf16[256,512]{1,0:T(8,128)(2,1)S(1)} collective-permute-done((bf16[256,512]{1,0:T(8,128)(2,1)S(1)}, bf16[256,512]{1,0:T(8,128)(2,1)S(1)}, u32[]{:S(2)}, u32[]{:S(2)}) %collective-permute-start.10) | collective-permute-done | bytes 262176 | tf_op jit(solution)/shard_map/ppermute | solution.py:38
  30.7 3.8 %collective-permute-done.8.first = bf16[256,512]{1,0:T(8,128)(2,1)S(1)} collective-permute-done((bf16[256,512]{1,0:T(8,128)(2,1)S(1)}, bf16[256,512]{1,0:T(8,128)(2,1)S(1)}, u32[]{:S(2)}, u32[]{:S(2)}) %collective-permute-start.8) | collective-permute-done | bytes 262176 | tf_op jit(solution)/shard_map/ppermute | solution.py:38
  35.6 6.1 %collective-permute-start.12 = (bf16[128,512]{1,0:T(8,128)(2,1)S(1)}, bf16[128,512]{1,0:T(8,128)(2,1)S(1)}, u32[]{:S(2)}, u32[]{:S(2)}) collective-permute-start(bf16[128,512]{1,0:T(8,128)(2,1)S(1)} %get-tuple-element.55), channel_id=1, source_target_pairs={{0,1},{1,137},{64,65},{65,201},{128,129},{129,9},{192,193},{193,73... | collective-permute-start | bytes 393224 | tf_op jit(solution)/shard_map/ppermute | solution.py:59
  41.7 6.1 %collective-permute-start.13 = (bf16[128,512]{1,0:T(8,128)(2,1)S(1)}, bf16[128,512]{1,0:T(8,128)(2,1)S(1)}, u32[]{:S(2)}, u32[]{:S(2)}) collective-permute-start(bf16[128,512]{1,0:T(8,128)(2,1)S(1)} %get-tuple-element.56), channel_id=1, source_target_pairs={{1,136},{65,200},{129,8},{193,72},{8,129},{72,193},{136,1},{200,65... | collective-permute-start | bytes 393224 | tf_op jit(solution)/shard_map/ppermute | solution.py:59
  47.9 3.2 %collective-permute-done.13.far = bf16[128,512]{1,0:T(8,128)(2,1)S(1)} collective-permute-done((bf16[128,512]{1,0:T(8,128)(2,1)S(1)}, bf16[128,512]{1,0:T(8,128)(2,1)S(1)}, u32[]{:S(2)}, u32[]{:S(2)}) %collective-permute-start.13) | collective-permute-done | bytes 131104 | tf_op jit(solution)/shard_map/ppermute | solution.py:59
  51.2 2.6 %collective-permute-start.14 = (bf16[128,512]{1,0:T(8,128)(2,1)S(1)}, bf16[128,512]{1,0:T(8,128)(2,1)S(1)}, u32[]{:S(2)}, u32[]{:S(2)}) collective-permute-start(bf16[128,512]{1,0:T(8,128)(2,1)S(1)} %mirror_sum.1), channel_id=1, source_target_pairs={{0,64},{64,0},{128,192},{192,128},{8,72},{72,8},{136,200},{200,136... | collective-permute-start | bytes 393224 | tf_op jit(solution)/shard_map/ppermute | solution.py:47
  53.8 3.2 %collective-permute-done.14 = bf16[128,512]{1,0:T(8,128)(2,1)S(1)} collective-permute-done((bf16[128,512]{1,0:T(8,128)(2,1)S(1)}, bf16[128,512]{1,0:T(8,128)(2,1)S(1)}, u32[]{:S(2)}, u32[]{:S(2)}) %collective-permute-start.14) | collective-permute-done | bytes 131104 | tf_op jit(solution)/shard_map/ppermute | solution.py:47
  57.1 1.1 %collective-permute-start.16 = (bf16[128,512]{1,0:T(8,128)(2,1)S(1)}, bf16[128,512]{1,0:T(8,128)(2,1)S(1)}, u32[]{:S(2)}, u32[]{:S(2)}) collective-permute-start(bf16[128,512]{1,0:T(8,128)(2,1)S(1)} %add_convert_fusion.1), channel_id=1, source_target_pairs={{0,128},{64,192},{128,0},{192,64},{8,136},{72,200},{136,8},{200,72... | collective-permute-start | bytes 393224 | tf_op jit(solution)/shard_map/ppermute | solution.py:47
  58.2 7.6 %collective-permute-done.16 = bf16[128,512]{1,0:T(8,128)(2,1)S(1)} collective-permute-done((bf16[128,512]{1,0:T(8,128)(2,1)S(1)}, bf16[128,512]{1,0:T(8,128)(2,1)S(1)}, u32[]{:S(2)}, u32[]{:S(2)}) %collective-permute-start.16) | collective-permute-done | bytes 131104 | tf_op jit(solution)/shard_map/ppermute | solution.py:47
  65.9 1.1 %collective-permute-start.18 = (bf16[128,512]{1,0:T(8,128)(2,1)S(1)}, bf16[128,512]{1,0:T(8,128)(2,1)S(1)}, u32[]{:S(2)}, u32[]{:S(2)}) collective-permute-start(bf16[128,512]{1,0:T(8,128)(2,1)S(1)} %add_convert_fusion.g0), channel_id=1, source_target_pairs={{0,1},{1,0},{2,3},{3,2},{4,5},{5,4},{6,7},{7,6},{8,9},{9,8},{10,11... | collective-permute-start | bytes 393224 | tf_op jit(solution)/shard_map/ppermute | solution.py:64
  67.0 2.7 %collective-permute-done.17.g1 = bf16[128,512]{1,0:T(8,128)(2,1)S(1)} collective-permute-done((bf16[128,512]{1,0:T(8,128)(2,1)S(1)}, bf16[128,512]{1,0:T(8,128)(2,1)S(1)}, u32[]{:S(2)}, u32[]{:S(2)}) %collective-permute-start.17) | collective-permute-done | bytes 131104 | tf_op jit(solution)/shard_map/ppermute | solution.py:64
  69.7 2.2 %collective-permute-start.19 = (bf16[128,512]{1,0:T(8,128)(2,1)S(1)}, bf16[128,512]{1,0:T(8,128)(2,1)S(1)}, u32[]{:S(2)}, u32[]{:S(2)}) collective-permute-start(bf16[128,512]{1,0:T(8,128)(2,1)S(1)} %collective-permute-done.17.g1), channel_id=1, source_target_pairs={{0,1},{1,0},{2,3},{3,2},{4,5},{5,4},{6,7},{7,6},{8,9},{9,8},{10,11... | collective-permute-start | bytes 393224 | tf_op jit(solution)/shard_map/ppermute | solution.py:64
  72.9 7.3 %finish.1 = (bf16[128,512]{1,0:T(8,128)(2,1)}, f32[2,128,512]{2,1,0:T(8,128)}, bf16[2,128,512]{2,1,0:T(8,128)(2,1)}) custom-call(f32[32]{0:T(128)S(1)} %convert_power_fusion.decays, s32[32]{0:T(128)S(1)} %copy-done.1, bf16[128,512]{1,0:T(8,128)(2,1)S(1)} %add_convert_fusion.g0, bf16[128,512]{1,0:T(8,128)(2,1)S(1)} %collective-permute-done.17.g1, ...), custom_call_target="tpu_custom_call" | custom-call | flops 4831838208 | bytes 6291456 | tf_op jit(solution)/shard_map/finish/pallas_call | solution.py:156
  (41 shorter events, 7.1 us)
Async XLA Ops:
  2.4 7.5 %collective-permute-start = (bf16[3,128,1536]{2,1,0:T(8,128)(2,1)S(1)}, bf16[3,128,1536]{2,1,0:T(8,128)(2,1)S(1)}, u32[]{:S(2)}, u32[]{:S(2)}) collective-permute-start(bf16[3,128,1536]{2,1,0:T(8,128)(2,1)S(1)} %get-tuple-element.33), channel_id=1, source_target_pairs={{0,1},{1,0},{2,3},{3,2},{4,5},{5,4},{6,7},{7,6},{8,9},{9,8},{10,11... | collective-permute-start | bytes 3538952 | tf_op jit(solution)/shard_map/ppermute | solution.py:64
  3.1 8.7 %collective-permute-start.5 = (bf16[128,1536]{1,0:T(8,128)(2,1)S(1)}, bf16[128,1536]{1,0:T(8,128)(2,1)S(1)}, u32[]{:S(2)}, u32[]{:S(2)}) collective-permute-start(bf16[128,1536]{1,0:T(8,128)(2,1)S(1)} %get-tuple-element.39), channel_id=1, source_target_pairs={{0,32},{1,5},{2,34},{3,7},{4,36},{5,1},{6,38},{7,3},{16,48},{17,21... | collective-permute-start | bytes 1179656 | tf_op jit(solution)/shard_map/ppermute | solution.py:38
  5.9 9.6 %collective-permute-start.6 = (bf16[128,1536]{1,0:T(8,128)(2,1)S(1)}, bf16[128,1536]{1,0:T(8,128)(2,1)S(1)}, u32[]{:S(2)}, u32[]{:S(2)}) collective-permute-start(bf16[128,1536]{1,0:T(8,128)(2,1)S(1)} %get-tuple-element.40), channel_id=1, source_target_pairs={{0,16},{1,3},{2,18},{3,5},{4,20},{5,7},{6,22},{7,1},{16,32},{17,19... | collective-permute-start | bytes 1179656 | tf_op jit(solution)/shard_map/ppermute | solution.py:38
  6.2 9.9 %copy-start.2 = (bf16[2,128,512]{2,1,0:T(8,128)(2,1)S(1)}, bf16[2,128,512]{2,1,0:T(8,128)(2,1)}, u32[]{:S(2)}) copy-start(bf16[2,128,512]{2,1,0:T(8,128)(2,1)} %param.9) | copy-start | bytes 786436
  6.2 10.0 %collective-permute-start.7 = (bf16[128,1536]{1,0:T(8,128)(2,1)S(1)}, bf16[128,1536]{1,0:T(8,128)(2,1)S(1)}, u32[]{:S(2)}, u32[]{:S(2)}) collective-permute-start(bf16[128,1536]{1,0:T(8,128)(2,1)S(1)} %get-tuple-element.41), channel_id=1, source_target_pairs={{0,48},{1,7},{2,50},{3,1},{4,52},{5,3},{6,54},{7,5},{16,0},{17,23}... | collective-permute-start | bytes 1179656 | tf_op jit(solution)/shard_map/ppermute | solution.py:38
  9.8 9.3 %collective-permute-start.4 = (bf16[1,128,1536]{2,1,0:T(8,128)(2,1)S(1)}, bf16[1,128,1536]{2,1,0:T(8,128)(2,1)S(1)}, u32[]{:S(2)}, u32[]{:S(2)}) collective-permute-start(bf16[1,128,1536]{2,1,0:T(8,128)(2,1)S(1)} %get-tuple-element.38), channel_id=1, source_target_pairs={{0,1},{1,0},{2,3},{3,2},{4,5},{5,4},{6,7},{7,6},{8,9},{9,8},{10,11... | collective-permute-start | bytes 1179656 | tf_op jit(solution)/shard_map/ppermute | solution.py:64
  10.0 10.1 %collective-permute-start.1 = (bf16[128,1536]{1,0:T(8,128)(2,1)S(1)}, bf16[128,1536]{1,0:T(8,128)(2,1)S(1)}, u32[]{:S(2)}, u32[]{:S(2)}) collective-permute-start(bf16[128,1536]{1,0:T(8,128)(2,1)S(1)} %get-tuple-element.34), channel_id=1, source_target_pairs={{0,32},{1,5},{2,34},{3,7},{4,36},{5,1},{6,38},{7,3},{16,48},{17,21... | collective-permute-start | bytes 1179656 | tf_op jit(solution)/shard_map/ppermute | solution.py:38
  11.8 12.1 %collective-permute-start.2 = (bf16[128,1536]{1,0:T(8,128)(2,1)S(1)}, bf16[128,1536]{1,0:T(8,128)(2,1)S(1)}, u32[]{:S(2)}, u32[]{:S(2)}) collective-permute-start(bf16[128,1536]{1,0:T(8,128)(2,1)S(1)} %get-tuple-element.35), channel_id=1, source_target_pairs={{0,16},{1,3},{2,18},{3,5},{4,20},{5,7},{6,22},{7,1},{16,32},{17,19... | collective-permute-start | bytes 1179656 | tf_op jit(solution)/shard_map/ppermute | solution.py:38
  15.5 8.9 %collective-permute-start.3 = (bf16[128,1536]{1,0:T(8,128)(2,1)S(1)}, bf16[128,1536]{1,0:T(8,128)(2,1)S(1)}, u32[]{:S(2)}, u32[]{:S(2)}) collective-permute-start(bf16[128,1536]{1,0:T(8,128)(2,1)S(1)} %get-tuple-element.36), channel_id=1, source_target_pairs={{0,48},{1,7},{2,50},{3,1},{4,52},{5,3},{6,54},{7,5},{16,0},{17,23}... | collective-permute-start | bytes 1179656 | tf_op jit(solution)/shard_map/ppermute | solution.py:38
  16.2 13.1 %collective-permute-start.11 = (bf16[3,128,512]{2,1,0:T(8,128)(2,1)S(1)}, bf16[3,128,512]{2,1,0:T(8,128)(2,1)S(1)}, u32[]{:S(2)}, u32[]{:S(2)}) collective-permute-start(bf16[3,128,512]{2,1,0:T(8,128)(2,1)S(1)} %pad_maximum_fusion.p0), channel_id=1, source_target_pairs={{0,1},{1,0},{2,3},{3,2},{4,5},{5,4},{6,7},{7,6},{8,9},{9,8},{10,11... | collective-permute-start | bytes 1179656 | tf_op jit(solution)/shard_map/ppermute | solution.py:64
  25.1 46.8 %copy-start.3 = (s32[32]{0:T(128)S(1)}, s32[32]{0:T(128)}, u32[]{:S(2)}) copy-start(s32[32]{0:T(128)} %param.10) | copy-start | bytes 388
  25.1 5.6 %collective-permute-start.10 = (bf16[256,512]{1,0:T(8,128)(2,1)S(1)}, bf16[256,512]{1,0:T(8,128)(2,1)S(1)}, u32[]{:S(2)}, u32[]{:S(2)}) collective-permute-start(bf16[256,512]{1,0:T(8,128)(2,1)S(1)} %get-tuple-element.48), channel_id=1, source_target_pairs={{0,6},{1,49},{2,0},{3,51},{4,2},{5,53},{6,4},{7,55},{16,22},{17,1}... | collective-permute-start | bytes 786440 | tf_op jit(solution)/shard_map/ppermute | solution.py:38
  27.0 7.5 %collective-permute-start.8 = (bf16[256,512]{1,0:T(8,128)(2,1)S(1)}, bf16[256,512]{1,0:T(8,128)(2,1)S(1)}, u32[]{:S(2)}, u32[]{:S(2)}) collective-permute-start(bf16[256,512]{1,0:T(8,128)(2,1)S(1)} %get-tuple-element.46), channel_id=1, source_target_pairs={{0,4},{1,33},{2,6},{3,35},{4,0},{5,37},{6,2},{7,39},{16,20},{17,49... | collective-permute-start | bytes 786440 | tf_op jit(solution)/shard_map/ppermute | solution.py:38
  27.7 7.7 %collective-permute-start.9 = (bf16[256,512]{1,0:T(8,128)(2,1)S(1)}, bf16[256,512]{1,0:T(8,128)(2,1)S(1)}, u32[]{:S(2)}, u32[]{:S(2)}) collective-permute-start(bf16[256,512]{1,0:T(8,128)(2,1)S(1)} %get-tuple-element.47), channel_id=1, source_target_pairs={{0,2},{1,17},{2,4},{3,19},{4,6},{5,21},{6,0},{7,23},{16,18},{17,33... | collective-permute-start | bytes 786440 | tf_op jit(solution)/shard_map/ppermute | solution.py:38
  35.6 37.3 %copy-start.1 = (s32[32]{0:T(128)S(1)}, s32[32]{0:T(128)}, u32[]{:S(2)}) copy-start(s32[32]{0:T(128)} %refresh.1) | copy-start | bytes 388
  35.6 12.4 %collective-permute-start.12 = (bf16[128,512]{1,0:T(8,128)(2,1)S(1)}, bf16[128,512]{1,0:T(8,128)(2,1)S(1)}, u32[]{:S(2)}, u32[]{:S(2)}) collective-permute-start(bf16[128,512]{1,0:T(8,128)(2,1)S(1)} %get-tuple-element.55), channel_id=1, source_target_pairs={{0,1},{1,137},{64,65},{65,201},{128,129},{129,9},{192,193},{193,73... | collective-permute-start | bytes 393224 | tf_op jit(solution)/shard_map/ppermute | solution.py:59
  41.7 9.4 %collective-permute-start.13 = (bf16[128,512]{1,0:T(8,128)(2,1)S(1)}, bf16[128,512]{1,0:T(8,128)(2,1)S(1)}, u32[]{:S(2)}, u32[]{:S(2)}) collective-permute-start(bf16[128,512]{1,0:T(8,128)(2,1)S(1)} %get-tuple-element.56), channel_id=1, source_target_pairs={{1,136},{65,200},{129,8},{193,72},{8,129},{72,193},{136,1},{200,65... | collective-permute-start | bytes 393224 | tf_op jit(solution)/shard_map/ppermute | solution.py:59
  47.8 9.2 %collective-permute-start.15 = (bf16[3,128,512]{2,1,0:T(8,128)(2,1)S(1)}, bf16[3,128,512]{2,1,0:T(8,128)(2,1)S(1)}, u32[]{:S(2)}, u32[]{:S(2)}) collective-permute-start(bf16[3,128,512]{2,1,0:T(8,128)(2,1)S(1)} %pad_maximum_fusion.p0), channel_id=1, source_target_pairs={{0,2},{2,0},{1,3},{3,1},{4,6},{6,4},{5,7},{7,5},{8,10},{10,8},{9,1... | collective-permute-start | bytes 1179656 | tf_op jit(solution)/shard_map/ppermute | solution.py:64
  51.2 5.9 %collective-permute-start.14 = (bf16[128,512]{1,0:T(8,128)(2,1)S(1)}, bf16[128,512]{1,0:T(8,128)(2,1)S(1)}, u32[]{:S(2)}, u32[]{:S(2)}) collective-permute-start(bf16[128,512]{1,0:T(8,128)(2,1)S(1)} %mirror_sum.1), channel_id=1, source_target_pairs={{0,64},{64,0},{128,192},{192,128},{8,72},{72,8},{136,200},{200,136... | collective-permute-start | bytes 393224 | tf_op jit(solution)/shard_map/ppermute | solution.py:47
  57.1 8.7 %collective-permute-start.16 = (bf16[128,512]{1,0:T(8,128)(2,1)S(1)}, bf16[128,512]{1,0:T(8,128)(2,1)S(1)}, u32[]{:S(2)}, u32[]{:S(2)}) collective-permute-start(bf16[128,512]{1,0:T(8,128)(2,1)S(1)} %add_convert_fusion.1), channel_id=1, source_target_pairs={{0,128},{64,192},{128,0},{192,64},{8,136},{72,200},{136,8},{200,72... | collective-permute-start | bytes 393224 | tf_op jit(solution)/shard_map/ppermute | solution.py:47
  58.2 13.7 %collective-permute-start.20 = (bf16[3,128,512]{2,1,0:T(8,128)(2,1)S(1)}, bf16[3,128,512]{2,1,0:T(8,128)(2,1)S(1)}, u32[]{:S(2)}, u32[]{:S(2)}) collective-permute-start(bf16[3,128,512]{2,1,0:T(8,128)(2,1)S(1)} %collective-permute-done.15.p1), channel_id=1, source_target_pairs={{0,1},{1,0},{2,3},{3,2},{4,5},{5,4},{6,7},{7,6},{8,9},{9,8},{10,11... | collective-permute-start | bytes 1179656 | tf_op jit(solution)/shard_map/ppermute | solution.py:64
  65.8 3.9 %collective-permute-start.17 = (bf16[128,512]{1,0:T(8,128)(2,1)S(1)}, bf16[128,512]{1,0:T(8,128)(2,1)S(1)}, u32[]{:S(2)}, u32[]{:S(2)}) collective-permute-start(bf16[128,512]{1,0:T(8,128)(2,1)S(1)} %add_convert_fusion.g0), channel_id=1, source_target_pairs={{0,2},{2,0},{1,3},{3,1},{4,6},{6,4},{5,7},{7,5},{8,10},{10,8},{9,1... | collective-permute-start | bytes 393224 | tf_op jit(solution)/shard_map/ppermute | solution.py:64
  65.9 6.2 %collective-permute-start.18 = (bf16[128,512]{1,0:T(8,128)(2,1)S(1)}, bf16[128,512]{1,0:T(8,128)(2,1)S(1)}, u32[]{:S(2)}, u32[]{:S(2)}) collective-permute-start(bf16[128,512]{1,0:T(8,128)(2,1)S(1)} %add_convert_fusion.g0), channel_id=1, source_target_pairs={{0,1},{1,0},{2,3},{3,2},{4,5},{5,4},{6,7},{7,6},{8,9},{9,8},{10,11... | collective-permute-start | bytes 393224 | tf_op jit(solution)/shard_map/ppermute | solution.py:64
  69.7 3.2 %collective-permute-start.19 = (bf16[128,512]{1,0:T(8,128)(2,1)S(1)}, bf16[128,512]{1,0:T(8,128)(2,1)S(1)}, u32[]{:S(2)}, u32[]{:S(2)}) collective-permute-start(bf16[128,512]{1,0:T(8,128)(2,1)S(1)} %collective-permute-done.17.g1), channel_id=1, source_target_pairs={{0,1},{1,0},{2,3},{3,2},{4,5},{5,4},{6,7},{7,6},{8,9},{9,8},{10,11... | collective-permute-start | bytes 393224 | tf_op jit(solution)/shard_map/ppermute | solution.py:64
  (1 other events, 9.2 us)

commit v11 on v7

--- a/solution.py
+++ b/solution.py
@@ -38,24 +38,27 @@
     return lax.ppermute(x, ("y",) + X + ("core",), pairs)
 
 
-def ring_spot(z, core=None):
-    spot = (z % 4) * 2 + z // 4
-    return spot if core is None else spot * 2 + core
-
-
-def swap_z(x, bits):
-    return lax.ppermute(x, Z, [(ring_spot(z), ring_spot(z ^ bits)) for z in range(8)])
-
-
-def mirror(near, far):
-    first, second = [], []
+def ring_spot(z):
+    return (z % 4) * 2 + z // 4
+
+
+def between_holders(x, to):
+    pairs = []
     for z in range(8):
-        stays = z // 4
-        first.append((ring_spot(z, stays), ring_spot(z, 1 - stays)))
-        first.append((ring_spot(z, 1 - stays), ring_spot(7 - z, 1 - stays)))
-        second.append((ring_spot(z, 1 - stays), ring_spot(7 - z, stays)))
-    axes = Z + ("core",)
-    return lax.ppermute(near, axes, first), lax.ppermute(far, axes, second)
+        for side in range(2):
+            z_to, side_to = to(z, side)
+            core = z // 4
+            pairs.append(((ring_spot(z) * 2 + side) * 2 + core, (ring_spot(z_to) * 2 + side_to) * 2 + core))
+    return lax.ppermute(x, Z + ("x_lo", "core"), pairs)
+
+
+def mirror(x):
+    pairs = [(ring_spot(z) * 2 + 1 - z // 4, ring_spot(7 - z) * 2 + 1 - z // 4) for z in range(8)]
+    return lax.ppermute(x, Z + ("core",), pairs)
+
+
+def hand_over(x):
+    return lax.ppermute(x, ("z_hi", "core"), [(0, 1), (3, 2)])
 
 
 def partner(x, axis, bits=1):
@@ -76,7 +79,7 @@
     return lax.optimization_barrier(narrow(x))
 
 
-def finish_kernel(decays, refresh, g0, g1, g2, g3, old_stats, old_right, left_old,
+def finish_kernel(decays, refresh, held, held_x, given, given_x, old_stats, old_right, left_old,
                   update, new_stats, new_roots, grad, full, right, left, result, work, sem):
     at = places()
     quarter = at["x_lo"] * 2 + at["core"]
@@ -84,9 +87,21 @@
     factor = 2 * (at["y"] * 4 + at["z_hi"] * 2 + at["x_hi"])
     decay = (decays[factor], decays[factor + 1])
     fresh = (refresh[factor], refresh[factor + 1])
-    for a in range(2):
-        for b in range(2):
-            grad[quarter_rows(at, a, b), :] = (g0, g1, g2, g3)[2 * b + a][...]
+    holds = at["core"] == at["z_hi"]
+
+    def place(near, far):
+        for i, rows in enumerate((near, far)):
+            top = (at["x_lo"] ^ i) * HALF
+            grad[pl.ds(pl.multiple_of(top, HALF), HALF), :] = rows[...]
+
+    @pl.when(holds)
+    def _():
+        place(held, held_x)
+
+    @pl.when(jnp.logical_not(holds))
+    def _():
+        place(given, given_x)
+
     g = grad[...]
     writes = []
 
@@ -269,98 +284,51 @@
     )(*parts, *before)
 
 
-def plane_sum_kernel(first, second, third, own, keep, near, far):
-    total = own[...]
+def plane_sum_kernel(first, second, third, own, total, send):
+    t = own[...]
     for part in (first, second, third):
-        total += part[...].astype(jnp.float32)
-    core = lax.axis_index("core")
-    stays = core == lax.axis_index("z_hi")
-
-    @pl.when(core == 0)
-    def _():
-        keep[...] = total[:ROWS]
-        far[...] = total[ROWS:].astype(SEND)
-
-    @pl.when(core == 1)
-    def _():
-        keep[...] = total[ROWS:]
-        far[...] = total[:ROWS].astype(SEND)
-
-    @pl.when(stays)
-    def _():
-        near[...] = far[...]
-
-    @pl.when(jnp.logical_not(stays))
-    def _():
-        near[...] = keep[...].astype(SEND)
+        t += part[...].astype(jnp.float32)
+    total[...] = t
+    send[...] = t.astype(SEND)
 
 
 def plane_sum(parts):
     return pl.pallas_call(
         plane_sum_kernel,
         name="plane_sum",
-        out_shape=(
-            jax.ShapeDtypeStruct((ROWS, B), jnp.float32),
-            jax.ShapeDtypeStruct((ROWS, B), SEND),
-            jax.ShapeDtypeStruct((ROWS, B), SEND),
-        ),
+        out_shape=(jax.ShapeDtypeStruct((HALF, B), jnp.float32), jax.ShapeDtypeStruct((HALF, B), SEND)),
         in_specs=[VMEM] * 4,
-        out_specs=(VMEM,) * 3,
+        out_specs=(VMEM,) * 2,
         compiler_params=pltpu.CompilerParams(vmem_limit_bytes=2 << 20),
         cost_estimate=pl.CostEstimate(flops=8 * ROWS * B, bytes_accessed=2 << 20, transcendentals=0),
     )(*parts)
 
 
-def mirror_sum_kernel(keep, near, far, out):
-    stays = lax.axis_index("core") == lax.axis_index("z_hi")
-
-    @pl.when(stays)
-    def _():
-        out[...] = narrow(keep[...] + near[...].astype(jnp.float32))
-
-    @pl.when(jnp.logical_not(stays))
-    def _():
-        out[...] = narrow(far[...].astype(jnp.float32) + near[...].astype(jnp.float32))
-
-
-def mirror_sum(keep, near, far):
-    return pl.pallas_call(
-        mirror_sum_kernel,
-        name="mirror_sum",
-        out_shape=jax.ShapeDtypeStruct((ROWS, B), jnp.bfloat16),
-        in_specs=[VMEM] * 3,
-        out_specs=VMEM,
-        compiler_params=pltpu.CompilerParams(vmem_limit_bytes=1 << 20),
-        cost_estimate=pl.CostEstimate(flops=2 * ROWS * B, bytes_accessed=1 << 19, transcendentals=0),
-    )(keep, near, far)
-
-
 def quarter_rows(at, a, b):
     top = ((at["x_lo"] ^ a) * 2 + (at["core"] ^ b)) * ROWS
     return pl.ds(pl.multiple_of(top, ROWS), ROWS)
 
 
-def assemble_kernel(own, p0, p1, p2, p3, full, right):
+def assemble_kernel(own, own_right, s1, s2, s3, r1, r2, r3, full, right):
     at = places()
     for a in range(2):
         for b in range(2):
-            pack = (p0, p1, p2, p3)[2 * b + a]
             here = quarter_rows(at, a, b)
-            right[here, :] = pack[2]
+            right[here, :] = (own_right, r1, r2, r3)[2 * b + a][...]
             for layer in range(2):
-                full[layer, here, :] = pack[layer].astype(jnp.float32) if a + b else own[layer]
-
-
-def assemble(own, packs):
+                full[layer, here, :] = (own, s1, s2, s3)[2 * b + a][layer].astype(jnp.float32)
+
+
+def assemble(*arrays):
     return pl.pallas_call(
         assemble_kernel,
         name="assemble",
         out_shape=(jax.ShapeDtypeStruct((2, B, B), jnp.float32), jax.ShapeDtypeStruct((B, B), jnp.bfloat16)),
-        in_specs=[VMEM] * 5,
+        in_specs=[VMEM] * 8,
         out_specs=(VMEM,) * 2,
         compiler_params=pltpu.CompilerParams(vmem_limit_bytes=1 << 20),
         cost_estimate=pl.CostEstimate(flops=0, bytes_accessed=4 << 20, transcendentals=0),
-    )(own, *packs)
+    )(*arrays)
 
 
 def per_device(activations, cotangents, statistics, roots, ages, refresh):
@@ -373,18 +341,21 @@
     early = product([own_pieces[3], pieces[3]] + own_came)
     *sends, own = product(came, early)
     came = [shift(sends[i], False, ORDER[i]) for i in range(3)]
-    pack = jnp.concatenate([narrow(statistics), roots[1:]], axis=0)
-    own, pack_core = lax.optimization_barrier((own, partner(pack, "core")))
-    keep, near, far = plane_sum(came + [own])
-    keep, near, far, pack = lax.optimization_barrier((keep, near, far, pack))
-    part = mirror_sum(keep, *mirror(near, far))
-    pack_x = partner(pack, "x_lo")
-    part = rounded(part.astype(jnp.float32) + swap_z(part, 1).astype(jnp.float32))
-    part, pack_x = lax.optimization_barrier((part, pack_x))
-    part = rounded(part.astype(jnp.float32) + swap_z(part, 2).astype(jnp.float32))
-    part_x, part_core = partner(part, "x_lo"), partner(part, "core")
-    grads = (part, part_x, part_core, partner(part_x, "core"))
-    full, right = assemble(statistics, (pack, pack_x, pack_core, partner(pack_x, "core")))
+    stats, right = narrow(statistics), roots[1]
+    own, stats_core, right_core = lax.optimization_barrier((own, partner(stats, "core"), partner(right, "core")))
+    total, send = plane_sum(came + [own])
+    total, send, stats, right = lax.optimization_barrier((total, send, stats, right))
+    stats_x, right_x = partner(stats, "x_lo"), partner(right, "x_lo")
+    part = rounded(total + mirror(send).astype(jnp.float32))
+    part, stats_x = lax.optimization_barrier((part, stats_x))
+    part = rounded(part.astype(jnp.float32) + between_holders(part, lambda z, a: (z ^ 1, a)).astype(jnp.float32))
+    part, right_x = lax.optimization_barrier((part, right_x))
+    part = rounded(part.astype(jnp.float32) + between_holders(part, lambda z, a: (z ^ 2, a)).astype(jnp.float32))
+    part_x = between_holders(part, lambda z, a: (z, 1 - a))
+    grads = (part, part_x, hand_over(part), hand_over(part_x))
+    full, right = assemble(
+        statistics, roots[1], stats_x, stats_core, partner(stats_x, "core"), right_x, right_core, partner(right_x, "core")
+    )
     return finish(decays, refresh, *grads, full, right, roots[0])
 
 

time: 76.5 us -> 91.9 us (1.20)
  starting transfers between devices: 31.2 us -> 52.9 us
  waiting for transfers between devices: 32.4 us -> 26 us
    ppermute x7, starting transfers between devices: 6.86 us -> 32.5 us  [partner(): return lax.ppermute(x, axis, [(i, i ^ bits) for i in range(n)])]
    ppermute x4 -> x6, waiting for transfers between devices: 9.23 us -> 4.82 us  [the longest x1 4.81 us: mirror(): return lax.ppermute(x, Z + ('core',), pairs)]
    ppermute x4 -> x6, starting transfers between devices: 15 us -> 11 us  [the longest x1 6.24 us: mirror(): return lax.ppermute(x, Z + ('core',), pairs)]
    ppermute x9, waiting for transfers between devices: 19.5 us -> 16.5 us  [shift(): return lax.ppermute(x, ('y',) + X + ('core',), pairs)]
  transfers between devices with their start and end apart: 20 -> 22, of which waited for: 11 -> 10; matrix products, arithmetic and copies ran while one was open for 0% -> 0% of each run, Pallas kernels for 3% -> 2%
where the time goes in v11:
time: 91.9 us; the launch traced here: 91.6 us
  starting transfers between devices  52.9 us (58%)
  waiting for transfers between devices  26 us (28%)
  Pallas kernels  11.5 us (13%)
  between operations  0.99 us (1%)
    ppermute x7, starting transfers between devices, partner(): return lax.ppermute(x, axis, [(i, i ^ bits) for i in range(n)])  32.5 us
    ppermute x9, waiting for transfers between devices, shift(): return lax.ppermute(x, ('y',) + X + ('core',), pairs)  16.5 us
    ppermute x9, starting transfers between devices, shift(): return lax.ppermute(x, ('y',) + X + ('core',), pairs)  9.31 us
    pallas_call x1, Pallas kernels, finish(): pl.pallas_call(finish_kernel, name='finish', out_shape=(jax.ShapeDtypeStr...  7.36 us
    ppermute x1, starting transfers between devices, mirror(): return lax.ppermute(x, Z + ('core',), pairs)  6.24 us
    ppermute x1, waiting for transfers between devices, mirror(): return lax.ppermute(x, Z + ('core',), pairs)  4.81 us
    ppermute x7, waiting for transfers between devices, partner(): return lax.ppermute(x, axis, [(i, i ^ bits) for i in range(n)])  4.62 us
    ppermute x2, starting transfers between devices, hand_over(): return lax.ppermute(x, ('z_hi', 'core'), [(0, 1), (3, 2)])  2.75 us
  transfers between devices with their start and end apart: 22, of which 10 were waited for; matrix products, arithmetic and copies ran while one was open for 0% of the time, Pallas kernels for 2%

profile of v11, /device:TPU:1, one launch (start us, length us, event | category | flops | bytes accessed | tf_op | source)
XLA Modules:
  0.0 91.6 jit_solution(7206883778875009618)
XLA Ops:
  0.6 2.0 %cut.1 = (bf16[128,1536]{1,0:T(8,128)(2,1)S(1)}, bf16[128,1536]{1,0:T(8,128)(2,1)S(1)}, bf16[128,1536]{1,0:T(8,128)(2,1)S(1)}, bf16[128,1536]{1,0:T(8,128)(2,1)S(1)}, bf16[4,128,1536]{2,1,0:T(8,128)(2,1)S(1)}) custom-call(bf16[128,8192]{1,0:T(8,128)(2,1)} %cotangents.1, bf16[128,512]{1,0:T(8,128)(2,1)} %activations.1), custom_call_target="tpu_custom_call" | custom-call | bytes 6291456 | tf_op jit(solution)/shard_map/cut/pallas_call | solution.py:230
  2.6 3.3 %collective-permute-start = (bf16[4,128,1536]{2,1,0:T(8,128)(2,1)S(1)}, bf16[4,128,1536]{2,1,0:T(8,128)(2,1)S(1)}, u32[]{:S(2)}, u32[]{:S(2)}) collective-permute-start(bf16[4,128,1536]{2,1,0:T(8,128)(2,1)S(1)} %get-tuple-element.35), channel_id=1, source_target_pairs={{0,1},{1,0},{2,3},{3,2},{4,5},{5,4},{6,7},{7,6},{8,9},{9,8},{10,11... | collective-permute-start | bytes 4718600 | tf_op jit(solution)/shard_map/ppermute | solution.py:66
  5.9 1.0 %collective-permute-start.4 = (bf16[128,1536]{1,0:T(8,128)(2,1)S(1)}, bf16[128,1536]{1,0:T(8,128)(2,1)S(1)}, u32[]{:S(2)}, u32[]{:S(2)}) collective-permute-start(bf16[128,1536]{1,0:T(8,128)(2,1)S(1)} %get-tuple-element.41), channel_id=1, source_target_pairs={{0,32},{1,5},{2,34},{3,7},{4,36},{5,1},{6,38},{7,3},{16,48},{17,21... | collective-permute-start | bytes 1179656 | tf_op jit(solution)/shard_map/ppermute | solution.py:38
  7.3 2.4 %collective-permute-start.6 = (bf16[128,1536]{1,0:T(8,128)(2,1)S(1)}, bf16[128,1536]{1,0:T(8,128)(2,1)S(1)}, u32[]{:S(2)}, u32[]{:S(2)}) collective-permute-start(bf16[128,1536]{1,0:T(8,128)(2,1)S(1)} %get-tuple-element.43), channel_id=1, source_target_pairs={{0,48},{1,7},{2,50},{3,1},{4,52},{5,3},{6,54},{7,5},{16,0},{17,23}... | collective-permute-start | bytes 1179656 | tf_op jit(solution)/shard_map/ppermute | solution.py:38
  10.6 3.8 %collective-permute-done.4.refs_2_ = bf16[128,1536]{1,0:T(8,128)(2,1)S(1)} collective-permute-done((bf16[128,1536]{1,0:T(8,128)(2,1)S(1)}, bf16[128,1536]{1,0:T(8,128)(2,1)S(1)}, u32[]{:S(2)}, u32[]{:S(2)}) %collective-permute-start.4) | collective-permute-done | bytes 393248 | tf_op jit(solution)/shard_map/ppermute | solution.py:38
  15.2 3.4 %collective-permute-done.5.refs_3_ = bf16[128,1536]{1,0:T(8,128)(2,1)S(1)} collective-permute-done((bf16[128,1536]{1,0:T(8,128)(2,1)S(1)}, bf16[128,1536]{1,0:T(8,128)(2,1)S(1)}, u32[]{:S(2)}, u32[]{:S(2)}) %collective-permute-start.5) | collective-permute-done | bytes 393248 | tf_op jit(solution)/shard_map/ppermute | solution.py:38
  19.5 1.0 %product.2 = (f32[256,512]{1,0:T(8,128)S(1)}, f32[256,512]{1,0:T(8,128)S(1)}, f32[256,512]{1,0:T(8,128)S(1)}, f32[256,512]{1,0:T(8,128)S(1)}) custom-call(bf16[128,1536]{1,0:T(8,128)(2,1)S(1)} %get-tuple-element.39.refs_0_, bf16[128,1536]{1,0:T(8,128)(2,1)S(1)} %get-tuple-element.40.refs_1_, bf16[128,1536]{1,0:T(8,128)(2,1)S(1)} %collective-permute-done.4.refs_2_, ...), custom_call_target="tpu_custom_call" | custom-call | flops 671088640 | bytes 4194304 | tf_op jit(solution)/shard_map/product/pallas_call | solution.py:276
  20.6 2.3 %collective-permute-done.1.refs_0_ = bf16[128,1536]{1,0:T(8,128)(2,1)S(1)} collective-permute-done((bf16[128,1536]{1,0:T(8,128)(2,1)S(1)}, bf16[128,1536]{1,0:T(8,128)(2,1)S(1)}, u32[]{:S(2)}, u32[]{:S(2)}) %collective-permute-start.1) | collective-permute-done | bytes 393248 | tf_op jit(solution)/shard_map/ppermute | solution.py:38
  22.9 4.1 %collective-permute-done.2.refs_1_ = bf16[128,1536]{1,0:T(8,128)(2,1)S(1)} collective-permute-done((bf16[128,1536]{1,0:T(8,128)(2,1)S(1)}, bf16[128,1536]{1,0:T(8,128)(2,1)S(1)}, u32[]{:S(2)}, u32[]{:S(2)}) %collective-permute-start.2) | collective-permute-done | bytes 393248 | tf_op jit(solution)/shard_map/ppermute | solution.py:38
  27.8 1.4 %collective-permute-start.7 = (bf16[256,512]{1,0:T(8,128)(2,1)S(1)}, bf16[256,512]{1,0:T(8,128)(2,1)S(1)}, u32[]{:S(2)}, u32[]{:S(2)}) collective-permute-start(bf16[256,512]{1,0:T(8,128)(2,1)S(1)} %get-tuple-element.48), channel_id=1, source_target_pairs={{0,4},{1,33},{2,6},{3,35},{4,0},{5,37},{6,2},{7,39},{16,20},{17,49... | collective-permute-start | bytes 786440 | tf_op jit(solution)/shard_map/ppermute | solution.py:38
  29.6 2.3 %collective-permute-start.9 = (bf16[256,512]{1,0:T(8,128)(2,1)S(1)}, bf16[256,512]{1,0:T(8,128)(2,1)S(1)}, u32[]{:S(2)}, u32[]{:S(2)}) collective-permute-start(bf16[256,512]{1,0:T(8,128)(2,1)S(1)} %get-tuple-element.50), channel_id=1, source_target_pairs={{0,6},{1,49},{2,0},{3,51},{4,2},{5,53},{6,4},{7,55},{16,22},{17,1}... | collective-permute-start | bytes 786440 | tf_op jit(solution)/shard_map/ppermute | solution.py:38
  31.9 2.0 %collective-permute-start.11 = (bf16[128,512]{1,0:T(8,128)(2,1)S(1)}, bf16[128,512]{1,0:T(8,128)(2,1)S(1)}, u32[]{:S(2)}, u32[]{:S(2)}) collective-permute-start(bf16[128,512]{1,0:T(8,128)(2,1)S(1)} %get-tuple-element.59.own_right), channel_id=1, source_target_pairs={{0,1},{1,0},{2,3},{3,2},{4,5},{5,4},{6,7},{7,6},{8,9},{9,8},{10,11... | collective-permute-start | bytes 393224 | tf_op jit(solution)/shard_map/ppermute | solution.py:66
  34.9 2.8 %collective-permute-done.8.second = bf16[256,512]{1,0:T(8,128)(2,1)S(1)} collective-permute-done((bf16[256,512]{1,0:T(8,128)(2,1)S(1)}, bf16[256,512]{1,0:T(8,128)(2,1)S(1)}, u32[]{:S(2)}, u32[]{:S(2)}) %collective-permute-start.8) | collective-permute-done | bytes 262176 | tf_op jit(solution)/shard_map/ppermute | solution.py:38
  37.8 6.2 %collective-permute-start.12 = (bf16[256,512]{1,0:T(8,128)(2,1)S(1)}, bf16[256,512]{1,0:T(8,128)(2,1)S(1)}, u32[]{:S(2)}, u32[]{:S(2)}) collective-permute-start(bf16[256,512]{1,0:T(8,128)(2,1)S(1)} %get-tuple-element.56), channel_id=1, source_target_pairs={{1,201},{65,137},{129,73},{193,9},{8,192},{72,128},{136,64},{200,0... | collective-permute-start | bytes 786440 | tf_op jit(solution)/shard_map/ppermute | solution.py:57
  44.1 1.3 %collective-permute-start.13 = (bf16[2,128,512]{2,1,0:T(8,128)(2,1)S(1)}, bf16[2,128,512]{2,1,0:T(8,128)(2,1)S(1)}, u32[]{:S(2)}, u32[]{:S(2)}) collective-permute-start(bf16[2,128,512]{2,1,0:T(8,128)(2,1)S(1)} %convert_element_type.31), channel_id=1, source_target_pairs={{0,2},{2,0},{1,3},{3,1},{4,6},{6,4},{5,7},{7,5},{8,10},{10,8},{9,1... | collective-permute-start | bytes 786440 | tf_op jit(solution)/shard_map/ppermute | solution.py:66
  45.4 4.8 %collective-permute-done.12 = bf16[256,512]{1,0:T(8,128)(2,1)S(1)} collective-permute-done((bf16[256,512]{1,0:T(8,128)(2,1)S(1)}, bf16[256,512]{1,0:T(8,128)(2,1)S(1)}, u32[]{:S(2)}, u32[]{:S(2)}) %collective-permute-start.12) | collective-permute-done | bytes 262176 | tf_op jit(solution)/shard_map/ppermute | solution.py:57
  51.0 1.3 %collective-permute-start.15 = (bf16[128,512]{1,0:T(8,128)(2,1)S(1)}, bf16[128,512]{1,0:T(8,128)(2,1)S(1)}, u32[]{:S(2)}, u32[]{:S(2)}) collective-permute-start(bf16[128,512]{1,0:T(8,128)(2,1)S(1)} %get-tuple-element.59.own_right), channel_id=1, source_target_pairs={{0,2},{2,0},{1,3},{3,1},{4,6},{6,4},{5,7},{7,5},{8,10},{10,8},{9,1... | collective-permute-start | bytes 393224 | tf_op jit(solution)/shard_map/ppermute | solution.py:66
  52.3 2.5 %collective-permute-done.15.r1 = bf16[128,512]{1,0:T(8,128)(2,1)S(1)} collective-permute-done((bf16[128,512]{1,0:T(8,128)(2,1)S(1)}, bf16[128,512]{1,0:T(8,128)(2,1)S(1)}, u32[]{:S(2)}, u32[]{:S(2)}) %collective-permute-start.15) | collective-permute-done | bytes 131104 | tf_op jit(solution)/shard_map/ppermute | solution.py:66
  56.3 20.3 %collective-permute-start.20 = (bf16[2,128,512]{2,1,0:T(8,128)(2,1)S(1)}, bf16[2,128,512]{2,1,0:T(8,128)(2,1)S(1)}, u32[]{:S(2)}, u32[]{:S(2)}) collective-permute-start(bf16[2,128,512]{2,1,0:T(8,128)(2,1)S(1)} %collective-permute-done.13.s1), channel_id=1, source_target_pairs={{0,1},{1,0},{2,3},{3,2},{4,5},{5,4},{6,7},{7,6},{8,9},{9,8},{10,11... | collective-permute-start | bytes 786440 | tf_op jit(solution)/shard_map/ppermute | solution.py:66
  76.6 1.5 %collective-permute-start.18 = (bf16[256,512]{1,0:T(8,128)(2,1)S(1)}, bf16[256,512]{1,0:T(8,128)(2,1)S(1)}, u32[]{:S(2)}, u32[]{:S(2)}) collective-permute-start(bf16[256,512]{1,0:T(8,128)(2,1)S(1)} %add_convert_fusion.held), channel_id=1, source_target_pairs={{0,1},{9,8},{2,3},{11,10},{4,5},{13,12},{6,7},{15,14},{16,17},{25,... | collective-permute-start | bytes 786440 | tf_op jit(solution)/shard_map/ppermute | solution.py:61
  78.1 1.3 %collective-permute-start.19 = (bf16[256,512]{1,0:T(8,128)(2,1)S(1)}, bf16[256,512]{1,0:T(8,128)(2,1)S(1)}, u32[]{:S(2)}, u32[]{:S(2)}) collective-permute-start(bf16[256,512]{1,0:T(8,128)(2,1)S(1)} %collective-permute-done.17.held_x), channel_id=1, source_target_pairs={{0,1},{9,8},{2,3},{11,10},{4,5},{13,12},{6,7},{15,14},{16,17},{25,... | collective-permute-start | bytes 786440 | tf_op jit(solution)/shard_map/ppermute | solution.py:61
  79.4 3.4 %collective-permute-start.21 = (bf16[128,512]{1,0:T(8,128)(2,1)S(1)}, bf16[128,512]{1,0:T(8,128)(2,1)S(1)}, u32[]{:S(2)}, u32[]{:S(2)}) collective-permute-start(bf16[128,512]{1,0:T(8,128)(2,1)S(1)} %collective-permute-done.15.r1), channel_id=1, source_target_pairs={{0,1},{1,0},{2,3},{3,2},{4,5},{5,4},{6,7},{7,6},{8,9},{9,8},{10,11... | collective-permute-start | bytes 393224 | tf_op jit(solution)/shard_map/ppermute | solution.py:66
  82.8 1.1 %collective-permute-done.21.r3 = bf16[128,512]{1,0:T(8,128)(2,1)S(1)} collective-permute-done((bf16[128,512]{1,0:T(8,128)(2,1)S(1)}, bf16[128,512]{1,0:T(8,128)(2,1)S(1)}, u32[]{:S(2)}, u32[]{:S(2)}) %collective-permute-start.21) | collective-permute-done | bytes 131104 | tf_op jit(solution)/shard_map/ppermute | solution.py:66
  84.1 7.4 %finish.1 = (bf16[128,512]{1,0:T(8,128)(2,1)}, f32[2,128,512]{2,1,0:T(8,128)}, bf16[2,128,512]{2,1,0:T(8,128)(2,1)}) custom-call(f32[32]{0:T(128)S(1)} %convert_power_fusion.decays, s32[32]{0:T(128)S(1)} %copy-done.1, bf16[256,512]{1,0:T(8,128)(2,1)S(1)} %add_convert_fusion.held, bf16[256,512]{1,0:T(8,128)(2,1)S(1)} %collective-permute-done.17.held_x, ...), custom_call_target="tpu_custom_call" | custom-call | flops 4831838208 | bytes 6291456 | tf_op jit(solution)/shard_map/finish/pallas_call | solution.py:170
  (41 shorter events, 7.8 us)
Async XLA Ops:
  2.6 7.0 %collective-permute-start = (bf16[4,128,1536]{2,1,0:T(8,128)(2,1)S(1)}, bf16[4,128,1536]{2,1,0:T(8,128)(2,1)S(1)}, u32[]{:S(2)}, u32[]{:S(2)}) collective-permute-start(bf16[4,128,1536]{2,1,0:T(8,128)(2,1)S(1)} %get-tuple-element.35), channel_id=1, source_target_pairs={{0,1},{1,0},{2,3},{3,2},{4,5},{5,4},{6,7},{7,6},{8,9},{9,8},{10,11... | collective-permute-start | bytes 4718600 | tf_op jit(solution)/shard_map/ppermute | solution.py:66
  5.9 8.5 %collective-permute-start.4 = (bf16[128,1536]{1,0:T(8,128)(2,1)S(1)}, bf16[128,1536]{1,0:T(8,128)(2,1)S(1)}, u32[]{:S(2)}, u32[]{:S(2)}) collective-permute-start(bf16[128,1536]{1,0:T(8,128)(2,1)S(1)} %get-tuple-element.41), channel_id=1, source_target_pairs={{0,32},{1,5},{2,34},{3,7},{4,36},{5,1},{6,38},{7,3},{16,48},{17,21... | collective-permute-start | bytes 1179656 | tf_op jit(solution)/shard_map/ppermute | solution.py:38
  7.0 11.6 %collective-permute-start.5 = (bf16[128,1536]{1,0:T(8,128)(2,1)S(1)}, bf16[128,1536]{1,0:T(8,128)(2,1)S(1)}, u32[]{:S(2)}, u32[]{:S(2)}) collective-permute-start(bf16[128,1536]{1,0:T(8,128)(2,1)S(1)} %get-tuple-element.42), channel_id=1, source_target_pairs={{0,16},{1,3},{2,18},{3,5},{4,20},{5,7},{6,22},{7,1},{16,32},{17,19... | collective-permute-start | bytes 1179656 | tf_op jit(solution)/shard_map/ppermute | solution.py:38
  7.3 12.3 %collective-permute-start.6 = (bf16[128,1536]{1,0:T(8,128)(2,1)S(1)}, bf16[128,1536]{1,0:T(8,128)(2,1)S(1)}, u32[]{:S(2)}, u32[]{:S(2)}) collective-permute-start(bf16[128,1536]{1,0:T(8,128)(2,1)S(1)} %get-tuple-element.43), channel_id=1, source_target_pairs={{0,48},{1,7},{2,50},{3,1},{4,52},{5,3},{6,54},{7,5},{16,0},{17,23}... | collective-permute-start | bytes 1179656 | tf_op jit(solution)/shard_map/ppermute | solution.py:38
  9.7 13.1 %collective-permute-start.1 = (bf16[128,1536]{1,0:T(8,128)(2,1)S(1)}, bf16[128,1536]{1,0:T(8,128)(2,1)S(1)}, u32[]{:S(2)}, u32[]{:S(2)}) collective-permute-start(bf16[128,1536]{1,0:T(8,128)(2,1)S(1)} %get-tuple-element.36), channel_id=1, source_target_pairs={{0,32},{1,5},{2,34},{3,7},{4,36},{5,1},{6,38},{7,3},{16,48},{17,21... | collective-permute-start | bytes 1179656 | tf_op jit(solution)/shard_map/ppermute | solution.py:38
  10.6 16.4 %collective-permute-start.2 = (bf16[128,1536]{1,0:T(8,128)(2,1)S(1)}, bf16[128,1536]{1,0:T(8,128)(2,1)S(1)}, u32[]{:S(2)}, u32[]{:S(2)}) collective-permute-start(bf16[128,1536]{1,0:T(8,128)(2,1)S(1)} %get-tuple-element.37), channel_id=1, source_target_pairs={{0,16},{1,3},{2,18},{3,5},{4,20},{5,7},{6,22},{7,1},{16,32},{17,19... | collective-permute-start | bytes 1179656 | tf_op jit(solution)/shard_map/ppermute | solution.py:38
  14.4 12.6 %collective-permute-start.3 = (bf16[128,1536]{1,0:T(8,128)(2,1)S(1)}, bf16[128,1536]{1,0:T(8,128)(2,1)S(1)}, u32[]{:S(2)}, u32[]{:S(2)}) collective-permute-start(bf16[128,1536]{1,0:T(8,128)(2,1)S(1)} %get-tuple-element.38), channel_id=1, source_target_pairs={{0,48},{1,7},{2,50},{3,1},{4,52},{5,3},{6,54},{7,5},{16,0},{17,23}... | collective-permute-start | bytes 1179656 | tf_op jit(solution)/shard_map/ppermute | solution.py:38
  18.6 16.3 %collective-permute-start.10 = (bf16[2,128,512]{2,1,0:T(8,128)(2,1)S(1)}, bf16[2,128,512]{2,1,0:T(8,128)(2,1)S(1)}, u32[]{:S(2)}, u32[]{:S(2)}) collective-permute-start(bf16[2,128,512]{2,1,0:T(8,128)(2,1)S(1)} %convert_element_type.31), channel_id=1, source_target_pairs={{0,1},{1,0},{2,3},{3,2},{4,5},{5,4},{6,7},{7,6},{8,9},{9,8},{10,11... | collective-permute-start | bytes 786440 | tf_op jit(solution)/shard_map/ppermute | solution.py:66
  27.8 7.1 %collective-permute-start.7 = (bf16[256,512]{1,0:T(8,128)(2,1)S(1)}, bf16[256,512]{1,0:T(8,128)(2,1)S(1)}, u32[]{:S(2)}, u32[]{:S(2)}) collective-permute-start(bf16[256,512]{1,0:T(8,128)(2,1)S(1)} %get-tuple-element.48), channel_id=1, source_target_pairs={{0,4},{1,33},{2,6},{3,35},{4,0},{5,37},{6,2},{7,39},{16,20},{17,49... | collective-permute-start | bytes 786440 | tf_op jit(solution)/shard_map/ppermute | solution.py:38
  29.2 8.5 %collective-permute-start.8 = (bf16[256,512]{1,0:T(8,128)(2,1)S(1)}, bf16[256,512]{1,0:T(8,128)(2,1)S(1)}, u32[]{:S(2)}, u32[]{:S(2)}) collective-permute-start(bf16[256,512]{1,0:T(8,128)(2,1)S(1)} %get-tuple-element.49), channel_id=1, source_target_pairs={{0,2},{1,17},{2,4},{3,19},{4,6},{5,21},{6,0},{7,23},{16,18},{17,33... | collective-permute-start | bytes 786440 | tf_op jit(solution)/shard_map/ppermute | solution.py:38
  29.6 8.1 %collective-permute-start.9 = (bf16[256,512]{1,0:T(8,128)(2,1)S(1)}, bf16[256,512]{1,0:T(8,128)(2,1)S(1)}, u32[]{:S(2)}, u32[]{:S(2)}) collective-permute-start(bf16[256,512]{1,0:T(8,128)(2,1)S(1)} %get-tuple-element.50), channel_id=1, source_target_pairs={{0,6},{1,49},{2,0},{3,51},{4,2},{5,53},{6,4},{7,55},{16,22},{17,1}... | collective-permute-start | bytes 786440 | tf_op jit(solution)/shard_map/ppermute | solution.py:38
  31.9 50.9 %copy-start.3 = (s32[32]{0:T(128)S(1)}, s32[32]{0:T(128)}, u32[]{:S(2)}) copy-start(s32[32]{0:T(128)} %param.10) | copy-start | bytes 388
  31.9 2.9 %collective-permute-start.11 = (bf16[128,512]{1,0:T(8,128)(2,1)S(1)}, bf16[128,512]{1,0:T(8,128)(2,1)S(1)}, u32[]{:S(2)}, u32[]{:S(2)}) collective-permute-start(bf16[128,512]{1,0:T(8,128)(2,1)S(1)} %get-tuple-element.59.own_right), channel_id=1, source_target_pairs={{0,1},{1,0},{2,3},{3,2},{4,5},{5,4},{6,7},{7,6},{8,9},{9,8},{10,11... | collective-permute-start | bytes 393224 | tf_op jit(solution)/shard_map/ppermute | solution.py:66
  37.8 46.3 %copy-start.1 = (s32[32]{0:T(128)S(1)}, s32[32]{0:T(128)}, u32[]{:S(2)}) copy-start(s32[32]{0:T(128)} %refresh.1) | copy-start | bytes 388
  37.8 12.3 %collective-permute-start.12 = (bf16[256,512]{1,0:T(8,128)(2,1)S(1)}, bf16[256,512]{1,0:T(8,128)(2,1)S(1)}, u32[]{:S(2)}, u32[]{:S(2)}) collective-permute-start(bf16[256,512]{1,0:T(8,128)(2,1)S(1)} %get-tuple-element.56), channel_id=1, source_target_pairs={{1,201},{65,137},{129,73},{193,9},{8,192},{72,128},{136,64},{200,0... | collective-permute-start | bytes 786440 | tf_op jit(solution)/shard_map/ppermute | solution.py:57
  44.1 6.2 %collective-permute-start.13 = (bf16[2,128,512]{2,1,0:T(8,128)(2,1)S(1)}, bf16[2,128,512]{2,1,0:T(8,128)(2,1)S(1)}, u32[]{:S(2)}, u32[]{:S(2)}) collective-permute-start(bf16[2,128,512]{2,1,0:T(8,128)(2,1)S(1)} %convert_element_type.31), channel_id=1, source_target_pairs={{0,2},{2,0},{1,3},{3,1},{4,6},{6,4},{5,7},{7,5},{8,10},{10,8},{9,1... | collective-permute-start | bytes 786440 | tf_op jit(solution)/shard_map/ppermute | solution.py:66
  50.3 2.0 %collective-permute-start.14 = (bf16[256,512]{1,0:T(8,128)(2,1)S(1)}, bf16[256,512]{1,0:T(8,128)(2,1)S(1)}, u32[]{:S(2)}, u32[]{:S(2)}) collective-permute-start(bf16[256,512]{1,0:T(8,128)(2,1)S(1)} %add_convert_fusion.2), channel_id=1, source_target_pairs={{0,64},{2,66},{64,0},{66,2},{128,192},{130,194},{192,128},{194,130... | collective-permute-start | bytes 786440 | tf_op jit(solution)/shard_map/ppermute | solution.py:52
  51.0 3.9 %collective-permute-start.15 = (bf16[128,512]{1,0:T(8,128)(2,1)S(1)}, bf16[128,512]{1,0:T(8,128)(2,1)S(1)}, u32[]{:S(2)}, u32[]{:S(2)}) collective-permute-start(bf16[128,512]{1,0:T(8,128)(2,1)S(1)} %get-tuple-element.59.own_right), channel_id=1, source_target_pairs={{0,2},{2,0},{1,3},{3,1},{4,6},{6,4},{5,7},{7,5},{8,10},{10,8},{9,1... | collective-permute-start | bytes 393224 | tf_op jit(solution)/shard_map/ppermute | solution.py:66
  54.9 0.7 collective-permute-start.16
  55.6 22.5 %collective-permute-start.17 = (bf16[256,512]{1,0:T(8,128)(2,1)S(1)}, bf16[256,512]{1,0:T(8,128)(2,1)S(1)}, u32[]{:S(2)}, u32[]{:S(2)}) collective-permute-start(bf16[256,512]{1,0:T(8,128)(2,1)S(1)} %add_convert_fusion.held), channel_id=1, source_target_pairs={{0,2},{2,0},{64,66},{66,64},{128,130},{130,128},{192,194},{194,192... | collective-permute-start | bytes 786440 | tf_op jit(solution)/shard_map/ppermute | solution.py:52
  56.3 26.5 %collective-permute-start.20 = (bf16[2,128,512]{2,1,0:T(8,128)(2,1)S(1)}, bf16[2,128,512]{2,1,0:T(8,128)(2,1)S(1)}, u32[]{:S(2)}, u32[]{:S(2)}) collective-permute-start(bf16[2,128,512]{2,1,0:T(8,128)(2,1)S(1)} %collective-permute-done.13.s1), channel_id=1, source_target_pairs={{0,1},{1,0},{2,3},{3,2},{4,5},{5,4},{6,7},{7,6},{8,9},{9,8},{10,11... | collective-permute-start | bytes 786440 | tf_op jit(solution)/shard_map/ppermute | solution.py:66
  76.6 7.5 %collective-permute-start.18 = (bf16[256,512]{1,0:T(8,128)(2,1)S(1)}, bf16[256,512]{1,0:T(8,128)(2,1)S(1)}, u32[]{:S(2)}, u32[]{:S(2)}) collective-permute-start(bf16[256,512]{1,0:T(8,128)(2,1)S(1)} %add_convert_fusion.held), channel_id=1, source_target_pairs={{0,1},{9,8},{2,3},{11,10},{4,5},{13,12},{6,7},{15,14},{16,17},{25,... | collective-permute-start | bytes 786440 | tf_op jit(solution)/shard_map/ppermute | solution.py:61
  78.1 6.0 %collective-permute-start.19 = (bf16[256,512]{1,0:T(8,128)(2,1)S(1)}, bf16[256,512]{1,0:T(8,128)(2,1)S(1)}, u32[]{:S(2)}, u32[]{:S(2)}) collective-permute-start(bf16[256,512]{1,0:T(8,128)(2,1)S(1)} %collective-permute-done.17.held_x), channel_id=1, source_target_pairs={{0,1},{9,8},{2,3},{11,10},{4,5},{13,12},{6,7},{15,14},{16,17},{25,... | collective-permute-start | bytes 786440 | tf_op jit(solution)/shard_map/ppermute | solution.py:61
  79.4 4.5 %collective-permute-start.21 = (bf16[128,512]{1,0:T(8,128)(2,1)S(1)}, bf16[128,512]{1,0:T(8,128)(2,1)S(1)}, u32[]{:S(2)}, u32[]{:S(2)}) collective-permute-start(bf16[128,512]{1,0:T(8,128)(2,1)S(1)} %collective-permute-done.15.r1), channel_id=1, source_target_pairs={{0,1},{1,0},{2,3},{3,2},{4,5},{5,4},{6,7},{7,6},{8,9},{9,8},{10,11... | collective-permute-start | bytes 393224 | tf_op jit(solution)/shard_map/ppermute | solution.py:66
  (2 other events, 25.8 us)

commit v12 on v8

--- a/solution.py
+++ b/solution.py
@@ -52,7 +52,7 @@
     first, second = [], []
     for z in range(8):
         stays = z // 4
-        across = (6 + 2 * (z % 2) - z) % 8
+        across = 7 - z
         first.append((ring_spot(z, stays), ring_spot(z, 1 - stays)))
         first.append((ring_spot(z, 1 - stays), ring_spot(across, 1 - stays)))
         second.append((ring_spot(z, 1 - stays), ring_spot(across, stays)))
@@ -91,7 +91,7 @@
     factor = 2 * (at["y"] * 4 + at["z_hi"] * 2 + at["x_hi"])
     decay = (decays[factor], decays[factor + 1])
     fresh = (refresh[factor], refresh[factor + 1])
-    side = lax.rem(at["z_lo"], 2)
+    side = lax.rem(at["z_lo"] + at["z_hi"], 2)
     for i in range(4):
         for b, pieces in enumerate((g_own, g_core)):
             top = ((at["x_lo"] ^ (i // 2)) * 2 + (at["core"] ^ b)) * ROWS + (side ^ (i % 2)) * PART
@@ -283,7 +283,7 @@
     for part in (first, second, third):
         t += part[...].astype(jnp.float32)
     total[...] = t
-    side = lax.rem(lax.axis_index("z_lo"), 2)
+    side = lax.rem(lax.axis_index("z_lo") + lax.axis_index("z_hi"), 2)
     for i in range(2):
         here = pl.ds(pl.multiple_of(i * ROWS + side * PART, PART), PART)
         there = pl.ds(pl.multiple_of(i * ROWS + (1 - side) * PART, PART), PART)
@@ -386,27 +386,26 @@
     return pl.ds(pl.multiple_of(top, ROWS), ROWS)
 
 
-def assemble_kernel(own, p0, p1, p2, p3, full, right):
+def assemble_kernel(own, own_right, s1, s2, s3, r1, r2, r3, full, right):
     at = places()
     for a in range(2):
         for b in range(2):
-            pack = (p0, p1, p2, p3)[2 * b + a]
             here = quarter_rows(at, a, b)
-            right[here, :] = pack[2]
+            right[here, :] = (own_right, r1, r2, r3)[2 * b + a][...]
             for layer in range(2):
-                full[layer, here, :] = pack[layer].astype(jnp.float32) if a + b else own[layer]
-
-
-def assemble(own, packs):
+                full[layer, here, :] = (own, s1, s2, s3)[2 * b + a][layer].astype(jnp.float32)
+
+
+def assemble(*arrays):
     return pl.pallas_call(
         assemble_kernel,
         name="assemble",
         out_shape=(jax.ShapeDtypeStruct((2, B, B), jnp.float32), jax.ShapeDtypeStruct((B, B), jnp.bfloat16)),
-        in_specs=[VMEM] * 5,
+        in_specs=[VMEM] * 8,
         out_specs=(VMEM,) * 2,
         compiler_params=pltpu.CompilerParams(vmem_limit_bytes=1 << 20),
         cost_estimate=pl.CostEstimate(flops=0, bytes_accessed=4 << 20, transcendentals=0),
-    )(own, *packs)
+    )(*arrays)
 
 
 def per_device(activations, cotangents, statistics, roots, ages, refresh):
@@ -419,17 +418,24 @@
     early = product([own_pieces[3], pieces[3]] + own_came)
     *sends, own = product(came, early)
     came = [shift(sends[i], False, ORDER[i]) for i in range(3)]
-    pack = jnp.concatenate([narrow(statistics), roots[1:]], axis=0)
-    own, pack_core = lax.optimization_barrier((own, partner(pack, "core")))
+    stats, right = narrow(statistics), roots[1]
+    own, stats_core, right_core = lax.optimization_barrier((own, partner(stats, "core"), partner(right, "core")))
     keep, send = plane_sum(came + [own])
-    keep, send, pack = lax.optimization_barrier((keep, send, pack))
     base, near, far = pair_sum(keep, swap_z(send, 1))
-    pack_x = partner(pack, "x_lo")
-    part, pack_x = lax.optimization_barrier((mirror_sum(base, *mirror(near, far)), pack_x))
+    base, near, far, stats, right = lax.optimization_barrier((base, near, far, stats, right))
+    stats_x = partner(stats, "x_lo")
+    part, stats_x, right = lax.optimization_barrier((mirror_sum(base, *mirror(near, far)), stats_x, right))
+    right_x = partner(right, "x_lo")
     part = rounded(part.astype(jnp.float32) + swap_z(part, 2).astype(jnp.float32))
-    grad = stack((part, swap_z(part, 1), partner(part, "x_lo"), diagonal(part)))
+    part, right_x = lax.optimization_barrier((part, right_x))
+    part_z, stats_far, right_far = lax.optimization_barrier(
+        (swap_z(part, 1), partner(stats_x, "core"), partner(right_x, "core"))
+    )
+    grad = stack((part, part_z, partner(part, "x_lo"), diagonal(part)))
     grads = (grad, partner(grad, "core"))
-    full, right = assemble(statistics, (pack, pack_x, pack_core, partner(pack_x, "core")))
+    full, right = assemble(
+        statistics, roots[1], stats_x, stats_core, stats_far, right_x, right_core, right_far
+    )
     return finish(decays, refresh, *grads, full, right, roots[0])
 
 

time: 76 us -> 78.2 us (1.029)
  starting transfers between devices: 31.4 us -> 35.8 us
  waiting for transfers between devices: 31.8 us -> 29.6 us
    ppermute x6 -> x9, starting transfers between devices: 4.92 us -> 8.56 us  [partner(): return lax.ppermute(x, axis, [(i, i ^ bits) for i in range(n)])]
    ppermute x9, waiting for transfers between devices: 19.4 us -> 16.6 us  [shift(): return lax.ppermute(x, ('y',) + X + ('core',), pairs)]
    ppermute x1, waiting for transfers between devices: 0.01 us -> 1.75 us  [diagonal(): return lax.ppermute(x, ('z_lo', 'x_lo'), pairs)]
    ppermute x2, waiting for transfers between devices: 3.02 us -> 1.93 us  [mirror(): return (lax.ppermute(near, axes, first), lax.ppermute(far, axes, second))]
    ppermute x1, starting transfers between devices: 1.31 us -> 2.37 us  [diagonal(): return lax.ppermute(x, ('z_lo', 'x_lo'), pairs)]
    ppermute x6 -> x9, waiting for transfers between devices: 4.15 us -> 4.1 us  [partner(): return lax.ppermute(x, axis, [(i, i ^ bits) for i in range(n)])]
  transfers between devices with their start and end apart: 21 -> 24, of which waited for: 12 -> 14; matrix products, arithmetic and copies ran while one was open for 0% -> 0% of each run, Pallas kernels for 3% -> 3%
where the time goes in v12:
time: 78.2 us; the launch traced here: 78.1 us
  starting transfers between devices  35.8 us (46%)
  waiting for transfers between devices  29.6 us (38%)
  Pallas kernels  11.7 us (15%)
  between operations  0.93 us (1%)
    ppermute x9, waiting for transfers between devices, shift(): return lax.ppermute(x, ('y',) + X + ('core',), pairs)  16.6 us
    ppermute x2, starting transfers between devices, mirror(): return (lax.ppermute(near, axes, first), lax.ppermute(far, axes, second))  10.4 us
    ppermute x9, starting transfers between devices, shift(): return lax.ppermute(x, ('y',) + X + ('core',), pairs)  9.31 us
    ppermute x9, starting transfers between devices, partner(): return lax.ppermute(x, axis, [(i, i ^ bits) for i in range(n)])  8.56 us
    pallas_call x1, Pallas kernels, finish(): pl.pallas_call(finish_kernel, name='finish', out_shape=(jax.ShapeDtypeStr...  7.34 us
    ppermute x3, waiting for transfers between devices, swap_z(): lax.ppermute(x, Z, [(ring_spot(z), ring_spot(z ^ bits)) for z in range(8)])  5.29 us
    ppermute x3, starting transfers between devices, swap_z(): lax.ppermute(x, Z, [(ring_spot(z), ring_spot(z ^ bits)) for z in range(8)])  5.09 us
    ppermute x9, waiting for transfers between devices, partner(): return lax.ppermute(x, axis, [(i, i ^ bits) for i in range(n)])  4.1 us
  transfers between devices with their start and end apart: 24, of which 14 were waited for; matrix products, arithmetic and copies ran while one was open for 0% of the time, Pallas kernels for 3%

profile of v12, /device:TPU:1, one launch (start us, length us, event | category | flops | bytes accessed | tf_op | source)
XLA Modules:
  0.0 78.1 jit_solution(16730733176375800876)
XLA Ops:
  0.6 2.0 %cut.1 = (bf16[128,1536]{1,0:T(8,128)(2,1)S(1)}, bf16[128,1536]{1,0:T(8,128)(2,1)S(1)}, bf16[128,1536]{1,0:T(8,128)(2,1)S(1)}, bf16[128,1536]{1,0:T(8,128)(2,1)S(1)}, bf16[4,128,1536]{2,1,0:T(8,128)(2,1)S(1)}) custom-call(bf16[128,8192]{1,0:T(8,128)(2,1)} %cotangents.1, bf16[128,512]{1,0:T(8,128)(2,1)} %activations.1), custom_call_target="tpu_custom_call" | custom-call | bytes 6291456 | tf_op jit(solution)/shard_map/cut/pallas_call | solution.py:224
  2.6 3.3 %collective-permute-start = (bf16[4,128,1536]{2,1,0:T(8,128)(2,1)S(1)}, bf16[4,128,1536]{2,1,0:T(8,128)(2,1)S(1)}, u32[]{:S(2)}, u32[]{:S(2)}) collective-permute-start(bf16[4,128,1536]{2,1,0:T(8,128)(2,1)S(1)} %get-tuple-element.43), channel_id=1, source_target_pairs={{0,1},{1,0},{2,3},{3,2},{4,5},{5,4},{6,7},{7,6},{8,9},{9,8},{10,11... | collective-permute-start | bytes 4718600 | tf_op jit(solution)/shard_map/ppermute | solution.py:70
  5.9 1.0 %collective-permute-start.4 = (bf16[128,1536]{1,0:T(8,128)(2,1)S(1)}, bf16[128,1536]{1,0:T(8,128)(2,1)S(1)}, u32[]{:S(2)}, u32[]{:S(2)}) collective-permute-start(bf16[128,1536]{1,0:T(8,128)(2,1)S(1)} %get-tuple-element.49), channel_id=1, source_target_pairs={{0,32},{1,5},{2,34},{3,7},{4,36},{5,1},{6,38},{7,3},{16,48},{17,21... | collective-permute-start | bytes 1179656 | tf_op jit(solution)/shard_map/ppermute | solution.py:39
  7.3 2.4 %collective-permute-start.6 = (bf16[128,1536]{1,0:T(8,128)(2,1)S(1)}, bf16[128,1536]{1,0:T(8,128)(2,1)S(1)}, u32[]{:S(2)}, u32[]{:S(2)}) collective-permute-start(bf16[128,1536]{1,0:T(8,128)(2,1)S(1)} %get-tuple-element.51), channel_id=1, source_target_pairs={{0,48},{1,7},{2,50},{3,1},{4,52},{5,3},{6,54},{7,5},{16,0},{17,23}... | collective-permute-start | bytes 1179656 | tf_op jit(solution)/shard_map/ppermute | solution.py:39
  10.6 3.8 %collective-permute-done.4.refs_2_ = bf16[128,1536]{1,0:T(8,128)(2,1)S(1)} collective-permute-done((bf16[128,1536]{1,0:T(8,128)(2,1)S(1)}, bf16[128,1536]{1,0:T(8,128)(2,1)S(1)}, u32[]{:S(2)}, u32[]{:S(2)}) %collective-permute-start.4) | collective-permute-done | bytes 393248 | tf_op jit(solution)/shard_map/ppermute | solution.py:39
  15.2 3.4 %collective-permute-done.5.refs_3_ = bf16[128,1536]{1,0:T(8,128)(2,1)S(1)} collective-permute-done((bf16[128,1536]{1,0:T(8,128)(2,1)S(1)}, bf16[128,1536]{1,0:T(8,128)(2,1)S(1)}, u32[]{:S(2)}, u32[]{:S(2)}) %collective-permute-start.5) | collective-permute-done | bytes 393248 | tf_op jit(solution)/shard_map/ppermute | solution.py:39
  19.5 1.0 %product.2 = (f32[256,512]{1,0:T(8,128)S(1)}, f32[256,512]{1,0:T(8,128)S(1)}, f32[256,512]{1,0:T(8,128)S(1)}, f32[256,512]{1,0:T(8,128)S(1)}) custom-call(bf16[128,1536]{1,0:T(8,128)(2,1)S(1)} %get-tuple-element.47.refs_0_, bf16[128,1536]{1,0:T(8,128)(2,1)S(1)} %get-tuple-element.48.refs_1_, bf16[128,1536]{1,0:T(8,128)(2,1)S(1)} %collective-permute-done.4.refs_2_, ...), custom_call_target="tpu_custom_call" | custom-call | flops 671088640 | bytes 4194304 | tf_op jit(solution)/shard_map/product/pallas_call | solution.py:270
  20.6 2.3 %collective-permute-done.1.refs_0_ = bf16[128,1536]{1,0:T(8,128)(2,1)S(1)} collective-permute-done((bf16[128,1536]{1,0:T(8,128)(2,1)S(1)}, bf16[128,1536]{1,0:T(8,128)(2,1)S(1)}, u32[]{:S(2)}, u32[]{:S(2)}) %collective-permute-start.1) | collective-permute-done | bytes 393248 | tf_op jit(solution)/shard_map/ppermute | solution.py:39
  22.9 4.1 %collective-permute-done.2.refs_1_ = bf16[128,1536]{1,0:T(8,128)(2,1)S(1)} collective-permute-done((bf16[128,1536]{1,0:T(8,128)(2,1)S(1)}, bf16[128,1536]{1,0:T(8,128)(2,1)S(1)}, u32[]{:S(2)}, u32[]{:S(2)}) %collective-permute-start.2) | collective-permute-done | bytes 393248 | tf_op jit(solution)/shard_map/ppermute | solution.py:39
  27.8 1.4 %collective-permute-start.7 = (bf16[256,512]{1,0:T(8,128)(2,1)S(1)}, bf16[256,512]{1,0:T(8,128)(2,1)S(1)}, u32[]{:S(2)}, u32[]{:S(2)}) collective-permute-start(bf16[256,512]{1,0:T(8,128)(2,1)S(1)} %get-tuple-element.56), channel_id=1, source_target_pairs={{0,4},{1,33},{2,6},{3,35},{4,0},{5,37},{6,2},{7,39},{16,20},{17,49... | collective-permute-start | bytes 786440 | tf_op jit(solution)/shard_map/ppermute | solution.py:39
  29.6 2.3 %collective-permute-start.9 = (bf16[256,512]{1,0:T(8,128)(2,1)S(1)}, bf16[256,512]{1,0:T(8,128)(2,1)S(1)}, u32[]{:S(2)}, u32[]{:S(2)}) collective-permute-start(bf16[256,512]{1,0:T(8,128)(2,1)S(1)} %get-tuple-element.58), channel_id=1, source_target_pairs={{0,6},{1,49},{2,0},{3,51},{4,2},{5,53},{6,4},{7,55},{16,22},{17,1}... | collective-permute-start | bytes 786440 | tf_op jit(solution)/shard_map/ppermute | solution.py:39
  31.9 2.0 %collective-permute-start.11 = (bf16[128,512]{1,0:T(8,128)(2,1)S(1)}, bf16[128,512]{1,0:T(8,128)(2,1)S(1)}, u32[]{:S(2)}, u32[]{:S(2)}) collective-permute-start(bf16[128,512]{1,0:T(8,128)(2,1)S(1)} %get-tuple-element.72.own_right), channel_id=1, source_target_pairs={{0,1},{1,0},{2,3},{3,2},{4,5},{5,4},{6,7},{7,6},{8,9},{9,8},{10,11... | collective-permute-start | bytes 393224 | tf_op jit(solution)/shard_map/ppermute | solution.py:70
  34.9 2.8 %collective-permute-done.8.second = bf16[256,512]{1,0:T(8,128)(2,1)S(1)} collective-permute-done((bf16[256,512]{1,0:T(8,128)(2,1)S(1)}, bf16[256,512]{1,0:T(8,128)(2,1)S(1)}, u32[]{:S(2)}, u32[]{:S(2)}) %collective-permute-start.8) | collective-permute-done | bytes 262176 | tf_op jit(solution)/shard_map/ppermute | solution.py:39
  38.4 3.4 %collective-permute-done.12.came = bf16[2,64,512]{2,1,0:T(8,128)(2,1)S(1)} collective-permute-done((bf16[2,64,512]{2,1,0:T(8,128)(2,1)S(1)}, bf16[2,64,512]{2,1,0:T(8,128)(2,1)S(1)}, u32[]{:S(2)}, u32[]{:S(2)}) %collective-permute-start.12) | collective-permute-done | bytes 131104 | tf_op jit(solution)/shard_map/ppermute | solution.py:48
  42.1 5.4 %collective-permute-start.13 = (bf16[64,512]{1,0:T(8,128)(2,1)S(1)}, bf16[64,512]{1,0:T(8,128)(2,1)S(1)}, u32[]{:S(2)}, u32[]{:S(2)}) collective-permute-start(bf16[64,512]{1,0:T(8,128)(2,1)S(1)} %get-tuple-element.67), channel_id=1, source_target_pairs={{0,1},{1,201},{64,65},{65,137},{128,129},{129,73},{192,193},{193,9... | collective-permute-start | bytes 196616 | tf_op jit(solution)/shard_map/ppermute | solution.py:60
  47.5 5.0 %collective-permute-start.14 = (bf16[64,512]{1,0:T(8,128)(2,1)S(1)}, bf16[64,512]{1,0:T(8,128)(2,1)S(1)}, u32[]{:S(2)}, u32[]{:S(2)}) collective-permute-start(bf16[64,512]{1,0:T(8,128)(2,1)S(1)} %get-tuple-element.68), channel_id=1, source_target_pairs={{1,200},{65,136},{129,72},{193,8},{8,193},{72,129},{136,65},{200,1... | collective-permute-start | bytes 196616 | tf_op jit(solution)/shard_map/ppermute | solution.py:60
  52.5 1.9 %collective-permute-done.14.far = bf16[64,512]{1,0:T(8,128)(2,1)S(1)} collective-permute-done((bf16[64,512]{1,0:T(8,128)(2,1)S(1)}, bf16[64,512]{1,0:T(8,128)(2,1)S(1)}, u32[]{:S(2)}, u32[]{:S(2)}) %collective-permute-start.14) | collective-permute-done | bytes 65568 | tf_op jit(solution)/shard_map/ppermute | solution.py:60
  54.5 4.6 %collective-permute-start.16 = (bf16[64,512]{1,0:T(8,128)(2,1)S(1)}, bf16[64,512]{1,0:T(8,128)(2,1)S(1)}, u32[]{:S(2)}, u32[]{:S(2)}) collective-permute-start(bf16[64,512]{1,0:T(8,128)(2,1)S(1)} %mirror_sum.1), channel_id=1, source_target_pairs={{0,128},{64,192},{128,0},{192,64},{8,136},{72,200},{136,8},{200,72... | collective-permute-start | bytes 196616 | tf_op jit(solution)/shard_map/ppermute | solution.py:48
  59.4 1.4 %collective-permute-done.16 = bf16[64,512]{1,0:T(8,128)(2,1)S(1)} collective-permute-done((bf16[64,512]{1,0:T(8,128)(2,1)S(1)}, bf16[64,512]{1,0:T(8,128)(2,1)S(1)}, u32[]{:S(2)}, u32[]{:S(2)}) %collective-permute-start.16) | collective-permute-done | bytes 65568 | tf_op jit(solution)/shard_map/ppermute | solution.py:48
  60.8 2.1 %collective-permute-done.17.r1 = bf16[128,512]{1,0:T(8,128)(2,1)S(1)} collective-permute-done((bf16[128,512]{1,0:T(8,128)(2,1)S(1)}, bf16[128,512]{1,0:T(8,128)(2,1)S(1)}, u32[]{:S(2)}, u32[]{:S(2)}) %collective-permute-start.17) | collective-permute-done | bytes 131104 | tf_op jit(solution)/shard_map/ppermute | solution.py:70
  63.2 2.4 %collective-permute-start.22 = (bf16[64,512]{1,0:T(8,128)(2,1)S(1)}, bf16[64,512]{1,0:T(8,128)(2,1)S(1)}, u32[]{:S(2)}, u32[]{:S(2)}) collective-permute-start(bf16[64,512]{1,0:T(8,128)(2,1)S(1)} %add_convert_fusion.refs_0_), channel_id=1, source_target_pairs={{0,66},{2,64},{64,2},{66,0},{128,194},{130,192},{192,130},{194,128... | collective-permute-start | bytes 196616 | tf_op jit(solution)/shard_map/ppermute | solution.py:65
  66.0 1.8 %collective-permute-done.22.refs_3_ = bf16[64,512]{1,0:T(8,128)(2,1)S(1)} collective-permute-done((bf16[64,512]{1,0:T(8,128)(2,1)S(1)}, bf16[64,512]{1,0:T(8,128)(2,1)S(1)}, u32[]{:S(2)}, u32[]{:S(2)}) %collective-permute-start.22) | collective-permute-done | bytes 65568 | tf_op jit(solution)/shard_map/ppermute | solution.py:65
  67.8 1.6 %collective-permute-start.23 = (bf16[4,64,512]{2,1,0:T(8,128)(2,1)S(1)}, bf16[4,64,512]{2,1,0:T(8,128)(2,1)S(1)}, u32[]{:S(2)}, u32[]{:S(2)}) collective-permute-start(bf16[4,64,512]{2,1,0:T(8,128)(2,1)S(1)} %stack.1.g_own), channel_id=1, source_target_pairs={{0,1},{1,0},{2,3},{3,2},{4,5},{5,4},{6,7},{7,6},{8,9},{9,8},{10,11... | collective-permute-start | bytes 786440 | tf_op jit(solution)/shard_map/ppermute | solution.py:70
  70.6 7.3 %finish.1 = (bf16[128,512]{1,0:T(8,128)(2,1)}, f32[2,128,512]{2,1,0:T(8,128)}, bf16[2,128,512]{2,1,0:T(8,128)(2,1)}) custom-call(f32[32]{0:T(128)S(1)} %convert_power_fusion.decays, s32[32]{0:T(128)S(1)} %copy-done.1, bf16[4,64,512]{2,1,0:T(8,128)(2,1)S(1)} %stack.1.g_own, bf16[4,64,512]{2,1,0:T(8,128)(2,1)S(1)} %collective-permute-done.23.g_core, ...), custom_call_target="tpu_custom_call" | custom-call | flops 4831838208 | bytes 6291456 | tf_op jit(solution)/shard_map/finish/pallas_call | solution.py:164
  (46 shorter events, 8.4 us)
Async XLA Ops:
  2.6 7.0 %collective-permute-start = (bf16[4,128,1536]{2,1,0:T(8,128)(2,1)S(1)}, bf16[4,128,1536]{2,1,0:T(8,128)(2,1)S(1)}, u32[]{:S(2)}, u32[]{:S(2)}) collective-permute-start(bf16[4,128,1536]{2,1,0:T(8,128)(2,1)S(1)} %get-tuple-element.43), channel_id=1, source_target_pairs={{0,1},{1,0},{2,3},{3,2},{4,5},{5,4},{6,7},{7,6},{8,9},{9,8},{10,11... | collective-permute-start | bytes 4718600 | tf_op jit(solution)/shard_map/ppermute | solution.py:70
  5.9 8.5 %collective-permute-start.4 = (bf16[128,1536]{1,0:T(8,128)(2,1)S(1)}, bf16[128,1536]{1,0:T(8,128)(2,1)S(1)}, u32[]{:S(2)}, u32[]{:S(2)}) collective-permute-start(bf16[128,1536]{1,0:T(8,128)(2,1)S(1)} %get-tuple-element.49), channel_id=1, source_target_pairs={{0,32},{1,5},{2,34},{3,7},{4,36},{5,1},{6,38},{7,3},{16,48},{17,21... | collective-permute-start | bytes 1179656 | tf_op jit(solution)/shard_map/ppermute | solution.py:39
  7.0 11.6 %collective-permute-start.5 = (bf16[128,1536]{1,0:T(8,128)(2,1)S(1)}, bf16[128,1536]{1,0:T(8,128)(2,1)S(1)}, u32[]{:S(2)}, u32[]{:S(2)}) collective-permute-start(bf16[128,1536]{1,0:T(8,128)(2,1)S(1)} %get-tuple-element.50), channel_id=1, source_target_pairs={{0,16},{1,3},{2,18},{3,5},{4,20},{5,7},{6,22},{7,1},{16,32},{17,19... | collective-permute-start | bytes 1179656 | tf_op jit(solution)/shard_map/ppermute | solution.py:39
  7.3 12.3 %collective-permute-start.6 = (bf16[128,1536]{1,0:T(8,128)(2,1)S(1)}, bf16[128,1536]{1,0:T(8,128)(2,1)S(1)}, u32[]{:S(2)}, u32[]{:S(2)}) collective-permute-start(bf16[128,1536]{1,0:T(8,128)(2,1)S(1)} %get-tuple-element.51), channel_id=1, source_target_pairs={{0,48},{1,7},{2,50},{3,1},{4,52},{5,3},{6,54},{7,5},{16,0},{17,23}... | collective-permute-start | bytes 1179656 | tf_op jit(solution)/shard_map/ppermute | solution.py:39
  9.7 13.1 %collective-permute-start.1 = (bf16[128,1536]{1,0:T(8,128)(2,1)S(1)}, bf16[128,1536]{1,0:T(8,128)(2,1)S(1)}, u32[]{:S(2)}, u32[]{:S(2)}) collective-permute-start(bf16[128,1536]{1,0:T(8,128)(2,1)S(1)} %get-tuple-element.44), channel_id=1, source_target_pairs={{0,32},{1,5},{2,34},{3,7},{4,36},{5,1},{6,38},{7,3},{16,48},{17,21... | collective-permute-start | bytes 1179656 | tf_op jit(solution)/shard_map/ppermute | solution.py:39
  10.6 16.4 %collective-permute-start.2 = (bf16[128,1536]{1,0:T(8,128)(2,1)S(1)}, bf16[128,1536]{1,0:T(8,128)(2,1)S(1)}, u32[]{:S(2)}, u32[]{:S(2)}) collective-permute-start(bf16[128,1536]{1,0:T(8,128)(2,1)S(1)} %get-tuple-element.45), channel_id=1, source_target_pairs={{0,16},{1,3},{2,18},{3,5},{4,20},{5,7},{6,22},{7,1},{16,32},{17,19... | collective-permute-start | bytes 1179656 | tf_op jit(solution)/shard_map/ppermute | solution.py:39
  14.4 12.6 %collective-permute-start.3 = (bf16[128,1536]{1,0:T(8,128)(2,1)S(1)}, bf16[128,1536]{1,0:T(8,128)(2,1)S(1)}, u32[]{:S(2)}, u32[]{:S(2)}) collective-permute-start(bf16[128,1536]{1,0:T(8,128)(2,1)S(1)} %get-tuple-element.46), channel_id=1, source_target_pairs={{0,48},{1,7},{2,50},{3,1},{4,52},{5,3},{6,54},{7,5},{16,0},{17,23}... | collective-permute-start | bytes 1179656 | tf_op jit(solution)/shard_map/ppermute | solution.py:39
  18.6 16.3 %collective-permute-start.10 = (bf16[2,128,512]{2,1,0:T(8,128)(2,1)S(1)}, bf16[2,128,512]{2,1,0:T(8,128)(2,1)S(1)}, u32[]{:S(2)}, u32[]{:S(2)}) collective-permute-start(bf16[2,128,512]{2,1,0:T(8,128)(2,1)S(1)} %convert_element_type.16), channel_id=1, source_target_pairs={{0,1},{1,0},{2,3},{3,2},{4,5},{5,4},{6,7},{7,6},{8,9},{9,8},{10,11... | collective-permute-start | bytes 786440 | tf_op jit(solution)/shard_map/ppermute | solution.py:70
  27.8 7.1 %collective-permute-start.7 = (bf16[256,512]{1,0:T(8,128)(2,1)S(1)}, bf16[256,512]{1,0:T(8,128)(2,1)S(1)}, u32[]{:S(2)}, u32[]{:S(2)}) collective-permute-start(bf16[256,512]{1,0:T(8,128)(2,1)S(1)} %get-tuple-element.56), channel_id=1, source_target_pairs={{0,4},{1,33},{2,6},{3,35},{4,0},{5,37},{6,2},{7,39},{16,20},{17,49... | collective-permute-start | bytes 786440 | tf_op jit(solution)/shard_map/ppermute | solution.py:39
  29.2 8.5 %collective-permute-start.8 = (bf16[256,512]{1,0:T(8,128)(2,1)S(1)}, bf16[256,512]{1,0:T(8,128)(2,1)S(1)}, u32[]{:S(2)}, u32[]{:S(2)}) collective-permute-start(bf16[256,512]{1,0:T(8,128)(2,1)S(1)} %get-tuple-element.57), channel_id=1, source_target_pairs={{0,2},{1,17},{2,4},{3,19},{4,6},{5,21},{6,0},{7,23},{16,18},{17,33... | collective-permute-start | bytes 786440 | tf_op jit(solution)/shard_map/ppermute | solution.py:39
  29.6 8.1 %collective-permute-start.9 = (bf16[256,512]{1,0:T(8,128)(2,1)S(1)}, bf16[256,512]{1,0:T(8,128)(2,1)S(1)}, u32[]{:S(2)}, u32[]{:S(2)}) collective-permute-start(bf16[256,512]{1,0:T(8,128)(2,1)S(1)} %get-tuple-element.58), channel_id=1, source_target_pairs={{0,6},{1,49},{2,0},{3,51},{4,2},{5,53},{6,4},{7,55},{16,22},{17,1}... | collective-permute-start | bytes 786440 | tf_op jit(solution)/shard_map/ppermute | solution.py:39
  31.9 2.9 %collective-permute-start.11 = (bf16[128,512]{1,0:T(8,128)(2,1)S(1)}, bf16[128,512]{1,0:T(8,128)(2,1)S(1)}, u32[]{:S(2)}, u32[]{:S(2)}) collective-permute-start(bf16[128,512]{1,0:T(8,128)(2,1)S(1)} %get-tuple-element.72.own_right), channel_id=1, source_target_pairs={{0,1},{1,0},{2,3},{3,2},{4,5},{5,4},{6,7},{7,6},{8,9},{9,8},{10,11... | collective-permute-start | bytes 393224 | tf_op jit(solution)/shard_map/ppermute | solution.py:70
  37.9 3.9 %collective-permute-start.12 = (bf16[2,64,512]{2,1,0:T(8,128)(2,1)S(1)}, bf16[2,64,512]{2,1,0:T(8,128)(2,1)S(1)}, u32[]{:S(2)}, u32[]{:S(2)}) collective-permute-start(bf16[2,64,512]{2,1,0:T(8,128)(2,1)S(1)} %get-tuple-element.62), channel_id=1, source_target_pairs={{0,64},{64,0},{128,192},{192,128},{8,72},{72,8},{136,200},{200,136... | collective-permute-start | bytes 393224 | tf_op jit(solution)/shard_map/ppermute | solution.py:48
  41.9 12.6 %collective-permute-start.15 = (bf16[2,128,512]{2,1,0:T(8,128)(2,1)S(1)}, bf16[2,128,512]{2,1,0:T(8,128)(2,1)S(1)}, u32[]{:S(2)}, u32[]{:S(2)}) collective-permute-start(bf16[2,128,512]{2,1,0:T(8,128)(2,1)S(1)} %convert_element_type.16), channel_id=1, source_target_pairs={{0,2},{2,0},{1,3},{3,1},{4,6},{6,4},{5,7},{7,5},{8,10},{10,8},{9,1... | collective-permute-start | bytes 786440 | tf_op jit(solution)/shard_map/ppermute | solution.py:70
  42.1 10.4 %collective-permute-start.13 = (bf16[64,512]{1,0:T(8,128)(2,1)S(1)}, bf16[64,512]{1,0:T(8,128)(2,1)S(1)}, u32[]{:S(2)}, u32[]{:S(2)}) collective-permute-start(bf16[64,512]{1,0:T(8,128)(2,1)S(1)} %get-tuple-element.67), channel_id=1, source_target_pairs={{0,1},{1,201},{64,65},{65,137},{128,129},{129,73},{192,193},{193,9... | collective-permute-start | bytes 196616 | tf_op jit(solution)/shard_map/ppermute | solution.py:60
  47.5 7.0 %collective-permute-start.14 = (bf16[64,512]{1,0:T(8,128)(2,1)S(1)}, bf16[64,512]{1,0:T(8,128)(2,1)S(1)}, u32[]{:S(2)}, u32[]{:S(2)}) collective-permute-start(bf16[64,512]{1,0:T(8,128)(2,1)S(1)} %get-tuple-element.68), channel_id=1, source_target_pairs={{1,200},{65,136},{129,72},{193,8},{8,193},{72,129},{136,65},{200,1... | collective-permute-start | bytes 196616 | tf_op jit(solution)/shard_map/ppermute | solution.py:60
  54.5 6.3 %collective-permute-start.16 = (bf16[64,512]{1,0:T(8,128)(2,1)S(1)}, bf16[64,512]{1,0:T(8,128)(2,1)S(1)}, u32[]{:S(2)}, u32[]{:S(2)}) collective-permute-start(bf16[64,512]{1,0:T(8,128)(2,1)S(1)} %mirror_sum.1), channel_id=1, source_target_pairs={{0,128},{64,192},{128,0},{192,64},{8,136},{72,200},{136,8},{200,72... | collective-permute-start | bytes 196616 | tf_op jit(solution)/shard_map/ppermute | solution.py:48
  59.1 3.8 %collective-permute-start.17 = (bf16[128,512]{1,0:T(8,128)(2,1)S(1)}, bf16[128,512]{1,0:T(8,128)(2,1)S(1)}, u32[]{:S(2)}, u32[]{:S(2)}) collective-permute-start(bf16[128,512]{1,0:T(8,128)(2,1)S(1)} %get-tuple-element.72.own_right), channel_id=1, source_target_pairs={{0,2},{2,0},{1,3},{3,1},{4,6},{6,4},{5,7},{7,5},{8,10},{10,8},{9,1... | collective-permute-start | bytes 393224 | tf_op jit(solution)/shard_map/ppermute | solution.py:70
  59.4 6.7 %collective-permute-start.19 = (bf16[2,128,512]{2,1,0:T(8,128)(2,1)S(1)}, bf16[2,128,512]{2,1,0:T(8,128)(2,1)S(1)}, u32[]{:S(2)}, u32[]{:S(2)}) collective-permute-start(bf16[2,128,512]{2,1,0:T(8,128)(2,1)S(1)} %collective-permute-done.15.s1), channel_id=1, source_target_pairs={{0,1},{1,0},{2,3},{3,2},{4,5},{5,4},{6,7},{7,6},{8,9},{9,8},{10,11... | collective-permute-start | bytes 786440 | tf_op jit(solution)/shard_map/ppermute | solution.py:70
  62.9 3.1 %collective-permute-start.20 = (bf16[128,512]{1,0:T(8,128)(2,1)S(1)}, bf16[128,512]{1,0:T(8,128)(2,1)S(1)}, u32[]{:S(2)}, u32[]{:S(2)}) collective-permute-start(bf16[128,512]{1,0:T(8,128)(2,1)S(1)} %collective-permute-done.17.r1), channel_id=1, source_target_pairs={{0,1},{1,0},{2,3},{3,2},{4,5},{5,4},{6,7},{7,6},{8,9},{9,8},{10,11... | collective-permute-start | bytes 393224 | tf_op jit(solution)/shard_map/ppermute | solution.py:70
  62.9 3.1 %collective-permute-start.18 = (bf16[64,512]{1,0:T(8,128)(2,1)S(1)}, bf16[64,512]{1,0:T(8,128)(2,1)S(1)}, u32[]{:S(2)}, u32[]{:S(2)}) collective-permute-start(bf16[64,512]{1,0:T(8,128)(2,1)S(1)} %add_convert_fusion.refs_0_), channel_id=1, source_target_pairs={{0,64},{64,0},{128,192},{192,128},{8,72},{72,8},{136,200},{200,136... | collective-permute-start | bytes 196616 | tf_op jit(solution)/shard_map/ppermute | solution.py:48
  62.9 3.1 %collective-permute-start.21 = (bf16[64,512]{1,0:T(8,128)(2,1)S(1)}, bf16[64,512]{1,0:T(8,128)(2,1)S(1)}, u32[]{:S(2)}, u32[]{:S(2)}) collective-permute-start(bf16[64,512]{1,0:T(8,128)(2,1)S(1)} %add_convert_fusion.refs_0_), channel_id=1, source_target_pairs={{0,2},{2,0},{1,3},{3,1},{4,6},{6,4},{5,7},{7,5},{8,10},{10,8},{9,1... | collective-permute-start | bytes 196616 | tf_op jit(solution)/shard_map/ppermute | solution.py:70
  63.2 4.6 %collective-permute-start.22 = (bf16[64,512]{1,0:T(8,128)(2,1)S(1)}, bf16[64,512]{1,0:T(8,128)(2,1)S(1)}, u32[]{:S(2)}, u32[]{:S(2)}) collective-permute-start(bf16[64,512]{1,0:T(8,128)(2,1)S(1)} %add_convert_fusion.refs_0_), channel_id=1, source_target_pairs={{0,66},{2,64},{64,2},{66,0},{128,194},{130,192},{192,130},{194,128... | collective-permute-start | bytes 196616 | tf_op jit(solution)/shard_map/ppermute | solution.py:65
  67.8 2.7 %collective-permute-start.23 = (bf16[4,64,512]{2,1,0:T(8,128)(2,1)S(1)}, bf16[4,64,512]{2,1,0:T(8,128)(2,1)S(1)}, u32[]{:S(2)}, u32[]{:S(2)}) collective-permute-start(bf16[4,64,512]{2,1,0:T(8,128)(2,1)S(1)} %stack.1.g_own), channel_id=1, source_target_pairs={{0,1},{1,0},{2,3},{3,2},{4,5},{5,4},{6,7},{7,6},{8,9},{9,8},{10,11... | collective-permute-start | bytes 786440 | tf_op jit(solution)/shard_map/ppermute | solution.py:70
  (4 other events, 103.1 us)
